TPU v7x, 32 devices: a whole 2x2x4 slice. The times are simulated.
32 devices in a mesh: ctx: 8 (over z, y), wt: 4 (over x, core).
Axes of the slice: x: 2, y: 2, z: 4, core: 2. Of those that a mesh axis runs over, the one named last changes fastest.
Arguments:
- hidden_in: bfloat16 [2, 4096, 1792], P(None, 'ctx', 'wt'), may hold values from -6 to 6
- lengths: int32 [2], replicated, may hold values from 1024 to 4096, as said below
- gain_attn: bfloat16 [1792], P('wt'), may hold values from 0.5 to 1.5
- gain_ffn: bfloat16 [1792], P('wt'), may hold values from 0.5 to 1.5
- w_query: bfloat16 [1792, 256], P('ctx', 'wt'), may hold values from -0.125 to 0.125
- w_key: bfloat16 [1792, 256], P('ctx', 'wt'), may hold values from -0.125 to 0.125
- w_value: bfloat16 [1792, 1792], P('ctx', 'wt'), may hold values from -0.125 to 0.125
- w_output: bfloat16 [1792, 1792], P('wt', 'ctx'), may hold values from -6 to 6
- w_gate: bfloat16 [1792, 4864], P('ctx', 'wt'), may hold values from -0.125 to 0.125
- w_up: bfloat16 [1792, 4864], P('ctx', 'wt'), may hold values from -0.125 to 0.125
- w_down: bfloat16 [4864, 1792], P('wt', 'ctx'), may hold values from -0.078125 to 0.078125
- cotangent: bfloat16 [2, 4096, 1792], P(None, 'ctx', 'wt'), may hold values from -6 to 6
Outputs:
- layer_out: bfloat16 [2, 4096, 1792], P(None, 'ctx', 'wt')
- grad_input: float32 [2, 4096, 1792], P(None, 'ctx', 'wt')
- grad_gain_attn: float32 [1792], P('wt')
- grad_gain_ffn: float32 [1792], P('wt')
- grad_query: float32 [1792, 256], P('ctx', 'wt')
- grad_key: float32 [1792, 256], P('ctx', 'wt')
- grad_value: float32 [1792, 1792], P('ctx', 'wt')
- grad_output: float32 [1792, 1792], P('wt', 'ctx')
- grad_gate: float32 [1792, 4864], P('ctx', 'wt')
- grad_up: float32 [1792, 4864], P('ctx', 'wt')
- grad_down: float32 [4864, 1792], P('wt', 'ctx')
Inputs may be any that keep to these rules, and one draw needn't show every extreme that they name: `lengths`: one sequence, drawn from the seed, has all 4096 positions valid and another a quarter of 4096.
All inputs are finite; a program needn't handle non-finite values.
Results may differ from a plain program's by a relative error of at most 0.024.
Values may be sent and summed in bfloat16 or wider, within the bound.
No kernel may reach another device: no remote copies, remote signals or barrier semaphores. Data moves between devices by JAX's collectives and lax.ppermute only.
A program may use at most 320 MiB of HBM per device.

v0:
```python
from functools import partial

import jax
import jax.numpy as jnp
from jax import lax
from jax.sharding import PartitionSpec as P

D = 1792
FEAT = 16
HEAD_DIM = 112


exact_mode = lax.Precision.HIGHEST
epsilon = 1e-05


def carried_in(value, axis, combine, identity):
    length, index = (lax.axis_size(axis), lax.axis_index(axis))
    everything = jax.tree.map(
        lambda part, kind: lax.all_gather(part.astype(kind), axis),
        value,
        (jnp.bfloat16, jnp.bfloat16),
    )
    start = jax.tree.map(
        lambda part, zero: jnp.broadcast_to(jnp.asarray(zero, part.dtype), part.shape),
        value,
        identity,
    )

    def carried_turn(k, before):
        reached = k < index
        new = combine(
            before, jax.tree.map(lambda part, own: part[k].astype(own.dtype), everything, value)
        )
        return jax.tree.map(lambda a, b: jnp.where(reached, a, b), new, before)

    return lax.fori_loop(0, length, carried_turn, start)


def entering(value, axis, combine, identity):
    length, index = (lax.axis_size(axis), lax.axis_index(axis))
    everything = jax.tree.map(
        lambda part, kind: lax.all_gather(part.astype(kind), axis),
        value,
        jax.tree.map(lambda a: jnp.bfloat16 if a.dtype == jnp.float32 else a.dtype, value),
    )
    start = jax.tree.map(
        lambda part, zero: jnp.broadcast_to(jnp.asarray(zero, part.dtype), part.shape),
        value,
        identity,
    )

    def entering_turn(k, before):
        at = length - 1 - k
        reached = at > index
        new = combine(
            before, jax.tree.map(lambda part, own: part[at].astype(own.dtype), everything, value)
        )
        return jax.tree.map(lambda a, b: jnp.where(reached, a, b), new, before)

    return lax.fori_loop(0, length, entering_turn, start)


def features(vectors):
    feat_dim = vectors.shape[-1]
    outer_prod = (vectors[..., :, None] * vectors[..., None, :]).reshape(
        vectors.shape[:-1] + (feat_dim * feat_dim,)
    )
    ones_col = jnp.ones(vectors.shape[:-1] + (1,), jnp.float32)
    return jnp.concatenate(
        [ones_col, vectors * feat_dim ** (-0.25), outer_prod * (0.5 / feat_dim) ** 0.5], -1
    )


def attend(query, key_in, value_in, state_sum, norm_sum, valid_mask):
    feat_dim = query.shape[-1]
    size = query.shape[1]
    mapped = features(query)
    numer = jnp.einsum("slhp,sphe->slhe", mapped, state_sum, precision=exact_mode)
    denom = jnp.einsum("slhp,sph->slh", mapped, norm_sum, precision=exact_mode)
    scores = jnp.einsum("sbhf,schf->shbc", query, key_in, precision=exact_mode) * feat_dim ** (-0.5)
    causal = (jnp.arange(size)[:, None] >= jnp.arange(size)[None, :]).astype(jnp.float32)
    weights = (1.0 + scores + 0.5 * scores * scores) * causal * valid_mask[:, None, None, :]
    numer = numer + jnp.einsum("shbc,sche->sbhe", weights, value_in, precision=exact_mode)
    denom = denom + jnp.einsum("shbc->sbh", weights)
    return numer / denom[..., None]


def block_state(key_in, value_in, valid_mask):
    mapped = features(key_in) * valid_mask[:, :, None, None]
    state_sum = jnp.einsum("slhp,slhe->sphe", mapped, value_in, precision=exact_mode)
    norm_sum = jnp.einsum("slhp->sph", mapped)
    return (state_sum, norm_sum)


def add_pair(earlier, later_part):
    return (earlier[0] + later_part[0], earlier[1] + later_part[1])


def to_full(local_part):
    return lax.all_gather(local_part, "wt", axis=2, tiled=True)


def narrow(partial_sum):
    return lax.psum_scatter(
        partial_sum.astype(jnp.bfloat16), "wt", scatter_dimension=2, tiled=True
    ).astype(jnp.float32)


def row_total(local_sum):
    return lax.psum(local_sum, "wt")


def fetch_rows(w_query, w_key, w_value, w_gate, w_up):
    return (
        lax.all_gather(w_query, "ctx", axis=0, tiled=True),
        lax.all_gather(w_key, "ctx", axis=0, tiled=True),
        lax.all_gather(w_value, "ctx", axis=0, tiled=True),
        lax.all_gather(w_gate, "ctx", axis=0, tiled=True),
        lax.all_gather(w_up, "ctx", axis=0, tiled=True),
    )


def fetch_cols(w_output, w_down):
    return (
        lax.all_gather(w_output, "ctx", axis=1, tiled=True),
        lax.all_gather(w_down, "ctx", axis=1, tiled=True),
    )


def matmul_bf(left, right):
    return jnp.dot(left, right, preferred_element_type=jnp.float32)


def right_trans(left, right):
    return jnp.einsum("rk,dk->rd", left, right, preferred_element_type=jnp.float32)


def left_trans(left, right):
    return jnp.einsum("rk,rd->kd", left, right, preferred_element_type=jnp.float32)


def body(
    hidden_in,
    lengths,
    gain_attn,
    gain_ffn,
    w_query,
    w_key,
    w_value,
    w_output,
    w_gate,
    w_up,
    w_down,
    cotangent,
):
    seq_count, local_len, width_part = hidden_in.shape
    row_count = seq_count * local_len
    heads_here = w_value.shape[1] // HEAD_DIM
    my_index = lax.axis_index("ctx")
    position = my_index * local_len + jnp.arange(local_len, dtype=jnp.int32)
    valid_mask = (position[None, :] < lengths[:, None]).astype(jnp.float32)
    x_float = hidden_in.astype(jnp.float32)
    gain_one = gain_attn.astype(jnp.float32)
    gain_two = gain_ffn.astype(jnp.float32)
    inv_one = lax.rsqrt(row_total(jnp.sum(x_float * x_float, -1)) / D + epsilon)
    normed_one = to_full((x_float * inv_one[..., None] * gain_one).astype(jnp.bfloat16)).reshape(
        row_count, D
    )
    query_full, key_full, value_full, gate_full, up_full = fetch_rows(
        w_query, w_key, w_value, w_gate, w_up
    )
    output_full, down_full = fetch_cols(w_output, w_down)
    query = matmul_bf(normed_one, query_full).astype(jnp.bfloat16)
    key_in = matmul_bf(normed_one, key_full).astype(jnp.bfloat16)
    value_in = matmul_bf(normed_one, value_full).astype(jnp.bfloat16)
    query_f = query.astype(jnp.float32).reshape(seq_count, local_len, heads_here, FEAT)
    key_f = key_in.astype(jnp.float32).reshape(seq_count, local_len, heads_here, FEAT)
    value_f = value_in.astype(jnp.float32).reshape(seq_count, local_len, heads_here, HEAD_DIM)
    own_state, own_norm = block_state(key_f, value_f, valid_mask)
    prior_sums = carried_in(
        (own_state, own_norm),
        "ctx",
        add_pair,
        (jnp.zeros_like(own_state), jnp.zeros_like(own_norm)),
    )
    attn, attend_pull = jax.vjp(
        partial(attend, valid_mask=valid_mask),
        query_f,
        key_f,
        value_f,
        prior_sums[0],
        prior_sums[1],
    )
    mixed_heads = attn.reshape(row_count, heads_here * HEAD_DIM).astype(jnp.bfloat16)
    attn_branch = lax.psum_scatter(
        matmul_bf(mixed_heads, output_full).reshape(seq_count, local_len, D).astype(jnp.bfloat16),
        "wt",
        scatter_dimension=2,
        tiled=True,
    ).astype(jnp.float32)
    residual = x_float + attn_branch
    inv_two = lax.rsqrt(row_total(jnp.sum(residual * residual, -1)) / D + epsilon)
    normed_two = to_full((residual * inv_two[..., None] * gain_two).astype(jnp.bfloat16)).reshape(
        row_count, D
    )
    gate_pre = matmul_bf(normed_two, gate_full)
    up_pre = matmul_bf(normed_two, up_full)
    sigmoid_gate = jax.nn.sigmoid(gate_pre)
    silu_gate = gate_pre * sigmoid_gate
    activation = (silu_gate * up_pre).astype(jnp.bfloat16)
    ffn_out = narrow(matmul_bf(activation, down_full).reshape(seq_count, local_len, D))
    layer_out = (residual + ffn_out).astype(jnp.bfloat16)
    grad_out_f = cotangent.astype(jnp.float32) * valid_mask[..., None]
    query_full, key_full, value_full, gate_full, up_full = fetch_rows(
        w_query, w_key, w_value, w_gate, w_up
    )
    output_full, down_full = fetch_cols(w_output, w_down)
    grad_out_bf = to_full(grad_out_f.astype(jnp.bfloat16)).reshape(row_count, D)
    grad_down = left_trans(activation, grad_out_bf)
    grad_act = right_trans(grad_out_bf, down_full)
    grad_gate_bf = (
        grad_act * up_pre * sigmoid_gate * (1.0 + gate_pre * (1.0 - sigmoid_gate))
    ).astype(jnp.bfloat16)
    grad_up_bf = (grad_act * silu_gate).astype(jnp.bfloat16)
    grad_gate = left_trans(normed_two, grad_gate_bf)
    grad_up = left_trans(normed_two, grad_up_bf)
    norm_two_part = right_trans(grad_gate_bf, gate_full) + right_trans(grad_up_bf, up_full)
    grad_norm_two = narrow(norm_two_part.reshape(seq_count, local_len, D))
    gain_two_grad = jnp.sum(residual * inv_two[..., None] * grad_norm_two, axis=(0, 1))
    inner_two = row_total(jnp.sum(residual * gain_two * grad_norm_two, -1))
    grad_resid = (
        grad_out_f
        + inv_two[..., None] * gain_two * grad_norm_two
        - residual * (inv_two * inv_two * inv_two * inner_two / D)[..., None]
    )
    grad_resid_bf = to_full(grad_resid.astype(jnp.bfloat16)).reshape(row_count, D)
    grad_output = left_trans(mixed_heads, grad_resid_bf)
    grad_attn_bf = right_trans(grad_resid_bf, output_full).astype(jnp.bfloat16)
    grad_attn = (
        lax.optimization_barrier(grad_attn_bf)
        .astype(jnp.float32)
        .reshape(seq_count, local_len, heads_here, HEAD_DIM)
    )
    grad_query_f, grad_key_f, grad_value_f, grad_state, grad_norm = attend_pull(grad_attn)
    later_sums = entering(
        (grad_state, grad_norm),
        "ctx",
        add_pair,
        (jnp.zeros_like(grad_state), jnp.zeros_like(grad_norm)),
    )
    _, state_pull = jax.vjp(partial(block_state, valid_mask=valid_mask), key_f, value_f)
    extra_key, extra_value = state_pull(later_sums)
    query_bf = grad_query_f.reshape(row_count, -1).astype(jnp.bfloat16)
    key_bf = (grad_key_f + extra_key).reshape(row_count, -1).astype(jnp.bfloat16)
    value_bf = (grad_value_f + extra_value).reshape(row_count, -1).astype(jnp.bfloat16)
    grad_query = left_trans(normed_one, query_bf)
    grad_key = left_trans(normed_one, key_bf)
    grad_value = left_trans(normed_one, value_bf)
    norm_one_part = (
        right_trans(query_bf, query_full)
        + right_trans(key_bf, key_full)
        + right_trans(value_bf, value_full)
    )
    grad_norm_one = narrow(norm_one_part.reshape(seq_count, local_len, D))
    gain_one_grad = jnp.sum(x_float * inv_one[..., None] * grad_norm_one, axis=(0, 1))
    inner_one = row_total(jnp.sum(x_float * gain_one * grad_norm_one, -1))
    grad_input = (
        grad_resid
        + inv_one[..., None] * gain_one * grad_norm_one
        - x_float * (inv_one * inv_one * inv_one * inner_one / D)[..., None]
    )
    row_grads = (
        lax.psum_scatter(
            grad_query.astype(jnp.bfloat16), "ctx", scatter_dimension=0, tiled=True
        ).astype(jnp.float32),
        lax.psum_scatter(
            grad_key.astype(jnp.bfloat16), "ctx", scatter_dimension=0, tiled=True
        ).astype(jnp.float32),
        lax.psum_scatter(
            grad_value.astype(jnp.bfloat16), "ctx", scatter_dimension=0, tiled=True
        ).astype(jnp.float32),
        lax.psum_scatter(
            grad_gate.astype(jnp.bfloat16), "ctx", scatter_dimension=0, tiled=True
        ).astype(jnp.float32),
        lax.psum_scatter(
            grad_up.astype(jnp.bfloat16), "ctx", scatter_dimension=0, tiled=True
        ).astype(jnp.float32),
    )
    col_grads = (
        lax.psum_scatter(
            grad_output.astype(jnp.bfloat16), "ctx", scatter_dimension=1, tiled=True
        ).astype(jnp.float32),
        lax.psum_scatter(
            grad_down.astype(jnp.bfloat16), "ctx", scatter_dimension=1, tiled=True
        ).astype(jnp.float32),
    )
    gain_grads = lax.psum((gain_one_grad, gain_two_grad), "ctx")
    return (
        layer_out,
        grad_input,
        gain_grads[0],
        gain_grads[1],
        row_grads[0],
        row_grads[1],
        row_grads[2],
        col_grads[0],
        row_grads[3],
        row_grads[4],
        col_grads[1],
    )


def solution(mesh):
    in_specs = (
        P(None, "ctx", "wt"),
        P(),
        P("wt"),
        P("wt"),
        P("ctx", "wt"),
        P("ctx", "wt"),
        P("ctx", "wt"),
        P("wt", "ctx"),
        P("ctx", "wt"),
        P("ctx", "wt"),
        P("wt", "ctx"),
        P(None, "ctx", "wt"),
    )
    out_specs = (
        P(None, "ctx", "wt"),
        P(None, "ctx", "wt"),
        P("wt"),
        P("wt"),
        P("ctx", "wt"),
        P("ctx", "wt"),
        P("ctx", "wt"),
        P("wt", "ctx"),
        P("ctx", "wt"),
        P("ctx", "wt"),
        P("wt", "ctx"),
    )
    return jax.shard_map(body, mesh=mesh, in_specs=in_specs, out_specs=out_specs, check_vma=False)
```

profile of v0, /device:TPU:0, one launch (start us, length us, event | category | flops | bytes accessed | tf_op | source)
XLA Modules:
  0.0 1464.6 jit_solution(5562700198579323586)
XLA Ops:
  20.9 31.2 %all-gather.4 = bf16[8,224,64]{1,2,0:T(8,128)(2,1)S(1)} all-gather(bf16[1,224,64]{1,2,0:T(8,128)(2,1)S(1)} %bitcast.252), channel_id=1, replica_groups=mesh['ctx'=8,'wt'=4] {'ctx'}, dimensions={0}, use_global_device_ids=true | all-gather | bytes 258048 | tf_op jit(solution)/shard_map/all_gather | solution.py:117
  64.7 35.8 %all-gather.20.cloned.1.call-done = bf16[1792,448]{1,0:T(8,128)(2,1)} async-done(((bf16[224,448]{1,0:T(8,128)(2,1)}), bf16[1792,448]{1,0:T(8,128)(2,1)}) %all-gather.20.cloned.1.call-update) | async-done | bytes 1605648 | tf_op jit(solution)/shard_map/all_gather | solution.py:118
  114.2 31.8 %all-gather.5 = bf16[8,224,64]{1,2,0:T(8,128)(2,1)S(1)} all-gather(bf16[1,224,64]{1,2,0:T(8,128)(2,1)S(1)} %bitcast.253), channel_id=1, replica_groups=mesh['ctx'=8,'wt'=4] {'ctx'}, dimensions={0}, use_global_device_ids=true | all-gather | bytes 258048 | tf_op jit(solution)/shard_map/all_gather | solution.py:116
  151.8 41.5 %all-gather.1 = bf16[16,273,4]{1,2,0:T(4,128)(2,1)S(1)} all-gather(bf16[2,273,4]{1,2,0:T(4,128)(2,1)S(1)} %bitcast.254), channel_id=3, replica_groups=mesh['ctx'=8,'wt'=4] {'ctx'}, dimensions={0}, use_global_device_ids=true | all-gather | bytes 39312 | tf_op jit(solution)/shard_map/all_gather | solution.py:20
  200.9 14.7 %while.37 = (s32[]{:T(128)}, f32[2,273,4,112]{3,2,1,0:T(4,128)S(1)}, f32[2,273,4]{1,2,0:T(4,128)S(1)}, s32[]{:T(128)}, bf16[8,2,273,4,112]{4,3,2,1,0:T(4,128)(2,...) while((s32[]{:T(128)}, f32[2,273,4,112]{3,2,1,0:T(4,128)S(1)}, ...), condition=%wide.region_4.5_spmd.clone, body=%wide.region_3.4_spmd.clone.sunk | while | flops 987172 | bytes 2468035 | solution.py:37
  225.8 10.3 fusion.21
  245.3 38.0 %reduce-scatter.18.cloned.1.call-done = bf16[2,512,448]{1,2,0:T(8,128)(2,1)} async-done(((bf16[2,512,1792]{1,2,0:T(8,128)(2,1)}), bf16[2,512,448]{1,2,0:T(8,128)(2,1)}) %reduce-scatter.18.cloned.1.call-update) | async-done | bytes 917520 | tf_op jit(solution)/shard_map/reduce_scatter | solution.py:196
  295.3 21.7 %all-gather.32.cloned.1.call-done = bf16[2,512,1792]{1,2,0:T(8,128)(2,1)} async-done(((bf16[2,512,448]{1,2,0:T(8,128)(2,1)}), bf16[2,512,1792]{1,2,0:T(8,128)(2,1)}) %all-gather.32.cloned.1.call-update) | async-done | bytes 3670032 | tf_op jit(solution)/shard_map/all_gather | solution.py:101
  323.0 27.8 %all-gather.24.cloned.1.call-done = bf16[2,512,1792]{1,2,0:T(8,128)(2,1)} async-done(((bf16[2,512,448]{1,2,0:T(8,128)(2,1)}), bf16[2,512,1792]{1,2,0:T(8,128)(2,1)}) %all-gather.24.cloned.1.call-update) | async-done | bytes 3670032 | tf_op jit(solution)/shard_map/all_gather | solution.py:101
  356.7 74.8 %all-gather.26.cloned.1.call-done = bf16[1792,1216]{1,0:T(8,128)(2,1)} async-done(((bf16[224,1216]{1,0:T(8,128)(2,1)}), bf16[1792,1216]{1,0:T(8,128)(2,1)}) %all-gather.26.cloned.1.call-update) | async-done | bytes 4358160 | tf_op jit(solution)/shard_map/all_gather | solution.py:119
  431.5 10.4 fusion.80
  442.0 68.4 %all-gather.28.cloned.1.call-done = bf16[1792,1216]{1,0:T(8,128)(2,1)} async-done(((bf16[224,1216]{1,0:T(8,128)(2,1)}), bf16[1792,1216]{1,0:T(8,128)(2,1)}) %all-gather.28.cloned.1.call-update) | async-done | bytes 4358160 | tf_op jit(solution)/shard_map/all_gather | solution.py:120
  510.4 10.3 fusion.81
  520.7 68.4 %all-gather.30.cloned.1.call-done = bf16[1216,1792]{0,1:T(8,128)(2,1)} async-done(((bf16[1216,224]{0,1:T(8,128)(2,1)}), bf16[1216,1792]{0,1:T(8,128)(2,1)}) %all-gather.30.cloned.1.call-update) | async-done | bytes 4358160 | tf_op jit(solution)/shard_map/all_gather | solution.py:127
  589.1 13.2 multiply_convert_fusion
  624.3 39.5 %reduce-scatter.22.cloned.1.call-done = bf16[2,512,448]{1,2,0:T(8,128)(2,1)} async-done(((bf16[2,512,1792]{1,2,0:T(8,128)(2,1)}), bf16[2,512,448]{1,2,0:T(8,128)(2,1)}) %reduce-scatter.22.cloned.1.call-update) | async-done | bytes 917520 | tf_op jit(solution)/shard_map/reduce_scatter | solution.py:105
  675.8 32.7 %all-gather.34.cloned.1.call-done = bf16[2,512,1792]{1,2,0:T(8,128)(2,1)} async-done(((bf16[2,512,448]{1,2,0:T(8,128)(2,1)}), bf16[2,512,1792]{1,2,0:T(8,128)(2,1)}) %all-gather.34.cloned.1.call-update) | async-done | bytes 3670032 | tf_op jit(solution)/shard_map/all_gather | solution.py:101
  732.0 10.0 convolution_convert_fusion.2
  742.0 9.9 convolution_convert_fusion.1
  752.0 9.9 convolution_convert_fusion
  806.7 31.4 %all-gather.3 = bf16[16,273,4]{1,2,0:T(4,128)(2,1)S(1)} all-gather(bf16[2,273,4]{1,2,0:T(4,128)(2,1)S(1)} %bitcast.255), channel_id=5, replica_groups=mesh['ctx'=8,'wt'=4] {'ctx'}, dimensions={0}, use_global_device_ids=true | all-gather | bytes 39312 | tf_op jit(solution)/shard_map/all_gather | solution.py:43
  838.1 15.2 %while.38 = (s32[]{:T(128)}, f32[2,273,4,112]{3,2,1,0:T(4,128)S(1)}, f32[2,273,4]{1,2,0:T(4,128)S(1)}, s32[]{:T(128)}, bf16[8,2,273,4,112]{4,3,2,1,0:T(4,128)(2,...) while((s32[]{:T(128)}, ...), condition=%wide.region_17.18_spmd.clone, body=%wide.region_16.17_spmd.clone.sunk | while | flops 987176 | bytes 2468097 | solution.py:61
  868.4 12.2 fusion.26
  922.2 78.8 %reduce-scatter.30.cloned.1.call-done = bf16[224,1216]{1,0:T(8,128)(2,1)} async-done(((bf16[1792,1216]{1,0:T(8,128)(2,1)}), bf16[224,1216]{1,0:T(8,128)(2,1)}) %reduce-scatter.30.cloned.1.call-update) | async-done | bytes 544784 | tf_op jit(solution)/shard_map/reduce_scatter | solution.py:286
  1003.1 94.7 %reduce-scatter.32.cloned.1.call-done = bf16[1216,224]{0,1:T(8,128)(2,1)} async-done(((bf16[1216,1792]{0,1:T(8,128)(2,1)}), bf16[1216,224]{0,1:T(8,128)(2,1)}) %reduce-scatter.32.cloned.1.call-update) | async-done | bytes 544784 | tf_op jit(solution)/shard_map/reduce_scatter | solution.py:294
  1099.9 63.1 %reduce-scatter.34.cloned.1.call-done = bf16[224,64]{1,0:T(8,128)(2,1)} async-done(((bf16[1792,64]{1,0:T(8,128)(2,1)}), bf16[224,64]{1,0:T(8,128)(2,1)}) %reduce-scatter.34.cloned.1.call-update) | async-done | bytes 28688
  1164.6 67.4 %reduce-scatter.38.cloned.1.call-done = bf16[224,448]{1,0:T(8,128)(2,1)} async-done(((bf16[1792,448]{1,0:T(8,128)(2,1)}), bf16[224,448]{1,0:T(8,128)(2,1)}) %reduce-scatter.38.cloned.1.call-update) | async-done | bytes 200720
  1233.8 62.6 %reduce-scatter.36.cloned.1.call-done = bf16[224,64]{1,0:T(8,128)(2,1)} async-done(((bf16[1792,64]{1,0:T(8,128)(2,1)}), bf16[224,64]{1,0:T(8,128)(2,1)}) %reduce-scatter.36.cloned.1.call-update) | async-done | bytes 28688
  1298.0 68.2 %reduce-scatter.26.cloned.1.call-done = bf16[224,448]{1,0:T(8,128)(2,1)} async-done(((bf16[1792,448]{1,0:T(8,128)(2,1)}), bf16[224,448]{1,0:T(8,128)(2,1)}) %reduce-scatter.26.cloned.1.call-update) | async-done | bytes 200720 | tf_op jit(solution)/shard_map/reduce_scatter | solution.py:280
  1367.9 40.9 %reduce-scatter.24.cloned.1.call-done = bf16[2,512,448]{1,2,0:T(8,128)(2,1)} async-done(((bf16[2,512,1792]{1,2,0:T(8,128)(2,1)}), bf16[2,512,448]{1,2,0:T(8,128)(2,1)}) %reduce-scatter.24.cloned.1.call-update) | async-done | bytes 917520 | tf_op jit(solution)/shard_map/reduce_scatter | solution.py:105
  1410.8 22.0 %all-reduce = (f32[448]{0:T(512)}, f32[448]{0:T(512)}) all-reduce(f32[448]{0:T(512)S(1)} %get-tuple-element.348, f32[448]{0:T(512)S(1)} %copy-done.56), channel_id=1, replica_groups=mesh['ctx'=8,'wt'=4] {'ctx'}, use_global_device_ids=true, to_apply=%region_24.25 | all-reduce | flops 896 | bytes 7168 | tf_op jit(solution)/shard_map/psum | solution.py:298
  1438.9 14.0 reduce-scatter.20.cloned.1.call-done
  (322 shorter events, 307.3 us)
Async XLA Ops:
  7.2 45.5 %all-gather.18.cloned.1.call-start = ((), (), s32[]{:S(2)}) async-start(), calls=%async_computation.11 | async-start | bytes 4587520 | tf_op jit(solution)/shard_map/all_gather | solution.py:101
  20.0 80.5 %all-gather.20.cloned.1.call-start = ((), (), s32[]{:S(2)}) async-start(), calls=%async_computation.12 | async-start | bytes 2064384 | tf_op jit(solution)/shard_map/all_gather | solution.py:118
  20.8 180.1 %all-gather.36.cloned.1.call-start = ((), (), s32[]{:S(2)}) async-start(), calls=%async_computation.28 | async-start | bytes 5031936 | tf_op jit(solution)/shard_map/all_gather | solution.py:20
  112.1 125.5 %all-gather.22.cloned.1.call-start = ((), (), s32[]{:S(2)}) async-start(), calls=%async_computation.13 | async-start | bytes 2064384 | tf_op jit(solution)/shard_map/all_gather | solution.py:126
  113.0 170.4 %reduce-scatter.18.cloned.1.call-start = ((), (), s32[]{:S(2)}) async-start(), calls=%async_computation.14 | async-start | bytes 4587520 | tf_op jit(solution)/shard_map/reduce_scatter | solution.py:196
  221.5 502.0 %copy-start.53 = (f32[2,512,4]{1,2,0:T(4,128)}, f32[2,512,4]{1,2,0:T(4,128)S(1)}, u32[]{:S(2)}) copy-start(f32[2,512,4]{1,2,0:T(4,128)S(1)} %get-tuple-element.381) | copy-start | bytes 49156
  243.0 74.0 %all-gather.32.cloned.1.call-start = ((), (), s32[]{:S(2)}) async-start(), calls=%async_computation.20 | async-start | bytes 4587520 | tf_op jit(solution)/shard_map/all_gather | solution.py:101
  245.3 105.5 %all-gather.24.cloned.1.call-start = ((), (), s32[]{:S(2)}) async-start(), calls=%async_computation.15 | async-start | bytes 4587520 | tf_op jit(solution)/shard_map/all_gather | solution.py:101
  293.2 138.3 %all-gather.26.cloned.1.call-start = ((), (), s32[]{:S(2)}) async-start(), calls=%async_computation.16 | async-start | bytes 5160960 | tf_op jit(solution)/shard_map/all_gather | solution.py:119
  294.0 216.4 %all-gather.28.cloned.1.call-start = ((), (), s32[]{:S(2)}) async-start(), calls=%async_computation.17 | async-start | bytes 5160960 | tf_op jit(solution)/shard_map/all_gather | solution.py:120
  294.7 294.4 %all-gather.30.cloned.1.call-start = ((), (), s32[]{:S(2)}) async-start(), calls=%async_computation.18 | async-start | bytes 5160960 | tf_op jit(solution)/shard_map/all_gather | solution.py:127
  295.3 368.5 %reduce-scatter.22.cloned.1.call-start = ((), (), s32[]{:S(2)}) async-start(), calls=%async_computation.21 | async-start | bytes 4587520 | tf_op jit(solution)/shard_map/reduce_scatter | solution.py:105
  624.2 84.3 %all-gather.34.cloned.1.call-start = ((), (), s32[]{:S(2)}) async-start(), calls=%async_computation.22 | async-start | bytes 4587520 | tf_op jit(solution)/shard_map/all_gather | solution.py:101
  675.7 162.4 %all-gather.38.cloned.1.call-start = ((), (), s32[]{:S(2)}) async-start(), calls=%async_computation.29 | async-start | bytes 5031936 | tf_op jit(solution)/shard_map/all_gather | solution.py:43
  731.7 188.2 %reduce-scatter.28.cloned.1.call-start = ((), (), s32[]{:S(2)}) async-start(), calls=%async_computation.25 | async-start | bytes 5160960 | tf_op jit(solution)/shard_map/reduce_scatter | solution.py:283
  742.0 258.9 %reduce-scatter.30.cloned.1.call-start = ((), (), s32[]{:S(2)}) async-start(), calls=%async_computation.26 | async-start | bytes 5160960 | tf_op jit(solution)/shard_map/reduce_scatter | solution.py:286
  752.0 345.8 %reduce-scatter.32.cloned.1.call-start = ((), (), s32[]{:S(2)}) async-start(), calls=%async_computation.27 | async-start | bytes 5160960 | tf_op jit(solution)/shard_map/reduce_scatter | solution.py:294
  762.0 401.0 %reduce-scatter.34.cloned.1.call-start = ((), (), s32[]{:S(2)}) async-start(), calls=%async_computation.30 | async-start | bytes 516096
  797.5 434.4 %reduce-scatter.38.cloned.1.call-start = ((), (), s32[]{:S(2)}) async-start(), calls=%async_computation.32 | async-start | bytes 2064384
  838.1 458.4 %reduce-scatter.36.cloned.1.call-start = ((), (), s32[]{:S(2)}) async-start(), calls=%async_computation.31 | async-start | bytes 516096
  884.7 481.4 %reduce-scatter.26.cloned.1.call-start = ((), (), s32[]{:S(2)}) async-start(), calls=%async_computation.24 | async-start | bytes 2064384 | tf_op jit(solution)/shard_map/reduce_scatter | solution.py:280
  890.2 518.6 %reduce-scatter.24.cloned.1.call-start = ((), (), s32[]{:S(2)}) async-start(), calls=%async_computation.23 | async-start | bytes 4587520 | tf_op jit(solution)/shard_map/reduce_scatter | solution.py:105
  903.2 549.7 %reduce-scatter.20.cloned.1.call-start = ((), (), s32[]{:S(2)}) async-start(), calls=%async_computation.19 | async-start | bytes 4587520 | tf_op jit(solution)/shard_map/reduce_scatter | solution.py:105
  919.9 488.9 %copy-start.41 = (f32[2,512]{1,0:T(2,128)S(1)}, f32[2,512]{1,0:T(2,128)}, u32[]{:S(2)}) copy-start(f32[2,512]{1,0:T(2,128)} %copy-done.40) | copy-start | bytes 12292
  919.9 488.9 %copy-start.51 = (f32[448]{0:T(512)S(1)}, f32[448]{0:T(512)}, u32[]{:S(2)}) copy-start(f32[448]{0:T(512)} %copy-done.50) | copy-start | bytes 5380
  922.1 488.7 %copy-start.56 = (f32[448]{0:T(512)S(1)}, f32[448]{0:T(512)}, u32[]{:S(2)}) copy-start(f32[448]{0:T(512)} %get-tuple-element.346) | copy-start | bytes 5380
  922.1 516.8 %copy-start.47 = (f32[2,512]{1,0:T(2,128)S(1)}, f32[2,512]{1,0:T(2,128)}, u32[]{:S(2)}) copy-start(f32[2,512]{1,0:T(2,128)} %copy-done.46) | copy-start | bytes 12292
  922.1 530.8 %copy-start.9 = (bf16[2,512,448]{1,2,0:T(8,128)(2,1)S(1)}, bf16[2,512,448]{1,2,0:T(8,128)(2,1)}, u32[]{:S(2)}) copy-start(bf16[2,512,448]{1,2,0:T(8,128)(2,1)} %reduce-scatter.18.cloned.1.call-done) | copy-start | bytes 2752516
  922.1 530.8 %copy-start.11 = (bf16[2,512,448]{1,2,0:T(8,128)(2,1)S(1)}, bf16[2,512,448]{1,2,0:T(8,128)(2,1)}, u32[]{:S(2)}) copy-start(bf16[2,512,448]{1,2,0:T(8,128)(2,1)} %param.27) | copy-start | bytes 2752516
  922.1 530.8 %copy-start.39 = (f32[2,512]{1,0:T(2,128)S(1)}, f32[2,512]{1,0:T(2,128)}, u32[]{:S(2)}) copy-start(f32[2,512]{1,0:T(2,128)} %copy-done.38) | copy-start | bytes 12292
  922.1 530.8 %copy-start.43 = (f32[448]{0:T(512)S(1)}, f32[448]{0:T(512)}, u32[]{:S(2)}) copy-start(f32[448]{0:T(512)} %copy-done.42) | copy-start | bytes 5380
  922.2 530.8 %copy-start.45 = (f32[2,512]{1,0:T(2,128)S(1)}, f32[2,512]{1,0:T(2,128)}, u32[]{:S(2)}) copy-start(f32[2,512]{1,0:T(2,128)} %copy-done.44) | copy-start | bytes 12292
  (56 other events, 1646.8 us)
Sparse Core Ops, SparseCore 0:
  20.2 31.8 all-gather.17
  54.2 46.2 all-gather.19
  112.2 78.1 all-gather.35
  193.0 44.5 all-gather.21
  243.1 40.2 reduce-scatter.17
  285.5 31.5 all-gather.31
  319.2 31.4 all-gather.23
  353.2 78.2 all-gather.25
  433.9 76.4 all-gather.27
  512.7 76.4 all-gather.29
  624.4 39.3 reduce-scatter.21
  675.9 32.6 all-gather.33
  731.9 76.8 all-gather.37
  812.2 91.7 reduce-scatter.27
  907.6 93.3 reduce-scatter.29
  1004.4 93.3 reduce-scatter.31
  1101.5 61.5 reduce-scatter.33
  1166.8 65.1 reduce-scatter.37
  1235.8 60.6 reduce-scatter.35
  1300.8 65.3 reduce-scatter.25
  1368.7 40.0 reduce-scatter.23
  1411.5 41.3 reduce-scatter.19
where the time goes:
time: 1480 us; the launch traced here: 1460 us
  waiting for transfers between devices  901 us (61%)
  matrix products  207 us (14%)
  blocking collectives  184 us (12%)
  other arithmetic  82.7 us (6%)
  local copies, waits for them, and re-layouts  70.9 us (5%)
  between operations  15.6 us (1%)
    unnamed x25, waiting for transfers between devices  196 us
    reduce_scatter x1, waiting for transfers between devices, body(): lax.psum_scatter(grad_down.astype(jnp.bfloat16), 'ctx', scatter_dimension...  94.7 us
    reduce_scatter x3, waiting for transfers between devices, narrow(): lax.psum_scatter(partial_sum.astype(jnp.bfloat16), 'wt', scatter_dimensio...  94.3 us
    all_gather x4, waiting for transfers between devices, to_full(): return lax.all_gather(local_part, 'wt', axis=2, tiled=True)  82.2 us
    reduce_scatter x1, waiting for transfers between devices, body(): lax.psum_scatter(grad_up.astype(jnp.bfloat16), 'ctx', scatter_dimension=0...  78.8 us
    all_gather x1, waiting for transfers between devices, fetch_rows(): lax.all_gather(w_gate, 'ctx', axis=0, tiled=True)  74.8 us
    all_gather x1, waiting for transfers between devices, fetch_rows(): lax.all_gather(w_up, 'ctx', axis=0, tiled=True)  68.4 us
    all_gather x1, waiting for transfers between devices, fetch_cols(): lax.all_gather(w_down, 'ctx', axis=1, tiled=True)  68.4 us
  transfers between devices with their start and end apart: 22, of which 18 were waited for; matrix products, arithmetic and copies ran while one was open for 18% of the time, Pallas kernels for 0%

commit v1 on v0

v1 whole, which is shorter than its diff:
```python
from functools import partial

import jax
import jax.numpy as jnp
from jax import lax
from jax.experimental import pallas as pl
from jax.experimental.pallas import tpu as pltpu
from jax.sharding import PartitionSpec as P

D = 1792
FEAT = 16
HEAD_DIM = 112
EXT = 128
PHI = 160
EPS = 1e-05
BF = jnp.bfloat16
F32 = jnp.float32


def mm_nn(left, right):
    return lax.dot_general(left, right, (((1,), (0,)), ((), ())), preferred_element_type=F32)


def mm_tn(left, right):
    return lax.dot_general(left, right, (((0,), (0,)), ((), ())), preferred_element_type=F32)


def mm_nt(left, right):
    return lax.dot_general(left, right, (((1,), (1,)), ((), ())), preferred_element_type=F32)


def swap(value, bit):
    count = lax.axis_size("wt")
    return lax.ppermute(value, "wt", [(i, i ^ bit) for i in range(count)])


def wt_gather(block):
    me = lax.axis_index("wt")
    far = swap(block, 2)
    near = swap(block, 1)
    both = swap(far, 1)
    odd, high = (me & 1) == 1, me >= 2
    first = jnp.where(high, far, block), jnp.where(high, both, near)
    second = jnp.where(high, block, far), jnp.where(high, near, both)
    return jnp.concatenate(
        [
            jnp.where(odd, first[1], first[0]),
            jnp.where(odd, first[0], first[1]),
            jnp.where(odd, second[1], second[0]),
            jnp.where(odd, second[0], second[1]),
        ],
        0,
    )


def wt_scatter(partial_sum):
    me = lax.axis_index("wt")
    core, chip = me & 1, me >> 1
    rows, columns = partial_sum.shape
    shaped = partial_sum.reshape(2, 2, rows // 4, columns)
    sent = lax.dynamic_index_in_dim(shaped, 1 - core, 1, keepdims=False)
    kept = lax.dynamic_index_in_dim(shaped, core, 1, keepdims=False)
    got = swap(sent, 1)
    other = lax.dynamic_index_in_dim(kept, 1 - chip, 0, keepdims=False).astype(
        F32
    ) + lax.dynamic_index_in_dim(got, 1 - chip, 0, keepdims=False).astype(F32)
    mine = lax.dynamic_index_in_dim(kept, chip, 0, keepdims=False).astype(
        F32
    ) + lax.dynamic_index_in_dim(got, chip, 0, keepdims=False).astype(F32)
    return mine + swap(other.astype(BF), 2).astype(F32)


def wt_total(value):
    value = value + swap(value, 1)
    return value + swap(value, 2)


def ring_order(count):
    half = count // 2
    return [2 * r for r in range(half)] + [2 * r + 1 for r in reversed(range(half))]


def ringed():
    return lax.axis_size("ctx") == 8


def hop(value, step):
    order = ring_order(lax.axis_size("ctx"))
    count = len(order)
    pairs = [(order[r], order[(r + step) % count]) for r in range(count)]
    return lax.ppermute(value, "ctx", pairs)


def ring_index(offset):
    order = ring_order(lax.axis_size("ctx"))
    count = len(order)
    place = {device: r for r, device in enumerate(order)}
    table = jnp.array([order[(place[i] + offset) % count] for i in range(count)], jnp.int32)
    return table[lax.axis_index("ctx")]


def ctx_gather(shard):
    if not ringed():
        return lax.all_gather(shard, "ctx", axis=0, tiled=True)
    rows = shard.shape[0]
    half = rows // 2
    pieces = [(shard, 0, 0)]
    right, left = shard, shard
    for step in range(1, 4):
        right, left = hop(right, 1), hop(left, -1)
        pieces += [(right, -step, 0), (left, step, 0)]
    pieces += [(hop(right[:half], 1), 4, 0), (hop(left[half:], -1), 4, half)]
    full = jnp.zeros((rows * 8,) + shard.shape[1:], shard.dtype)
    for piece, offset, start in pieces:
        full = lax.dynamic_update_slice_in_dim(full, piece, ring_index(offset) * rows + start, 0)
    return full


def ctx_scatter(full):
    if not ringed():
        return lax.psum_scatter(full, "ctx", scatter_dimension=0, tiled=True).astype(F32)
    rows = full.shape[0] // 8
    half = rows // 2

    def own(offset):
        return lax.dynamic_slice_in_dim(full, ring_index(offset) * rows, rows, 0)

    opposite = own(4)
    right, left = hop(opposite[:half], 1), hop(opposite[half:], -1)
    zero = jnp.zeros((half, full.shape[1]), full.dtype)
    right, left = jnp.concatenate([right, zero], 0), jnp.concatenate([zero, left], 0)
    for step in (3, 2, 1):
        right = hop((right.astype(F32) + own(step).astype(F32)).astype(BF), 1)
        left = hop((left.astype(F32) + own(-step).astype(F32)).astype(BF), -1)
    return own(0).astype(F32) + right.astype(F32) + left.astype(F32)


def shifted(value, by):
    count = lax.axis_size("ctx")
    pairs = [(i, i + by) for i in range(count) if 0 <= i + by < count]
    return lax.ppermute(value, "ctx", pairs)


def ctx_before(value, sign):
    count, index = lax.axis_size("ctx"), lax.axis_index("ctx")
    if not ringed():
        everything = lax.all_gather(value, "ctx").astype(F32)
        place = jnp.arange(count)
        keep = (place < index) if sign > 0 else (place > index)
        keep = keep.reshape((count,) + (1,) * value.ndim)
        return jnp.sum(jnp.where(keep, everything, 0.0), 0).astype(BF)
    other = lax.ppermute(value, "ctx", [(i, i ^ 1) for i in range(count)])
    behind = (index & 1) == (1 if sign > 0 else 0)
    total = (value.astype(F32) + other.astype(F32)).astype(BF)
    first = shifted(total, 2 * sign)
    two = (total.astype(F32) + first.astype(F32)).astype(BF)
    second = shifted(two, 4 * sign)
    result = first.astype(F32) + second.astype(F32)
    return (result + jnp.where(behind, other.astype(F32), 0.0)).astype(BF)


def ctx_total(value):
    if not ringed():
        return lax.psum(value, "ctx")
    for bit in (1, 2, 4):
        value = value + lax.ppermute(value, "ctx", [(i, i ^ bit) for i in range(8)])
    return value


def turned(rows, by):
    return jnp.concatenate([rows[by:], rows[:by]], 0)


def feature_rows(vectors, square, cross, linear):
    length = vectors.shape[1]
    half = FEAT // 2
    pieces = [vectors * vectors * square]
    pieces += [vectors * turned(vectors, by) * cross for by in range(1, half)]
    pieces += [vectors[:half] * vectors[half:] * cross]
    place = lax.broadcasted_iota(jnp.int32, (half, length), 0)
    pieces += [jnp.where(place == 0, 1.0, 0.0), vectors * linear]
    return jnp.concatenate(pieces, 0).astype(BF)


def feature_pull(grad, vectors, square, cross, linear):
    half = FEAT // 2
    total = 2.0 * square * grad[:FEAT] * vectors
    for by in range(1, half):
        part = grad[FEAT * by : FEAT * (by + 1)] * cross
        total += part * turned(vectors, by) + turned(part * vectors, FEAT - by)
    part = grad[FEAT * half : FEAT * half + half] * cross
    total += jnp.concatenate([part * vectors[half:], part * vectors[:half]], 0)
    return total + grad[PHI - FEAT :] * linear


QUERY_SCALE = (1.0 / 32.0, 1.0 / 16.0, 0.25)
KEY_SCALE = (1.0, 1.0, 1.0)


def extended(value, valid):
    place = lax.broadcasted_iota(jnp.int32, (EXT - HEAD_DIM, value.shape[1]), 0)
    tail = jnp.where(place == 0, jnp.broadcast_to(valid, place.shape), 0.0)
    return jnp.concatenate([(value.astype(F32) * valid).astype(BF), tail.astype(BF)], 0)


def causal_of(length):
    key_place = lax.broadcasted_iota(jnp.int32, (length, length), 0)
    query_place = lax.broadcasted_iota(jnp.int32, (length, length), 1)
    return key_place <= query_place


def state_kernel(key_ref, value_ref, valid_ref, state_ref):
    mapped = feature_rows(key_ref[...].astype(F32), *KEY_SCALE)
    state_ref[0] = mm_nt(mapped, extended(value_ref[...], valid_ref[...])).astype(BF)


def attend_kernel(query_ref, key_ref, value_ref, valid_ref, state_ref, mixed_ref, denom_ref):
    query = query_ref[...]
    scores = mm_tn(key_ref[...], query) * 0.25
    weights = jnp.where(causal_of(query.shape[1]), 1.0 + scores + 0.5 * scores * scores, 0.0)
    total = mm_nn(extended(value_ref[...], valid_ref[...]), weights.astype(BF))
    mapped = feature_rows(query.astype(F32), *QUERY_SCALE)
    total += mm_tn(state_ref[0], mapped)
    denom = total[HEAD_DIM : HEAD_DIM + 1]
    denom_ref[0] = denom
    mixed_ref[...] = (total[:HEAD_DIM] / denom).astype(BF)


def spread_kernel(query_ref, grad_ref, mixed_ref, denom_ref, weighted_ref, state_ref):
    weighted = grad_ref[...].astype(F32) / denom_ref[0]
    shift = jnp.sum(weighted * mixed_ref[...].astype(F32), 0, keepdims=True)
    place = lax.broadcasted_iota(jnp.int32, (EXT - HEAD_DIM, weighted.shape[1]), 0)
    tail = jnp.where(place == 0, -jnp.broadcast_to(shift, place.shape), 0.0)
    whole = jnp.concatenate([weighted, tail], 0).astype(BF)
    weighted_ref[0] = whole
    mapped = feature_rows(query_ref[...].astype(F32), *QUERY_SCALE)
    state_ref[0] = mm_nt(mapped, whole).astype(BF)


def local_kernel(
    query_ref, key_ref, value_ref, valid_ref, state_ref, weighted_ref, dq_ref, dk_ref, dv_ref
):
    query, key_in, weighted = query_ref[...], key_ref[...], weighted_ref[0]
    causal = causal_of(query.shape[1])
    scores = mm_tn(key_in, query) * 0.25
    weights = jnp.where(causal, 1.0 + scores + 0.5 * scores * scores, 0.0).astype(BF)
    dv_ref[...] = mm_nt(weighted[:HEAD_DIM], weights) * valid_ref[...]
    slope = mm_tn(extended(value_ref[...], valid_ref[...]), weighted)
    slope = jnp.where(causal, slope * (1.0 + scores), 0.0).astype(BF)
    mapped = mm_nn(state_ref[0], weighted)
    pulled = feature_pull(mapped, query.astype(F32), *QUERY_SCALE)
    dq_ref[...] = (mm_nn(key_in, slope) * 0.25 + pulled).astype(BF)
    dk_ref[...] = mm_nt(query, slope) * 0.25


def later_kernel(key_ref, value_ref, valid_ref, state_ref, dk_in, dv_in, dk_ref, dv_ref):
    key_in = key_ref[...].astype(F32)
    valid = valid_ref[...]
    mapped = mm_nn(state_ref[0], extended(value_ref[...], valid))
    dk_ref[...] = (dk_in[...] + feature_pull(mapped, key_in, *KEY_SCALE)).astype(BF)
    spread = mm_tn(state_ref[0], feature_rows(key_in, *KEY_SCALE))
    dv_ref[...] = (dv_in[...] + spread[:HEAD_DIM] * valid).astype(BF)


def head_call(kernel, name, heads, length, ins, outs, cost):
    specs = {
        "feat": (pl.BlockSpec((FEAT, length), lambda h: (h, 0)), (heads * FEAT, length)),
        "head": (pl.BlockSpec((HEAD_DIM, length), lambda h: (h, 0)), (heads * HEAD_DIM, length)),
        "valid": (pl.BlockSpec((1, length), lambda h: (0, 0)), (1, length)),
        "state": (pl.BlockSpec((1, PHI, EXT), lambda h: (h, 0, 0)), (heads, PHI, EXT)),
        "row": (pl.BlockSpec((1, 1, length), lambda h: (h, 0, 0)), (heads, 1, length)),
        "ext": (pl.BlockSpec((1, EXT, length), lambda h: (h, 0, 0)), (heads, EXT, length)),
    }
    return pl.pallas_call(
        kernel,
        name=name,
        grid=(heads,),
        in_specs=[specs[i][0] for i in ins],
        out_specs=[specs[o][0] for o, _ in outs],
        out_shape=[jax.ShapeDtypeStruct(specs[o][1], kind) for o, kind in outs],
        compiler_params=pltpu.CompilerParams(vmem_limit_bytes=32 << 20),
        cost_estimate=pl.CostEstimate(flops=cost, bytes_accessed=4 << 20, transcendentals=0),
    )


def body(
    hidden_in,
    lengths,
    gain_attn,
    gain_ffn,
    w_query,
    w_key,
    w_value,
    w_output,
    w_gate,
    w_up,
    w_down,
    cotangent,
):
    seqs, length, width = hidden_in.shape
    heads = w_value.shape[1] // HEAD_DIM
    q_rows = heads * FEAT
    both = range(seqs)
    position = lax.axis_index("ctx") * length + jnp.arange(length, dtype=jnp.int32)
    valid = [(position < lengths[s]).astype(F32)[None, :] for s in both]

    hidden = [hidden_in[s].T for s in both]
    full_in = [wt_gather(hidden[s]) for s in both]
    gains = wt_gather(jnp.stack([gain_attn, gain_ffn], 1)).astype(F32)
    attn_shard = jnp.concatenate([w_query, w_key, w_value, w_output.T], 1)
    w_attn = ctx_gather(attn_shard)
    qkv_columns = 2 * q_rows + heads * HEAD_DIM
    w_qkv, w_out = w_attn[:, :qkv_columns], w_attn[:, qkv_columns:]
    gate_full = ctx_gather(w_gate)
    up_full = ctx_gather(w_up)
    down_full = ctx_gather(w_down.T)
    grad_out = [(cotangent[s].T.astype(F32) * valid[s]).astype(BF) for s in both]
    grad_out_full = [wt_gather(grad_out[s]) for s in both]

    def normed(full, gain):
        value = full.astype(F32)
        inverse = lax.rsqrt(jnp.sum(value * value, 0, keepdims=True) / D + EPS)
        return inverse, (value * inverse * gain[:, None]).astype(BF)

    call = partial(head_call, heads=heads, length=length)
    flops = heads * 2 * length * length * 256

    inv_one, normed_one, query, key_in, value_in, state = [], [], [], [], [], []
    for s in both:
        inverse, normal = normed(full_in[s], gains[:, 0])
        qkv = mm_tn(w_qkv, normal).astype(BF)
        inv_one.append(inverse)
        normed_one.append(normal)
        query.append(qkv[:q_rows])
        key_in.append(qkv[q_rows : 2 * q_rows])
        value_in.append(qkv[2 * q_rows :])
        (own,) = call(
            state_kernel, "state", ins=("feat", "head", "valid"), outs=(("state", BF),), cost=flops // 2
        )(key_in[s], value_in[s], valid[s])
        state.append(ctx_before(own, 1))

    mixed, denom, resid, inv_two, normed_two = [], [], [], [], []
    for s in both:
        mix, den = call(
            attend_kernel,
            "attend",
            ins=("feat", "feat", "head", "valid", "state"),
            outs=(("head", BF), ("row", F32)),
            cost=flops,
        )(query[s], key_in[s], value_in[s], valid[s], state[s])
        mixed.append(mix)
        denom.append(den)
        resid.append(hidden[s].astype(F32) + wt_scatter(mm_nn(w_out, mix).astype(BF)))
        inverse, normal = normed(wt_gather(resid[s].astype(BF)), gains[:, 1])
        inv_two.append(inverse)
        normed_two.append(normal)

    layer_out, grad_gate, grad_up, act, d_norm_two, inner_two = [], [], [], [], [], []
    for s in both:
        gate = mm_tn(gate_full, normed_two[s])
        up = mm_tn(up_full, normed_two[s])
        sig = jax.nn.sigmoid(gate)
        silu = gate * sig
        act.append((silu * up).astype(BF))
        layer_out.append(
            (resid[s] + wt_scatter(mm_nn(down_full, act[s]).astype(BF))).astype(BF)
        )
        d_act = mm_tn(down_full, grad_out_full[s])
        g_gate = (d_act * up * sig * (1.0 + gate * (1.0 - sig))).astype(BF)
        g_up = (d_act * silu).astype(BF)
        grad_gate.append(g_gate)
        grad_up.append(g_up)
        inner_two.append(
            wt_total(
                jnp.sum(g_gate.astype(F32) * gate + g_up.astype(F32) * up, 0, keepdims=True)
            )
        )
        d_norm_two.append(
            wt_scatter((mm_nn(gate_full, g_gate) + mm_nn(up_full, g_up)).astype(BF))
        )

    down_grad = ctx_scatter(sum(mm_nt(grad_out_full[s], act[s]) for s in both).astype(BF))
    gate_grad = ctx_scatter(sum(mm_nt(normed_two[s], grad_gate[s]) for s in both).astype(BF))
    up_grad = ctx_scatter(sum(mm_nt(normed_two[s], grad_up[s]) for s in both).astype(BF))

    gain_two = gain_ffn.astype(F32)[:, None]
    gain_one = gain_attn.astype(F32)[:, None]
    gain_two_part, d_resid, resid_full, weighted, d_state = 0.0, [], [], [], []
    for s in both:
        gain_two_part += jnp.sum(resid[s] * inv_two[s] * d_norm_two[s], 1)
        d_resid.append(
            grad_out[s].astype(F32)
            + inv_two[s] * gain_two * d_norm_two[s]
            - resid[s] * (inv_two[s] * inv_two[s] * inner_two[s] / D)
        )
        resid_full.append(wt_gather(d_resid[s].astype(BF)))
        g_attn = mm_tn(w_out, resid_full[s]).astype(BF)
        whole, spread = call(
            spread_kernel,
            "spread",
            ins=("feat", "head", "head", "row"),
            outs=(("ext", BF), ("state", BF)),
            cost=flops // 2,
        )(query[s], g_attn, mixed[s], denom[s])
        weighted.append(whole)
        d_state.append(ctx_before(spread, -1))
    gain_two_grad = ctx_total(gain_two_part)

    gain_one_part, grad_input, d_qkv = 0.0, [], []
    for s in both:
        dq, dk_part, dv_part = call(
            local_kernel,
            "local",
            ins=("feat", "feat", "head", "valid", "state", "ext"),
            outs=(("feat", BF), ("feat", F32), ("head", F32)),
            cost=flops * 2,
        )(query[s], key_in[s], value_in[s], valid[s], state[s], weighted[s])
        dk, dv = call(
            later_kernel,
            "later",
            ins=("feat", "head", "valid", "state", "feat", "head"),
            outs=(("feat", BF), ("head", BF)),
            cost=flops // 2,
        )(key_in[s], value_in[s], valid[s], d_state[s], dk_part, dv_part)
        d_qkv.append(jnp.concatenate([dq, dk, dv], 0))
        inner = 0.0
        for grad, made in ((dq, query[s]), (dk, key_in[s]), (dv, value_in[s])):
            inner += jnp.sum(grad.astype(F32) * made.astype(F32), 0, keepdims=True)
        inner = wt_total(inner)
        d_norm_one = wt_scatter(mm_nn(w_qkv, d_qkv[s]).astype(BF))
        value = hidden[s].astype(F32)
        gain_one_part += jnp.sum(value * inv_one[s] * d_norm_one, 1)
        grad_input.append(
            d_resid[s]
            + inv_one[s] * gain_one * d_norm_one
            - value * (inv_one[s] * inv_one[s] * inner / D)
        )
    attn_part = jnp.concatenate(
        [
            sum(mm_nt(normed_one[s], d_qkv[s]) for s in both).astype(BF),
            sum(mm_nt(resid_full[s], mixed[s]) for s in both).astype(BF),
        ],
        1,
    )
    attn_grad = ctx_scatter(attn_part)
    gain_one_grad = ctx_total(gain_one_part)

    return (
        jnp.stack([v.T for v in layer_out]),
        jnp.stack([v.T for v in grad_input]),
        gain_one_grad,
        gain_two_grad,
        attn_grad[:, :q_rows],
        attn_grad[:, q_rows : 2 * q_rows],
        attn_grad[:, 2 * q_rows : qkv_columns],
        attn_grad[:, qkv_columns:].T,
        gate_grad,
        up_grad,
        down_grad.T,
    )


def solution(mesh):
    acts, rows, columns = P(None, "ctx", "wt"), P("ctx", "wt"), P("wt", "ctx")
    in_specs = (acts, P(), P("wt"), P("wt"), rows, rows, rows, columns, rows, rows, columns, acts)
    out_specs = (acts, acts, P("wt"), P("wt"), rows, rows, rows, columns, rows, rows, columns)
    return jax.shard_map(body, mesh=mesh, in_specs=in_specs, out_specs=out_specs, check_vma=False)
```

time: 1480 us -> 721 us (0.49)
  waiting for transfers between devices: 901 us -> 273 us
  blocking collectives: 184 us -> 0 us
  starting transfers between devices: 1.66 us -> 142 us
  matrix products: 207 us -> 116 us
  local copies, waits for them, and re-layouts: 70.9 us -> 112 us
  other arithmetic: 82.7 us -> 42 us
  Pallas kernels: 0 us -> 17.2 us
    reduce_scatter x8 -> x0, waiting for transfers between devices: 374 us -> none  [the longest x1 94.7 us: body(): lax.psum_scatter(grad_down.astype(jnp.bfloat16), 'ctx', scatter_dimension...]
    all_gather x11 -> x0, waiting for transfers between devices: 331 us -> none  [the longest x4 82.2 us: to_full(): return lax.all_gather(local_part, 'wt', axis=2, tiled=True)]
    ppermute x0 -> x133, waiting for transfers between devices: none -> 273 us  [the longest x64 101 us: hop(): return lax.ppermute(value, 'ctx', pairs)]
    unnamed x25 -> x0, waiting for transfers between devices: 196 us -> none
    ppermute x0 -> x133, starting transfers between devices: none -> 142 us  [the longest x64 80.4 us: hop(): return lax.ppermute(value, 'ctx', pairs)]
    all_gather x4 -> x0, blocking collectives: 136 us -> none  [the longest x1 41.5 us: carried_in(): lax.all_gather(part.astype(kind), axis)]
    dot_general x35 -> x30, matrix products: 207 us -> 116 us  [the longest x10 62.6 us: mm_nt(): lax.dot_general(left, right, (((1,), (1,)), ((), ())), preferred_element_...]
    dynamic_update_slice x0 -> x36, local copies, waits for them, and re-layouts: none -> 79.7 us  [ctx_gather(): lax.dynamic_update_slice_in_dim(full, piece, ring_index(offset) * rows +...]
  transfers between devices with their start and end apart: 22 -> 133, of which waited for: 18 -> 55; matrix products, arithmetic and copies ran while one was open for 18% -> 31% of each run, Pallas kernels for 0% -> 2%
where the time goes in v1:
time: 721 us; the launch traced here: 711 us
  waiting for transfers between devices  273 us (38%)
  starting transfers between devices  142 us (20%)
  matrix products  116 us (16%)
  local copies, waits for them, and re-layouts  112 us (16%)
  other arithmetic  42 us (6%)
  Pallas kernels  17.2 us (2%)
  between operations  8.41 us (1%)
    ppermute x64, waiting for transfers between devices, hop(): return lax.ppermute(value, 'ctx', pairs)  101 us
    ppermute x51, waiting for transfers between devices, swap(): return lax.ppermute(value, 'wt', [(i, i ^ bit) for i in range(count)])  100 us
    ppermute x64, starting transfers between devices, hop(): return lax.ppermute(value, 'ctx', pairs)  80.4 us
    dynamic_update_slice x36, local copies, waits for them, and re-layouts, ctx_gather(): lax.dynamic_update_slice_in_dim(full, piece, ring_index(offset) * rows +...  79.7 us
    dot_general x10, matrix products, mm_nt(): lax.dot_general(left, right, (((1,), (1,)), ((), ())), preferred_element_...  62.6 us
    ppermute x6, waiting for transfers between devices, ctx_total(): value = value + lax.ppermute(value, 'ctx', [(i, i ^ bit) for i in range(8)])  41.1 us
    ppermute x51, starting transfers between devices, swap(): return lax.ppermute(value, 'wt', [(i, i ^ bit) for i in range(count)])  32.2 us
    dot_general x10, matrix products, mm_tn(): lax.dot_general(left, right, (((0,), (0,)), ((), ())), preferred_element_...  30.5 us
  transfers between devices with their start and end apart: 133, of which 55 were waited for; matrix products, arithmetic and copies ran while one was open for 31% of the time, Pallas kernels for 2%

profile of v1, /device:TPU:0, one launch (start us, length us, event | category | flops | bytes accessed | tf_op | source)
XLA Modules:
  0.0 710.6 jit_solution(11838414583317492482)
XLA Ops:
  40.7 6.5 dynamic_update_slice.109
  47.9 6.5 dynamic_update_slice.110
  70.8 7.9 %collective-permute-done.48 = bf16[448,512]{1,0:T(8,128)(2,1)S(1)} collective-permute-done((bf16[448,512]{1,0:T(8,128)(2,1)}, bf16[448,512]{1,0:T(8,128)(2,1)S(1)}, u32[]{:S(2)}, u32[]{:S(2)}) %collective-permute-start.48) | collective-permute-done | bytes 458784 | tf_op jit(solution)/shard_map/ppermute | solution.py:34
  100.0 6.5 dynamic_update_slice.111
  138.7 7.1 %collective-permute-done.4 = bf16[224,1024]{0,1:T(8,128)(2,1)S(1)} collective-permute-done((bf16[224,1024]{0,1:T(8,128)(2,1)}, bf16[224,1024]{0,1:T(8,128)(2,1)S(1)}, u32[]{:S(2)}, u32[]{:S(2)}) %collective-permute-start.4) | collective-permute-done | bytes 458784 | tf_op jit(solution)/shard_map/ppermute | solution.py:91
  157.1 6.3 dynamic_update_slice.113
  163.4 6.5 dynamic_update_slice.114
  169.9 6.0 collective-permute-done.6
  246.1 7.9 %collective-permute-done.55 = bf16[448,512]{1,0:T(8,128)(2,1)S(1)} collective-permute-done((bf16[448,512]{1,0:T(8,128)(2,1)S(1)}, bf16[448,512]{1,0:T(8,128)(2,1)S(1)}, u32[]{:S(2)}, u32[]{:S(2)}) %collective-permute-start.55) | collective-permute-done | bytes 458784 | tf_op jit(solution)/shard_map/ppermute | solution.py:34
  256.1 9.3 %collective-permute-done.56 = bf16[448,512]{1,0:T(8,128)(2,1)S(1)} collective-permute-done((bf16[448,512]{1,0:T(8,128)(2,1)S(1)}, bf16[448,512]{1,0:T(8,128)(2,1)S(1)}, u32[]{:S(2)}, u32[]{:S(2)}) %collective-permute-start.56) | collective-permute-done | bytes 458784 | tf_op jit(solution)/shard_map/ppermute | solution.py:34
  291.9 17.9 %collective-permute-done.84 = f32[1,512]{1,0:T(1,128)S(1)} collective-permute-done((f32[1,512]{1,0:T(1,128)S(1)}, f32[1,512]{1,0:T(1,128)S(1)}, u32[]{:S(2)}, u32[]{:S(2)}) %collective-permute-start.84) | collective-permute-done | bytes 2080 | tf_op jit(solution)/shard_map/ppermute | solution.py:34
  317.1 6.5 collective-permute-done.85
  359.2 6.2 collective-permute-done.90
  381.0 7.1 %collective-permute-done.94 = f32[1,512]{1,0:T(1,128)S(1)} collective-permute-done((f32[1,512]{1,0:T(1,128)S(1)}, f32[1,512]{1,0:T(1,128)S(1)}, u32[]{:S(2)}, u32[]{:S(2)}) %collective-permute-start.94) | collective-permute-done | bytes 2080 | tf_op jit(solution)/shard_map/ppermute | solution.py:34
  388.1 8.9 %collective-permute-done.92 = bf16[448,512]{1,0:T(8,128)(2,1)S(1)} collective-permute-done((bf16[448,512]{1,0:T(8,128)(2,1)S(1)}, bf16[448,512]{1,0:T(8,128)(2,1)S(1)}, u32[]{:S(2)}, u32[]{:S(2)}) %collective-permute-start.92) | collective-permute-done | bytes 458784 | tf_op jit(solution)/shard_map/ppermute | solution.py:34
  410.8 6.2 fusion.93
  430.2 7.8 %fusion.119 = f32[1792,1216]{1,0:T(8,128)} fusion(bf16[1216,512]{1,0:T(8,128)(2,1)S(1)} %get-tuple-element.103, f32[1792]{0:T(1024)S(1)} %copy-done.86, f32[512]{0:T(512)S(1)} %get-tuple-element.204, bf16[448,512]{1,0:T(8,128)(2,1)S(1)} %get-tuple-element.171, bf16[448,512]{1,0:T(8,128)(2,1)S(1)} %get-tuple-element.170, ...), kind=kOutput, calls=%fused_computation.384 | convolution fusion | flops 2241462272 | bytes 11805696 | tf_op jit(solution)/shard_map/dot_general | solution.py:29
  438.4 8.0 %fusion.121 = f32[1792,1216]{1,0:T(8,128)} fusion(bf16[1216,512]{1,0:T(8,128)(2,1)S(1)} %get-tuple-element.102, f32[1792]{0:T(1024)S(1)} %copy-done.86, f32[512]{0:T(512)S(1)} %get-tuple-element.204, bf16[448,512]{1,0:T(8,128)(2,1)S(1)} %get-tuple-element.171, bf16[448,512]{1,0:T(8,128)(2,1)S(1)} %get-tuple-element.170, ...), kind=kOutput, calls=%fused_computation.385 | convolution fusion | flops 2241462272 | bytes 11805696 | tf_op jit(solution)/shard_map/dot_general | solution.py:29
  453.2 8.1 %add_convert_fusion.2 = bf16[1792,1216]{1,0:T(8,128)(2,1)S(1)} fusion(f32[1792,1216]{1,0:T(8,128)} %fusion.121, bf16[1216,512]{1,0:T(8,128)(2,1)S(1)} %copy-done.102, f32[512]{0:T(512)S(1)} %get-tuple-element.208, f32[1792]{0:T(1024)S(1)} %copy-done.86, bf16[448,512]{1,0:T(8,128)(2,1)S(1)} %copy-done.27, bf16[448,512]{1,0:T(8,128)(2,1)S(1)} %copy-done.25, ...), kind=kOutput, calls=%fused_computation.2 | convolution fusion | flops 2245820416 | bytes 16163840 | tf_op jit(solution)/shard_map/dot_general | solution.py:29
  464.2 8.0 %add_convert_fusion.1 = bf16[1792,1216]{1,0:T(8,128)(2,1)S(1)} fusion(f32[1792,1216]{1,0:T(8,128)} %fusion.119, bf16[1216,512]{1,0:T(8,128)(2,1)S(1)} %copy-done.100, f32[512]{0:T(512)S(1)} %get-tuple-element.208, f32[1792]{0:T(1024)S(1)} %copy-done.86, bf16[448,512]{1,0:T(8,128)(2,1)S(1)} %copy-done.27, bf16[448,512]{1,0:T(8,128)(2,1)S(1)} %copy-done.25, ...), kind=kOutput, calls=%fused_computation.1 | convolution fusion | flops 2245820416 | bytes 16163840 | tf_op jit(solution)/shard_map/dot_general | solution.py:29
  474.3 6.9 add_convert_fusion
  494.6 9.8 %collective-permute-done.110 = bf16[224,1216]{1,0:T(8,128)(2,1)S(1)} collective-permute-done((bf16[224,1216]{1,0:T(8,128)(2,1)S(1)}, bf16[224,1216]{1,0:T(8,128)(2,1)S(1)}, u32[]{:S(2)}, u32[]{:S(2)}) %collective-permute-start.110) | collective-permute-done | bytes 544800 | tf_op jit(solution)/shard_map/ppermute | solution.py:91
  505.4 11.3 %collective-permute-done.118 = bf16[224,1216]{1,0:T(8,128)(2,1)S(1)} collective-permute-done((bf16[224,1216]{1,0:T(8,128)(2,1)S(1)}, bf16[224,1216]{1,0:T(8,128)(2,1)S(1)}, u32[]{:S(2)}, u32[]{:S(2)}) %collective-permute-start.118) | collective-permute-done | bytes 544800 | tf_op jit(solution)/shard_map/ppermute | solution.py:91
  521.4 7.6 %collective-permute-done.126 = bf16[224,1216]{1,0:T(8,128)(2,1)S(1)} collective-permute-done((bf16[224,1216]{1,0:T(8,128)(2,1)S(1)}, bf16[224,1216]{1,0:T(8,128)(2,1)S(1)}, u32[]{:S(2)}, u32[]{:S(2)}) %collective-permute-start.126) | collective-permute-done | bytes 544800 | tf_op jit(solution)/shard_map/ppermute | solution.py:91
  534.4 8.0 %collective-permute-done.65 = bf16[448,512]{1,0:T(8,128)(2,1)S(1)} collective-permute-done((bf16[448,512]{1,0:T(8,128)(2,1)S(1)}, bf16[448,512]{1,0:T(8,128)(2,1)S(1)}, u32[]{:S(2)}, u32[]{:S(2)}) %collective-permute-start.65) | collective-permute-done | bytes 458784 | tf_op jit(solution)/shard_map/ppermute | solution.py:34
  572.7 16.8 %collective-permute-done.99 = f32[448]{0:T(512)S(1)} collective-permute-done((f32[448]{0:T(512)S(1)}, f32[448]{0:T(512)S(1)}, u32[]{:S(2)}, u32[]{:S(2)}) %collective-permute-start.99) | collective-permute-done | bytes 1824 | tf_op jit(solution)/shard_map/ppermute | solution.py:166
  618.4 6.1 add_convert_fusion.3
  633.0 9.9 %collective-permute-done.102 = bf16[224,1024]{0,1:T(8,128)(2,1)S(1)} collective-permute-done((bf16[224,1024]{0,1:T(8,128)(2,1)S(1)}, bf16[224,1024]{0,1:T(8,128)(2,1)S(1)}, u32[]{:S(2)}, u32[]{:S(2)}) %collective-permute-start.102) | collective-permute-done | bytes 458784 | tf_op jit(solution)/shard_map/ppermute | solution.py:91
  654.5 6.6 collective-permute-done.103
  666.1 6.8 collective-permute-done.75
  682.6 6.6 collective-permute-done.95
  698.7 7.8 %collective-permute-done.97 = f32[448]{0:T(512)S(1)} collective-permute-done((f32[448]{0:T(512)S(1)}, f32[448]{0:T(512)S(1)}, u32[]{:S(2)}, u32[]{:S(2)}) %collective-permute-start.97) | collective-permute-done | bytes 1824 | tf_op jit(solution)/shard_map/ppermute | solution.py:166
  (693 shorter events, 442.5 us)
Async XLA Ops:
  2.8 37.0 %collective-permute-start = (bf16[224,1024]{0,1:T(8,128)(2,1)S(1)}, bf16[224,1024]{0,1:T(8,128)(2,1)}, u32[]{:S(2)}, u32[]{:S(2)}) collective-permute-start(bf16[224,1024]{0,1:T(8,128)(2,1)S(1)} %pad_maximum_fusion.10), channel_id=1, source_target_pairs={{0,8},{8,16},{16,24},{24,28},{28,20},{20,12},{12,4},{4,0},{1,9},{9... | collective-permute-start | bytes 1376264 | tf_op jit(solution)/shard_map/ppermute | solution.py:91
  5.9 41.3 %collective-permute-start.1 = (bf16[224,1024]{0,1:T(8,128)(2,1)S(1)}, bf16[224,1024]{0,1:T(8,128)(2,1)}, u32[]{:S(2)}, u32[]{:S(2)}) collective-permute-start(bf16[224,1024]{0,1:T(8,128)(2,1)S(1)} %pad_maximum_fusion.10), channel_id=1, source_target_pairs={{0,4},{8,0},{16,8},{24,16},{28,24},{20,28},{12,20},{4,12},{1,5},{9... | collective-permute-start | bytes 1376264 | tf_op jit(solution)/shard_map/ppermute | solution.py:91
  7.3 29.9 %collective-permute-start.13 = (bf16[448,2]{0,1:T(2,128)(2,1)S(1)}, bf16[448,2]{0,1:T(2,128)(2,1)S(1)}, u32[]{:S(2)}, u32[]{:S(2)}) collective-permute-start(bf16[448,2]{0,1:T(2,128)(2,1)S(1)} %pad_maximum_fusion.19), channel_id=1, source_target_pairs={{0,1},{1,0},{2,3},{3,2},{4,5},{5,4},{6,7},{7,6},{8,9},{9,8},{10,11... | collective-permute-start | bytes 5384 | tf_op jit(solution)/shard_map/ppermute | solution.py:34
  9.4 45.0 %collective-permute-start.27 = (bf16[224,1216]{1,0:T(8,128)(2,1)}, bf16[224,1216]{1,0:T(8,128)(2,1)}, u32[]{:S(2)}, u32[]{:S(2)}) collective-permute-start(bf16[224,1216]{1,0:T(8,128)(2,1)} %param.88), channel_id=1, source_target_pairs={{0,8},{8,16},{16,24},{24,28},{28,20},{20,12},{12,4},{4,0},{1,9},{9... | collective-permute-start | bytes 1634312 | tf_op jit(solution)/shard_map/ppermute | solution.py:91
  47.2 32.0 %collective-permute-start.38 = (bf16[224,1216]{1,0:T(8,128)(2,1)S(1)}, bf16[224,1216]{1,0:T(8,128)(2,1)}, u32[]{:S(2)}, u32[]{:S(2)}) collective-permute-start(bf16[224,1216]{1,0:T(8,128)(2,1)S(1)} %copy-done.52), channel_id=1, source_target_pairs={{0,8},{8,16},{16,24},{24,28},{28,20},{20,12},{12,4},{4,0},{1,9},{9... | collective-permute-start | bytes 1634312 | tf_op jit(solution)/shard_map/ppermute | solution.py:91
  94.9 27.6 %collective-permute-start.21 = (bf16[224,1216]{1,0:T(8,128)(2,1)}, bf16[224,1216]{1,0:T(8,128)(2,1)}, u32[]{:S(2)}, u32[]{:S(2)}) collective-permute-start(bf16[224,1216]{1,0:T(8,128)(2,1)} %collective-permute-done.19), channel_id=1, source_target_pairs={{0,8},{8,16},{16,24},{24,28},{28,20},{20,12},{12,4},{4,0},{1,9},{9... | collective-permute-start | bytes 1634312 | tf_op jit(solution)/shard_map/ppermute | solution.py:91
  97.9 31.2 %collective-permute-start.22 = (bf16[224,1216]{1,0:T(8,128)(2,1)}, bf16[224,1216]{1,0:T(8,128)(2,1)}, u32[]{:S(2)}, u32[]{:S(2)}) collective-permute-start(bf16[224,1216]{1,0:T(8,128)(2,1)} %collective-permute-done.20), channel_id=1, source_target_pairs={{0,4},{8,0},{16,8},{24,16},{28,24},{20,28},{12,20},{4,12},{1,5},{9... | collective-permute-start | bytes 1634312 | tf_op jit(solution)/shard_map/ppermute | solution.py:91
  106.5 28.3 %collective-permute-start.40 = (bf16[224,1216]{1,0:T(8,128)(2,1)}, bf16[224,1216]{1,0:T(8,128)(2,1)}, u32[]{:S(2)}, u32[]{:S(2)}) collective-permute-start(bf16[224,1216]{1,0:T(8,128)(2,1)} %collective-permute-done.38), channel_id=1, source_target_pairs={{0,8},{8,16},{16,24},{24,28},{28,20},{20,12},{12,4},{4,0},{1,9},{9... | collective-permute-start | bytes 1634312 | tf_op jit(solution)/shard_map/ppermute | solution.py:91
  112.3 42.8 %collective-permute-start.41 = (bf16[224,1216]{1,0:T(8,128)(2,1)}, bf16[224,1216]{1,0:T(8,128)(2,1)S(1)}, u32[]{:S(2)}, u32[]{:S(2)}) collective-permute-start(bf16[224,1216]{1,0:T(8,128)(2,1)} %copy-done.53), channel_id=1, source_target_pairs={{0,4},{8,0},{16,8},{24,16},{28,24},{20,28},{12,20},{4,12},{1,5},{9... | collective-permute-start | bytes 1634312 | tf_op jit(solution)/shard_map/ppermute | solution.py:91
  116.9 29.0 %collective-permute-start.4 = (bf16[224,1024]{0,1:T(8,128)(2,1)}, bf16[224,1024]{0,1:T(8,128)(2,1)S(1)}, u32[]{:S(2)}, u32[]{:S(2)}) collective-permute-start(bf16[224,1024]{0,1:T(8,128)(2,1)} %collective-permute-done.2), channel_id=1, source_target_pairs={{0,8},{8,16},{16,24},{24,28},{28,20},{20,12},{12,4},{4,0},{1,9},{9... | collective-permute-start | bytes 1376264 | tf_op jit(solution)/shard_map/ppermute | solution.py:91
  122.5 30.1 %collective-permute-start.5 = (bf16[224,1024]{0,1:T(8,128)(2,1)}, bf16[224,1024]{0,1:T(8,128)(2,1)S(1)}, u32[]{:S(2)}, u32[]{:S(2)}) collective-permute-start(bf16[224,1024]{0,1:T(8,128)(2,1)} %collective-permute-done.3), channel_id=1, source_target_pairs={{0,4},{8,0},{16,8},{24,16},{28,24},{20,28},{12,20},{4,12},{1,5},{9... | collective-permute-start | bytes 1376264 | tf_op jit(solution)/shard_map/ppermute | solution.py:91
  129.1 61.3 %collective-permute-start.31 = (bf16[224,1216]{1,0:T(8,128)(2,1)}, bf16[224,1216]{1,0:T(8,128)(2,1)}, u32[]{:S(2)}, u32[]{:S(2)}) collective-permute-start(bf16[224,1216]{1,0:T(8,128)(2,1)} %collective-permute-done.29), channel_id=1, source_target_pairs={{0,8},{8,16},{16,24},{24,28},{28,20},{20,12},{12,4},{4,0},{1,9},{9... | collective-permute-start | bytes 1634312 | tf_op jit(solution)/shard_map/ppermute | solution.py:91
  134.8 59.1 %collective-permute-start.32 = (bf16[224,1216]{1,0:T(8,128)(2,1)}, bf16[224,1216]{1,0:T(8,128)(2,1)}, u32[]{:S(2)}, u32[]{:S(2)}) collective-permute-start(bf16[224,1216]{1,0:T(8,128)(2,1)} %collective-permute-done.30), channel_id=1, source_target_pairs={{0,4},{8,0},{16,8},{24,16},{28,24},{20,28},{12,20},{4,12},{1,5},{9... | collective-permute-start | bytes 1634312 | tf_op jit(solution)/shard_map/ppermute | solution.py:91
  145.9 52.5 %collective-permute-start.23 = (bf16[224,1216]{1,0:T(8,128)(2,1)}, bf16[224,1216]{1,0:T(8,128)(2,1)}, u32[]{:S(2)}, u32[]{:S(2)}) collective-permute-start(bf16[224,1216]{1,0:T(8,128)(2,1)} %collective-permute-done.21), channel_id=1, source_target_pairs={{0,8},{8,16},{16,24},{24,28},{28,20},{20,12},{12,4},{4,0},{1,9},{9... | collective-permute-start | bytes 1634312 | tf_op jit(solution)/shard_map/ppermute | solution.py:91
  155.2 26.5 %collective-permute-start.7 = (bf16[112,1024]{0,1:T(8,128)(2,1)}, bf16[112,1024]{0,1:T(8,128)(2,1)}, u32[]{:S(2)}, u32[]{:S(2)}) collective-permute-start(bf16[112,1024]{0,1:T(8,128)(2,1)} %slice.147), channel_id=1, source_target_pairs={{0,4},{8,0},{16,8},{24,16},{28,24},{20,28},{12,20},{4,12},{1,5},{9... | collective-permute-start | bytes 688136 | tf_op jit(solution)/shard_map/ppermute | solution.py:91
  175.9 38.8 %collective-permute-start.24 = (bf16[224,1216]{1,0:T(8,128)(2,1)}, bf16[224,1216]{1,0:T(8,128)(2,1)}, u32[]{:S(2)}, u32[]{:S(2)}) collective-permute-start(bf16[224,1216]{1,0:T(8,128)(2,1)} %collective-permute-done.22), channel_id=1, source_target_pairs={{0,4},{8,0},{16,8},{24,16},{28,24},{20,28},{12,20},{4,12},{1,5},{9... | collective-permute-start | bytes 1634312 | tf_op jit(solution)/shard_map/ppermute | solution.py:91
  181.6 48.5 %collective-permute-start.42 = (bf16[224,1216]{1,0:T(8,128)(2,1)}, bf16[224,1216]{1,0:T(8,128)(2,1)}, u32[]{:S(2)}, u32[]{:S(2)}) collective-permute-start(bf16[224,1216]{1,0:T(8,128)(2,1)} %collective-permute-done.40), channel_id=1, source_target_pairs={{0,8},{8,16},{16,24},{24,28},{28,20},{20,12},{12,4},{4,0},{1,9},{9... | collective-permute-start | bytes 1634312 | tf_op jit(solution)/shard_map/ppermute | solution.py:91
  190.4 42.1 %collective-permute-start.43 = (bf16[224,1216]{1,0:T(8,128)(2,1)S(1)}, bf16[224,1216]{1,0:T(8,128)(2,1)S(1)}, u32[]{:S(2)}, u32[]{:S(2)}) collective-permute-start(bf16[224,1216]{1,0:T(8,128)(2,1)S(1)} %copy-done.55), channel_id=1, source_target_pairs={{0,4},{8,0},{16,8},{24,16},{28,24},{20,28},{12,20},{4,12},{1,5},{9... | collective-permute-start | bytes 1634312 | tf_op jit(solution)/shard_map/ppermute | solution.py:91
  198.4 57.6 %collective-permute-start.33 = (bf16[112,1216]{1,0:T(8,128)(2,1)S(1)}, bf16[112,1216]{1,0:T(8,128)(2,1)S(1)}, u32[]{:S(2)}, u32[]{:S(2)}) collective-permute-start(bf16[112,1216]{1,0:T(8,128)(2,1)S(1)} %slice.156), channel_id=1, source_target_pairs={{0,8},{8,16},{16,24},{24,28},{28,20},{20,12},{12,4},{4,0},{1,9},{9... | collective-permute-start | bytes 817160 | tf_op jit(solution)/shard_map/ppermute | solution.py:91
  211.9 44.1 %collective-permute-start.34 = (bf16[112,1216]{1,0:T(8,128)(2,1)S(1)}, bf16[112,1216]{1,0:T(8,128)(2,1)S(1)}, u32[]{:S(2)}, u32[]{:S(2)}) collective-permute-start(bf16[112,1216]{1,0:T(8,128)(2,1)S(1)} %slice.157), channel_id=1, source_target_pairs={{0,4},{8,0},{16,8},{24,16},{28,24},{20,28},{12,20},{4,12},{1,5},{9... | collective-permute-start | bytes 817160 | tf_op jit(solution)/shard_map/ppermute | solution.py:91
  233.6 31.9 %collective-permute-start.44 = (bf16[112,1216]{1,0:T(8,128)(2,1)S(1)}, bf16[112,1216]{1,0:T(8,128)(2,1)S(1)}, u32[]{:S(2)}, u32[]{:S(2)}) collective-permute-start(bf16[112,1216]{1,0:T(8,128)(2,1)S(1)} %slice.159), channel_id=1, source_target_pairs={{0,8},{8,16},{16,24},{24,28},{28,20},{20,12},{12,4},{4,0},{1,9},{9... | collective-permute-start | bytes 817160 | tf_op jit(solution)/shard_map/ppermute | solution.py:91
  328.2 42.3 %collective-permute-start.61 = (bf16[448,512]{1,0:T(8,128)(2,1)S(1)}, bf16[448,512]{1,0:T(8,128)(2,1)}, u32[]{:S(2)}, u32[]{:S(2)}) collective-permute-start(bf16[448,512]{1,0:T(8,128)(2,1)S(1)} %get-tuple-element.181), channel_id=1, source_target_pairs={{0,2},{1,3},{2,0},{3,1},{4,6},{5,7},{6,4},{7,5},{8,10},{9,11},{10,... | collective-permute-start | bytes 1376264 | tf_op jit(solution)/shard_map/ppermute | solution.py:34
  438.0 44.6 %collective-permute-start.66 = (f32[1,512]{1,0:T(1,128)S(1)}, f32[1,512]{1,0:T(1,128)S(1)}, u32[]{:S(2)}, u32[]{:S(2)}) collective-permute-start(f32[1,512]{1,0:T(1,128)S(1)} %bitcast.314), channel_id=1, source_target_pairs={{0,1},{1,0},{2,3},{3,2},{4,5},{5,4},{6,7},{7,6},{8,9},{9,8},{10,11... | collective-permute-start | bytes 6152 | tf_op jit(solution)/shard_map/ppermute | solution.py:34
  490.5 28.5 %collective-permute-start.64 = (bf16[2,448,512]{2,1,0:T(8,128)(2,1)S(1)}, bf16[2,448,512]{2,1,0:T(8,128)(2,1)S(1)}, u32[]{:S(2)}, u32[]{:S(2)}) collective-permute-start(bf16[2,448,512]{2,1,0:T(8,128)(2,1)S(1)} %dynamic-slice_bitcast_fusion.3), channel_id=1, source_target_pairs={{0,1},{1,0},{2,3},{3,2},{4,5},{5,4},{6,7},{7,6},{8,9},{9,8},{10,11... | collective-permute-start | bytes 2752520 | tf_op jit(solution)/shard_map/ppermute | solution.py:34
  518.3 30.4 %collective-permute-start.111 = (bf16[224,1216]{1,0:T(8,128)(2,1)S(1)}, bf16[224,1216]{1,0:T(8,128)(2,1)S(1)}, u32[]{:S(2)}, u32[]{:S(2)}) collective-permute-start(bf16[224,1216]{1,0:T(8,128)(2,1)S(1)} %get-tuple-element.133), channel_id=1, source_target_pairs={{0,8},{8,16},{16,24},{24,28},{28,20},{20,12},{12,4},{4,0},{1,9},{9... | collective-permute-start | bytes 1634312 | tf_op jit(solution)/shard_map/ppermute | solution.py:91
  519.0 31.4 %collective-permute-start.115 = (bf16[224,1216]{1,0:T(8,128)(2,1)S(1)}, bf16[224,1216]{1,0:T(8,128)(2,1)S(1)}, u32[]{:S(2)}, u32[]{:S(2)}) collective-permute-start(bf16[224,1216]{1,0:T(8,128)(2,1)S(1)} %get-tuple-element.134), channel_id=1, source_target_pairs={{0,4},{8,0},{16,8},{24,16},{28,24},{20,28},{12,20},{4,12},{1,5},{9... | collective-permute-start | bytes 1634312 | tf_op jit(solution)/shard_map/ppermute | solution.py:91
  520.8 32.8 %collective-permute-start.119 = (bf16[224,1216]{1,0:T(8,128)(2,1)S(1)}, bf16[224,1216]{1,0:T(8,128)(2,1)S(1)}, u32[]{:S(2)}, u32[]{:S(2)}) collective-permute-start(bf16[224,1216]{1,0:T(8,128)(2,1)S(1)} %get-tuple-element.125), channel_id=1, source_target_pairs={{0,8},{8,16},{16,24},{24,28},{28,20},{20,12},{12,4},{4,0},{1,9},{9... | collective-permute-start | bytes 1634312 | tf_op jit(solution)/shard_map/ppermute | solution.py:91
  565.2 78.3 %collective-permute-start.116 = (bf16[224,1216]{1,0:T(8,128)(2,1)S(1)}, bf16[224,1216]{1,0:T(8,128)(2,1)S(1)}, u32[]{:S(2)}, u32[]{:S(2)}) collective-permute-start(bf16[224,1216]{1,0:T(8,128)(2,1)S(1)} %get-tuple-element.132), channel_id=1, source_target_pairs={{0,4},{8,0},{16,8},{24,16},{28,24},{20,28},{12,20},{4,12},{1,5},{9... | collective-permute-start | bytes 1634312 | tf_op jit(solution)/shard_map/ppermute | solution.py:91
  567.7 78.7 %collective-permute-start.112 = (bf16[224,1216]{1,0:T(8,128)(2,1)S(1)}, bf16[224,1216]{1,0:T(8,128)(2,1)}, u32[]{:S(2)}, u32[]{:S(2)}) collective-permute-start(bf16[224,1216]{1,0:T(8,128)(2,1)S(1)} %get-tuple-element.131), channel_id=1, source_target_pairs={{0,8},{8,16},{16,24},{24,28},{28,20},{20,12},{12,4},{4,0},{1,9},{9... | collective-permute-start | bytes 1634312 | tf_op jit(solution)/shard_map/ppermute | solution.py:91
  567.7 111.5 %collective-permute-start.124 = (bf16[224,1216]{1,0:T(8,128)(2,1)S(1)}, bf16[224,1216]{1,0:T(8,128)(2,1)S(1)}, u32[]{:S(2)}, u32[]{:S(2)}) collective-permute-start(bf16[224,1216]{1,0:T(8,128)(2,1)S(1)} %get-tuple-element.124), channel_id=1, source_target_pairs={{0,4},{8,0},{16,8},{24,16},{28,24},{20,28},{12,20},{4,12},{1,5},{9... | collective-permute-start | bytes 1634312 | tf_op jit(solution)/shard_map/ppermute | solution.py:91
  648.7 30.8 %collective-permute-start.120 = (bf16[224,1216]{1,0:T(8,128)(2,1)S(1)}, bf16[224,1216]{1,0:T(8,128)(2,1)S(1)}, u32[]{:S(2)}, u32[]{:S(2)}) collective-permute-start(bf16[224,1216]{1,0:T(8,128)(2,1)S(1)} %get-tuple-element.123), channel_id=1, source_target_pairs={{0,8},{8,16},{16,24},{24,28},{28,20},{20,12},{12,4},{4,0},{1,9},{9... | collective-permute-start | bytes 1634312 | tf_op jit(solution)/shard_map/ppermute | solution.py:91
  648.7 43.8 %collective-permute-start.132 = (bf16[224,1216]{1,0:T(8,128)(2,1)S(1)}, bf16[224,1216]{1,0:T(8,128)(2,1)S(1)}, u32[]{:S(2)}, u32[]{:S(2)}) collective-permute-start(bf16[224,1216]{1,0:T(8,128)(2,1)S(1)} %get-tuple-element.116), channel_id=1, source_target_pairs={{0,4},{8,0},{16,8},{24,16},{28,24},{20,28},{12,20},{4,12},{1,5},{9... | collective-permute-start | bytes 1634312 | tf_op jit(solution)/shard_map/ppermute | solution.py:91
  (218 other events, 3394.3 us)

commit v2 on v1

v2 whole, which is shorter than its diff:
```python
from functools import partial

import jax
import jax.numpy as jnp
from jax import lax
from jax.experimental import pallas as pl
from jax.experimental.pallas import tpu as pltpu
from jax.sharding import PartitionSpec as P

D = 1792
FEAT = 16
HEAD_DIM = 112
EXT = 128
PHI = 160
EPS = 1e-05
BF = jnp.bfloat16
F32 = jnp.float32


def mm_nn(left, right):
    return lax.dot_general(left, right, (((1,), (0,)), ((), ())), preferred_element_type=F32)


def mm_tn(left, right):
    return lax.dot_general(left, right, (((0,), (0,)), ((), ())), preferred_element_type=F32)


def mm_nt(left, right):
    return lax.dot_general(left, right, (((1,), (1,)), ((), ())), preferred_element_type=F32)


def swap(value, bit):
    count = lax.axis_size("wt")
    return lax.ppermute(value, "wt", [(i, i ^ bit) for i in range(count)])


def in_order(own, near, far, both):
    me = lax.axis_index("wt")
    odd, high = (me & 1) == 1, me >= 2
    first = jnp.where(high, far, own), jnp.where(high, both, near)
    second = jnp.where(high, own, far), jnp.where(high, near, both)
    return jnp.concatenate(
        [
            jnp.where(odd, first[1], first[0]),
            jnp.where(odd, first[0], first[1]),
            jnp.where(odd, second[1], second[0]),
            jnp.where(odd, second[0], second[1]),
        ],
        0,
    )


class Spread:
    def __init__(self, block):
        self.block, self.far, self.near = block, swap(block, 2), swap(block, 1)

    def cross(self):
        self.both = swap(self.far, 1)

    def full(self, s=None):
        found = self.block, self.near, self.far, self.both
        return in_order(*(found if s is None else [v[s] for v in found]))


def wt_gather(block):
    spread = Spread(block)
    spread.cross()
    return spread.full()


class Scatter:
    def __init__(self, partial_sum, row=None):
        core = lax.axis_index("wt") & 1
        self.rows, self.columns = partial_sum.shape[0] // 4, partial_sum.shape[1]
        shaped = partial_sum.reshape(2, 2, self.rows, self.columns)
        sent = lax.dynamic_index_in_dim(shaped, 1 - core, 1, keepdims=False)
        self.kept = lax.dynamic_index_in_dim(shaped, core, 1, keepdims=False)
        self.row = row
        self.got = swap(self._with_row(sent, row), 1)

    def _with_row(self, blocks, row):
        if row is None:
            return blocks
        high = row.astype(BF)
        low = (row - high.astype(F32)).astype(BF)
        tail = jnp.concatenate([high, low, jnp.zeros((6, self.columns), BF)], 0)
        tail = jnp.broadcast_to(tail, blocks.shape[:-2] + tail.shape)
        return jnp.concatenate([blocks, tail], -2)

    def _row_of(self, block):
        two = block[self.rows : self.rows + 2].astype(F32)
        return two[:1] + two[1:]

    def _pair(self, which):
        kept = lax.dynamic_index_in_dim(self.kept, which, 0, keepdims=False)
        got = lax.dynamic_index_in_dim(self.got, which, 0, keepdims=False)
        return kept.astype(F32) + got[: self.rows].astype(F32)

    def cross(self):
        self.chip = lax.axis_index("wt") >> 1
        self.half = None if self.row is None else self.row + self._row_of(self.got[0])
        self.last = swap(self._with_row(self._pair(1 - self.chip).astype(BF), self.half), 2)

    def sums(self):
        total = self._pair(self.chip) + self.last[: self.rows].astype(F32)
        return total if self.row is None else (total, self.half + self._row_of(self.last))


def ring_order(count):
    half = count // 2
    return [2 * r for r in range(half)] + [2 * r + 1 for r in reversed(range(half))]


def ringed():
    return lax.axis_size("ctx") == 8


def hop(value, step):
    order = ring_order(lax.axis_size("ctx"))
    count = len(order)
    pairs = [(order[r], order[(r + step) % count]) for r in range(count)]
    return lax.ppermute(value, "ctx", pairs)


def ring_index(*offsets):
    order = ring_order(lax.axis_size("ctx"))
    count = len(order)
    place = {device: r for r, device in enumerate(order)}
    table = [[order[(place[i] + offset) % count] for offset in offsets] for i in range(count)]
    return jnp.array(table, jnp.int32)[lax.axis_index("ctx")]


ANY = pl.BlockSpec(memory_space=pl.ANY)


def assembled(pieces, starts, rows):
    count = len(pieces)

    def kernel(start_ref, *refs):
        out, sems = refs[count], refs[count + 1]
        copies = []
        for k in range(count):
            size = pieces[k].shape[-2]
            at = pl.ds(pl.multiple_of(start_ref[k], 16), size)
            where = out.at[at, :] if len(out.shape) == 2 else out.at[:, at, :]
            copies.append(pltpu.make_async_copy(refs[k], where, sems.at[k]))
            copies[-1].start()
        for copy in copies:
            copy.wait()

    shape = pieces[0].shape[:-2] + (rows, pieces[0].shape[-1])
    return pl.pallas_call(
        kernel,
        name="assemble",
        in_specs=[pl.BlockSpec(memory_space=pltpu.SMEM)] + [ANY] * count,
        out_specs=pl.BlockSpec(memory_space=pltpu.VMEM),
        out_shape=jax.ShapeDtypeStruct(shape, pieces[0].dtype),
        scratch_shapes=[pltpu.SemaphoreType.DMA((count,))],
        compiler_params=pltpu.CompilerParams(vmem_limit_bytes=24 << 20),
        cost_estimate=pl.CostEstimate(flops=0, bytes_accessed=8 << 20, transcendentals=0),
    )(starts, *pieces)


def tie(value, *others):
    return lax.optimization_barrier((value,) + others)[0] if others else value


class Gather:
    def __init__(self, shard):
        self.shard, self.axis = shard, shard.ndim - 2
        self.right, self.left = [shard], [shard]

    def advance(self, *others):
        if not ringed():
            return
        right, left = self.right[-1], self.left[-1]
        if len(self.right) == 4:
            rows = right.shape[self.axis]
            right = lax.slice_in_dim(right, 0, rows // 2, axis=self.axis)
            left = lax.slice_in_dim(left, rows // 2, rows, axis=self.axis)
        if others:
            right, left = lax.optimization_barrier((right, left) + others)[:2]
        self.right.append(hop(right, 1))
        self.left.append(hop(left, -1))

    def here(self):
        return (self.right[-1], self.left[-1]) if ringed() else ()

    def full(self):
        if not ringed():
            return lax.all_gather(self.shard, "ctx", axis=self.axis, tiled=True)
        rows = self.shard.shape[self.axis]
        starts = ring_index(0, -1, -2, -3, 4, 1, 2, 3, 4) * rows
        starts += jnp.array([0] * 8 + [rows // 2], jnp.int32)
        return assembled(self.right + self.left[1:], starts, rows * 8)


def grad_products(lefts, rights, index, got, rows, out, name):
    seqs = len(lefts[0])
    widths = [r[0].shape[0] for r in rights]
    columns = sum(widths)
    chunks = index.shape[0]
    length = lefts[0][0].shape[1]
    half = rows // 2
    n_left, n_right = len(lefts) * seqs, len(rights) * seqs
    same = [k for k in range(len(lefts)) if k and lefts[k][0] is lefts[k - 1][0]]
    unique = [k for k in range(len(lefts)) if k not in same]
    source = []
    for k in range(len(lefts)):
        source.append(len([u for u in unique if u <= k]) - 1)
    if out == "halves":
        shapes = [((half, columns), BF)] * 2
    elif out == "sums":
        shapes = [((rows, columns), BF)] * chunks
    else:
        shapes = [((rows, w), F32) for w in widths]

    def kernel(index_ref, *refs):
        n_l = len(unique) * seqs
        left_refs = refs[:n_l]
        right_refs = refs[n_l : n_l + n_right]
        got_refs = refs[n_l + n_right : n_l + n_right + len(got)]
        rest = refs[n_l + n_right + len(got) :]
        outs, scratch = rest[: len(shapes)], rest[len(shapes) :]
        left_bufs, right_bufs, sems = scratch[:n_l], scratch[n_l : n_l + n_right], scratch[-1]
        copies = {}
        for k in range(len(lefts)):
            for s in range(seqs):
                if k in unique:
                    u = source[k] * seqs + s
                    for c in range(chunks):
                        at = pl.ds(pl.multiple_of(index_ref[c] * rows, 16), rows)
                        key = ("l", u, c)
                        copies[key] = pltpu.make_async_copy(
                            left_refs[u].at[at, :], left_bufs[u].at[c], sems.at[len(copies)]
                        )
                        copies[key].start()
                r = k * seqs + s
                copies["r", r] = pltpu.make_async_copy(
                    right_refs[r], right_bufs[r], sems.at[len(copies)]
                )
                copies["r", r].start()
        first = 0
        for k in range(len(lefts)):
            for s in range(seqs):
                if k in unique:
                    for c in range(chunks):
                        copies["l", source[k] * seqs + s, c].wait()
                copies["r", k * seqs + s].wait()
            for c in range(chunks):
                total = 0.0
                for s in range(seqs):
                    total += mm_nt(
                        left_bufs[source[k] * seqs + s][c], right_bufs[k * seqs + s][...]
                    )
                span = pl.ds(first, widths[k])
                if out == "final":
                    for ref in got_refs:
                        total += ref[:, span].astype(F32)
                    outs[k][...] = total
                elif out == "halves":
                    outs[0][:, span] = total[:half].astype(BF)
                    outs[1][:, span] = total[half:].astype(BF)
                elif got_refs[c].shape[0] == rows:
                    outs[c][:, span] = (total + got_refs[c][:, span].astype(F32)).astype(BF)
                else:
                    more = got_refs[c][:, span].astype(F32)
                    top = total[:half] + more if c == 0 else total[:half]
                    low = total[half:] + more if c == 1 else total[half:]
                    outs[c][:half, span] = top.astype(BF)
                    outs[c][half:, span] = low.astype(BF)
            first += widths[k]

    whole = pl.BlockSpec(memory_space=pltpu.VMEM)
    left_arrays = [lefts[k][s] for k in unique for s in range(seqs)]
    right_arrays = [r[s] for r in rights for s in range(seqs)]
    n_copies = len(left_arrays) * chunks + len(right_arrays)
    flops = 2 * chunks * rows * columns * length * seqs
    return pl.pallas_call(
        kernel,
        name=name,
        in_specs=[pl.BlockSpec(memory_space=pltpu.SMEM)]
        + [ANY] * (len(left_arrays) + len(right_arrays))
        + [whole] * len(got),
        out_specs=[whole] * len(shapes),
        out_shape=[jax.ShapeDtypeStruct(*s) for s in shapes],
        scratch_shapes=[pltpu.VMEM((chunks, rows, length), BF)] * len(left_arrays)
        + [pltpu.VMEM(a.shape, BF) for a in right_arrays]
        + [pltpu.SemaphoreType.DMA((n_copies,))],
        compiler_params=pltpu.CompilerParams(vmem_limit_bytes=40 << 20),
        cost_estimate=pl.CostEstimate(
            flops=flops, bytes_accessed=2 * length * seqs * columns + 4 * rows * columns, transcendentals=0
        ),
    )(index, *left_arrays, *right_arrays, *got)


class Products:
    def __init__(self, lefts, rights, name):
        self.given = lefts, rights
        self.name, self.step = name, 4

    def _kernel(self, index, got, out):
        lefts, rights = self.given
        rows = lefts[0][0].shape[0] // 8
        return grad_products(lefts, rights, index, got, rows, out, f"{self.name}_{self.step}")

    def advance(self, *others):
        if not ringed():
            return others
        if self.step == 4:
            sent = self._kernel(tie(ring_index(4), *others), [], "halves")
        else:
            index = tie(ring_index(self.step, -self.step), *others)
            sent = self._kernel(index, self.got, "sums")
        self.got = [hop(sent[0], 1), hop(sent[1], -1)]
        self.step -= 1
        return tuple(sent)

    def final(self):
        if not ringed():
            found = []
            for left, right in zip(*self.given):
                total = sum(mm_nt(a, b) for a, b in zip(left, right)).astype(BF)
                found.append(lax.psum_scatter(total, "ctx", scatter_dimension=0, tiled=True).astype(F32))
            return found
        return self._kernel(ring_index(0), self.got, "final")


def shifted(value, by):
    count = lax.axis_size("ctx")
    pairs = [(i, i + by) for i in range(count) if 0 <= i + by < count]
    return lax.ppermute(value, "ctx", pairs)


class Before:
    def __init__(self, value, sign):
        self.value, self.sign = value, sign
        if ringed():
            count = lax.axis_size("ctx")
            self.other = lax.ppermute(value, "ctx", [(i, i ^ 1) for i in range(count)])

    def first(self):
        if ringed():
            self.total = (self.value.astype(F32) + self.other.astype(F32)).astype(BF)
            self.one = shifted(self.total, 2 * self.sign)

    def second(self):
        if ringed():
            two = (self.total.astype(F32) + self.one.astype(F32)).astype(BF)
            self.two = shifted(two, 4 * self.sign)

    def result(self):
        count, index = lax.axis_size("ctx"), lax.axis_index("ctx")
        if not ringed():
            everything = lax.all_gather(self.value, "ctx").astype(F32)
            place = jnp.arange(count)
            keep = (place < index) if self.sign > 0 else (place > index)
            keep = keep.reshape((count,) + (1,) * self.value.ndim)
            return jnp.sum(jnp.where(keep, everything, 0.0), 0).astype(BF)
        behind = (index & 1) == (1 if self.sign > 0 else 0)
        result = self.one.astype(F32) + self.two.astype(F32)
        return (result + jnp.where(behind, self.other.astype(F32), 0.0)).astype(BF)


def ctx_total(value):
    if not ringed():
        return lax.psum(value, "ctx")
    for bit in (1, 2, 4):
        value = value + lax.ppermute(value, "ctx", [(i, i ^ bit) for i in range(8)])
    return value


def turned(rows, by):
    return jnp.concatenate([rows[by:], rows[:by]], 0)


def feature_rows(vectors, square, cross, linear):
    length = vectors.shape[1]
    half = FEAT // 2
    pieces = [vectors * vectors * square]
    pieces += [vectors * turned(vectors, by) * cross for by in range(1, half)]
    pieces += [vectors[:half] * vectors[half:] * cross]
    place = lax.broadcasted_iota(jnp.int32, (half, length), 0)
    pieces += [jnp.where(place == 0, 1.0, 0.0), vectors * linear]
    return jnp.concatenate(pieces, 0).astype(BF)


def feature_pull(grad, vectors, square, cross, linear):
    half = FEAT // 2
    total = 2.0 * square * grad[:FEAT] * vectors
    for by in range(1, half):
        part = grad[FEAT * by : FEAT * (by + 1)] * cross
        total += part * turned(vectors, by) + turned(part * vectors, FEAT - by)
    part = grad[FEAT * half : FEAT * half + half] * cross
    total += jnp.concatenate([part * vectors[half:], part * vectors[:half]], 0)
    return total + grad[PHI - FEAT :] * linear


QUERY_SCALE = (1.0 / 32.0, 1.0 / 16.0, 0.25)
KEY_SCALE = (1.0, 1.0, 1.0)


def extended(value, valid):
    place = lax.broadcasted_iota(jnp.int32, (EXT - HEAD_DIM, value.shape[1]), 0)
    tail = jnp.where(place == 0, jnp.broadcast_to(valid, place.shape), 0.0)
    return jnp.concatenate([(value.astype(F32) * valid).astype(BF), tail.astype(BF)], 0)


def causal_of(length):
    key_place = lax.broadcasted_iota(jnp.int32, (length, length), 0)
    query_place = lax.broadcasted_iota(jnp.int32, (length, length), 1)
    return key_place <= query_place


def state_kernel(key_ref, value_ref, valid_ref, state_ref):
    mapped = feature_rows(key_ref[...].astype(F32), *KEY_SCALE)
    state_ref[0] = mm_nt(mapped, extended(value_ref[...], valid_ref[...])).astype(BF)


def attend_kernel(query_ref, key_ref, value_ref, valid_ref, state_ref, mixed_ref, denom_ref):
    query = query_ref[...]
    scores = mm_tn(key_ref[...], query) * 0.25
    weights = jnp.where(causal_of(query.shape[1]), 1.0 + scores + 0.5 * scores * scores, 0.0)
    total = mm_nn(extended(value_ref[...], valid_ref[...]), weights.astype(BF))
    mapped = feature_rows(query.astype(F32), *QUERY_SCALE)
    total += mm_tn(state_ref[0], mapped)
    denom = total[HEAD_DIM : HEAD_DIM + 1]
    denom_ref[0] = denom
    mixed_ref[...] = (total[:HEAD_DIM] / denom).astype(BF)


def spread_kernel(query_ref, grad_ref, mixed_ref, denom_ref, weighted_ref, state_ref):
    weighted = grad_ref[...].astype(F32) / denom_ref[0]
    shift = jnp.sum(weighted * mixed_ref[...].astype(F32), 0, keepdims=True)
    place = lax.broadcasted_iota(jnp.int32, (EXT - HEAD_DIM, weighted.shape[1]), 0)
    tail = jnp.where(place == 0, -jnp.broadcast_to(shift, place.shape), 0.0)
    whole = jnp.concatenate([weighted, tail], 0).astype(BF)
    weighted_ref[0] = whole
    mapped = feature_rows(query_ref[...].astype(F32), *QUERY_SCALE)
    state_ref[0] = mm_nt(mapped, whole).astype(BF)


def local_kernel(
    query_ref, key_ref, value_ref, valid_ref, state_ref, weighted_ref, dq_ref, dk_ref, dv_ref
):
    query, key_in, weighted = query_ref[...], key_ref[...], weighted_ref[0]
    causal = causal_of(query.shape[1])
    scores = mm_tn(key_in, query) * 0.25
    weights = jnp.where(causal, 1.0 + scores + 0.5 * scores * scores, 0.0).astype(BF)
    dv_ref[...] = mm_nt(weighted[:HEAD_DIM], weights) * valid_ref[...]
    slope = mm_tn(extended(value_ref[...], valid_ref[...]), weighted)
    slope = jnp.where(causal, slope * (1.0 + scores), 0.0).astype(BF)
    mapped = mm_nn(state_ref[0], weighted)
    pulled = feature_pull(mapped, query.astype(F32), *QUERY_SCALE)
    dq_ref[...] = (mm_nn(key_in, slope) * 0.25 + pulled).astype(BF)
    dk_ref[...] = mm_nt(query, slope) * 0.25


def later_kernel(key_ref, value_ref, valid_ref, state_ref, dk_in, dv_in, dk_ref, dv_ref):
    key_in = key_ref[...].astype(F32)
    valid = valid_ref[...]
    mapped = mm_nn(state_ref[0], extended(value_ref[...], valid))
    dk_ref[...] = (dk_in[...] + feature_pull(mapped, key_in, *KEY_SCALE)).astype(BF)
    spread = mm_tn(state_ref[0], feature_rows(key_in, *KEY_SCALE))
    dv_ref[...] = (dv_in[...] + spread[:HEAD_DIM] * valid).astype(BF)


def head_call(kernel, name, heads, length, ins, outs, cost):
    specs = {
        "feat": (pl.BlockSpec((FEAT, length), lambda h: (h, 0)), (heads * FEAT, length)),
        "head": (pl.BlockSpec((HEAD_DIM, length), lambda h: (h, 0)), (heads * HEAD_DIM, length)),
        "valid": (pl.BlockSpec((1, length), lambda h: (0, 0)), (1, length)),
        "state": (pl.BlockSpec((1, PHI, EXT), lambda h: (h, 0, 0)), (heads, PHI, EXT)),
        "row": (pl.BlockSpec((1, 1, length), lambda h: (h, 0, 0)), (heads, 1, length)),
        "ext": (pl.BlockSpec((1, EXT, length), lambda h: (h, 0, 0)), (heads, EXT, length)),
    }
    return pl.pallas_call(
        kernel,
        name=name,
        grid=(heads,),
        in_specs=[specs[i][0] for i in ins],
        out_specs=[specs[o][0] for o, _ in outs],
        out_shape=[jax.ShapeDtypeStruct(specs[o][1], kind) for o, kind in outs],
        compiler_params=pltpu.CompilerParams(vmem_limit_bytes=32 << 20),
        cost_estimate=pl.CostEstimate(flops=cost, bytes_accessed=4 << 20, transcendentals=0),
    )


def body(
    hidden_in,
    lengths,
    gain_attn,
    gain_ffn,
    w_query,
    w_key,
    w_value,
    w_output,
    w_gate,
    w_up,
    w_down,
    cotangent,
):
    seqs, length, width = hidden_in.shape
    heads = w_value.shape[1] // HEAD_DIM
    q_rows = heads * FEAT
    both = range(seqs)
    position = lax.axis_index("ctx") * length + jnp.arange(length, dtype=jnp.int32)
    valid = [(position < lengths[s]).astype(F32)[None, :] for s in both]

    hidden = [hidden_in[s].T for s in both]
    call = partial(head_call, heads=heads, length=length)
    flops = heads * 2 * length * length * 256
    qkv_columns = 2 * q_rows + heads * HEAD_DIM
    last = []

    def turn(value, *others):
        return tie(value, *(tuple(last) + others))

    def mark(value):
        last[:] = [value]
        return value

    def normed(full, gain):
        value = full.astype(F32)
        inverse = lax.rsqrt(jnp.sum(value * value, 0, keepdims=True) / D + EPS)
        return inverse, (value * inverse * gain[:, None]).astype(BF)

    spread_in = Spread(hidden_in.transpose(0, 2, 1))
    ring_attn = Gather(jnp.concatenate([w_query, w_key, w_value, w_output.T], 1))
    ring_gate_up = Gather(jnp.stack([w_gate, w_up]))
    ring_down = Gather(w_down.T)
    ring_attn.advance()
    gains = wt_gather(jnp.stack([gain_attn, gain_ffn], 1)).astype(F32)
    ring_attn.advance()
    ring_gate_up.advance(*ring_attn.here())
    spread_in.cross()
    ring_attn.advance()
    grad_out = (cotangent.transpose(0, 2, 1).astype(F32) * jnp.stack(valid)).astype(BF)
    spread_out = Spread(tie(grad_out, spread_in.far))
    ring_attn.advance()
    w_attn = ring_attn.full()
    w_qkv, w_out = w_attn[:, :qkv_columns], w_attn[:, qkv_columns:]
    spread_out.cross()

    inv_one, normed_one, query, key_in, value_in, before = [], [], [], [], [], []
    for s in both:
        inverse, normal = normed(spread_in.full(s), gains[:, 0])
        inv_one.append(inverse)
        normed_one.append(normal)
        qkv = mm_tn(w_qkv, turn(normal)).astype(BF)
        query.append(qkv[:q_rows])
        key_in.append(qkv[q_rows : 2 * q_rows])
        value_in.append(qkv[2 * q_rows :])
        (own,) = call(
            state_kernel, "state", ins=("feat", "head", "valid"), outs=(("state", BF),), cost=flops // 2
        )(key_in[s], value_in[s], valid[s])
        mark(own)
        before.append(Before(own, 1))
    ring_gate_up.advance(*last)
    for s in both:
        before[s].first()
    for s in both:
        before[s].second()
    grad_out_full = [spread_out.full(s) for s in both]

    state, mixed, denom, scatter_attn = [], [], [], []
    for s in both:
        state.append(before[s].result())
        mix, den = call(
            attend_kernel,
            "attend",
            ins=("feat", "feat", "head", "valid", "state"),
            outs=(("head", BF), ("row", F32)),
            cost=flops,
        )(turn(query[s]), key_in[s], value_in[s], valid[s], state[s])
        mixed.append(mix)
        denom.append(den)
        scatter_attn.append(Scatter(mark(mm_nn(w_out, mix).astype(BF))))
    ring_gate_up.advance(*last)
    resid, spread_resid = [], []
    for s in both:
        scatter_attn[s].cross()
    for s in both:
        resid.append(hidden[s].astype(F32) + scatter_attn[s].sums())
        spread_resid.append(Spread(resid[s].astype(BF)))
    ring_gate_up.advance(*last)
    ring_down.advance(*last)
    ring_down.advance()
    for s in both:
        spread_resid[s].cross()

    gate_up = ring_gate_up.full()
    gate_full, up_full = gate_up[0], gate_up[1]
    inv_two, normed_two, gate, up, act = [], [], [], [], []
    for s in both:
        inverse, normal = normed(spread_resid[s].full(), gains[:, 1])
        inv_two.append(inverse)
        normed_two.append(normal)
        ready = turn(normal)
        gate.append(mm_tn(gate_full, ready))
        up.append(mm_tn(up_full, ready))
        act.append(mark((gate[s] * jax.nn.sigmoid(gate[s]) * up[s]).astype(BF)))
    ring_down.advance()
    ring_down.advance()
    down_full = ring_down.full()

    grad_gate, grad_up, scatter_two = [], [], []
    for s in both:
        sig = jax.nn.sigmoid(gate[s])
        d_act = mm_tn(down_full, turn(grad_out_full[s]))
        g_gate = (d_act * up[s] * sig * (1.0 + gate[s] * (1.0 - sig))).astype(BF)
        g_up = (d_act * gate[s] * sig).astype(BF)
        grad_gate.append(g_gate)
        grad_up.append(g_up)
        inner = jnp.sum(
            g_gate.astype(F32) * gate[s] + g_up.astype(F32) * up[s], 0, keepdims=True
        )
        d_norm = mark((mm_nn(gate_full, g_gate) + mm_nn(up_full, g_up)).astype(BF))
        scatter_two.append(Scatter(d_norm, inner))
    scatter_two[0].cross()
    ffn_products = Products(
        [grad_out_full, normed_two, normed_two], [act, grad_gate, grad_up], "ffn_grad"
    )
    mark(ffn_products.advance(*last)[0])
    scatter_two[1].cross()
    scatter_out = []
    for s in both:
        scatter_out.append(Scatter(mark(mm_nn(down_full, turn(act[s])).astype(BF))))

    gain_two = gain_ffn.astype(F32)[:, None]
    gain_one = gain_attn.astype(F32)[:, None]
    gain_two_part, d_resid, spread_grad = 0.0, [], []
    for s in both:
        d_norm, inner = scatter_two[s].sums()
        gain_two_part += jnp.sum(resid[s] * inv_two[s] * d_norm, 1)
        d_resid.append(
            grad_out[s].astype(F32)
            + inv_two[s] * gain_two * d_norm
            - resid[s] * (inv_two[s] * inv_two[s] * inner / D)
        )
        spread_grad.append(Spread(d_resid[s].astype(BF)))
    for s in both:
        spread_grad[s].cross()
    for s in both:
        scatter_out[s].cross()
    resid_full, weighted, after = [], [], []
    for s in both:
        resid_full.append(turn(spread_grad[s].full()))
        g_attn = mm_tn(w_out, resid_full[s]).astype(BF)
        whole, spread = call(
            spread_kernel,
            "spread",
            ins=("feat", "head", "head", "row"),
            outs=(("ext", BF), ("state", BF)),
            cost=flops // 2,
        )(query[s], g_attn, mixed[s], denom[s])
        mark(spread)
        weighted.append(whole)
        after.append(Before(spread, -1))
    mark(ffn_products.advance(*last)[0])
    for s in both:
        after[s].first()
    local = []
    for s in both:
        found = call(
            local_kernel,
            "local",
            ins=("feat", "feat", "head", "valid", "state", "ext"),
            outs=(("feat", BF), ("feat", F32), ("head", F32)),
            cost=flops * 2,
        )(turn(query[s]), key_in[s], value_in[s], valid[s], state[s], weighted[s])
        mark(found[0])
        local.append(found)
        after[s].second()
    layer_out = [(resid[s] + scatter_out[s].sums()).astype(BF) for s in both]

    d_qkv, scatter_one = [], []
    for s in both:
        dq, dk_part, dv_part = local[s]
        dk, dv = call(
            later_kernel,
            "later",
            ins=("feat", "head", "valid", "state", "feat", "head"),
            outs=(("feat", BF), ("head", BF)),
            cost=flops // 2,
        )(turn(key_in[s]), value_in[s], valid[s], after[s].result(), dk_part, dv_part)
        d_qkv.append(jnp.concatenate([dq, dk, dv], 0))
        inner = 0.0
        for grad, made in ((dq, query[s]), (dk, key_in[s]), (dv, value_in[s])):
            inner += jnp.sum(grad.astype(F32) * made.astype(F32), 0, keepdims=True)
        scatter_one.append(Scatter(mark(mm_nn(w_qkv, d_qkv[s]).astype(BF)), inner))
    attn_products = Products([normed_one, resid_full], [d_qkv, mixed], "attn_grad")
    mark(attn_products.advance(*last)[0])
    for s in both:
        scatter_one[s].cross()
    mark(ffn_products.advance(*last)[0])
    mark(attn_products.advance(*last)[0])
    gain_one_part, grad_input = 0.0, []
    for s in both:
        value = hidden[s].astype(F32)
        d_norm, inner = scatter_one[s].sums()
        gain_one_part += jnp.sum(value * inv_one[s] * d_norm, 1)
        grad_input.append(
            d_resid[s]
            + inv_one[s] * gain_one * d_norm
            - value * (inv_one[s] * inv_one[s] * inner / D)
        )
    mark(attn_products.advance(*last)[0])
    mark(ffn_products.advance(*last)[0])
    mark(attn_products.advance(*last)[0])
    gain_grads = ctx_total(jnp.stack([gain_one_part, gain_two_part]))
    down_grad, gate_grad, up_grad = ffn_products.final()
    qkv_grad, out_grad = attn_products.final()

    return (
        jnp.stack([v.T for v in layer_out]),
        jnp.stack([v.T for v in grad_input]),
        gain_grads[0],
        gain_grads[1],
        qkv_grad[:, :q_rows],
        qkv_grad[:, q_rows : 2 * q_rows],
        qkv_grad[:, 2 * q_rows :],
        out_grad.T,
        gate_grad,
        up_grad,
        down_grad.T,
    )


def solution(mesh):
    acts, rows, columns = P(None, "ctx", "wt"), P("ctx", "wt"), P("wt", "ctx")
    in_specs = (acts, P(), P("wt"), P("wt"), rows, rows, rows, columns, rows, rows, columns, acts)
    out_specs = (acts, acts, P("wt"), P("wt"), rows, rows, rows, columns, rows, rows, columns)
    return jax.shard_map(body, mesh=mesh, in_specs=in_specs, out_specs=out_specs, check_vma=False)
```

time: 721 us -> 678 us (0.940)
  Pallas kernels: 17.2 us -> 94.2 us
  matrix products: 116 us -> 48.7 us
  local copies, waits for them, and re-layouts: 112 us -> 47.3 us
  starting transfers between devices: 142 us -> 100 us
  other arithmetic: 42 us -> 72.7 us
  waiting for transfers between devices: 273 us -> 302 us
    ppermute x64 -> x40, waiting for transfers between devices: 101 us -> 187 us  [hop(): return lax.ppermute(value, 'ctx', pairs)]
    dynamic_update_slice x36 -> x0, local copies, waits for them, and re-layouts: 79.7 us -> none  [ctx_gather(): lax.dynamic_update_slice_in_dim(full, piece, ring_index(offset) * rows +...]
    pallas_call x0 -> x13, Pallas kernels: none -> 77 us  [the longest x10 68.6 us: grad_products(): pl.pallas_call(kernel, name=name, in_specs=[pl.BlockSpec(memory_space=plt...]
    dot_general x10 -> x0, matrix products: 62.6 us -> none  [mm_nt(): lax.dot_general(left, right, (((1,), (1,)), ((), ())), preferred_element_...]
    ppermute x6 -> x3, waiting for transfers between devices: 41.1 us -> 5.09 us  [ctx_total(): value = value + lax.ppermute(value, 'ctx', [(i, i ^ bit) for i in range(8)])]
    ppermute x64 -> x40, starting transfers between devices: 80.4 us -> 47.3 us  [hop(): return lax.ppermute(value, 'ctx', pairs)]
    ppermute x51 -> x37, waiting for transfers between devices: 100 us -> 69.7 us  [swap(): return lax.ppermute(value, 'wt', [(i, i ^ bit) for i in range(count)])]
    unnamed x240 -> x236, local copies, waits for them, and re-layouts: 7.36 us -> 33.7 us
  transfers between devices with their start and end apart: 133 -> 92, of which waited for: 55 -> 40; matrix products, arithmetic and copies ran while one was open for 31% -> 15% of each run, Pallas kernels for 2% -> 10%
where the time goes in v2:
time: 678 us; the launch traced here: 669 us
  waiting for transfers between devices  302 us (45%)
  starting transfers between devices  100 us (15%)
  Pallas kernels  94.2 us (14%)
  other arithmetic  72.7 us (11%)
  matrix products  48.7 us (7%)
  local copies, waits for them, and re-layouts  47.3 us (7%)
    ppermute x40, waiting for transfers between devices, hop(): return lax.ppermute(value, 'ctx', pairs)  187 us
    ppermute x37, waiting for transfers between devices, swap(): return lax.ppermute(value, 'wt', [(i, i ^ bit) for i in range(count)])  69.7 us
    pallas_call x10, Pallas kernels, grad_products(): pl.pallas_call(kernel, name=name, in_specs=[pl.BlockSpec(memory_space=plt...  68.6 us
    ppermute x40, starting transfers between devices, hop(): return lax.ppermute(value, 'ctx', pairs)  47.3 us
    unnamed x236, local copies, waits for them, and re-layouts  33.7 us
    dot_general x10, matrix products, mm_tn(): lax.dot_general(left, right, (((0,), (0,)), ((), ())), preferred_element_...  26.8 us
    ppermute x8, waiting for transfers between devices, shifted(): return lax.ppermute(value, 'ctx', pairs)  25.9 us
    ppermute x8, starting transfers between devices, shifted(): return lax.ppermute(value, 'ctx', pairs)  25 us
  transfers between devices with their start and end apart: 92, of which 40 were waited for; matrix products, arithmetic and copies ran while one was open for 15% of the time, Pallas kernels for 10%

profile of v2, /device:TPU:0, one launch (start us, length us, event | category | flops | bytes accessed | tf_op | source)
XLA Modules:
  0.0 668.5 jit_solution(14289778045448853583)
XLA Ops:
  12.5 5.7 collective-permute-done.refs_1_
  23.8 6.1 collective-permute-done.8
  34.8 8.0 %collective-permute-done.2.refs_3_ = bf16[224,1024]{1,0:T(8,128)(2,1)S(1)} collective-permute-done((bf16[224,1024]{1,0:T(8,128)(2,1)S(1)}, bf16[224,1024]{1,0:T(8,128)(2,1)S(1)}, u32[]{:S(2)}, u32[]{:S(2)}) %collective-permute-start.2) | collective-permute-done | bytes 458784 | tf_op jit(solution)/shard_map/ppermute | solution.py:122
  70.8 6.4 fusion.2
  83.6 8.9 %collective-permute-done.14 = bf16[4,160,128]{2,1,0:T(8,128)(2,1)S(1)} collective-permute-done((bf16[4,160,128]{2,1,0:T(8,128)(2,1)S(1)}, bf16[4,160,128]{2,1,0:T(8,128)(2,1)S(1)}, u32[]{:S(2)}, u32[]{:S(2)}) %collective-permute-start.14) | collective-permute-done | bytes 163872 | tf_op jit(solution)/shard_map/ppermute | solution.py:340
  109.7 8.0 %collective-permute-start.16 = (bf16[4,160,128]{2,1,0:T(8,128)(2,1)S(1)}, bf16[4,160,128]{2,1,0:T(8,128)(2,1)S(1)}, u32[]{:S(2)}, u32[]{:S(2)}) collective-permute-start(bf16[4,160,128]{2,1,0:T(8,128)(2,1)S(1)} %fusion.76), channel_id=1, source_target_pairs={{0,16},{4,20},{8,24},{12,28},{1,17},{5,21},{9,25},{13,29},{2,18},{... | collective-permute-start | bytes 491528 | tf_op jit(solution)/shard_map/ppermute | solution.py:332
  120.9 5.8 collective-permute-start.21
  135.4 6.1 collective-permute-start.22
  144.6 10.6 %collective-permute-done.22.refs_1_ = bf16[224,1216]{1,0:T(8,128)(2,1)} collective-permute-done((bf16[224,1216]{1,0:T(8,128)(2,1)}, bf16[224,1216]{1,0:T(8,128)(2,1)}, u32[]{:S(2)}, u32[]{:S(2)}) %collective-permute-start.22) | collective-permute-done | bytes 544800 | tf_op jit(solution)/shard_map/ppermute | solution.py:122
  160.5 22.4 %collective-permute-done.26.refs_5_ = bf16[224,1216]{1,0:T(8,128)(2,1)} collective-permute-done((bf16[224,1216]{1,0:T(8,128)(2,1)}, bf16[224,1216]{1,0:T(8,128)(2,1)}, u32[]{:S(2)}, u32[]{:S(2)}) %collective-permute-start.26) | collective-permute-done | bytes 544800 | tf_op jit(solution)/shard_map/ppermute | solution.py:122
  187.9 7.0 %collective-permute-done.45 = bf16[448,512]{1,0:T(8,128)(2,1)} collective-permute-done((bf16[448,512]{1,0:T(8,128)(2,1)}, bf16[448,512]{1,0:T(8,128)(2,1)}, u32[]{:S(2)}, u32[]{:S(2)}) %collective-permute-start.45) | collective-permute-done | bytes 458784 | tf_op jit(solution)/shard_map/ppermute | solution.py:34
  207.1 27.5 %collective-permute-done.24.refs_3_ = bf16[224,1216]{1,0:T(8,128)(2,1)S(1)} collective-permute-done((bf16[224,1216]{1,0:T(8,128)(2,1)}, bf16[224,1216]{1,0:T(8,128)(2,1)S(1)}, u32[]{:S(2)}, u32[]{:S(2)}) %collective-permute-start.24) | collective-permute-done | bytes 544800 | tf_op jit(solution)/shard_map/ppermute | solution.py:122
  238.9 8.6 %collective-permute-done.38 = bf16[448,512]{1,0:T(8,128)(2,1)S(1)} collective-permute-done((bf16[448,512]{1,0:T(8,128)(2,1)S(1)}, bf16[448,512]{1,0:T(8,128)(2,1)S(1)}, u32[]{:S(2)}, u32[]{:S(2)}) %collective-permute-start.38) | collective-permute-done | bytes 458784 | tf_op jit(solution)/shard_map/ppermute | solution.py:34
  255.1 6.4 fusion.8
  290.4 5.4 add_reduce_fusion
  303.1 8.0 %ffn_grad_4.1 = (bf16[112,3648]{1,0:T(8,128)(2,1)}, bf16[112,3648]{1,0:T(8,128)(2,1)}) custom-call(s32[1]{0:T(128)} %bitcast.26.index_ref, bf16[1792,512]{1,0:T(8,128)(2,1)S(1)} %pad_maximum_fusion.4.refs_0_, bf16[1792,512]{1,0:T(8,128)(2,1)S(1)} %pad_maximum_fusion.3.refs_1_, bf16[1792,512]{1,0:T(8,128)(2,1)} %copy-done.72, bf16[1792,512]{1,0:T(8,128)(2,1)} %copy-done.73, ...), custom_call_target="tpu_custom_call" | custom-call | flops 1673527296 | bytes 10739712 | tf_op jit(solution)/shard_map/ffn_grad_4/pallas_call | solution.py:279
  325.6 9.0 %collective-permute-done.54 = bf16[456,512]{1,0:T(8,128)(2,1)S(1)} collective-permute-done((bf16[456,512]{1,0:T(8,128)(2,1)S(1)}, bf16[456,512]{1,0:T(8,128)(2,1)S(1)}, u32[]{:S(2)}, u32[]{:S(2)}) %collective-permute-start.54) | collective-permute-done | bytes 466976 | tf_op jit(solution)/shard_map/ppermute | solution.py:34
  334.7 9.8 %collective-permute-done.50 = bf16[448,512]{1,0:T(8,128)(2,1)S(1)} collective-permute-done((bf16[448,512]{1,0:T(8,128)(2,1)S(1)}, bf16[448,512]{1,0:T(8,128)(2,1)S(1)}, u32[]{:S(2)}, u32[]{:S(2)}) %collective-permute-start.50) | collective-permute-done | bytes 458784 | tf_op jit(solution)/shard_map/ppermute | solution.py:34
  348.8 15.5 %collective-permute-done.56 = bf16[456,512]{1,0:T(8,128)(2,1)S(1)} collective-permute-done((bf16[456,512]{1,0:T(8,128)(2,1)S(1)}, bf16[456,512]{1,0:T(8,128)(2,1)S(1)}, u32[]{:S(2)}, u32[]{:S(2)}) %collective-permute-start.56) | collective-permute-done | bytes 466976 | tf_op jit(solution)/shard_map/ppermute | solution.py:34
  368.5 5.7 collective-permute-done.60
  377.0 6.6 collective-permute-done.57
  396.4 8.8 %ffn_grad_3.1 = (bf16[224,3648]{1,0:T(8,128)(2,1)}, bf16[224,3648]{1,0:T(8,128)(2,1)S(1)}) custom-call(s32[2]{0:T(128)S(1)} %fusion.117.index_ref, bf16[1792,512]{1,0:T(8,128)(2,1)S(1)} %copy-done.3, bf16[1792,512]{1,0:T(8,128)(2,1)} %copy-done, bf16[1792,512]{1,0:T(8,128)(2,1)} %copy-done.72, bf16[1792,512]{1,0:T(8,128)(2,1)} %copy-done.73, ...), custom_call_target="tpu_custom_call" | custom-call | flops 3347054592 | bytes 10739712 | tf_op jit(solution)/shard_map/ffn_grad_3/pallas_call | solution.py:279
  428.2 11.3 %collective-permute-done.67 = bf16[4,160,128]{2,1,0:T(8,128)(2,1)S(1)} collective-permute-done((bf16[4,160,128]{2,1,0:T(8,128)(2,1)S(1)}, bf16[4,160,128]{2,1,0:T(8,128)(2,1)S(1)}, u32[]{:S(2)}, u32[]{:S(2)}) %collective-permute-start.67) | collective-permute-done | bytes 163872 | tf_op jit(solution)/shard_map/ppermute | solution.py:332
  463.4 25.6 %collective-permute-done.78.refs_10_ = bf16[224,3648]{1,0:T(8,128)(2,1)S(1)} collective-permute-done((bf16[224,3648]{1,0:T(8,128)(2,1)}, bf16[224,3648]{1,0:T(8,128)(2,1)S(1)}, u32[]{:S(2)}, u32[]{:S(2)}) %collective-permute-start.78) | collective-permute-done | bytes 1634336 | tf_op jit(solution)/shard_map/ppermute | solution.py:122
  491.6 8.3 %ffn_grad_2.1 = (bf16[224,3648]{1,0:T(8,128)(2,1)}, bf16[224,3648]{1,0:T(8,128)(2,1)S(1)}) custom-call(s32[2]{0:T(128)S(1)} %fusion.116.index_ref, bf16[1792,512]{1,0:T(8,128)(2,1)} %copy-done.2, bf16[1792,512]{1,0:T(8,128)(2,1)} %copy-done, bf16[1792,512]{1,0:T(8,128)(2,1)} %copy-done.72, bf16[1792,512]{1,0:T(8,128)(2,1)} %copy-done.73, ...), custom_call_target="tpu_custom_call" | custom-call | flops 3347054592 | bytes 10739712 | tf_op jit(solution)/shard_map/ffn_grad_2/pallas_call | solution.py:279
  509.2 34.4 %collective-permute-done.80.refs_8_ = bf16[112,1024]{1,0:T(8,128)(2,1)S(1)} collective-permute-done((bf16[112,1024]{1,0:T(8,128)(2,1)S(1)}, bf16[112,1024]{1,0:T(8,128)(2,1)S(1)}, u32[]{:S(2)}, u32[]{:S(2)}) %collective-permute-start.80) | collective-permute-done | bytes 229408 | tf_op jit(solution)/shard_map/ppermute | solution.py:122
  545.0 5.7 attn_grad_3.1
  561.8 5.9 attn_grad_2.1
  571.1 8.8 %ffn_grad_1.1 = (bf16[224,3648]{1,0:T(8,128)(2,1)}, bf16[224,3648]{1,0:T(8,128)(2,1)}) custom-call(s32[2]{0:T(128)S(1)} %fusion.115.index_ref, bf16[1792,512]{1,0:T(8,128)(2,1)} %copy-done.2, bf16[1792,512]{1,0:T(8,128)(2,1)} %copy-done, bf16[1792,512]{1,0:T(8,128)(2,1)} %copy-done.72, bf16[1792,512]{1,0:T(8,128)(2,1)} %copy-done.73, ...), custom_call_target="tpu_custom_call" | custom-call | flops 3347054592 | bytes 10739712 | tf_op jit(solution)/shard_map/ffn_grad_1/pallas_call | solution.py:279
  586.8 38.4 %collective-permute-done.86.refs_8_ = bf16[224,1024]{1,0:T(8,128)(2,1)S(1)} collective-permute-done((bf16[224,1024]{1,0:T(8,128)(2,1)S(1)}, bf16[224,1024]{1,0:T(8,128)(2,1)S(1)}, u32[]{:S(2)}, u32[]{:S(2)}) %collective-permute-start.86) | collective-permute-done | bytes 458784 | tf_op jit(solution)/shard_map/ppermute | solution.py:122
  625.9 5.7 attn_grad_1.1
  658.9 9.2 %ffn_grad_0.1 = (f32[224,1216]{1,0:T(8,128)}, f32[224,1216]{1,0:T(8,128)}, f32[224,1216]{1,0:T(8,128)}) custom-call(s32[1]{0:T(128)} %bitcast.114.index_ref, bf16[1792,512]{1,0:T(8,128)(2,1)S(1)} %copy-done.4, bf16[1792,512]{1,0:T(8,128)(2,1)S(1)} %copy-done.1, bf16[1792,512]{1,0:T(8,128)(2,1)} %copy-done.72, bf16[1792,512]{1,0:T(8,128)(2,1)} %copy-done.73, ...), custom_call_target="tpu_custom_call" | custom-call | flops 1673527296 | bytes 10739712 | tf_op jit(solution)/shard_map/ffn_grad_0/pallas_call | solution.py:279
  (579 shorter events, 305.6 us)
Async XLA Ops:
  9.6 55.3 %collective-permute-start.10 = (bf16[2,448,512]{2,1,0:T(8,128)(2,1)}, bf16[2,448,512]{2,1,0:T(8,128)(2,1)}, u32[]{:S(2)}, u32[]{:S(2)}) collective-permute-start(bf16[2,448,512]{2,1,0:T(8,128)(2,1)} %bitcast.365), channel_id=1, source_target_pairs={{0,1},{1,0},{2,3},{3,2},{4,5},{5,4},{6,7},{7,6},{8,9},{9,8},{10,11... | collective-permute-start | bytes 2752520 | tf_op jit(solution)/shard_map/ppermute | solution.py:34
  29.8 35.6 %collective-permute-start.9 = (bf16[2,448,512]{2,1,0:T(8,128)(2,1)}, bf16[2,448,512]{2,1,0:T(8,128)(2,1)}, u32[]{:S(2)}, u32[]{:S(2)}) collective-permute-start(bf16[2,448,512]{2,1,0:T(8,128)(2,1)} %collective-permute-done.8), channel_id=1, source_target_pairs={{0,1},{1,0},{2,3},{3,2},{4,5},{5,4},{6,7},{7,6},{8,9},{9,8},{10,11... | collective-permute-start | bytes 2752520 | tf_op jit(solution)/shard_map/ppermute | solution.py:34
  47.9 94.6 %collective-permute-start.43 = (bf16[2,448,512]{2,1,0:T(8,128)(2,1)}, bf16[2,448,512]{2,1,0:T(8,128)(2,1)}, u32[]{:S(2)}, u32[]{:S(2)}) collective-permute-start(bf16[2,448,512]{2,1,0:T(8,128)(2,1)} %fusion.34), channel_id=1, source_target_pairs={{0,1},{1,0},{2,3},{3,2},{4,5},{5,4},{6,7},{7,6},{8,9},{9,8},{10,11... | collective-permute-start | bytes 2752520 | tf_op jit(solution)/shard_map/ppermute | solution.py:34
  52.5 90.5 %collective-permute-start.41 = (bf16[2,448,512]{2,1,0:T(8,128)(2,1)}, bf16[2,448,512]{2,1,0:T(8,128)(2,1)}, u32[]{:S(2)}, u32[]{:S(2)}) collective-permute-start(bf16[2,448,512]{2,1,0:T(8,128)(2,1)} %fusion.34), channel_id=1, source_target_pairs={{0,2},{1,3},{2,0},{3,1},{4,6},{5,7},{6,4},{7,5},{8,10},{9,11},{10,... | collective-permute-start | bytes 2752520 | tf_op jit(solution)/shard_map/ppermute | solution.py:34
  55.2 80.1 %collective-permute-start.30 = (bf16[2,224,1216]{2,1,0:T(8,128)(2,1)S(1)}, bf16[2,224,1216]{2,1,0:T(8,128)(2,1)S(1)}, u32[]{:S(2)}, u32[]{:S(2)}) collective-permute-start(bf16[2,224,1216]{2,1,0:T(8,128)(2,1)S(1)} %pad_maximum_fusion.9.refs_0_), channel_id=1, source_target_pairs={{0,8},{8,16},{16,24},{24,28},{28,20},{20,12},{12,4},{4,0},{1,9},{9... | collective-permute-start | bytes 3268616 | tf_op jit(solution)/shard_map/ppermute | solution.py:122
  64.9 77.6 %collective-permute-start.31 = (bf16[2,224,1216]{2,1,0:T(8,128)(2,1)S(1)}, bf16[2,224,1216]{2,1,0:T(8,128)(2,1)}, u32[]{:S(2)}, u32[]{:S(2)}) collective-permute-start(bf16[2,224,1216]{2,1,0:T(8,128)(2,1)S(1)} %pad_maximum_fusion.9.refs_0_), channel_id=1, source_target_pairs={{0,4},{8,0},{16,8},{24,16},{28,24},{20,28},{12,20},{4,12},{1,5},{9... | collective-permute-start | bytes 3268616 | tf_op jit(solution)/shard_map/ppermute | solution.py:122
  142.5 41.1 %collective-permute-start.32 = (bf16[2,224,1216]{2,1,0:T(8,128)(2,1)S(1)}, bf16[2,224,1216]{2,1,0:T(8,128)(2,1)}, u32[]{:S(2)}, u32[]{:S(2)}) collective-permute-start(bf16[2,224,1216]{2,1,0:T(8,128)(2,1)S(1)} %collective-permute-done.30.refs_1_), channel_id=1, source_target_pairs={{0,8},{8,16},{16,24},{24,28},{28,20},{20,12},{12,4},{4,0},{1,9},{9... | collective-permute-start | bytes 3268616 | tf_op jit(solution)/shard_map/ppermute | solution.py:122
  143.0 41.5 %collective-permute-start.33 = (bf16[2,224,1216]{2,1,0:T(8,128)(2,1)}, bf16[2,224,1216]{2,1,0:T(8,128)(2,1)}, u32[]{:S(2)}, u32[]{:S(2)}) collective-permute-start(bf16[2,224,1216]{2,1,0:T(8,128)(2,1)} %collective-permute-done.31.refs_5_), channel_id=1, source_target_pairs={{0,4},{8,0},{16,8},{24,16},{28,24},{20,28},{12,20},{4,12},{1,5},{9... | collective-permute-start | bytes 3268616 | tf_op jit(solution)/shard_map/ppermute | solution.py:122
  155.2 27.7 %collective-permute-start.26 = (bf16[224,1216]{1,0:T(8,128)(2,1)}, bf16[224,1216]{1,0:T(8,128)(2,1)}, u32[]{:S(2)}, u32[]{:S(2)}) collective-permute-start(bf16[224,1216]{1,0:T(8,128)(2,1)} %bitcast.21.refs_0_), channel_id=1, source_target_pairs={{0,4},{8,0},{16,8},{24,16},{28,24},{20,28},{12,20},{4,12},{1,5},{9... | collective-permute-start | bytes 1634312 | tf_op jit(solution)/shard_map/ppermute | solution.py:122
  155.6 46.7 %collective-permute-start.42 = (bf16[2,448,512]{2,1,0:T(8,128)(2,1)}, bf16[2,448,512]{2,1,0:T(8,128)(2,1)}, u32[]{:S(2)}, u32[]{:S(2)}) collective-permute-start(bf16[2,448,512]{2,1,0:T(8,128)(2,1)} %collective-permute-done.41), channel_id=1, source_target_pairs={{0,1},{1,0},{2,3},{3,2},{4,5},{5,4},{6,7},{7,6},{8,9},{9,8},{10,11... | collective-permute-start | bytes 2752520 | tf_op jit(solution)/shard_map/ppermute | solution.py:34
  157.7 29.3 %collective-permute-start.18 = (bf16[448,512]{1,0:T(8,128)(2,1)}, bf16[448,512]{1,0:T(8,128)(2,1)S(1)}, u32[]{:S(2)}, u32[]{:S(2)}) collective-permute-start(bf16[448,512]{1,0:T(8,128)(2,1)} %fusion.56), channel_id=1, source_target_pairs={{0,2},{1,3},{2,0},{3,1},{4,6},{5,7},{6,4},{7,5},{8,10},{9,11},{10,... | collective-permute-start | bytes 1376264 | tf_op jit(solution)/shard_map/ppermute | solution.py:34
  186.9 49.6 %collective-permute-start.34 = (bf16[2,224,1216]{2,1,0:T(8,128)(2,1)}, bf16[2,224,1216]{2,1,0:T(8,128)(2,1)S(1)}, u32[]{:S(2)}, u32[]{:S(2)}) collective-permute-start(bf16[2,224,1216]{2,1,0:T(8,128)(2,1)} %collective-permute-done.32.refs_2_), channel_id=1, source_target_pairs={{0,8},{8,16},{16,24},{24,28},{28,20},{20,12},{12,4},{4,0},{1,9},{9... | collective-permute-start | bytes 3268616 | tf_op jit(solution)/shard_map/ppermute | solution.py:122
  194.8 42.4 %collective-permute-start.35 = (bf16[2,224,1216]{2,1,0:T(8,128)(2,1)}, bf16[2,224,1216]{2,1,0:T(8,128)(2,1)S(1)}, u32[]{:S(2)}, u32[]{:S(2)}) collective-permute-start(bf16[2,224,1216]{2,1,0:T(8,128)(2,1)} %collective-permute-done.33.refs_6_), channel_id=1, source_target_pairs={{0,4},{8,0},{16,8},{24,16},{28,24},{20,28},{12,20},{4,12},{1,5},{9... | collective-permute-start | bytes 3268616 | tf_op jit(solution)/shard_map/ppermute | solution.py:122
  200.2 34.3 %collective-permute-start.24 = (bf16[224,1216]{1,0:T(8,128)(2,1)}, bf16[224,1216]{1,0:T(8,128)(2,1)S(1)}, u32[]{:S(2)}, u32[]{:S(2)}) collective-permute-start(bf16[224,1216]{1,0:T(8,128)(2,1)} %collective-permute-done.23.refs_2_), channel_id=1, source_target_pairs={{0,8},{8,16},{16,24},{24,28},{28,20},{20,12},{12,4},{4,0},{1,9},{9... | collective-permute-start | bytes 1634312 | tf_op jit(solution)/shard_map/ppermute | solution.py:122
  200.8 34.3 %collective-permute-start.28 = (bf16[224,1216]{1,0:T(8,128)(2,1)}, bf16[224,1216]{1,0:T(8,128)(2,1)S(1)}, u32[]{:S(2)}, u32[]{:S(2)}) collective-permute-start(bf16[224,1216]{1,0:T(8,128)(2,1)} %collective-permute-done.27.refs_6_), channel_id=1, source_target_pairs={{0,4},{8,0},{16,8},{24,16},{28,24},{20,28},{12,20},{4,12},{1,5},{9... | collective-permute-start | bytes 1634312 | tf_op jit(solution)/shard_map/ppermute | solution.py:122
  202.3 34.0 %collective-permute-start.46 = (bf16[448,512]{1,0:T(8,128)(2,1)S(1)}, bf16[448,512]{1,0:T(8,128)(2,1)S(1)}, u32[]{:S(2)}, u32[]{:S(2)}) collective-permute-start(bf16[448,512]{1,0:T(8,128)(2,1)S(1)} %get-tuple-element.246), channel_id=1, source_target_pairs={{0,2},{1,3},{2,0},{3,1},{4,6},{5,7},{6,4},{7,5},{8,10},{9,11},{10,... | collective-permute-start | bytes 1376264 | tf_op jit(solution)/shard_map/ppermute | solution.py:34
  323.5 40.8 %collective-permute-start.52 = (bf16[448,512]{1,0:T(8,128)(2,1)S(1)}, bf16[448,512]{1,0:T(8,128)(2,1)S(1)}, u32[]{:S(2)}, u32[]{:S(2)}) collective-permute-start(bf16[448,512]{1,0:T(8,128)(2,1)S(1)} %fusion.45), channel_id=1, source_target_pairs={{0,2},{1,3},{2,0},{3,1},{4,6},{5,7},{6,4},{7,5},{8,10},{9,11},{10,... | collective-permute-start | bytes 1376264 | tf_op jit(solution)/shard_map/ppermute | solution.py:34
  324.8 39.5 %collective-permute-start.56 = (bf16[456,512]{1,0:T(8,128)(2,1)S(1)}, bf16[456,512]{1,0:T(8,128)(2,1)S(1)}, u32[]{:S(2)}, u32[]{:S(2)}) collective-permute-start(bf16[456,512]{1,0:T(8,128)(2,1)S(1)} %get-tuple-element.259), channel_id=1, source_target_pairs={{0,2},{1,3},{2,0},{3,1},{4,6},{5,7},{6,4},{7,5},{8,10},{9,11},{10,... | collective-permute-start | bytes 1400840 | tf_op jit(solution)/shard_map/ppermute | solution.py:34
  347.5 26.7 %collective-permute-start.60 = (bf16[448,512]{1,0:T(8,128)(2,1)}, bf16[448,512]{1,0:T(8,128)(2,1)}, u32[]{:S(2)}, u32[]{:S(2)}) collective-permute-start(bf16[448,512]{1,0:T(8,128)(2,1)} %get-tuple-element.191), channel_id=1, source_target_pairs={{0,2},{1,3},{2,0},{3,1},{4,6},{5,7},{6,4},{7,5},{8,10},{9,11},{10,... | collective-permute-start | bytes 1376264 | tf_op jit(solution)/shard_map/ppermute | solution.py:34
  450.5 38.4 %collective-permute-start.78 = (bf16[224,3648]{1,0:T(8,128)(2,1)}, bf16[224,3648]{1,0:T(8,128)(2,1)S(1)}, u32[]{:S(2)}, u32[]{:S(2)}) collective-permute-start(bf16[224,3648]{1,0:T(8,128)(2,1)} %get-tuple-element.116), channel_id=1, source_target_pairs={{0,8},{8,16},{16,24},{24,28},{28,20},{20,12},{12,4},{4,0},{1,9},{9... | collective-permute-start | bytes 4902920 | tf_op jit(solution)/shard_map/ppermute | solution.py:122
  450.5 38.4 %collective-permute-start.79 = (bf16[224,3648]{1,0:T(8,128)(2,1)S(1)}, bf16[224,3648]{1,0:T(8,128)(2,1)S(1)}, u32[]{:S(2)}, u32[]{:S(2)}) collective-permute-start(bf16[224,3648]{1,0:T(8,128)(2,1)S(1)} %copy-done.64), channel_id=1, source_target_pairs={{0,4},{8,0},{16,8},{24,16},{28,24},{20,28},{12,20},{4,12},{1,5},{9... | collective-permute-start | bytes 4902920 | tf_op jit(solution)/shard_map/ppermute | solution.py:122
  462.1 89.2 %collective-permute-start.69 = (bf16[456,512]{1,0:T(8,128)(2,1)}, bf16[456,512]{1,0:T(8,128)(2,1)}, u32[]{:S(2)}, u32[]{:S(2)}) collective-permute-start(bf16[456,512]{1,0:T(8,128)(2,1)} %get-tuple-element.254), channel_id=1, source_target_pairs={{0,2},{1,3},{2,0},{3,1},{4,6},{5,7},{6,4},{7,5},{8,10},{9,11},{10,... | collective-permute-start | bytes 1400840 | tf_op jit(solution)/shard_map/ppermute | solution.py:34
  501.2 67.3 %collective-permute-start.84 = (bf16[224,3648]{1,0:T(8,128)(2,1)}, bf16[224,3648]{1,0:T(8,128)(2,1)S(1)}, u32[]{:S(2)}, u32[]{:S(2)}) collective-permute-start(bf16[224,3648]{1,0:T(8,128)(2,1)} %get-tuple-element.137), channel_id=1, source_target_pairs={{0,8},{8,16},{16,24},{24,28},{28,20},{20,12},{12,4},{4,0},{1,9},{9... | collective-permute-start | bytes 4902920 | tf_op jit(solution)/shard_map/ppermute | solution.py:122
  501.5 67.0 %collective-permute-start.85 = (bf16[224,3648]{1,0:T(8,128)(2,1)}, bf16[224,3648]{1,0:T(8,128)(2,1)S(1)}, u32[]{:S(2)}, u32[]{:S(2)}) collective-permute-start(bf16[224,3648]{1,0:T(8,128)(2,1)} %copy-done.65), channel_id=1, source_target_pairs={{0,4},{8,0},{16,8},{24,16},{28,24},{20,28},{12,20},{4,12},{1,5},{9... | collective-permute-start | bytes 4902920 | tf_op jit(solution)/shard_map/ppermute | solution.py:122
  504.5 39.2 %collective-permute-start.80 = (bf16[112,1024]{1,0:T(8,128)(2,1)S(1)}, bf16[112,1024]{1,0:T(8,128)(2,1)S(1)}, u32[]{:S(2)}, u32[]{:S(2)}) collective-permute-start(bf16[112,1024]{1,0:T(8,128)(2,1)S(1)} %get-tuple-element.134), channel_id=1, source_target_pairs={{0,8},{8,16},{16,24},{24,28},{28,20},{20,12},{12,4},{4,0},{1,9},{9... | collective-permute-start | bytes 688136 | tf_op jit(solution)/shard_map/ppermute | solution.py:122
  504.8 40.3 %collective-permute-start.81 = (bf16[112,1024]{1,0:T(8,128)(2,1)S(1)}, bf16[112,1024]{1,0:T(8,128)(2,1)S(1)}, u32[]{:S(2)}, u32[]{:S(2)}) collective-permute-start(bf16[112,1024]{1,0:T(8,128)(2,1)S(1)} %get-tuple-element.139), channel_id=1, source_target_pairs={{0,4},{8,0},{16,8},{24,16},{28,24},{20,28},{12,20},{4,12},{1,5},{9... | collective-permute-start | bytes 688136 | tf_op jit(solution)/shard_map/ppermute | solution.py:122
  558.5 27.6 %collective-permute-start.75 = (f32[2,448]{1,0:T(2,128)S(1)}, f32[2,448]{1,0:T(2,128)S(1)}, u32[]{:S(2)}, u32[]{:S(2)}) collective-permute-start(f32[2,448]{1,0:T(2,128)S(1)} %pad_maximum_fusion.24), channel_id=1, source_target_pairs={{0,4},{4,0},{8,12},{12,8},{16,20},{20,16},{24,28},{28,24},{1,5},{5... | collective-permute-start | bytes 10760 | tf_op jit(solution)/shard_map/ppermute | solution.py:369
  579.9 71.0 %collective-permute-start.90 = (bf16[224,3648]{1,0:T(8,128)(2,1)}, bf16[224,3648]{1,0:T(8,128)(2,1)}, u32[]{:S(2)}, u32[]{:S(2)}) collective-permute-start(bf16[224,3648]{1,0:T(8,128)(2,1)} %get-tuple-element.146), channel_id=1, source_target_pairs={{0,8},{8,16},{16,24},{24,28},{28,20},{20,12},{12,4},{4,0},{1,9},{9... | collective-permute-start | bytes 4902920 | tf_op jit(solution)/shard_map/ppermute | solution.py:122
  580.5 70.4 %collective-permute-start.91 = (bf16[224,3648]{1,0:T(8,128)(2,1)}, bf16[224,3648]{1,0:T(8,128)(2,1)}, u32[]{:S(2)}, u32[]{:S(2)}) collective-permute-start(bf16[224,3648]{1,0:T(8,128)(2,1)} %get-tuple-element.153), channel_id=1, source_target_pairs={{0,4},{8,0},{16,8},{24,16},{28,24},{20,28},{12,20},{4,12},{1,5},{9... | collective-permute-start | bytes 4902920 | tf_op jit(solution)/shard_map/ppermute | solution.py:122
  582.0 43.3 %collective-permute-start.86 = (bf16[224,1024]{1,0:T(8,128)(2,1)S(1)}, bf16[224,1024]{1,0:T(8,128)(2,1)S(1)}, u32[]{:S(2)}, u32[]{:S(2)}) collective-permute-start(bf16[224,1024]{1,0:T(8,128)(2,1)S(1)} %copy-done.67), channel_id=1, source_target_pairs={{0,8},{8,16},{16,24},{24,28},{28,20},{20,12},{12,4},{4,0},{1,9},{9... | collective-permute-start | bytes 1376264 | tf_op jit(solution)/shard_map/ppermute | solution.py:122
  582.6 43.3 %collective-permute-start.87 = (bf16[224,1024]{1,0:T(8,128)(2,1)S(1)}, bf16[224,1024]{1,0:T(8,128)(2,1)S(1)}, u32[]{:S(2)}, u32[]{:S(2)}) collective-permute-start(bf16[224,1024]{1,0:T(8,128)(2,1)S(1)} %get-tuple-element.148), channel_id=1, source_target_pairs={{0,4},{8,0},{16,8},{24,16},{28,24},{20,28},{12,20},{4,12},{1,5},{9... | collective-permute-start | bytes 1376264 | tf_op jit(solution)/shard_map/ppermute | solution.py:122
  586.2 47.5 %collective-permute-start.76 = (f32[2,448]{1,0:T(2,128)S(1)}, f32[2,448]{1,0:T(2,128)S(1)}, u32[]{:S(2)}, u32[]{:S(2)}) collective-permute-start(f32[2,448]{1,0:T(2,128)S(1)} %fusion.122), channel_id=1, source_target_pairs={{0,8},{4,12},{8,0},{12,4},{16,24},{20,28},{24,16},{28,20},{1,9},{5... | collective-permute-start | bytes 10760 | tf_op jit(solution)/shard_map/ppermute | solution.py:369
  (173 other events, 2157.2 us)

commit v3 on v1

v3 whole, which is shorter than its diff:
```python
import jax
import jax.numpy as jnp
from jax import lax
from jax.experimental import pallas as pl
from jax.experimental.pallas import tpu as pltpu
from jax.sharding import PartitionSpec as P


D = 1792
FEAT = 16
HEAD_DIM = 112
EXT = 128
PHI = 160
EPS = 1e-05
BF = jnp.bfloat16
F32 = jnp.float32
ANY = pl.BlockSpec(memory_space=pl.ANY)
WHOLE = pl.BlockSpec(memory_space=pltpu.VMEM)
SMEM = pl.BlockSpec(memory_space=pltpu.SMEM)
OFFSETS = (0, 1, 2, 3, 4, -1, -2, -3)
PLACE = {offset: 1 + k for k, offset in enumerate(OFFSETS)}
PLACE[-4] = PLACE[4]


def mm_nn(left, right):
    return lax.dot_general(left, right, (((1,), (0,)), ((), ())), preferred_element_type=F32)


def mm_tn(left, right):
    return lax.dot_general(left, right, (((0,), (0,)), ((), ())), preferred_element_type=F32)


def mm_nt(left, right):
    return lax.dot_general(left, right, (((1,), (1,)), ((), ())), preferred_element_type=F32)


def tie(value, *others):
    others = jax.tree.leaves(others)
    return lax.optimization_barrier((value, *others))[0] if others else value


def params(mib=24):
    return pltpu.CompilerParams(vmem_limit_bytes=mib << 20)


def cost(flops=0, moved=4 << 20):
    return pl.CostEstimate(flops=flops, bytes_accessed=moved, transcendentals=0)


def swap(value, bit):
    count = lax.axis_size("wt")
    return lax.ppermute(value, "wt", [(i, i ^ bit) for i in range(count)])


class Spread:
    def __init__(self, block):
        self.block, self.far, self.near = block, swap(block, 2), swap(block, 1)

    def cross(self):
        self.both = swap(self.far, 1)

    def blocks(self):
        return self.block, self.near, self.far, self.both


def gathered(index, blocks, gains=None, column=0):
    seqs, rows, length = blocks[0].shape

    def kernel(index_ref, *refs):
        values = [ref[0] for ref in refs[:4]]
        out = refs[8 if gains is not None else 4]
        if gains is not None:
            values = [v.astype(F32) for v in values]
            total = sum(jnp.sum(v * v, 0, keepdims=True) for v in values)
            inverse = lax.rsqrt(total / D + EPS)
            refs[9][0] = inverse
            scaled = []
            for v, gain_ref in zip(values, refs[4:8]):
                gain = gain_ref[...][:, column : column + 1].astype(F32)
                scaled.append((v * inverse * gain).astype(BF))
            values = scaled
        me = index_ref[0]
        for bit in range(4):
            out[pl.ds(pl.multiple_of((me ^ bit) * rows, 16), rows), :] = values[bit]

    block = pl.BlockSpec((1, rows, length), lambda s, index_ref: (s, 0, 0))
    full = pl.BlockSpec((4 * rows, length), lambda s, index_ref: (0, s))
    row = pl.BlockSpec((1, 1, length), lambda s, index_ref: (s, 0, 0))
    gain = pl.BlockSpec((rows, 2), lambda s, index_ref: (0, 0))
    shape = jax.ShapeDtypeStruct((4 * rows, seqs * length), BF)
    inverse = jax.ShapeDtypeStruct((seqs, 1, length), F32)
    normed = gains is not None
    return pl.pallas_call(
        kernel,
        name="gather_norm" if normed else "gather",
        grid_spec=pltpu.PrefetchScalarGridSpec(
            num_scalar_prefetch=1,
            grid=(seqs,),
            in_specs=[block] * 4 + ([gain] * 4 if normed else []),
            out_specs=[full, row] if normed else full,
        ),
        out_shape=[shape, inverse] if normed else shape,
        compiler_params=params(),
        cost_estimate=cost(1 << 30),
    )(index, *blocks, *(gains if normed else ()))


def projected(index, weights, rights, name, columns=None, row=None):
    rows = D // 4
    depth, width = rights[0].shape
    extra = 0 if row is None else 8
    start = 0 if columns is None else columns
    stacked = weights.ndim == 3

    def kernel(index_ref, weight_ref, *refs):
        right_refs = refs[: len(rights)]
        sent, kept = refs[-2:]
        total = 0.0
        for k, right in enumerate(right_refs):
            left = weight_ref[k] if stacked else weight_ref[...][:, start : start + depth]
            total += mm_nn(left, right[...])
        step = pl.program_id(0)
        total = total.astype(BF)

        @pl.when(step < 2)
        def _():
            sent[0, :rows] = total
            if row is not None:
                value = refs[len(rights)][...]
                high = value.astype(BF).astype(F32)
                place = lax.broadcasted_iota(jnp.int32, (8, width), 0)
                tail = jnp.where(place == 0, high, jnp.where(place == 1, value - high, 0.0))
                sent[0, rows:] = tail.astype(BF)

        @pl.when(step >= 2)
        def _():
            kept[0] = total

    def of(i, index_ref):
        core = index_ref[0] % 2
        return (i % 2) * 2 + jnp.where(i < 2, 1 - core, core)

    if stacked:
        left_spec = pl.BlockSpec((len(rights), rows, depth), lambda i, r: (0, of(i, r), 0))
    else:
        left_spec = pl.BlockSpec((rows, weights.shape[1]), lambda i, r: (of(i, r), 0))
    in_specs = [left_spec] + [pl.BlockSpec((depth, width), lambda i, r: (0, 0))] * len(rights)
    if row is not None:
        in_specs.append(pl.BlockSpec((1, width), lambda i, r: (0, 0)))
    return pl.pallas_call(
        kernel,
        name=name,
        grid_spec=pltpu.PrefetchScalarGridSpec(
            num_scalar_prefetch=1,
            grid=(4,),
            in_specs=in_specs,
            out_specs=[
                pl.BlockSpec((1, rows + extra, width), lambda i, r: (jnp.minimum(i, 1), 0, 0)),
                pl.BlockSpec((1, rows, width), lambda i, r: (jnp.maximum(i - 2, 0), 0, 0)),
            ],
        ),
        out_shape=[
            jax.ShapeDtypeStruct((2, rows + extra, width), BF),
            jax.ShapeDtypeStruct((2, rows, width), BF),
        ],
        compiler_params=params(32),
        cost_estimate=cost(2 * D * depth * len(rights) * width, 8 << 20),
    )(index, weights, *rights, *(() if row is None else (row,)))


class Scatter:
    def __init__(self, index, parts, seqs, row=None):
        self.index, self.row, self.seqs = index, row, seqs
        self.sent, self.kept = parts
        self.got = swap(self.sent, 1)

    def cross(self):
        seqs, row = self.seqs, self.row
        rows, width = self.kept.shape[1:]
        length = width // seqs
        extra = 0 if row is None else 8

        def kernel(index_ref, kept_ref, got_ref, *refs):
            far, mine = refs[-2:] if row is None else refs[-3:-1]
            chip = index_ref[0] // 2
            other = kept_ref[1 - chip].astype(F32) + got_ref[1 - chip, :rows].astype(F32)
            far[0, :rows] = other.astype(BF)
            mine[0] = kept_ref[chip].astype(F32) + got_ref[chip, :rows].astype(F32)
            if row is not None:
                two = got_ref[0, rows:].astype(F32)
                value = refs[0][...] + two[:1] + two[1:2]
                refs[-1][0] = value
                high = value.astype(BF).astype(F32)
                place = lax.broadcasted_iota(jnp.int32, (8, length), 0)
                tail = jnp.where(place == 0, high, jnp.where(place == 1, value - high, 0.0))
                far[0, rows:] = tail.astype(BF)

        def spec(height):
            return pl.BlockSpec((1, height, length), lambda s, r: (s, 0, 0))

        out = [((seqs, rows + extra, length), BF), ((seqs, rows, length), F32)]
        out += [] if row is None else [((seqs, 1, length), F32)]
        in_specs = [
            pl.BlockSpec((2, rows, length), lambda s, r: (0, 0, s)),
            pl.BlockSpec((2, rows + extra, length), lambda s, r: (0, 0, s)),
        ]
        in_specs += [] if row is None else [pl.BlockSpec((1, length), lambda s, r: (0, s))]
        found = pl.pallas_call(
            kernel,
            name="pair_sum",
            grid_spec=pltpu.PrefetchScalarGridSpec(
                num_scalar_prefetch=1,
                grid=(seqs,),
                in_specs=in_specs,
                out_specs=[spec(shape[1]) for shape, _ in out],
            ),
            out_shape=[jax.ShapeDtypeStruct(*o) for o in out],
            compiler_params=params(),
            cost_estimate=cost(1 << 28),
        )(self.index, self.kept, self.got, *(() if row is None else (row,)))
        self.sent_far, self.mine, self.rows = found[0], found[1], rows
        self.half = None if row is None else found[2]
        self.last = swap(self.sent_far, 2)

    def sums(self, *others):
        last = tie(self.last, *others)
        total = self.mine + last[:, : self.rows].astype(F32)
        if self.row is None:
            return total
        two = last[:, self.rows : self.rows + 2].astype(F32)
        return total, self.half + two[:, :1] + two[:, 1:]


def ring_order(count):
    half = count // 2
    return [2 * r for r in range(half)] + [2 * r + 1 for r in reversed(range(half))]


def ringed():
    return lax.axis_size("ctx") == 8


def hop(value, step):
    order = ring_order(lax.axis_size("ctx"))
    count = len(order)
    pairs = [(order[r], order[(r + step) % count]) for r in range(count)]
    return lax.ppermute(value, "ctx", pairs)


def places():
    count = lax.axis_size("ctx")
    order = ring_order(count)
    place = {device: r for r, device in enumerate(order)}
    table = [[0] + [order[(place[i] + offset) % count] for offset in OFFSETS] for i in range(count)]
    found = jnp.array(table, jnp.int32)[lax.axis_index("ctx")]
    return found + jnp.where(jnp.arange(len(OFFSETS) + 1) == 0, lax.axis_index("wt"), 0)


class Gather:
    def __init__(self, shard):
        self.shard, self.axis = shard, shard.ndim - 2
        self.right, self.left = [shard], [shard]

    def advance(self, *others):
        if not ringed():
            return
        right, left = self.right[-1], self.left[-1]
        if len(self.right) == 4:
            rows = right.shape[self.axis]
            right = lax.slice_in_dim(right, 0, rows // 2, axis=self.axis)
            left = lax.slice_in_dim(left, rows // 2, rows, axis=self.axis)
        others = jax.tree.leaves(others)
        if others:
            right, left = lax.optimization_barrier((right, left, *others))[:2]
        self.right.append(hop(right, 1))
        self.left.append(hop(left, -1))

    def here(self):
        return (self.right[-1], self.left[-1]) if ringed() else ()

    def full(self, index):
        if not ringed():
            return lax.all_gather(self.shard, "ctx", axis=self.axis, tiled=True)
        rows = self.shard.shape[self.axis]
        pieces = self.right + self.left[1:]
        offsets = (0, -1, -2, -3, 4, 1, 2, 3, 4)
        count = len(pieces)

        def kernel(index_ref, *refs):
            out, sems = refs[count], refs[count + 1]
            copies = []
            for k in range(count):
                first = index_ref[PLACE[offsets[k]]] * rows + (rows // 2 if k == 8 else 0)
                at = pl.ds(pl.multiple_of(first, 16), pieces[k].shape[-2])
                where = out.at[at, :] if len(out.shape) == 2 else out.at[:, at, :]
                copies.append(pltpu.make_async_copy(refs[k], where, sems.at[k]))
                copies[-1].start()
            for copy in copies:
                copy.wait()

        shape = self.shard.shape[:-2] + (rows * 8, self.shard.shape[-1])
        return pl.pallas_call(
            kernel,
            name="assemble",
            in_specs=[SMEM] + [ANY] * count,
            out_specs=WHOLE,
            out_shape=jax.ShapeDtypeStruct(shape, BF),
            scratch_shapes=[pltpu.SemaphoreType.DMA((count,))],
            compiler_params=params(),
            cost_estimate=cost(),
        )(index, *pieces)


def products(lefts, rights, name):
    rows, length = lefts[0].shape
    widths = [r.shape[0] for r in rights]
    used = lefts[:1] if all(left is lefts[0] for left in lefts) else lefts

    def kernel(*refs):
        out = refs[-1]
        first = 0
        for k, width in enumerate(widths):
            left = refs[k if len(used) > 1 else 0]
            out[:, pl.ds(first, width)] = mm_nt(left[...], refs[len(used) + k][...]).astype(BF)
            first += width

    return pl.pallas_call(
        kernel,
        name=name,
        grid=(4,),
        in_specs=[pl.BlockSpec((rows // 4, length), lambda i: (i, 0))] * len(used)
        + [pl.BlockSpec((width, length), lambda i: (0, 0)) for width in widths],
        out_specs=pl.BlockSpec((rows // 4, sum(widths)), lambda i: (i, 0)),
        out_shape=jax.ShapeDtypeStruct((rows, sum(widths)), BF),
        compiler_params=params(32),
        cost_estimate=cost(2 * rows * length * sum(widths), 2 * rows * sum(widths)),
    )(*used, *rights)


class Products:
    def __init__(self, index, full):
        self.index, self.full, self.step, self.sent = index, full, 4, ()
        if ringed():
            self.rows, self.width = full.shape[0] // 8, full.shape[1]
            self._send()

    def _send(self):
        half, step = self.rows // 2, self.step
        first, second = step == 4, step == 3

        def kernel(index_ref, *refs):
            row = pl.program_id(0)
            if first:
                own, right, left = refs

                @pl.when(row == 0)
                def _():
                    right[...] = own[...]

                @pl.when(row == 1)
                def _():
                    left[...] = own[...]

                return
            from_right, from_left, own_right, own_left, right, left = refs
            more_right, more_left = from_right[...].astype(F32), from_left[...].astype(F32)
            if second:
                more_right = jnp.where(row == 0, more_right, 0.0)
                more_left = jnp.where(row == 1, more_left, 0.0)
            right[...] = (own_right[...].astype(F32) + more_right).astype(BF)
            left[...] = (own_left[...].astype(F32) + more_left).astype(BF)

        def own(offset):
            return pl.BlockSpec((half, self.width), lambda i, r: (r[PLACE[offset]] * 2 + i, 0))

        still = pl.BlockSpec((half, self.width), lambda i, r: (0, 0))
        moving = pl.BlockSpec((half, self.width), lambda i, r: (i, 0))
        if first:
            in_specs, out_spec, given, rows = [own(4)], still, (self.full,), half
        else:
            in_specs = [still if second else moving] * 2 + [own(step), own(-step)]
            out_spec, given, rows = moving, (self.right, self.left, self.full, self.full), self.rows
        self.sent = pl.pallas_call(
            kernel,
            name="ring_sum",
            grid_spec=pltpu.PrefetchScalarGridSpec(
                num_scalar_prefetch=1, grid=(2,), in_specs=in_specs, out_specs=[out_spec] * 2
            ),
            out_shape=[jax.ShapeDtypeStruct((rows, self.width), BF)] * 2,
            compiler_params=params(),
            cost_estimate=cost(1 << 24),
        )(self.index, *given)
        self.right, self.left = hop(self.sent[0], 1), hop(self.sent[1], -1)

    def here(self):
        return (self.right, self.left) if ringed() else ()

    def advance(self, *others):
        if ringed():
            self.step -= 1
            self.right = tie(self.right, self.left, *others)
            self._send()

    def final(self, *others):
        if not ringed():
            return lax.psum_scatter(self.full, "ctx", scatter_dimension=0, tiled=True).astype(F32)
        right = tie(self.right, self.left, *others)

        def kernel(index_ref, own, right_ref, left_ref, out):
            out[...] = own[...].astype(F32) + right_ref[...].astype(F32) + left_ref[...].astype(F32)

        half = self.rows // 2
        moving = pl.BlockSpec((half, self.width), lambda i, r: (i, 0))
        own = pl.BlockSpec((half, self.width), lambda i, r: (r[PLACE[0]] * 2 + i, 0))
        return pl.pallas_call(
            kernel,
            name="ring_end",
            grid_spec=pltpu.PrefetchScalarGridSpec(
                num_scalar_prefetch=1, grid=(2,), in_specs=[own, moving, moving], out_specs=moving
            ),
            out_shape=jax.ShapeDtypeStruct((self.rows, self.width), F32),
            compiler_params=params(),
            cost_estimate=cost(1 << 24),
        )(self.index, self.full, right, self.left)


def shifted(value, by):
    count = lax.axis_size("ctx")
    pairs = [(i, i + by) for i in range(count) if 0 <= i + by < count]
    return lax.ppermute(value, "ctx", pairs)


class Before:
    def __init__(self, value, sign):
        self.value, self.sign = value, sign
        self.other = self.one = self.two = self.sent = ()
        if ringed():
            count = lax.axis_size("ctx")
            self.other = lax.ppermute(value, "ctx", [(i, i ^ 1) for i in range(count)])

    def first(self):
        if ringed():
            self.total = (self.value.astype(F32) + self.other.astype(F32)).astype(BF)
            self.one = shifted(self.total, 2 * self.sign)

    def second(self):
        if ringed():
            self.sent = (self.total.astype(F32) + self.one.astype(F32)).astype(BF)
            self.two = shifted(self.sent, 4 * self.sign)

    def result(self):
        count, index = lax.axis_size("ctx"), lax.axis_index("ctx")
        if not ringed():
            everything = lax.all_gather(self.value, "ctx").astype(F32)
            place = jnp.arange(count)
            keep = (place < index) if self.sign > 0 else (place > index)
            keep = keep.reshape((count,) + (1,) * self.value.ndim)
            return jnp.sum(jnp.where(keep, everything, 0.0), 0).astype(BF)
        behind = (index & 1) == (1 if self.sign > 0 else 0)
        result = self.one.astype(F32) + self.two.astype(F32)
        return (result + jnp.where(behind, self.other.astype(F32), 0.0)).astype(BF)


def ctx_total(value):
    if not ringed():
        return lax.psum(value, "ctx")
    for bit in (1, 2, 4):
        value = value + lax.ppermute(value, "ctx", [(i, i ^ bit) for i in range(8)])
    return value


def turned(rows, by):
    return jnp.concatenate([rows[by:], rows[:by]], 0)


def feature_rows(vectors, square, cross, linear):
    length = vectors.shape[1]
    half = FEAT // 2
    pieces = [vectors * vectors * square]
    pieces += [vectors * turned(vectors, by) * cross for by in range(1, half)]
    pieces += [vectors[:half] * vectors[half:] * cross]
    place = lax.broadcasted_iota(jnp.int32, (half, length), 0)
    pieces += [jnp.where(place == 0, 1.0, 0.0), vectors * linear]
    return jnp.concatenate(pieces, 0).astype(BF)


def feature_pull(grad, vectors, square, cross, linear):
    half = FEAT // 2
    total = 2.0 * square * grad[:FEAT] * vectors
    for by in range(1, half):
        part = grad[FEAT * by : FEAT * (by + 1)] * cross
        total += part * turned(vectors, by) + turned(part * vectors, FEAT - by)
    part = grad[FEAT * half : FEAT * half + half] * cross
    total += jnp.concatenate([part * vectors[half:], part * vectors[:half]], 0)
    return total + grad[PHI - FEAT :] * linear


QUERY_SCALE = (1.0 / 32.0, 1.0 / 16.0, 0.25)
KEY_SCALE = (1.0, 1.0, 1.0)


def extended(value, valid):
    place = lax.broadcasted_iota(jnp.int32, (EXT - HEAD_DIM, value.shape[1]), 0)
    tail = jnp.where(place == 0, jnp.broadcast_to(valid, place.shape), 0.0)
    return jnp.concatenate([(value.astype(F32) * valid).astype(BF), tail.astype(BF)], 0)


def causal_of(length):
    key_place = lax.broadcasted_iota(jnp.int32, (length, length), 0)
    query_place = lax.broadcasted_iota(jnp.int32, (length, length), 1)
    return key_place <= query_place


def state_kernel(key_ref, value_ref, valid_ref, state_ref):
    mapped = feature_rows(key_ref[...].astype(F32), *KEY_SCALE)
    state_ref[0, 0] = mm_nt(mapped, extended(value_ref[...], valid_ref[0])).astype(BF)


def attend_kernel(query_ref, key_ref, value_ref, valid_ref, state_ref, mixed_ref, denom_ref):
    query = query_ref[...]
    scores = mm_tn(key_ref[...], query) * 0.25
    weights = jnp.where(causal_of(query.shape[1]), 1.0 + scores + 0.5 * scores * scores, 0.0)
    total = mm_nn(extended(value_ref[...], valid_ref[0]), weights.astype(BF))
    mapped = feature_rows(query.astype(F32), *QUERY_SCALE)
    total += mm_tn(state_ref[0, 0], mapped)
    denom = total[HEAD_DIM : HEAD_DIM + 1]
    denom_ref[0, 0] = denom
    mixed_ref[...] = (total[:HEAD_DIM] / denom).astype(BF)


def spread_kernel(query_ref, grad_ref, mixed_ref, denom_ref, weighted_ref, state_ref):
    weighted = grad_ref[...].astype(F32) / denom_ref[0, 0]
    shift = jnp.sum(weighted * mixed_ref[...].astype(F32), 0, keepdims=True)
    place = lax.broadcasted_iota(jnp.int32, (EXT - HEAD_DIM, weighted.shape[1]), 0)
    tail = jnp.where(place == 0, -jnp.broadcast_to(shift, place.shape), 0.0)
    whole = jnp.concatenate([weighted, tail], 0).astype(BF)
    weighted_ref[0, 0] = whole
    mapped = feature_rows(query_ref[...].astype(F32), *QUERY_SCALE)
    state_ref[0, 0] = mm_nt(mapped, whole).astype(BF)


def local_kernel(
    query_ref, key_ref, value_ref, valid_ref, state_ref, weighted_ref, dq_ref, dk_ref, dv_ref
):
    query, key_in, weighted = query_ref[...], key_ref[...], weighted_ref[0, 0]
    causal = causal_of(query.shape[1])
    scores = mm_tn(key_in, query) * 0.25
    weights = jnp.where(causal, 1.0 + scores + 0.5 * scores * scores, 0.0).astype(BF)
    dv_ref[...] = mm_nt(weighted[:HEAD_DIM], weights) * valid_ref[0]
    slope = mm_tn(extended(value_ref[...], valid_ref[0]), weighted)
    slope = jnp.where(causal, slope * (1.0 + scores), 0.0).astype(BF)
    mapped = mm_nn(state_ref[0, 0], weighted)
    pulled = feature_pull(mapped, query.astype(F32), *QUERY_SCALE)
    dq_ref[...] = (mm_nn(key_in, slope) * 0.25 + pulled).astype(BF)
    dk_ref[...] = mm_nt(query, slope) * 0.25


def later_kernel(heads, key_ref, value_ref, valid_ref, state_ref, dq_in, dk_in, dv_in, out_ref):
    head = pl.program_id(1)
    key_in = key_ref[...].astype(F32)
    valid = valid_ref[0]
    mapped = mm_nn(state_ref[0, 0], extended(value_ref[...], valid))
    d_key = (dk_in[...] + feature_pull(mapped, key_in, *KEY_SCALE)).astype(BF)
    spread = mm_tn(state_ref[0, 0], feature_rows(key_in, *KEY_SCALE))
    d_value = (dv_in[...] + spread[:HEAD_DIM] * valid).astype(BF)
    values, queries = heads * HEAD_DIM, heads * FEAT
    out_ref[pl.ds(pl.multiple_of(head * HEAD_DIM, 16), HEAD_DIM), :] = d_value
    out_ref[pl.ds(pl.multiple_of(values + head * FEAT, 16), FEAT), :] = dq_in[...]
    out_ref[pl.ds(pl.multiple_of(values + queries + head * FEAT, 16), FEAT), :] = d_key


def head_call(kernel, name, seqs, heads, length, ins, outs, flops):
    first_query = heads * HEAD_DIM // FEAT
    columns = heads * (HEAD_DIM + 2 * FEAT)
    specs = {
        "value": pl.BlockSpec((HEAD_DIM, length), lambda s, h: (h, s)),
        "query": pl.BlockSpec((FEAT, length), lambda s, h: (first_query + h, s)),
        "key": pl.BlockSpec((FEAT, length), lambda s, h: (first_query + heads + h, s)),
        "all": pl.BlockSpec((columns, length), lambda s, h: (0, s)),
        "feat": pl.BlockSpec((FEAT, length), lambda s, h: (h, s)),
        "head": pl.BlockSpec((HEAD_DIM, length), lambda s, h: (h, s)),
        "valid": pl.BlockSpec((1, 1, length), lambda s, h: (s, 0, 0)),
        "state": pl.BlockSpec((1, 1, PHI, EXT), lambda s, h: (s, h, 0, 0)),
        "row": pl.BlockSpec((1, 1, 1, length), lambda s, h: (s, h, 0, 0)),
        "ext": pl.BlockSpec((1, 1, EXT, length), lambda s, h: (s, h, 0, 0)),
    }
    shapes = {
        "all": (columns, seqs * length),
        "feat": (heads * FEAT, seqs * length),
        "head": (heads * HEAD_DIM, seqs * length),
        "state": (seqs, heads, PHI, EXT),
        "row": (seqs, heads, 1, length),
        "ext": (seqs, heads, EXT, length),
    }
    return pl.pallas_call(
        kernel,
        name=name,
        grid=(seqs, heads),
        in_specs=[specs[i] for i in ins],
        out_specs=[specs[o] for o, _ in outs],
        out_shape=[jax.ShapeDtypeStruct(shapes[o], kind) for o, kind in outs],
        compiler_params=params(),
        cost_estimate=cost(flops),
    )


def body(
    hidden_in,
    lengths,
    gain_attn,
    gain_ffn,
    w_query,
    w_key,
    w_value,
    w_output,
    w_gate,
    w_up,
    w_down,
    cotangent,
):
    seqs, length, width = hidden_in.shape
    heads = w_value.shape[1] // HEAD_DIM
    hidden_units = w_gate.shape[1]
    columns = heads * (HEAD_DIM + 2 * FEAT)
    index = places()
    position = lax.axis_index("ctx") * length + jnp.arange(length, dtype=jnp.int32)
    valid = (position[None, :] < lengths[:, None]).astype(F32)[:, None, :]
    hidden = hidden_in.transpose(0, 2, 1)
    unit = seqs * heads * 2 * length * length * 256
    token = [jnp.zeros((8, 128), F32)]

    def call(kernel, name, ins, outs, share):
        return head_call(kernel, name, seqs, heads, length, ins, outs, int(unit * share))

    def turn(value, *others):
        return tie(value, token[0], *others)

    def fence(*values):
        token[0] = tie(token[0], *values)

    ring_attn = Gather(jnp.concatenate([w_value, w_query, w_key, w_output.T], 1))
    ring_down = Gather(w_down.T)
    ring_gate_up = Gather(jnp.stack([w_gate, w_up]))
    ring_attn.advance()
    spread_in = Spread(hidden)
    gains = Spread(jnp.stack([gain_attn, gain_ffn], 1))
    gains.cross()
    fence(ring_attn.here())
    ring_attn.advance(*token)
    fence(ring_attn.here(), ring_gate_up.shard)
    ring_attn.advance(*token)
    ring_gate_up.advance(*token)
    fence(spread_in.far)
    spread_in.cross()
    grad_out = (cotangent.transpose(0, 2, 1).astype(F32) * valid).astype(BF)
    spread_out = Spread(turn(grad_out))
    fence(spread_in.near, spread_in.both)
    blocks = spread_in.blocks()
    normed_one, inv_one = gathered(index, (turn(blocks[0]),) + blocks[1:], gains.blocks(), 0)
    fence(ring_attn.here(), normed_one)
    ring_attn.advance(*token)
    fence(ring_attn.here())
    w_attn = ring_attn.full(turn(index))
    fence(w_attn, ring_gate_up.here())
    ring_gate_up.advance(*token)

    qkv = mm_tn(w_attn[:, :columns], turn(normed_one)).astype(BF)
    (own,) = call(state_kernel, "state", ("key", "value", "valid"), (("state", BF),), 0.5)(
        qkv, qkv, valid
    )
    before = Before(own, 1)
    fence(ring_gate_up.here(), before.other)
    before.first()
    fence(before.one)
    before.second()
    fence(before.sent)
    ring_gate_up.advance(*token)
    fence(spread_out.far)
    spread_out.cross()
    blocks = spread_out.blocks()
    grad_out_full = gathered(index, (turn(blocks[0]),) + blocks[1:])
    fence(grad_out_full)

    state = before.result()
    mixed, denom = call(
        attend_kernel,
        "attend",
        ("query", "key", "value", "valid", "state"),
        (("head", BF), ("row", F32)),
        1,
    )(turn(qkv), qkv, qkv, valid, state)
    scatter_attn = Scatter(index, projected(index, w_attn, [mixed], "out_proj", columns), seqs)
    fence(scatter_attn.got)
    scatter_attn.cross()
    fence(scatter_attn.sent_far, ring_gate_up.here())
    ring_down.advance(*token)
    ring_gate_up.advance(*token)
    resid = hidden.astype(F32) + scatter_attn.sums(*token)
    spread_resid = Spread(resid.astype(BF))
    fence(spread_resid.block, ring_down.here())
    ring_down.advance(*token)
    fence(ring_gate_up.here())
    gate_up = ring_gate_up.full(turn(index))
    fence(gate_up)
    fence(spread_resid.far)
    spread_resid.cross()
    fence(ring_down.here())
    ring_down.advance(*token)

    blocks = spread_resid.blocks()
    normed_two, inv_two = gathered(index, (turn(blocks[0]),) + blocks[1:], gains.blocks(), 1)
    fence(normed_two)
    gate = mm_tn(gate_up[0], turn(normed_two))
    fence(ring_down.here())
    ring_down.advance(*token)
    up = mm_tn(gate_up[1], normed_two)
    act = (gate * jax.nn.sigmoid(gate) * up).astype(BF)
    fence(act)
    fence(ring_down.here())
    down_full = ring_down.full(turn(index))
    fence(down_full)

    sig = jax.nn.sigmoid(gate)
    d_act = mm_tn(down_full, turn(grad_out_full))
    g_gate = (d_act * up * sig * (1.0 + gate * (1.0 - sig))).astype(BF)
    g_up = (d_act * gate * sig).astype(BF)
    inner = jnp.sum(g_gate.astype(F32) * gate + g_up.astype(F32) * up, 0, keepdims=True)
    fence(g_gate, g_up)
    scatter_two = Scatter(
        index, projected(index, gate_up, [turn(g_gate), g_up], "ffn_back", row=inner), seqs, inner
    )
    fence(scatter_two.sent)
    down_ring = Products(index, products([turn(grad_out_full)], [act], "down_grad"))
    fence(down_ring.sent)
    fence(scatter_two.got)
    scatter_two.cross()
    fence(scatter_two.sent_far)
    gate_up_ring = Products(
        index, products([normed_two, normed_two], [turn(g_gate), g_up], "gate_up_grad")
    )
    fence(gate_up_ring.sent)
    fence(down_ring.here())
    down_ring.advance(*token)
    fence(down_ring.sent)

    gain_one, gain_two = gain_attn.astype(F32)[:, None], gain_ffn.astype(F32)[:, None]
    d_norm, inner = scatter_two.sums(*token)
    gain_two_part = jnp.sum(resid * inv_two * d_norm, (0, 2))
    d_resid = (
        grad_out.astype(F32)
        + inv_two * gain_two * d_norm
        - resid * (inv_two * inv_two * inner / D)
    )
    spread_grad = Spread(d_resid.astype(BF))
    fence(spread_grad.block)
    fence(gate_up_ring.here())
    gate_up_ring.advance(*token)
    fence(gate_up_ring.sent)
    fence(down_ring.here())
    down_ring.advance(*token)
    fence(down_ring.sent)
    ffn_out = projected(index, down_full, [turn(act)], "ffn_out")
    fence(ffn_out)
    fence(spread_grad.far)
    spread_grad.cross()
    fence(down_ring.here())
    down_ring.advance(*token)
    fence(down_ring.sent)
    blocks = spread_grad.blocks()
    resid_full = gathered(index, (turn(blocks[0]),) + blocks[1:])
    g_attn = mm_tn(w_attn[:, columns:], resid_full).astype(BF)
    weighted, spread = call(
        spread_kernel, "spread", ("query", "head", "head", "row"), (("ext", BF), ("state", BF)), 0.5
    )(qkv, g_attn, mixed, denom)
    after = Before(spread, -1)
    fence(spread)
    scatter_out = Scatter(index, [tie(ffn_out[0], *token), ffn_out[1]], seqs)
    local = call(
        local_kernel,
        "local",
        ("query", "key", "value", "valid", "state", "ext"),
        (("feat", BF), ("feat", F32), ("head", F32)),
        2,
    )(turn(qkv), qkv, qkv, valid, state, weighted)
    fence(after.other)
    after.first()
    fence(after.one)
    after.second()
    fence(after.sent)
    fence(gate_up_ring.here(), local)
    gate_up_ring.advance(*token)
    fence(gate_up_ring.sent)
    fence(scatter_out.got)
    scatter_out.cross()
    down_grad = down_ring.final(*token)
    fence(down_grad)

    def later(*refs):
        later_kernel(heads, *refs)

    (d_qkv,) = call(
        later,
        "later",
        ("key", "value", "valid", "state", "feat", "feat", "head"),
        (("all", BF),),
        0.5,
    )(turn(qkv), qkv, valid, after.result(), *local)
    inner = jnp.sum(d_qkv.astype(F32) * qkv.astype(F32), 0, keepdims=True)
    scatter_one = Scatter(
        index, projected(index, w_attn, [d_qkv], "qkv_back", 0, row=inner), seqs, inner
    )
    fence(scatter_one.sent)
    attn_ring = Products(
        index, products([turn(normed_one), resid_full], [d_qkv, mixed], "attn_grad")
    )
    fence(attn_ring.sent)
    fence(scatter_one.got)
    scatter_one.cross()
    fence(scatter_one.sent_far)
    fence(attn_ring.here())
    attn_ring.advance(*token)
    fence(attn_ring.sent)
    fence(gate_up_ring.here())
    gate_up_ring.advance(*token)
    fence(gate_up_ring.sent)
    layer_out = (resid + scatter_out.sums(*token)).astype(BF)
    fence(layer_out)
    fence(attn_ring.here())
    attn_ring.advance(*token)
    fence(attn_ring.sent)
    d_norm, inner = scatter_one.sums(*token)
    value = hidden.astype(F32)
    gain_one_part = jnp.sum(value * inv_one * d_norm, (0, 2))
    grad_input = (
        d_resid + inv_one * gain_one * d_norm - value * (inv_one * inv_one * inner / D)
    )
    gain_grads = ctx_total(jnp.stack([gain_one_part, gain_two_part]))
    fence(grad_input)
    fence(attn_ring.here())
    attn_ring.advance(*token)
    fence(attn_ring.sent)
    gate_up_grad = gate_up_ring.final(*token)
    fence(gate_up_grad, gain_grads)
    attn_grad = attn_ring.final(*token)

    values, queries = heads * HEAD_DIM, heads * FEAT
    return (
        layer_out.transpose(0, 2, 1),
        grad_input.transpose(0, 2, 1),
        gain_grads[0],
        gain_grads[1],
        attn_grad[:, values : values + queries],
        attn_grad[:, values + queries : columns],
        attn_grad[:, :values],
        attn_grad[:, columns:].T,
        gate_up_grad[:, :hidden_units],
        gate_up_grad[:, hidden_units:],
        down_grad.T,
    )


def solution(mesh):
    acts, rows, columns = P(None, "ctx", "wt"), P("ctx", "wt"), P("wt", "ctx")
    in_specs = (acts, P(), P("wt"), P("wt"), rows, rows, rows, columns, rows, rows, columns, acts)
    out_specs = (acts, acts, P("wt"), P("wt"), rows, rows, rows, columns, rows, rows, columns)
    return jax.shard_map(body, mesh=mesh, in_specs=in_specs, out_specs=out_specs, check_vma=False)
```

time: 721 us -> 559 us (0.78)
  Pallas kernels: 17.2 us -> 109 us
  matrix products: 116 us -> 28.5 us
  local copies, waits for them, and re-layouts: 112 us -> 27.4 us
  starting transfers between devices: 142 us -> 87.1 us
  other arithmetic: 42 us -> 18.1 us
    ppermute x64 -> x48, waiting for transfers between devices: 101 us -> 193 us  [hop(): return lax.ppermute(value, 'ctx', pairs)]
    pallas_call x10 -> x38, Pallas kernels: 17.2 us -> 109 us  [the longest x4 27.4 us: projected(): pl.pallas_call(kernel, name=name, grid_spec=pltpu.PrefetchScalarGridSpec(...]
    dot_general x20 -> x0, matrix products: 85.5 us -> none  [the longest x10 62.6 us: mm_nt(): lax.dot_general(left, right, (((1,), (1,)), ((), ())), preferred_element_...]
    dynamic_update_slice x36 -> x0, local copies, waits for them, and re-layouts: 79.7 us -> none  [ctx_gather(): lax.dynamic_update_slice_in_dim(full, piece, ring_index(offset) * rows +...]
    ppermute x51 -> x23, waiting for transfers between devices: 100 us -> 24.1 us  [swap(): return lax.ppermute(value, 'wt', [(i, i ^ bit) for i in range(count)])]
    ppermute x6 -> x3, waiting for transfers between devices: 41.1 us -> 2.69 us  [ctx_total(): value = value + lax.ppermute(value, 'ctx', [(i, i ^ bit) for i in range(8)])]
    ppermute x51 -> x23, starting transfers between devices: 32.2 us -> 9.73 us  [swap(): return lax.ppermute(value, 'wt', [(i, i ^ bit) for i in range(count)])]
    ppermute x8 -> x4, waiting for transfers between devices: 22.9 us -> 44.9 us  [shifted(): return lax.ppermute(value, 'ctx', pairs)]
  transfers between devices with their start and end apart: 133 -> 80, of which waited for: 55 -> 43; matrix products, arithmetic and copies ran while one was open for 31% -> 6% of each run, Pallas kernels for 2% -> 14%
where the time goes in v3:
time: 559 us; the launch traced here: 551 us
  waiting for transfers between devices  279 us (50%)
  Pallas kernels  109 us (19%)
  starting transfers between devices  87.1 us (16%)
  matrix products  28.5 us (5%)
  local copies, waits for them, and re-layouts  27.4 us (5%)
  other arithmetic  18.1 us (3%)
    ppermute x48, waiting for transfers between devices, hop(): return lax.ppermute(value, 'ctx', pairs)  193 us
    ppermute x48, starting transfers between devices, hop(): return lax.ppermute(value, 'ctx', pairs)  59.2 us
    ppermute x4, waiting for transfers between devices, shifted(): return lax.ppermute(value, 'ctx', pairs)  44.9 us
    dot_general x5, matrix products, mm_tn(): lax.dot_general(left, right, (((0,), (0,)), ((), ())), preferred_element_...  28.5 us
    pallas_call x4, Pallas kernels, projected(): pl.pallas_call(kernel, name=name, grid_spec=pltpu.PrefetchScalarGridSpec(...  27.4 us
    ppermute x23, waiting for transfers between devices, swap(): return lax.ppermute(value, 'wt', [(i, i ^ bit) for i in range(count)])  24.1 us
    pallas_call x3, Pallas kernels, products(): pl.pallas_call(kernel, name=name, grid=(4,), in_specs=[pl.BlockSpec((rows...  22.1 us
    unnamed x140, local copies, waits for them, and re-layouts  21.5 us
  transfers between devices with their start and end apart: 80, of which 43 were waited for; matrix products, arithmetic and copies ran while one was open for 6% of the time, Pallas kernels for 14%

profile of v3, /device:TPU:0, one launch (start us, length us, event | category | flops | bytes accessed | tf_op | source)
XLA Modules:
  0.0 551.0 jit_solution(9603646469271270430)
XLA Ops:
  9.7 9.9 %collective-permute-done.refs_1_ = bf16[224,1024]{1,0:T(8,128)(2,1)S(1)} collective-permute-done((bf16[224,1024]{1,0:T(8,128)(2,1)S(1)}, bf16[224,1024]{1,0:T(8,128)(2,1)S(1)}, u32[]{:S(2)}, u32[]{:S(2)}) %collective-permute-start) | collective-permute-done | bytes 458784 | tf_op jit(solution)/shard_map/ppermute | solution.py:247
  27.0 4.9 collective-permute-done.2.refs_2_
  57.6 15.0 %collective-permute-done.12.refs_4_ = bf16[112,1024]{1,0:T(8,128)(2,1)S(1)} collective-permute-done((bf16[112,1024]{1,0:T(8,128)(2,1)S(1)}, bf16[112,1024]{1,0:T(8,128)(2,1)S(1)}, u32[]{:S(2)}, u32[]{:S(2)}) %collective-permute-start.12) | collective-permute-done | bytes 229408 | tf_op jit(solution)/shard_map/ppermute | solution.py:247
  82.2 6.6 %collective-permute-done.18 = bf16[2,4,160,128]{3,2,1,0:T(8,128)(2,1)S(1)} collective-permute-done((bf16[2,4,160,128]{3,2,1,0:T(8,128)(2,1)S(1)}, bf16[2,4,160,128]{3,2,1,0:T(8,128)(2,1)S(1)}, u32[]{:S(2)}, u32[]{:S(2)}) %collective-permute-start.18) | collective-permute-done | bytes 327712 | tf_op jit(solution)/shard_map/ppermute | solution.py:439
  95.6 5.5 %collective-permute-done.19 = bf16[2,4,160,128]{3,2,1,0:T(8,128)(2,1)S(1)} collective-permute-done((bf16[2,4,160,128]{3,2,1,0:T(8,128)(2,1)S(1)}, bf16[2,4,160,128]{3,2,1,0:T(8,128)(2,1)S(1)}, u32[]{:S(2)}, u32[]{:S(2)}) %collective-permute-start.19) | collective-permute-done | bytes 327712 | tf_op jit(solution)/shard_map/ppermute | solution.py:430
  102.6 5.3 collective-permute-start.23
  108.0 18.8 %collective-permute-done.23 = bf16[2,4,160,128]{3,2,1,0:T(8,128)(2,1)} collective-permute-done((bf16[2,4,160,128]{3,2,1,0:T(8,128)(2,1)}, bf16[2,4,160,128]{3,2,1,0:T(8,128)(2,1)}, u32[]{:S(2)}, u32[]{:S(2)}) %collective-permute-start.23) | collective-permute-done | bytes 327712 | tf_op jit(solution)/shard_map/ppermute | solution.py:430
  131.1 4.8 attend.1
  139.8 8.0 %collective-permute-start.26 = (bf16[2,224,1216]{2,1,0:T(8,128)(2,1)}, bf16[2,224,1216]{2,1,0:T(8,128)(2,1)S(1)}, u32[]{:S(2)}, u32[]{:S(2)}) collective-permute-start(bf16[2,224,1216]{2,1,0:T(8,128)(2,1)} %collective-permute-done.16.refs_2_), channel_id=1, source_target_pairs={{0,8},{8,16},{16,24},{24,28},{28,20},{20,12},{12,4},{4,0},{1,9},{9... | collective-permute-start | bytes 3268616 | tf_op jit(solution)/shard_map/ppermute | solution.py:247
  149.6 23.6 %collective-permute-done.26.refs_3_ = bf16[2,224,1216]{2,1,0:T(8,128)(2,1)S(1)} collective-permute-done((bf16[2,224,1216]{2,1,0:T(8,128)(2,1)}, bf16[2,224,1216]{2,1,0:T(8,128)(2,1)S(1)}, u32[]{:S(2)}, u32[]{:S(2)}) %collective-permute-start.26) | collective-permute-done | bytes 1089568 | tf_op jit(solution)/shard_map/ppermute | solution.py:247
  182.0 11.5 %collective-permute-done.28.refs_1_ = bf16[224,1216]{1,0:T(8,128)(2,1)S(1)} collective-permute-done((bf16[224,1216]{1,0:T(8,128)(2,1)S(1)}, bf16[224,1216]{1,0:T(8,128)(2,1)S(1)}, u32[]{:S(2)}, u32[]{:S(2)}) %collective-permute-start.28) | collective-permute-done | bytes 544800 | tf_op jit(solution)/shard_map/ppermute | solution.py:247
  197.8 8.0 %collective-permute-done.30.refs_4_ = bf16[2,112,1216]{2,1,0:T(8,128)(2,1)S(1)} collective-permute-done((bf16[2,112,1216]{2,1,0:T(8,128)(2,1)S(1)}, bf16[2,112,1216]{2,1,0:T(8,128)(2,1)S(1)}, u32[]{:S(2)}, u32[]{:S(2)}) %collective-permute-start.30) | collective-permute-done | bytes 544800 | tf_op jit(solution)/shard_map/ppermute | solution.py:247
  211.1 5.0 collective-permute-done.33.refs_2_
  220.6 10.9 %collective-permute-done.37.refs_3_ = bf16[224,1216]{1,0:T(8,128)(2,1)S(1)} collective-permute-done((bf16[224,1216]{1,0:T(8,128)(2,1)S(1)}, bf16[224,1216]{1,0:T(8,128)(2,1)S(1)}, u32[]{:S(2)}, u32[]{:S(2)}) %collective-permute-start.37) | collective-permute-done | bytes 544800 | tf_op jit(solution)/shard_map/ppermute | solution.py:247
  234.6 4.8 fusion.1
  241.5 7.5 %multiply_convert_fusion.2 = (bf16[1216,1024]{1,0:T(8,128)(2,1)}, f32[1216,1024]{1,0:T(8,128)}) fusion(f32[1216,1024]{1,0:T(8,128)S(1)} %fusion.1, bf16[1792,1024]{1,0:T(8,128)(2,1)S(1)} %get-tuple-element.217.refs_0_, bf16[2,1792,1216]{2,1,0:T(8,128)(2,1)S(1)} %assemble.4.weight_ref), kind=kOutput, calls=%fused_computation.3 | convolution fusion | flops 4470210560 | bytes 20709376 | tf_op jit(solution)/shard_map/dot_general | solution.py:30
  250.5 11.8 %add_reduce_fusion = (f32[1024]{0:T(1024)S(1)}, bf16[1216,1024]{1,0:T(8,128)(2,1)S(1)}, bf16[1216,1024]{1,0:T(8,128)(2,1)}) fusion(f32[1216,1024]{1,0:T(8,128)} %get-tuple-element.361, f32[1216,1024]{1,0:T(8,128)S(1)} %fusion.1, bf16[1792,1216]{1,0:T(8,128)(2,1)S(1)} %assemble.5.weight_ref, bf16[1792,1024]{1,0:T(8,128)(2,1)S(1)} %gather.2.refs_0_), kind=kOutput, calls=%fused_computation | convolution fusion | flops 4486396928 | bytes 22974464 | tf_op jit(solution)/shard_map/dot_general | solution.py:30
  265.0 11.9 %ffn_back.1 = (bf16[2,456,1024]{2,1,0:T(8,128)(2,1)S(1)}, bf16[2,448,1024]{2,1,0:T(8,128)(2,1)S(1)}) custom-call(s32[9]{0:T(128)S(1)} %fusion.30.index_ref, bf16[2,1792,1216]{2,1,0:T(8,128)(2,1)S(1)} %assemble.4.weight_ref, bf16[1216,1024]{1,0:T(8,128)(2,1)S(1)} %copy-done.45, bf16[1216,1024]{1,0:T(8,128)(2,1)S(1)} %get-tuple-element.345.refs_1_.refs_2_, ...), custom_call_target="tpu_custom_call" | custom-call | flops 8925478912 | bytes 8388608 | tf_op jit(solution)/shard_map/ffn_back/pallas_call | solution.py:150
  283.6 5.6 %down_grad.1.refs_0_.refs_2_.refs_3_.own = bf16[1792,1216]{1,0:T(8,128)(2,1)S(1)} custom-call(bf16[1792,1024]{1,0:T(8,128)(2,1)S(1)} %copy-done.10, bf16[1216,1024]{1,0:T(8,128)(2,1)S(1)} %copy-done.41), custom_call_target="tpu_custom_call" | custom-call | flops 4462739456 | bytes 4358144 | tf_op jit(solution)/shard_map/down_grad/pallas_call | solution.py:327
  292.9 10.6 %gate_up_grad.1.refs_0_.refs_2_.refs_3_.own = bf16[1792,2432]{1,0:T(8,128)(2,1)S(1)} custom-call(bf16[1792,1024]{1,0:T(8,128)(2,1)S(1)} %copy-done.34, bf16[1216,1024]{1,0:T(8,128)(2,1)S(1)} %copy-done.46, bf16[1216,1024]{1,0:T(8,128)(2,1)S(1)} %copy-done.44), custom_call_target="tpu_custom_call" | custom-call | flops 8925478912 | bytes 8716288 | tf_op jit(solution)/shard_map/gate_up_grad/pallas_call | solution.py:327
  314.9 11.2 %collective-permute-done.45.refs_0_ = bf16[112,2432]{1,0:T(8,128)(2,1)S(1)} collective-permute-done((bf16[112,2432]{1,0:T(8,128)(2,1)S(1)}, bf16[112,2432]{1,0:T(8,128)(2,1)S(1)}, u32[]{:S(2)}, u32[]{:S(2)}) %collective-permute-start.45) | collective-permute-done | bytes 544800 | tf_op jit(solution)/shard_map/ppermute | solution.py:247
  326.1 6.2 %collective-permute-done.49.refs_2_ = bf16[2,448,512]{2,1,0:T(8,128)(2,1)S(1)} collective-permute-done((bf16[2,448,512]{2,1,0:T(8,128)(2,1)S(1)}, bf16[2,448,512]{2,1,0:T(8,128)(2,1)S(1)}, u32[]{:S(2)}, u32[]{:S(2)}) %collective-permute-start.49) | collective-permute-done | bytes 917536 | tf_op jit(solution)/shard_map/ppermute | solution.py:52
  341.0 7.3 %ffn_out.1 = (bf16[2,448,1024]{2,1,0:T(8,128)(2,1)}, bf16[2,448,1024]{2,1,0:T(8,128)(2,1)S(1)}) custom-call(s32[9]{0:T(128)S(1)} %fusion.30.index_ref, bf16[1792,1216]{1,0:T(8,128)(2,1)S(1)} %bitcast.62, bf16[1216,1024]{1,0:T(8,128)(2,1)S(1)} %copy-done.42), custom_call_target="tpu_custom_call" | custom-call | flops 4462739456 | bytes 8388608 | tf_op jit(solution)/shard_map/ffn_out/pallas_call | solution.py:150
  364.8 7.2 %collective-permute-done.56 = bf16[2,4,160,128]{3,2,1,0:T(8,128)(2,1)S(1)} collective-permute-done((bf16[2,4,160,128]{3,2,1,0:T(8,128)(2,1)S(1)}, bf16[2,4,160,128]{3,2,1,0:T(8,128)(2,1)S(1)}, u32[]{:S(2)}, u32[]{:S(2)}) %collective-permute-start.56) | collective-permute-done | bytes 327712 | tf_op jit(solution)/shard_map/ppermute | solution.py:439
  373.4 20.6 %collective-permute-done.57 = bf16[2,4,160,128]{3,2,1,0:T(8,128)(2,1)S(1)} collective-permute-done((bf16[2,4,160,128]{3,2,1,0:T(8,128)(2,1)S(1)}, bf16[2,4,160,128]{3,2,1,0:T(8,128)(2,1)S(1)}, u32[]{:S(2)}, u32[]{:S(2)}) %collective-permute-start.57) | collective-permute-done | bytes 327712 | tf_op jit(solution)/shard_map/ppermute | solution.py:430
  405.8 7.8 %local.1 = (bf16[64,1024]{1,0:T(8,128)(2,1)S(1)}, f32[64,1024]{1,0:T(8,128)S(1)}, f32[448,1024]{1,0:T(8,128)S(1)}) custom-call(bf16[576,1024]{1,0:T(8,128)(2,1)S(1)} %fusion.10.key_ref.value_ref.query_ref.refs_0_.refs_1_, bf16[576,1024]{1,0:T(8,128)(2,1)S(1)} %fusion.10.key_ref.value_ref.query_ref.refs_0_.refs_1_, ...), custom_call_target="tpu_custom_call" | custom-call | flops 2147483648 | bytes 4194304 | tf_op jit(solution)/shard_map/local/pallas_call | solution.py:778
  418.1 4.5 qkv_back.1
  424.7 5.9 %attn_grad.1.refs_0_.refs_2_.refs_3_.own = bf16[1792,1024]{1,0:T(8,128)(2,1)S(1)} custom-call(bf16[1792,1024]{1,0:T(8,128)(2,1)S(1)} %copy-done.32, bf16[1792,1024]{1,0:T(8,128)(2,1)S(1)} %copy-done.12, bf16[576,1024]{1,0:T(8,128)(2,1)S(1)} %later.1.refs_0_.refs_2_, bf16[448,1024]{1,0:T(8,128)(2,1)S(1)} %copy-done.19), custom_call_target="tpu_custom_call" | custom-call | flops 3758096384 | bytes 3670016 | tf_op jit(solution)/shard_map/attn_grad/pallas_call | solution.py:327
  440.3 7.3 %collective-permute-done.65.refs_1_ = bf16[112,1024]{1,0:T(8,128)(2,1)S(1)} collective-permute-done((bf16[112,1024]{1,0:T(8,128)(2,1)S(1)}, bf16[112,1024]{1,0:T(8,128)(2,1)S(1)}, u32[]{:S(2)}, u32[]{:S(2)}) %collective-permute-start.65) | collective-permute-done | bytes 229408 | tf_op jit(solution)/shard_map/ppermute | solution.py:247
  453.7 8.5 %collective-permute-done.66.refs_0_ = bf16[224,1024]{1,0:T(8,128)(2,1)S(1)} collective-permute-done((bf16[224,1024]{1,0:T(8,128)(2,1)S(1)}, bf16[224,1024]{1,0:T(8,128)(2,1)S(1)}, u32[]{:S(2)}, u32[]{:S(2)}) %collective-permute-start.66) | collective-permute-done | bytes 458784 | tf_op jit(solution)/shard_map/ppermute | solution.py:247
  465.3 35.1 %collective-permute-done.79.left_ref = bf16[224,1216]{1,0:T(8,128)(2,1)S(1)} collective-permute-done((bf16[224,1216]{1,0:T(8,128)(2,1)S(1)}, bf16[224,1216]{1,0:T(8,128)(2,1)S(1)}, u32[]{:S(2)}, u32[]{:S(2)}) %collective-permute-start.79) | collective-permute-done | bytes 544800 | tf_op jit(solution)/shard_map/ppermute | solution.py:247
  537.7 6.6 %collective-permute-done.55 = bf16[2,448,512]{2,1,0:T(8,128)(2,1)S(1)} collective-permute-done((bf16[2,448,512]{2,1,0:T(8,128)(2,1)}, bf16[2,448,512]{2,1,0:T(8,128)(2,1)S(1)}, u32[]{:S(2)}, u32[]{:S(2)}) %collective-permute-start.55) | collective-permute-done | bytes 917536 | tf_op jit(solution)/shard_map/ppermute | solution.py:52
  (356 shorter events, 230.2 us)
Async XLA Ops:
  9.7 32.2 %collective-permute-start.5 = (bf16[2,448,512]{2,1,0:T(8,128)(2,1)}, bf16[2,448,512]{2,1,0:T(8,128)(2,1)}, u32[]{:S(2)}, u32[]{:S(2)}) collective-permute-start(bf16[2,448,512]{2,1,0:T(8,128)(2,1)} %bitcast.59), channel_id=1, source_target_pairs={{0,1},{1,0},{2,3},{3,2},{4,5},{5,4},{6,7},{7,6},{8,9},{9,8},{10,11... | collective-permute-start | bytes 2752520 | tf_op jit(solution)/shard_map/ppermute | solution.py:52
  24.3 26.0 %collective-permute-start.6 = (bf16[2,448,512]{2,1,0:T(8,128)(2,1)}, bf16[2,448,512]{2,1,0:T(8,128)(2,1)}, u32[]{:S(2)}, u32[]{:S(2)}) collective-permute-start(bf16[2,448,512]{2,1,0:T(8,128)(2,1)} %collective-permute-done.4.refs_2_), channel_id=1, source_target_pairs={{0,1},{1,0},{2,3},{3,2},{4,5},{5,4},{6,7},{7,6},{8,9},{9,8},{10,11... | collective-permute-start | bytes 2752520 | tf_op jit(solution)/shard_map/ppermute | solution.py:52
  40.3 36.8 %collective-permute-start.14 = (bf16[2,224,1216]{2,1,0:T(8,128)(2,1)S(1)}, bf16[2,224,1216]{2,1,0:T(8,128)(2,1)}, u32[]{:S(2)}, u32[]{:S(2)}) collective-permute-start(bf16[2,224,1216]{2,1,0:T(8,128)(2,1)S(1)} %pad_maximum_fusion.refs_0_), channel_id=1, source_target_pairs={{0,8},{8,16},{16,24},{24,28},{28,20},{20,12},{12,4},{4,0},{1,9},{9... | collective-permute-start | bytes 3268616 | tf_op jit(solution)/shard_map/ppermute | solution.py:247
  41.9 35.3 %collective-permute-start.15 = (bf16[2,224,1216]{2,1,0:T(8,128)(2,1)S(1)}, bf16[2,224,1216]{2,1,0:T(8,128)(2,1)}, u32[]{:S(2)}, u32[]{:S(2)}) collective-permute-start(bf16[2,224,1216]{2,1,0:T(8,128)(2,1)S(1)} %pad_maximum_fusion.refs_0_), channel_id=1, source_target_pairs={{0,4},{8,0},{16,8},{24,16},{28,24},{20,28},{12,20},{4,12},{1,5},{9... | collective-permute-start | bytes 3268616 | tf_op jit(solution)/shard_map/ppermute | solution.py:247
  57.1 38.0 %collective-permute-start.20 = (bf16[2,448,512]{2,1,0:T(8,128)(2,1)}, bf16[2,448,512]{2,1,0:T(8,128)(2,1)}, u32[]{:S(2)}, u32[]{:S(2)}) collective-permute-start(bf16[2,448,512]{2,1,0:T(8,128)(2,1)} %fusion.16.refs_0_), channel_id=1, source_target_pairs={{0,2},{1,3},{2,0},{3,1},{4,6},{5,7},{6,4},{7,5},{8,10},{9,11},{10,... | collective-permute-start | bytes 2752520 | tf_op jit(solution)/shard_map/ppermute | solution.py:52
  93.0 35.2 %collective-permute-start.16 = (bf16[2,224,1216]{2,1,0:T(8,128)(2,1)}, bf16[2,224,1216]{2,1,0:T(8,128)(2,1)}, u32[]{:S(2)}, u32[]{:S(2)}) collective-permute-start(bf16[2,224,1216]{2,1,0:T(8,128)(2,1)} %collective-permute-done.14.refs_1_), channel_id=1, source_target_pairs={{0,8},{8,16},{16,24},{24,28},{28,20},{20,12},{12,4},{4,0},{1,9},{9... | collective-permute-start | bytes 3268616 | tf_op jit(solution)/shard_map/ppermute | solution.py:247
  93.8 34.4 %collective-permute-start.17 = (bf16[2,224,1216]{2,1,0:T(8,128)(2,1)}, bf16[2,224,1216]{2,1,0:T(8,128)(2,1)}, u32[]{:S(2)}, u32[]{:S(2)}) collective-permute-start(bf16[2,224,1216]{2,1,0:T(8,128)(2,1)} %collective-permute-done.15.refs_5_), channel_id=1, source_target_pairs={{0,4},{8,0},{16,8},{24,16},{28,24},{20,28},{12,20},{4,12},{1,5},{9... | collective-permute-start | bytes 3268616 | tf_op jit(solution)/shard_map/ppermute | solution.py:247
  95.0 33.1 %collective-permute-start.21 = (bf16[2,448,512]{2,1,0:T(8,128)(2,1)}, bf16[2,448,512]{2,1,0:T(8,128)(2,1)}, u32[]{:S(2)}, u32[]{:S(2)}) collective-permute-start(bf16[2,448,512]{2,1,0:T(8,128)(2,1)} %fusion.16.refs_0_), channel_id=1, source_target_pairs={{0,1},{1,0},{2,3},{3,2},{4,5},{5,4},{6,7},{7,6},{8,9},{9,8},{10,11... | collective-permute-start | bytes 2752520 | tf_op jit(solution)/shard_map/ppermute | solution.py:52
  95.1 33.1 %collective-permute-start.22 = (bf16[2,448,512]{2,1,0:T(8,128)(2,1)}, bf16[2,448,512]{2,1,0:T(8,128)(2,1)}, u32[]{:S(2)}, u32[]{:S(2)}) collective-permute-start(bf16[2,448,512]{2,1,0:T(8,128)(2,1)} %collective-permute-done.20.refs_2_), channel_id=1, source_target_pairs={{0,1},{1,0},{2,3},{3,2},{4,5},{5,4},{6,7},{7,6},{8,9},{9,8},{10,11... | collective-permute-start | bytes 2752520 | tf_op jit(solution)/shard_map/ppermute | solution.py:52
  102.6 24.2 %collective-permute-start.23 = (bf16[2,4,160,128]{3,2,1,0:T(8,128)(2,1)}, bf16[2,4,160,128]{3,2,1,0:T(8,128)(2,1)}, u32[]{:S(2)}, u32[]{:S(2)}) collective-permute-start(bf16[2,4,160,128]{3,2,1,0:T(8,128)(2,1)} %fusion.21), channel_id=1, source_target_pairs={{0,16},{4,20},{8,24},{12,28},{1,17},{5,21},{9,25},{13,29},{2,18},{... | collective-permute-start | bytes 983048 | tf_op jit(solution)/shard_map/ppermute | solution.py:430
  139.8 33.5 %collective-permute-start.26 = (bf16[2,224,1216]{2,1,0:T(8,128)(2,1)}, bf16[2,224,1216]{2,1,0:T(8,128)(2,1)S(1)}, u32[]{:S(2)}, u32[]{:S(2)}) collective-permute-start(bf16[2,224,1216]{2,1,0:T(8,128)(2,1)} %collective-permute-done.16.refs_2_), channel_id=1, source_target_pairs={{0,8},{8,16},{16,24},{24,28},{28,20},{20,12},{12,4},{4,0},{1,9},{9... | collective-permute-start | bytes 3268616 | tf_op jit(solution)/shard_map/ppermute | solution.py:247
  147.8 27.5 %collective-permute-start.27 = (bf16[2,224,1216]{2,1,0:T(8,128)(2,1)}, bf16[2,224,1216]{2,1,0:T(8,128)(2,1)S(1)}, u32[]{:S(2)}, u32[]{:S(2)}) collective-permute-start(bf16[2,224,1216]{2,1,0:T(8,128)(2,1)} %collective-permute-done.17.refs_6_), channel_id=1, source_target_pairs={{0,4},{8,0},{16,8},{24,16},{28,24},{20,28},{12,20},{4,12},{1,5},{9... | collective-permute-start | bytes 3268616 | tf_op jit(solution)/shard_map/ppermute | solution.py:247
  149.1 26.3 %collective-permute-start.25 = (bf16[2,448,512]{2,1,0:T(8,128)(2,1)S(1)}, bf16[2,448,512]{2,1,0:T(8,128)(2,1)S(1)}, u32[]{:S(2)}, u32[]{:S(2)}) collective-permute-start(bf16[2,448,512]{2,1,0:T(8,128)(2,1)S(1)} %get-tuple-element.193), channel_id=1, source_target_pairs={{0,2},{1,3},{2,0},{3,1},{4,6},{5,7},{6,4},{7,5},{8,10},{9,11},{10,... | collective-permute-start | bytes 2752520 | tf_op jit(solution)/shard_map/ppermute | solution.py:52
  177.1 28.7 %collective-permute-start.32 = (bf16[2,448,512]{2,1,0:T(8,128)(2,1)S(1)}, bf16[2,448,512]{2,1,0:T(8,128)(2,1)S(1)}, u32[]{:S(2)}, u32[]{:S(2)}) collective-permute-start(bf16[2,448,512]{2,1,0:T(8,128)(2,1)S(1)} %get-tuple-element.211.refs_0_), channel_id=1, source_target_pairs={{0,2},{1,3},{2,0},{3,1},{4,6},{5,7},{6,4},{7,5},{8,10},{9,11},{10,... | collective-permute-start | bytes 2752520 | tf_op jit(solution)/shard_map/ppermute | solution.py:52
  179.9 25.9 %collective-permute-start.30 = (bf16[2,112,1216]{2,1,0:T(8,128)(2,1)S(1)}, bf16[2,112,1216]{2,1,0:T(8,128)(2,1)S(1)}, u32[]{:S(2)}, u32[]{:S(2)}) collective-permute-start(bf16[2,112,1216]{2,1,0:T(8,128)(2,1)S(1)} %slice.107), channel_id=1, source_target_pairs={{0,8},{8,16},{16,24},{24,28},{28,20},{20,12},{12,4},{4,0},{1,9},{9... | collective-permute-start | bytes 1634312 | tf_op jit(solution)/shard_map/ppermute | solution.py:247
  182.0 26.0 %collective-permute-start.31 = (bf16[2,112,1216]{2,1,0:T(8,128)(2,1)S(1)}, bf16[2,112,1216]{2,1,0:T(8,128)(2,1)S(1)}, u32[]{:S(2)}, u32[]{:S(2)}) collective-permute-start(bf16[2,112,1216]{2,1,0:T(8,128)(2,1)S(1)} %slice.108), channel_id=1, source_target_pairs={{0,4},{8,0},{16,8},{24,16},{28,24},{20,28},{12,20},{4,12},{1,5},{9... | collective-permute-start | bytes 1634312 | tf_op jit(solution)/shard_map/ppermute | solution.py:247
  205.8 26.6 %collective-permute-start.35 = (bf16[2,448,512]{2,1,0:T(8,128)(2,1)S(1)}, bf16[2,448,512]{2,1,0:T(8,128)(2,1)S(1)}, u32[]{:S(2)}, u32[]{:S(2)}) collective-permute-start(bf16[2,448,512]{2,1,0:T(8,128)(2,1)S(1)} %get-tuple-element.211.refs_0_), channel_id=1, source_target_pairs={{0,1},{1,0},{2,3},{3,2},{4,5},{5,4},{6,7},{7,6},{8,9},{9,8},{10,11... | collective-permute-start | bytes 2752520 | tf_op jit(solution)/shard_map/ppermute | solution.py:52
  205.8 26.6 %collective-permute-start.36 = (bf16[2,448,512]{2,1,0:T(8,128)(2,1)S(1)}, bf16[2,448,512]{2,1,0:T(8,128)(2,1)S(1)}, u32[]{:S(2)}, u32[]{:S(2)}) collective-permute-start(bf16[2,448,512]{2,1,0:T(8,128)(2,1)S(1)} %collective-permute-done.32.refs_2_), channel_id=1, source_target_pairs={{0,1},{1,0},{2,3},{3,2},{4,5},{5,4},{6,7},{7,6},{8,9},{9,8},{10,11... | collective-permute-start | bytes 2752520 | tf_op jit(solution)/shard_map/ppermute | solution.py:52
  312.9 24.4 %collective-permute-start.47 = (bf16[224,1216]{1,0:T(8,128)(2,1)S(1)}, bf16[224,1216]{1,0:T(8,128)(2,1)S(1)}, u32[]{:S(2)}, u32[]{:S(2)}) collective-permute-start(bf16[224,1216]{1,0:T(8,128)(2,1)S(1)} %get-tuple-element.243), channel_id=1, source_target_pairs={{0,8},{8,16},{16,24},{24,28},{28,20},{20,12},{12,4},{4,0},{1,9},{9... | collective-permute-start | bytes 1634312 | tf_op jit(solution)/shard_map/ppermute | solution.py:247
  313.8 24.1 %collective-permute-start.48 = (bf16[224,1216]{1,0:T(8,128)(2,1)S(1)}, bf16[224,1216]{1,0:T(8,128)(2,1)S(1)}, u32[]{:S(2)}, u32[]{:S(2)}) collective-permute-start(bf16[224,1216]{1,0:T(8,128)(2,1)S(1)} %get-tuple-element.244), channel_id=1, source_target_pairs={{0,4},{8,0},{16,8},{24,16},{28,24},{20,28},{12,20},{4,12},{1,5},{9... | collective-permute-start | bytes 1634312 | tf_op jit(solution)/shard_map/ppermute | solution.py:247
  326.1 27.6 %collective-permute-start.52 = (bf16[2,448,512]{2,1,0:T(8,128)(2,1)S(1)}, bf16[2,448,512]{2,1,0:T(8,128)(2,1)S(1)}, u32[]{:S(2)}, u32[]{:S(2)}) collective-permute-start(bf16[2,448,512]{2,1,0:T(8,128)(2,1)S(1)} %get-tuple-element.271.refs_0_), channel_id=1, source_target_pairs={{0,1},{1,0},{2,3},{3,2},{4,5},{5,4},{6,7},{7,6},{8,9},{9,8},{10,11... | collective-permute-start | bytes 2752520 | tf_op jit(solution)/shard_map/ppermute | solution.py:52
  362.8 34.0 %collective-permute-start.72 = (bf16[224,2432]{1,0:T(8,128)(2,1)}, bf16[224,2432]{1,0:T(8,128)(2,1)S(1)}, u32[]{:S(2)}, u32[]{:S(2)}) collective-permute-start(bf16[224,2432]{1,0:T(8,128)(2,1)} %get-tuple-element.253), channel_id=1, source_target_pairs={{0,8},{8,16},{16,24},{24,28},{28,20},{20,12},{12,4},{4,0},{1,9},{9... | collective-permute-start | bytes 3268616 | tf_op jit(solution)/shard_map/ppermute | solution.py:247
  363.9 32.9 %collective-permute-start.73 = (bf16[224,2432]{1,0:T(8,128)(2,1)}, bf16[224,2432]{1,0:T(8,128)(2,1)}, u32[]{:S(2)}, u32[]{:S(2)}) collective-permute-start(bf16[224,2432]{1,0:T(8,128)(2,1)} %get-tuple-element.254), channel_id=1, source_target_pairs={{0,4},{8,0},{16,8},{24,16},{28,24},{20,28},{12,20},{4,12},{1,5},{9... | collective-permute-start | bytes 3268616 | tf_op jit(solution)/shard_map/ppermute | solution.py:247
  403.5 46.9 %collective-permute-start.74 = (bf16[224,2432]{1,0:T(8,128)(2,1)}, bf16[224,2432]{1,0:T(8,128)(2,1)S(1)}, u32[]{:S(2)}, u32[]{:S(2)}) collective-permute-start(bf16[224,2432]{1,0:T(8,128)(2,1)} %get-tuple-element.302), channel_id=1, source_target_pairs={{0,8},{8,16},{16,24},{24,28},{28,20},{20,12},{12,4},{4,0},{1,9},{9... | collective-permute-start | bytes 3268616 | tf_op jit(solution)/shard_map/ppermute | solution.py:247
  404.4 46.1 %collective-permute-start.75 = (bf16[224,2432]{1,0:T(8,128)(2,1)}, bf16[224,2432]{1,0:T(8,128)(2,1)S(1)}, u32[]{:S(2)}, u32[]{:S(2)}) collective-permute-start(bf16[224,2432]{1,0:T(8,128)(2,1)} %get-tuple-element.303), channel_id=1, source_target_pairs={{0,4},{8,0},{16,8},{24,16},{28,24},{20,28},{12,20},{4,12},{1,5},{9... | collective-permute-start | bytes 3268616 | tf_op jit(solution)/shard_map/ppermute | solution.py:247
  422.5 79.8 %collective-permute-start.59 = (bf16[2,456,1024]{2,1,0:T(8,128)(2,1)S(1)}, bf16[2,456,1024]{2,1,0:T(8,128)(2,1)S(1)}, u32[]{:S(2)}, u32[]{:S(2)}) collective-permute-start(bf16[2,456,1024]{2,1,0:T(8,128)(2,1)S(1)} %get-tuple-element.285), channel_id=1, source_target_pairs={{0,1},{1,0},{2,3},{3,2},{4,5},{5,4},{6,7},{7,6},{8,9},{9,8},{10,11... | collective-permute-start | bytes 5603336 | tf_op jit(solution)/shard_map/ppermute | solution.py:52
  451.6 52.1 %collective-permute-start.76 = (bf16[224,2432]{1,0:T(8,128)(2,1)S(1)}, bf16[224,2432]{1,0:T(8,128)(2,1)S(1)}, u32[]{:S(2)}, u32[]{:S(2)}) collective-permute-start(bf16[224,2432]{1,0:T(8,128)(2,1)S(1)} %get-tuple-element.305), channel_id=1, source_target_pairs={{0,8},{8,16},{16,24},{24,28},{28,20},{20,12},{12,4},{4,0},{1,9},{9... | collective-permute-start | bytes 3268616 | tf_op jit(solution)/shard_map/ppermute | solution.py:247
  453.7 64.1 %collective-permute-start.54 = (bf16[2,448,1024]{2,1,0:T(8,128)(2,1)}, bf16[2,448,1024]{2,1,0:T(8,128)(2,1)S(1)}, u32[]{:S(2)}, u32[]{:S(2)}) collective-permute-start(bf16[2,448,1024]{2,1,0:T(8,128)(2,1)} %get-tuple-element.275), channel_id=1, source_target_pairs={{0,1},{1,0},{2,3},{3,2},{4,5},{5,4},{6,7},{7,6},{8,9},{9,8},{10,11... | collective-permute-start | bytes 5505032 | tf_op jit(solution)/shard_map/ppermute | solution.py:52
  462.1 43.9 %collective-permute-start.77 = (bf16[224,2432]{1,0:T(8,128)(2,1)S(1)}, bf16[224,2432]{1,0:T(8,128)(2,1)S(1)}, u32[]{:S(2)}, u32[]{:S(2)}) collective-permute-start(bf16[224,2432]{1,0:T(8,128)(2,1)S(1)} %get-tuple-element.306), channel_id=1, source_target_pairs={{0,4},{8,0},{16,8},{24,16},{28,24},{20,28},{12,20},{4,12},{1,5},{9... | collective-permute-start | bytes 3268616 | tf_op jit(solution)/shard_map/ppermute | solution.py:247
  462.4 38.0 %collective-permute-start.79 = (bf16[224,1216]{1,0:T(8,128)(2,1)S(1)}, bf16[224,1216]{1,0:T(8,128)(2,1)S(1)}, u32[]{:S(2)}, u32[]{:S(2)}) collective-permute-start(bf16[224,1216]{1,0:T(8,128)(2,1)S(1)} %copy-done.38), channel_id=1, source_target_pairs={{0,4},{8,0},{16,8},{24,16},{28,24},{20,28},{12,20},{4,12},{1,5},{9... | collective-permute-start | bytes 1634312 | tf_op jit(solution)/shard_map/ppermute | solution.py:247
  503.7 23.7 %collective-permute-start.60 = (bf16[2,456,512]{2,1,0:T(8,128)(2,1)S(1)}, bf16[2,456,512]{2,1,0:T(8,128)(2,1)S(1)}, u32[]{:S(2)}, u32[]{:S(2)}) collective-permute-start(bf16[2,456,512]{2,1,0:T(8,128)(2,1)S(1)} %get-tuple-element.287), channel_id=1, source_target_pairs={{0,2},{1,3},{2,0},{3,1},{4,6},{5,7},{6,4},{7,5},{8,10},{9,11},{10,... | collective-permute-start | bytes 2801672 | tf_op jit(solution)/shard_map/ppermute | solution.py:52
  519.7 24.6 %collective-permute-start.55 = (bf16[2,448,512]{2,1,0:T(8,128)(2,1)}, bf16[2,448,512]{2,1,0:T(8,128)(2,1)S(1)}, u32[]{:S(2)}, u32[]{:S(2)}) collective-permute-start(bf16[2,448,512]{2,1,0:T(8,128)(2,1)} %get-tuple-element.277), channel_id=1, source_target_pairs={{0,2},{1,3},{2,0},{3,1},{4,6},{5,7},{6,4},{7,5},{8,10},{9,11},{10,... | collective-permute-start | bytes 2752520 | tf_op jit(solution)/shard_map/ppermute | solution.py:52
  (113 other events, 1548.1 us)

commit v4 on v3

--- a/solution.py
+++ b/solution.py
@@ -56,7 +56,8 @@
     def __init__(self, block):
         self.block, self.far, self.near = block, swap(block, 2), swap(block, 1)
 
-    def cross(self):
+    def cross(self, *others):
+        self.far = tie(self.far, *others)
         self.both = swap(self.far, 1)
 
     def blocks(self):
@@ -105,6 +106,12 @@
     )(index, *blocks, *(gains if normed else ()))
 
 
+def halves(value):
+    high = value.astype(BF).astype(F32)
+    place = lax.broadcasted_iota(jnp.int32, (8, value.shape[1]), 0)
+    return jnp.where(place == 0, high, jnp.where(place == 1, value - high, 0.0)).astype(BF)
+
+
 def projected(index, weights, rights, name, columns=None, row=None):
     rows = D // 4
     depth, width = rights[0].shape
@@ -114,7 +121,7 @@
 
     def kernel(index_ref, weight_ref, *refs):
         right_refs = refs[: len(rights)]
-        sent, kept = refs[-2:]
+        kept = refs[-1]
         total = 0.0
         for k, right in enumerate(right_refs):
             left = weight_ref[k] if stacked else weight_ref[...][:, start : start + depth]
@@ -122,15 +129,13 @@
         step = pl.program_id(0)
         total = total.astype(BF)
 
-        @pl.when(step < 2)
-        def _():
-            sent[0, :rows] = total
+        def send(sent):
+            sent[:rows] = total
             if row is not None:
-                value = refs[len(rights)][...]
-                high = value.astype(BF).astype(F32)
-                place = lax.broadcasted_iota(jnp.int32, (8, width), 0)
-                tail = jnp.where(place == 0, high, jnp.where(place == 1, value - high, 0.0))
-                sent[0, rows:] = tail.astype(BF)
+                sent[rows:] = halves(refs[len(rights)][...])
+
+        for place in range(2):
+            pl.when(step == place)(lambda place=place: send(refs[place - 3]))
 
         @pl.when(step >= 2)
         def _():
@@ -154,56 +159,91 @@
             num_scalar_prefetch=1,
             grid=(4,),
             in_specs=in_specs,
-            out_specs=[
-                pl.BlockSpec((1, rows + extra, width), lambda i, r: (jnp.minimum(i, 1), 0, 0)),
-                pl.BlockSpec((1, rows, width), lambda i, r: (jnp.maximum(i - 2, 0), 0, 0)),
-            ],
+            out_specs=[pl.BlockSpec((rows + extra, width), lambda i, r: (0, 0))] * 2
+            + [pl.BlockSpec((1, rows, width), lambda i, r: (jnp.maximum(i - 2, 0), 0, 0))],
         ),
-        out_shape=[
-            jax.ShapeDtypeStruct((2, rows + extra, width), BF),
-            jax.ShapeDtypeStruct((2, rows, width), BF),
-        ],
+        out_shape=[jax.ShapeDtypeStruct((rows + extra, width), BF)] * 2
+        + [jax.ShapeDtypeStruct((2, rows, width), BF)],
         compiler_params=params(32),
         cost_estimate=cost(2 * D * depth * len(rights) * width, 8 << 20),
     )(index, weights, *rights, *(() if row is None else (row,)))
 
 
+class Reduce:
+    def __init__(self, index, parts, row=None):
+        self.index, self.row = index, row
+        self.sent, self.kept = tuple(parts[:2]), parts[2]
+        self.got = [swap(sent, 1) for sent in self.sent]
+        self.here, self.there = [], []
+
+    def cross(self, *others):
+        rows, width = self.kept.shape[1:]
+        extra = self.sent[0].shape[0] - rows
+        length = width // 2
+
+        def kernel(kept_ref, got_ref, *refs):
+            out = refs[-1]
+            out[:rows] = (kept_ref[0].astype(F32) + got_ref[:rows].astype(F32)).astype(BF)
+            if extra:
+                two = got_ref[rows:].astype(F32)
+                out[rows:] = halves(refs[0][...] + two[:1] + two[1:2])
+
+        for place in range(2):
+            given = (self.kept, tie(self.got[place], *others))
+            given += () if self.row is None else (self.row,)
+            tall = pl.BlockSpec((rows + extra, length), lambda i: (0, i))
+            kept = pl.BlockSpec((1, rows, length), lambda i, place=place: (place, 0, i))
+            found = pl.pallas_call(
+                kernel,
+                name="core_sum",
+                grid=(2,),
+                in_specs=[kept, tall]
+                + ([] if self.row is None else [pl.BlockSpec((1, length), lambda i: (0, i))]),
+                out_specs=tall,
+                out_shape=jax.ShapeDtypeStruct((rows + extra, width), BF),
+                compiler_params=params(),
+                cost_estimate=cost(1 << 28),
+            )(*given)
+            self.here.append(found)
+            self.there.append(swap(found, 2))
+
+
 class Scatter:
     def __init__(self, index, parts, seqs, row=None):
         self.index, self.row, self.seqs = index, row, seqs
-        self.sent, self.kept = parts
-        self.got = swap(self.sent, 1)
-
-    def cross(self):
+        self.sent, self.kept = tuple(parts[:2]), parts[2]
+        self.got = [swap(sent, 1) for sent in self.sent]
+
+    def cross(self, *others):
         seqs, row = self.seqs, self.row
         rows, width = self.kept.shape[1:]
         length = width // seqs
-        extra = 0 if row is None else 8
-
-        def kernel(index_ref, kept_ref, got_ref, *refs):
+        extra = self.sent[0].shape[0] - rows
+        got = (tie(self.got[0], *others), self.got[1])
+
+        def kernel(index_ref, kept_ref, first_ref, second_ref, *refs):
             far, mine = refs[-2:] if row is None else refs[-3:-1]
             chip = index_ref[0] // 2
-            other = kept_ref[1 - chip].astype(F32) + got_ref[1 - chip, :rows].astype(F32)
-            far[0, :rows] = other.astype(BF)
-            mine[0] = kept_ref[chip].astype(F32) + got_ref[chip, :rows].astype(F32)
+
+            def pair(place):
+                got = jnp.where(place == 0, first_ref[:rows], second_ref[:rows])
+                return kept_ref[place].astype(F32) + got.astype(F32)
+
+            far[0, :rows] = pair(1 - chip).astype(BF)
+            mine[0] = pair(chip)
             if row is not None:
-                two = got_ref[0, rows:].astype(F32)
+                two = first_ref[rows:].astype(F32)
                 value = refs[0][...] + two[:1] + two[1:2]
                 refs[-1][0] = value
-                high = value.astype(BF).astype(F32)
-                place = lax.broadcasted_iota(jnp.int32, (8, length), 0)
-                tail = jnp.where(place == 0, high, jnp.where(place == 1, value - high, 0.0))
-                far[0, rows:] = tail.astype(BF)
+                far[0, rows:] = halves(value)
 
         def spec(height):
             return pl.BlockSpec((1, height, length), lambda s, r: (s, 0, 0))
 
         out = [((seqs, rows + extra, length), BF), ((seqs, rows, length), F32)]
         out += [] if row is None else [((seqs, 1, length), F32)]
-        in_specs = [
-            pl.BlockSpec((2, rows, length), lambda s, r: (0, 0, s)),
-            pl.BlockSpec((2, rows + extra, length), lambda s, r: (0, 0, s)),
-        ]
+        in_specs = [pl.BlockSpec((2, rows, length), lambda s, r: (0, 0, s))]
+        in_specs += [pl.BlockSpec((rows + extra, length), lambda s, r: (0, s))] * 2
         in_specs += [] if row is None else [pl.BlockSpec((1, length), lambda s, r: (0, s))]
         found = pl.pallas_call(
             kernel,
@@ -217,7 +257,7 @@
             out_shape=[jax.ShapeDtypeStruct(*o) for o in out],
             compiler_params=params(),
             cost_estimate=cost(1 << 28),
-        )(self.index, self.kept, self.got, *(() if row is None else (row,)))
+        )(self.index, self.kept, *got, *(() if row is None else (row,)))
         self.sent_far, self.mine, self.rows = found[0], found[1], rows
         self.half = None if row is None else found[2]
         self.last = swap(self.sent_far, 2)
@@ -231,6 +271,151 @@
         return total, self.half + two[:, :1] + two[:, 1:]
 
 
+def resid_added(index, reduce, own, far, *others):
+    seqs, rows, length = own.shape
+    width = seqs * length
+
+    def kernel(index_ref, here_0, here_1, there_0, there_1, own_ref, far_ref, resid, both_0, both_1):
+        chip = index_ref[0] // 2
+        given = (here_0, there_0, both_0), (here_1, there_1, both_1)
+        for place, (here, there, both) in enumerate(given):
+            mine = chip == place
+            base = jnp.where(mine, own_ref[0].astype(F32), far_ref[0].astype(F32))
+            value = base + (here[...].astype(F32) + there[...].astype(F32))
+            both[...] = value.astype(BF)
+
+            @pl.when(mine)
+            def _():
+                resid[0] = value
+
+    wide = pl.BlockSpec((rows, length), lambda s, r: (0, s))
+    one = pl.BlockSpec((1, rows, length), lambda s, r: (s, 0, 0))
+    resid, *both = pl.pallas_call(
+        kernel,
+        name="resid",
+        grid_spec=pltpu.PrefetchScalarGridSpec(
+            num_scalar_prefetch=1,
+            grid=(seqs,),
+            in_specs=[wide] * 4 + [one, one],
+            out_specs=[one, wide, wide],
+        ),
+        out_shape=[jax.ShapeDtypeStruct((seqs, rows, length), F32)]
+        + [jax.ShapeDtypeStruct((rows, width), BF)] * 2,
+        compiler_params=params(),
+        cost_estimate=cost(1 << 28),
+    )(index, *reduce.here, tie(reduce.there[0], *others), reduce.there[1], own, far)
+    return resid, both
+
+
+def resid_back(index, reduce, grad_own, grad_far, resid, resid_both, inverse, gains, *others):
+    seqs, rows, length = grad_own.shape
+    width = seqs * length
+
+    def kernel(index_ref, *refs):
+        here, there, held_both, both = refs[:2], refs[2:4], refs[4:6], refs[-3:-1]
+        own_ref, far_ref, resid_ref, inverse_ref, own_gain_ref, far_gain_ref, grad = refs[6:13]
+        chip = index_ref[0] // 2
+        tail = here[0][rows:].astype(F32) + there[0][rows:].astype(F32)
+        inv = inverse_ref[0]
+        scale = inv * inv * (tail[:1] + tail[1:2]) / D
+        own_gain_column = own_gain_ref[...][:, 1:2].astype(F32)
+        far_gain_column = far_gain_ref[...][:, 1:2].astype(F32)
+        for place in range(2):
+            mine = chip == place
+            normed = here[place][:rows].astype(F32) + there[place][:rows].astype(F32)
+            base = jnp.where(mine, own_ref[0].astype(F32), far_ref[0].astype(F32))
+            gain = jnp.where(mine, own_gain_column, far_gain_column)
+            most = base + inv * gain * normed
+            both[place][...] = (most - held_both[place][...].astype(F32) * scale).astype(BF)
+
+            @pl.when(mine)
+            def _():
+                held = resid_ref[0]
+                grad[0] = most - held * scale
+                refs[-1][0] = jnp.sum(held * inv * normed, 1, keepdims=True)
+
+    wide = pl.BlockSpec((rows, length), lambda s, r: (0, s))
+    more = pl.BlockSpec((rows + 8, length), lambda s, r: (0, s))
+    one = pl.BlockSpec((1, rows, length), lambda s, r: (s, 0, 0))
+    row = pl.BlockSpec((1, 1, length), lambda s, r: (s, 0, 0))
+    gain = pl.BlockSpec((rows, 2), lambda s, r: (0, 0))
+    grad, *both, gain_sum = pl.pallas_call(
+        kernel,
+        name="resid_back",
+        grid_spec=pltpu.PrefetchScalarGridSpec(
+            num_scalar_prefetch=1,
+            grid=(seqs,),
+            in_specs=[more] * 4 + [wide] * 2 + [one, one, one, row, gain, gain],
+            out_specs=[one, wide, wide, pl.BlockSpec((1, rows, 1), lambda s, r: (s, 0, 0))],
+        ),
+        out_shape=[jax.ShapeDtypeStruct((seqs, rows, length), F32)]
+        + [jax.ShapeDtypeStruct((rows, width), BF)] * 2
+        + [jax.ShapeDtypeStruct((seqs, rows, 1), F32)],
+        compiler_params=params(),
+        cost_estimate=cost(1 << 28),
+    )(
+        index,
+        *reduce.here,
+        tie(reduce.there[0], *others),
+        reduce.there[1],
+        *resid_both,
+        grad_own,
+        grad_far,
+        resid,
+        inverse,
+        *gains,
+    )
+    return grad, both, gain_sum
+
+
+def gathered_pair(index, here, there, seqs, gains=None, column=0):
+    rows, width = here[0].shape
+    length = width // seqs
+    normed = gains is not None
+
+    def kernel(index_ref, *refs):
+        me = index_ref[0]
+        chip, core = me // 2, me % 2
+        blocks = refs[:2], refs[2:4]
+        out = refs[8 if normed else 4]
+        if normed:
+            total = 0.0
+            for ref in refs[:4]:
+                value = ref[...].astype(F32)
+                total += jnp.sum(value * value, 0, keepdims=True)
+            inverse = lax.rsqrt(total / D + EPS)
+            refs[9][0] = inverse
+            columns = [ref[...][:, column : column + 1].astype(F32) for ref in refs[4:8]]
+        for other in range(2):
+            for place in range(2):
+                value = blocks[other][place][...]
+                if normed:
+                    gain = jnp.where(chip == place, columns[other], columns[2 + other])
+                    value = (value.astype(F32) * inverse * gain).astype(BF)
+                row = 2 * place + (core ^ other)
+                out[pl.ds(pl.multiple_of(row * rows, 16), rows), :] = value
+
+    wide = pl.BlockSpec((rows, length), lambda s, r: (0, s))
+    full = pl.BlockSpec((4 * rows, length), lambda s, r: (0, s))
+    row = pl.BlockSpec((1, 1, length), lambda s, r: (s, 0, 0))
+    gain = pl.BlockSpec((rows, 2), lambda s, r: (0, 0))
+    shape = jax.ShapeDtypeStruct((4 * rows, width), BF)
+    inverse = jax.ShapeDtypeStruct((seqs, 1, length), F32)
+    return pl.pallas_call(
+        kernel,
+        name="pair_norm" if normed else "pair",
+        grid_spec=pltpu.PrefetchScalarGridSpec(
+            num_scalar_prefetch=1,
+            grid=(seqs,),
+            in_specs=[wide] * 4 + ([gain] * 4 if normed else []),
+            out_specs=[full, row] if normed else full,
+        ),
+        out_shape=[shape, inverse] if normed else shape,
+        compiler_params=params(),
+        cost_estimate=cost(1 << 30),
+    )(index, *here, *there, *(gains if normed else ()))
+
+
 def ring_order(count):
     half = count // 2
     return [2 * r for r in range(half)] + [2 * r + 1 for r in reversed(range(half))]
@@ -258,7 +443,7 @@
 
 class Gather:
     def __init__(self, shard):
-        self.shard, self.axis = shard, shard.ndim - 2
+        self.shard, self.axis, self.sent = shard, shard.ndim - 2, ()
         self.right, self.left = [shard], [shard]
 
     def advance(self, *others):
@@ -272,6 +457,7 @@
         others = jax.tree.leaves(others)
         if others:
             right, left = lax.optimization_barrier((right, left, *others))[:2]
+        self.sent = right, left
         self.right.append(hop(right, 1))
         self.left.append(hop(left, -1))
 
@@ -438,14 +624,16 @@
             count = lax.axis_size("ctx")
             self.other = lax.ppermute(value, "ctx", [(i, i ^ 1) for i in range(count)])
 
-    def first(self):
+    def first(self, *others):
         if ringed():
-            self.total = (self.value.astype(F32) + self.other.astype(F32)).astype(BF)
+            other = tie(self.other, *others)
+            self.total = (self.value.astype(F32) + other.astype(F32)).astype(BF)
             self.one = shifted(self.total, 2 * self.sign)
 
-    def second(self):
+    def second(self, *others):
         if ringed():
-            self.sent = (self.total.astype(F32) + self.one.astype(F32)).astype(BF)
+            one = tie(self.one, *others)
+            self.sent = (self.total.astype(F32) + one.astype(F32)).astype(BF)
             self.two = shifted(self.sent, 4 * self.sign)
 
     def result(self):
@@ -649,37 +837,39 @@
     ring_attn.advance(*token)
     fence(ring_attn.here(), ring_gate_up.shard)
     ring_attn.advance(*token)
-    ring_gate_up.advance(*token)
-    fence(spread_in.far)
-    spread_in.cross()
+    spread_in.cross(*token)
     grad_out = (cotangent.transpose(0, 2, 1).astype(F32) * valid).astype(BF)
-    spread_out = Spread(turn(grad_out))
+    spread_out = Spread(tie(grad_out, spread_in.far))
+    fence(ring_attn.here())
+    ring_attn.advance(*token)
+    ring_gate_up.advance(ring_attn.sent)
     fence(spread_in.near, spread_in.both)
     blocks = spread_in.blocks()
     normed_one, inv_one = gathered(index, (turn(blocks[0]),) + blocks[1:], gains.blocks(), 0)
-    fence(ring_attn.here(), normed_one)
-    ring_attn.advance(*token)
+    fence(normed_one)
     fence(ring_attn.here())
     w_attn = ring_attn.full(turn(index))
-    fence(w_attn, ring_gate_up.here())
-    ring_gate_up.advance(*token)
-
-    qkv = mm_tn(w_attn[:, :columns], turn(normed_one)).astype(BF)
+
+    qkv = mm_tn(w_attn[:, :columns], normed_one).astype(BF)
     (own,) = call(state_kernel, "state", ("key", "value", "valid"), (("state", BF),), 0.5)(
         qkv, qkv, valid
     )
     before = Before(own, 1)
-    fence(ring_gate_up.here(), before.other)
-    before.first()
+    fence(own)
+    fence(before.other)
+    before.first(*token)
+    fence(before.total if ringed() else ())
+    fence(ring_gate_up.here())
+    ring_gate_up.advance(*token)
     fence(before.one)
-    before.second()
+    before.second(*token)
     fence(before.sent)
-    ring_gate_up.advance(*token)
-    fence(spread_out.far)
-    spread_out.cross()
+    spread_out.cross(*token)
     blocks = spread_out.blocks()
     grad_out_full = gathered(index, (turn(blocks[0]),) + blocks[1:])
     fence(grad_out_full)
+    fence(ring_gate_up.here())
+    ring_gate_up.advance(*token)
 
     state = before.result()
     mixed, denom = call(
@@ -690,29 +880,29 @@
         1,
     )(turn(qkv), qkv, qkv, valid, state)
     scatter_attn = Scatter(index, projected(index, w_attn, [mixed], "out_proj", columns), seqs)
-    fence(scatter_attn.got)
-    scatter_attn.cross()
-    fence(scatter_attn.sent_far, ring_gate_up.here())
+    fence(scatter_attn.sent)
+    scatter_attn.cross(*token)
+    fence(scatter_attn.sent_far)
+    fence(ring_gate_up.here())
+    ring_gate_up.advance(*token)
     ring_down.advance(*token)
-    ring_gate_up.advance(*token)
     resid = hidden.astype(F32) + scatter_attn.sums(*token)
     spread_resid = Spread(resid.astype(BF))
-    fence(spread_resid.block, ring_down.here())
+    fence(spread_resid.block)
+    fence(ring_gate_up.here(), ring_down.here())
     ring_down.advance(*token)
-    fence(ring_gate_up.here())
     gate_up = ring_gate_up.full(turn(index))
     fence(gate_up)
-    fence(spread_resid.far)
-    spread_resid.cross()
     fence(ring_down.here())
     ring_down.advance(*token)
+    spread_resid.cross(*token)
 
     blocks = spread_resid.blocks()
-    normed_two, inv_two = gathered(index, (turn(blocks[0]),) + blocks[1:], gains.blocks(), 1)
+    normed_two, inv_two = gathered(index, blocks, gains.blocks(), 1)
     fence(normed_two)
-    gate = mm_tn(gate_up[0], turn(normed_two))
     fence(ring_down.here())
     ring_down.advance(*token)
+    gate = mm_tn(gate_up[0], turn(normed_two))
     up = mm_tn(gate_up[1], normed_two)
     act = (gate * jax.nn.sigmoid(gate) * up).astype(BF)
     fence(act)
@@ -732,8 +922,7 @@
     fence(scatter_two.sent)
     down_ring = Products(index, products([turn(grad_out_full)], [act], "down_grad"))
     fence(down_ring.sent)
-    fence(scatter_two.got)
-    scatter_two.cross()
+    scatter_two.cross(*token)
     fence(scatter_two.sent_far)
     gate_up_ring = Products(
         index, products([normed_two, normed_two], [turn(g_gate), g_up], "gate_up_grad")
@@ -756,25 +945,33 @@
     fence(gate_up_ring.here())
     gate_up_ring.advance(*token)
     fence(gate_up_ring.sent)
+    ffn_out = projected(index, down_full, [turn(act)], "ffn_out")
+    fence(ffn_out)
     fence(down_ring.here())
     down_ring.advance(*token)
     fence(down_ring.sent)
-    ffn_out = projected(index, down_full, [turn(act)], "ffn_out")
-    fence(ffn_out)
-    fence(spread_grad.far)
-    spread_grad.cross()
-    fence(down_ring.here())
-    down_ring.advance(*token)
-    fence(down_ring.sent)
+    spread_grad.cross(*token)
     blocks = spread_grad.blocks()
-    resid_full = gathered(index, (turn(blocks[0]),) + blocks[1:])
-    g_attn = mm_tn(w_attn[:, columns:], resid_full).astype(BF)
+    resid_full = gathered(index, blocks)
+    fence(resid_full)
+    g_attn = mm_tn(w_attn[:, columns:], turn(resid_full)).astype(BF)
     weighted, spread = call(
         spread_kernel, "spread", ("query", "head", "head", "row"), (("ext", BF), ("state", BF)), 0.5
-    )(qkv, g_attn, mixed, denom)
+    )(turn(qkv), g_attn, mixed, denom)
     after = Before(spread, -1)
     fence(spread)
-    scatter_out = Scatter(index, [tie(ffn_out[0], *token), ffn_out[1]], seqs)
+    fence(gate_up_ring.here())
+    fence(after.other)
+    after.first(*token)
+    fence(after.total if ringed() else ())
+    scatter_out = Scatter(index, [*lax.optimization_barrier((*ffn_out, *token))[:3]], seqs)
+    fence(after.one)
+    after.second(*token)
+    fence(after.sent)
+    gate_up_ring.advance(*token)
+    fence(gate_up_ring.sent)
+    scatter_out.cross(*token)
+    fence(scatter_out.sent_far)
     local = call(
         local_kernel,
         "local",
@@ -782,18 +979,7 @@
         (("feat", BF), ("feat", F32), ("head", F32)),
         2,
     )(turn(qkv), qkv, qkv, valid, state, weighted)
-    fence(after.other)
-    after.first()
-    fence(after.one)
-    after.second()
-    fence(after.sent)
-    fence(gate_up_ring.here(), local)
-    gate_up_ring.advance(*token)
-    fence(gate_up_ring.sent)
-    fence(scatter_out.got)
-    scatter_out.cross()
-    down_grad = down_ring.final(*token)
-    fence(down_grad)
+    fence(local)
 
     def later(*refs):
         later_kernel(heads, *refs)
@@ -807,40 +993,45 @@
     )(turn(qkv), qkv, valid, after.result(), *local)
     inner = jnp.sum(d_qkv.astype(F32) * qkv.astype(F32), 0, keepdims=True)
     scatter_one = Scatter(
-        index, projected(index, w_attn, [d_qkv], "qkv_back", 0, row=inner), seqs, inner
+        index, projected(index, w_attn, [d_qkv], "qkv_back", row=inner), seqs, inner
     )
     fence(scatter_one.sent)
+    fence(down_ring.here())
+    down_ring.advance(*token)
+    fence(down_ring.sent)
     attn_ring = Products(
         index, products([turn(normed_one), resid_full], [d_qkv, mixed], "attn_grad")
     )
     fence(attn_ring.sent)
-    fence(scatter_one.got)
-    scatter_one.cross()
+    fence(gate_up_ring.here())
+    gate_up_ring.advance(*token)
+    fence(gate_up_ring.sent)
+    scatter_one.cross(*token)
     fence(scatter_one.sent_far)
     fence(attn_ring.here())
     attn_ring.advance(*token)
     fence(attn_ring.sent)
-    fence(gate_up_ring.here())
-    gate_up_ring.advance(*token)
-    fence(gate_up_ring.sent)
     layer_out = (resid + scatter_out.sums(*token)).astype(BF)
     fence(layer_out)
-    fence(attn_ring.here())
-    attn_ring.advance(*token)
-    fence(attn_ring.sent)
     d_norm, inner = scatter_one.sums(*token)
     value = hidden.astype(F32)
     gain_one_part = jnp.sum(value * inv_one * d_norm, (0, 2))
     grad_input = (
         d_resid + inv_one * gain_one * d_norm - value * (inv_one * inv_one * inner / D)
     )
-    gain_grads = ctx_total(jnp.stack([gain_one_part, gain_two_part]))
-    fence(grad_input)
+    fence(gain_one_part, grad_input)
+    gain_grads = ctx_total(jnp.stack([gain_one_part, gain_two_part]) + token[0][:1, :1])
+    fence(attn_ring.here())
+    attn_ring.advance(*token)
+    fence(attn_ring.sent)
+    down_grad = down_ring.final(*token)
+    fence(down_grad)
     fence(attn_ring.here())
     attn_ring.advance(*token)
     fence(attn_ring.sent)
     gate_up_grad = gate_up_ring.final(*token)
-    fence(gate_up_grad, gain_grads)
+    fence(gate_up_grad)
+    fence(gain_grads)
     attn_grad = attn_ring.final(*token)
 
     values, queries = heads * HEAD_DIM, heads * FEAT

time: 559 us -> 532 us (0.952)
  waiting for transfers between devices: 279 us -> 240 us
    ppermute x48, waiting for transfers between devices: 193 us -> 156 us  [hop(): return lax.ppermute(value, 'ctx', pairs)]
    ppermute x23 -> x27, waiting for transfers between devices: 24.1 us -> 6.09 us  [swap(): return lax.ppermute(value, 'wt', [(i, i ^ bit) for i in range(count)])]
    ppermute x2, waiting for transfers between devices: 13.8 us -> 23.9 us  [__init__(): self.other = lax.ppermute(value, 'ctx', [(i, i ^ 1) for i in range(count)])]
    ppermute x3, waiting for transfers between devices: 2.69 us -> 8.48 us  [ctx_total(): value = value + lax.ppermute(value, 'ctx', [(i, i ^ bit) for i in range(8)])]
    ppermute x23 -> x27, starting transfers between devices: 9.73 us -> 15.1 us  [swap(): return lax.ppermute(value, 'wt', [(i, i ^ bit) for i in range(count)])]
    unnamed x140 -> x158, local copies, waits for them, and re-layouts: 21.5 us -> 21 us
  transfers between devices with their start and end apart: 80 -> 84, of which waited for: 43 -> 36; matrix products, arithmetic and copies ran while one was open for 6% -> 7% of each run, Pallas kernels for 14% -> 16%
where the time goes in v4:
time: 532 us; the launch traced here: 526 us
  waiting for transfers between devices  240 us (45%)
  Pallas kernels  113 us (21%)
  starting transfers between devices  91.6 us (17%)
  matrix products  32 us (6%)
  local copies, waits for them, and re-layouts  27.5 us (5%)
  other arithmetic  19.9 us (4%)
    ppermute x48, waiting for transfers between devices, hop(): return lax.ppermute(value, 'ctx', pairs)  156 us
    ppermute x48, starting transfers between devices, hop(): return lax.ppermute(value, 'ctx', pairs)  61.7 us
    ppermute x4, waiting for transfers between devices, shifted(): return lax.ppermute(value, 'ctx', pairs)  45.7 us
    dot_general x5, matrix products, mm_tn(): lax.dot_general(left, right, (((0,), (0,)), ((), ())), preferred_element_...  32 us
    pallas_call x4, Pallas kernels, projected(): pl.pallas_call(kernel, name=name, grid_spec=pltpu.PrefetchScalarGridSpec(...  29.1 us
    ppermute x2, waiting for transfers between devices, __init__(): self.other = lax.ppermute(value, 'ctx', [(i, i ^ 1) for i in range(count)])  23.9 us
    pallas_call x3, Pallas kernels, products(): pl.pallas_call(kernel, name=name, grid=(4,), in_specs=[pl.BlockSpec((rows...  22.3 us
    unnamed x158, local copies, waits for them, and re-layouts  21 us
  transfers between devices with their start and end apart: 84, of which 36 were waited for; matrix products, arithmetic and copies ran while one was open for 7% of the time, Pallas kernels for 16%

profile of v4, /device:TPU:0, one launch (start us, length us, event | category | flops | bytes accessed | tf_op | source)
XLA Modules:
  0.0 526.5 jit_solution(5011676233104456947)
XLA Ops:
  9.7 8.5 %collective-permute-done.refs_1_ = bf16[224,1024]{1,0:T(8,128)(2,1)S(1)} collective-permute-done((bf16[224,1024]{1,0:T(8,128)(2,1)S(1)}, bf16[224,1024]{1,0:T(8,128)(2,1)S(1)}, u32[]{:S(2)}, u32[]{:S(2)}) %collective-permute-start) | collective-permute-done | bytes 458784 | tf_op jit(solution)/shard_map/ppermute | solution.py:432
  23.1 7.9 %collective-permute-done.2.refs_2_ = bf16[224,1024]{1,0:T(8,128)(2,1)} collective-permute-done((bf16[224,1024]{1,0:T(8,128)(2,1)S(1)}, bf16[224,1024]{1,0:T(8,128)(2,1)}, u32[]{:S(2)}, u32[]{:S(2)}) %collective-permute-start.2) | collective-permute-done | bytes 458784 | tf_op jit(solution)/shard_map/ppermute | solution.py:432
  36.3 9.2 %collective-permute-done.4.refs_3_ = bf16[224,1024]{1,0:T(8,128)(2,1)S(1)} collective-permute-done((bf16[224,1024]{1,0:T(8,128)(2,1)}, bf16[224,1024]{1,0:T(8,128)(2,1)S(1)}, u32[]{:S(2)}, u32[]{:S(2)}) %collective-permute-start.4) | collective-permute-done | bytes 458784 | tf_op jit(solution)/shard_map/ppermute | solution.py:432
  69.5 18.3 %collective-permute-done.14 = bf16[2,4,160,128]{3,2,1,0:T(8,128)(2,1)S(1)} collective-permute-done((bf16[2,4,160,128]{3,2,1,0:T(8,128)(2,1)S(1)}, bf16[2,4,160,128]{3,2,1,0:T(8,128)(2,1)S(1)}, u32[]{:S(2)}, u32[]{:S(2)}) %collective-permute-start.14) | collective-permute-done | bytes 327712 | tf_op jit(solution)/shard_map/ppermute | solution.py:625
  91.5 5.9 %collective-permute-done.17 = bf16[2,4,160,128]{3,2,1,0:T(8,128)(2,1)S(1)} collective-permute-done((bf16[2,4,160,128]{3,2,1,0:T(8,128)(2,1)S(1)}, bf16[2,4,160,128]{3,2,1,0:T(8,128)(2,1)S(1)}, u32[]{:S(2)}, u32[]{:S(2)}) %collective-permute-start.17) | collective-permute-done | bytes 327712 | tf_op jit(solution)/shard_map/ppermute | solution.py:616
  98.9 5.7 %collective-permute-start.23 = (bf16[2,4,160,128]{3,2,1,0:T(8,128)(2,1)}, bf16[2,4,160,128]{3,2,1,0:T(8,128)(2,1)}, u32[]{:S(2)}, u32[]{:S(2)}) collective-permute-start(bf16[2,4,160,128]{3,2,1,0:T(8,128)(2,1)} %add_convert_fusion.5), channel_id=1, source_target_pairs={{0,16},{4,20},{8,24},{12,28},{1,17},{5,21},{9,25},{13,29},{2,18},{... | collective-permute-start | bytes 983048 | tf_op jit(solution)/shard_map/ppermute | solution.py:616
  104.6 23.1 %collective-permute-done.23 = bf16[2,4,160,128]{3,2,1,0:T(8,128)(2,1)} collective-permute-done((bf16[2,4,160,128]{3,2,1,0:T(8,128)(2,1)}, bf16[2,4,160,128]{3,2,1,0:T(8,128)(2,1)}, u32[]{:S(2)}, u32[]{:S(2)}) %collective-permute-start.23) | collective-permute-done | bytes 327712 | tf_op jit(solution)/shard_map/ppermute | solution.py:616
  141.1 4.9 collective-permute-start.27
  149.1 22.0 %collective-permute-done.27.refs_3_ = bf16[2,224,1216]{2,1,0:T(8,128)(2,1)S(1)} collective-permute-done((bf16[2,224,1216]{2,1,0:T(8,128)(2,1)}, bf16[2,224,1216]{2,1,0:T(8,128)(2,1)S(1)}, u32[]{:S(2)}, u32[]{:S(2)}) %collective-permute-start.27) | collective-permute-done | bytes 1089568 | tf_op jit(solution)/shard_map/ppermute | solution.py:432
  180.7 8.5 %collective-permute-done.29.refs_4_ = bf16[2,112,1216]{2,1,0:T(8,128)(2,1)S(1)} collective-permute-done((bf16[2,112,1216]{2,1,0:T(8,128)(2,1)S(1)}, bf16[2,112,1216]{2,1,0:T(8,128)(2,1)S(1)}, u32[]{:S(2)}, u32[]{:S(2)}) %collective-permute-start.29) | collective-permute-done | bytes 544800 | tf_op jit(solution)/shard_map/ppermute | solution.py:432
  191.4 8.0 %collective-permute-done.31.refs_1_ = bf16[224,1216]{1,0:T(8,128)(2,1)S(1)} collective-permute-done((bf16[224,1216]{1,0:T(8,128)(2,1)S(1)}, bf16[224,1216]{1,0:T(8,128)(2,1)S(1)}, u32[]{:S(2)}, u32[]{:S(2)}) %collective-permute-start.31) | collective-permute-done | bytes 544800 | tf_op jit(solution)/shard_map/ppermute | solution.py:432
  206.8 7.8 %collective-permute-done.33.refs_2_ = bf16[224,1216]{1,0:T(8,128)(2,1)S(1)} collective-permute-done((bf16[224,1216]{1,0:T(8,128)(2,1)S(1)}, bf16[224,1216]{1,0:T(8,128)(2,1)S(1)}, u32[]{:S(2)}, u32[]{:S(2)}) %collective-permute-start.33) | collective-permute-done | bytes 544800 | tf_op jit(solution)/shard_map/ppermute | solution.py:432
  217.6 13.1 %collective-permute-done.38.refs_3_ = bf16[224,1216]{1,0:T(8,128)(2,1)S(1)} collective-permute-done((bf16[224,1216]{1,0:T(8,128)(2,1)S(1)}, bf16[224,1216]{1,0:T(8,128)(2,1)S(1)}, u32[]{:S(2)}, u32[]{:S(2)}) %collective-permute-start.38) | collective-permute-done | bytes 544800 | tf_op jit(solution)/shard_map/ppermute | solution.py:432
  233.8 6.5 %fusion.1 = f32[1216,1024]{1,0:T(8,128)} fusion(bf16[1792,1024]{1,0:T(8,128)(2,1)S(1)} %get-tuple-element.263.refs_0_, bf16[2,1792,1216]{2,1,0:T(8,128)(2,1)S(1)} %assemble.4.weight_ref), kind=kOutput, calls=%fused_computation.8 | convolution fusion | flops 4462739456 | bytes 13238272 | tf_op jit(solution)/shard_map/dot_general | solution.py:30
  242.3 8.7 %multiply_convert_fusion.2 = (bf16[1216,1024]{1,0:T(8,128)(2,1)S(1)}, f32[1216,1024]{1,0:T(8,128)}) fusion(f32[1216,1024]{1,0:T(8,128)} %fusion.1, bf16[1792,1024]{1,0:T(8,128)(2,1)S(1)} %get-tuple-element.263.refs_0_, bf16[2,1792,1216]{2,1,0:T(8,128)(2,1)S(1)} %assemble.4.weight_ref), kind=kOutput, calls=%fused_computation.3 | convolution fusion | flops 4470210560 | bytes 20709376 | tf_op jit(solution)/shard_map/dot_general | solution.py:30
  252.5 12.5 %add_reduce_fusion = (f32[1024]{0:T(1024)S(1)}, bf16[1216,1024]{1,0:T(8,128)(2,1)S(1)}, bf16[1216,1024]{1,0:T(8,128)(2,1)}) fusion(f32[1216,1024]{1,0:T(8,128)} %get-tuple-element.439, f32[1216,1024]{1,0:T(8,128)} %fusion.1, bf16[1792,1216]{1,0:T(8,128)(2,1)S(1)} %assemble.5.weight_ref, bf16[1792,1024]{1,0:T(8,128)(2,1)S(1)} %gather.2.refs_0_), kind=kOutput, calls=%fused_computation | convolution fusion | flops 4486396928 | bytes 22974464 | tf_op jit(solution)/shard_map/dot_general | solution.py:30
  267.6 11.9 %ffn_back.1 = (bf16[456,1024]{1,0:T(8,128)(2,1)S(1)}, bf16[456,1024]{1,0:T(8,128)(2,1)S(1)}, bf16[2,448,1024]{2,1,0:T(8,128)(2,1)S(1)}) custom-call(s32[9]{0:T(128)S(1)} %fusion.20.index_ref, bf16[2,1792,1216]{2,1,0:T(8,128)(2,1)S(1)} %assemble.4.weight_ref, bf16[1216,1024]{1,0:T(8,128)(2,1)S(1)} %copy-done.53, ...), custom_call_target="tpu_custom_call" | custom-call | flops 8925478912 | bytes 8388608 | tf_op jit(solution)/shard_map/ffn_back/pallas_call | solution.py:155
  280.1 5.6 %down_grad.1.refs_0_.refs_2_.refs_3_.own = bf16[1792,1216]{1,0:T(8,128)(2,1)S(1)} custom-call(bf16[1792,1024]{1,0:T(8,128)(2,1)S(1)} %copy-done.10, bf16[1216,1024]{1,0:T(8,128)(2,1)S(1)} %get-tuple-element.303.refs_1_.refs_0_), custom_call_target="tpu_custom_call" | custom-call | flops 4462739456 | bytes 4358144 | tf_op jit(solution)/shard_map/down_grad/pallas_call | solution.py:513
  291.5 10.8 %gate_up_grad.1.refs_0_.refs_2_.refs_3_.own = bf16[1792,2432]{1,0:T(8,128)(2,1)S(1)} custom-call(bf16[1792,1024]{1,0:T(8,128)(2,1)S(1)} %copy-done.36, bf16[1216,1024]{1,0:T(8,128)(2,1)S(1)} %copy-done.53, bf16[1216,1024]{1,0:T(8,128)(2,1)S(1)} %copy-done.52), custom_call_target="tpu_custom_call" | custom-call | flops 8925478912 | bytes 8716288 | tf_op jit(solution)/shard_map/gate_up_grad/pallas_call | solution.py:513
  303.6 9.7 %collective-permute-start.48 = (bf16[112,2432]{1,0:T(8,128)(2,1)S(1)}, bf16[112,2432]{1,0:T(8,128)(2,1)S(1)}, u32[]{:S(2)}, u32[]{:S(2)}) collective-permute-start(bf16[112,2432]{1,0:T(8,128)(2,1)S(1)} %get-tuple-element.286), channel_id=1, source_target_pairs={{0,4},{8,0},{16,8},{24,16},{28,24},{20,28},{12,20},{4,12},{1,5},{9... | collective-permute-start | bytes 1634312 | tf_op jit(solution)/shard_map/ppermute | solution.py:432
  319.2 8.0 %collective-permute-done.48.refs_1_ = bf16[112,2432]{1,0:T(8,128)(2,1)S(1)} collective-permute-done((bf16[112,2432]{1,0:T(8,128)(2,1)S(1)}, bf16[112,2432]{1,0:T(8,128)(2,1)S(1)}, u32[]{:S(2)}, u32[]{:S(2)}) %collective-permute-start.48) | collective-permute-done | bytes 544800 | tf_op jit(solution)/shard_map/ppermute | solution.py:432
  329.4 7.6 %ffn_out.1 = (bf16[448,1024]{1,0:T(8,128)(2,1)}, bf16[448,1024]{1,0:T(8,128)(2,1)}, bf16[2,448,1024]{2,1,0:T(8,128)(2,1)S(1)}) custom-call(s32[9]{0:T(128)S(1)} %fusion.20.index_ref, bf16[1792,1216]{1,0:T(8,128)(2,1)S(1)} %bitcast.61, bf16[1216,1024]{1,0:T(8,128)(2,1)S(1)} %copy-done.50), custom_call_target="tpu_custom_call" | custom-call | flops 4462739456 | bytes 8388608 | tf_op jit(solution)/shard_map/ffn_out/pallas_call | solution.py:155
  351.2 15.6 %collective-permute-done.54.refs_0_ = bf16[224,2432]{1,0:T(8,128)(2,1)S(1)} collective-permute-done((bf16[224,2432]{1,0:T(8,128)(2,1)S(1)}, bf16[224,2432]{1,0:T(8,128)(2,1)S(1)}, u32[]{:S(2)}, u32[]{:S(2)}) %collective-permute-start.54) | collective-permute-done | bytes 1089568 | tf_op jit(solution)/shard_map/ppermute | solution.py:432
  367.9 5.6 %collective-permute-done.56 = bf16[2,4,160,128]{3,2,1,0:T(8,128)(2,1)S(1)} collective-permute-done((bf16[2,4,160,128]{3,2,1,0:T(8,128)(2,1)S(1)}, bf16[2,4,160,128]{3,2,1,0:T(8,128)(2,1)S(1)}, u32[]{:S(2)}, u32[]{:S(2)}) %collective-permute-start.56) | collective-permute-done | bytes 327712 | tf_op jit(solution)/shard_map/ppermute | solution.py:625
  375.4 9.3 %collective-permute-done.58 = bf16[2,4,160,128]{3,2,1,0:T(8,128)(2,1)S(1)} collective-permute-done((bf16[2,4,160,128]{3,2,1,0:T(8,128)(2,1)S(1)}, bf16[2,4,160,128]{3,2,1,0:T(8,128)(2,1)S(1)}, u32[]{:S(2)}, u32[]{:S(2)}) %collective-permute-start.58) | collective-permute-done | bytes 327712 | tf_op jit(solution)/shard_map/ppermute | solution.py:616
  396.5 7.4 %collective-permute-done.61 = bf16[2,4,160,128]{3,2,1,0:T(8,128)(2,1)} collective-permute-done((bf16[2,4,160,128]{3,2,1,0:T(8,128)(2,1)}, bf16[2,4,160,128]{3,2,1,0:T(8,128)(2,1)}, u32[]{:S(2)}, u32[]{:S(2)}) %collective-permute-start.61) | collective-permute-done | bytes 327712 | tf_op jit(solution)/shard_map/ppermute | solution.py:616
  411.5 7.8 %local.1 = (bf16[64,1024]{1,0:T(8,128)(2,1)S(1)}, f32[64,1024]{1,0:T(8,128)S(1)}, f32[448,1024]{1,0:T(8,128)S(1)}) custom-call(bf16[576,1024]{1,0:T(8,128)(2,1)S(1)} %fusion.9.key_ref.value_ref.query_ref.refs_0_.refs_1_, bf16[576,1024]{1,0:T(8,128)(2,1)S(1)} %fusion.9.key_ref.value_ref.query_ref.refs_0_.refs_1_, ...), custom_call_target="tpu_custom_call" | custom-call | flops 2147483648 | bytes 4194304 | tf_op jit(solution)/shard_map/local/pallas_call | solution.py:975
  422.5 5.8 %qkv_back.1 = (bf16[456,1024]{1,0:T(8,128)(2,1)}, bf16[456,1024]{1,0:T(8,128)(2,1)}, bf16[2,448,1024]{2,1,0:T(8,128)(2,1)S(1)}) custom-call(s32[9]{0:T(128)S(1)} %fusion.20.index_ref, bf16[1792,1024]{1,0:T(8,128)(2,1)S(1)} %copy-done.8, bf16[576,1024]{1,0:T(8,128)(2,1)S(1)} %later.1.refs_0_.refs_2_, f32[1,1024]{1,0:T(1,128)S(1)} %bitcast.65), custom_call_target="tpu_custom_call" | custom-call | flops 2113929216 | bytes 8388608 | tf_op jit(solution)/shard_map/qkv_back/pallas_call | solution.py:155
  431.8 5.9 %attn_grad.1.refs_0_.refs_2_.refs_3_.own = bf16[1792,1024]{1,0:T(8,128)(2,1)S(1)} custom-call(bf16[1792,1024]{1,0:T(8,128)(2,1)S(1)} %copy-done.34, bf16[1792,1024]{1,0:T(8,128)(2,1)S(1)} %copy-done.12, bf16[576,1024]{1,0:T(8,128)(2,1)S(1)} %later.1.refs_0_.refs_2_, bf16[448,1024]{1,0:T(8,128)(2,1)S(1)} %copy-done.21), custom_call_target="tpu_custom_call" | custom-call | flops 3758096384 | bytes 3670016 | tf_op jit(solution)/shard_map/attn_grad/pallas_call | solution.py:513
  452.5 8.8 %collective-permute-done.74.refs_0_ = bf16[224,1024]{1,0:T(8,128)(2,1)S(1)} collective-permute-done((bf16[224,1024]{1,0:T(8,128)(2,1)S(1)}, bf16[224,1024]{1,0:T(8,128)(2,1)S(1)}, u32[]{:S(2)}, u32[]{:S(2)}) %collective-permute-start.74) | collective-permute-done | bytes 458784 | tf_op jit(solution)/shard_map/ppermute | solution.py:432
  478.5 22.0 %collective-permute-done.83.left_ref = bf16[224,1216]{1,0:T(8,128)(2,1)S(1)} collective-permute-done((bf16[224,1216]{1,0:T(8,128)(2,1)S(1)}, bf16[224,1216]{1,0:T(8,128)(2,1)S(1)}, u32[]{:S(2)}, u32[]{:S(2)}) %collective-permute-start.83) | collective-permute-done | bytes 544800 | tf_op jit(solution)/shard_map/ppermute | solution.py:432
  515.4 6.1 %collective-permute-done.73 = f32[2,448]{1,0:T(2,128)S(1)} collective-permute-done((f32[2,448]{1,0:T(2,128)S(1)}, f32[2,448]{1,0:T(2,128)S(1)}, u32[]{:S(2)}, u32[]{:S(2)}) %collective-permute-start.73) | collective-permute-done | bytes 3616 | tf_op jit(solution)/shard_map/ppermute | solution.py:656
  (384 shorter events, 206.0 us)
Async XLA Ops:
  7.7 24.6 %collective-permute-start.7 = (bf16[2,448,512]{2,1,0:T(8,128)(2,1)}, bf16[2,448,512]{2,1,0:T(8,128)(2,1)}, u32[]{:S(2)}, u32[]{:S(2)}) collective-permute-start(bf16[2,448,512]{2,1,0:T(8,128)(2,1)} %bitcast.57), channel_id=1, source_target_pairs={{0,2},{1,3},{2,0},{3,1},{4,6},{5,7},{6,4},{7,5},{8,10},{9,11},{10,... | collective-permute-start | bytes 2752520 | tf_op jit(solution)/shard_map/ppermute | solution.py:52
  21.7 29.6 %collective-permute-start.6 = (bf16[2,448,512]{2,1,0:T(8,128)(2,1)}, bf16[2,448,512]{2,1,0:T(8,128)(2,1)}, u32[]{:S(2)}, u32[]{:S(2)}) collective-permute-start(bf16[2,448,512]{2,1,0:T(8,128)(2,1)} %bitcast.58), channel_id=1, source_target_pairs={{0,1},{1,0},{2,3},{3,2},{4,5},{5,4},{6,7},{7,6},{8,9},{9,8},{10,11... | collective-permute-start | bytes 2752520 | tf_op jit(solution)/shard_map/ppermute | solution.py:52
  52.5 36.8 %collective-permute-start.15 = (bf16[2,224,1216]{2,1,0:T(8,128)(2,1)S(1)}, bf16[2,224,1216]{2,1,0:T(8,128)(2,1)}, u32[]{:S(2)}, u32[]{:S(2)}) collective-permute-start(bf16[2,224,1216]{2,1,0:T(8,128)(2,1)S(1)} %pad_maximum_fusion.refs_0_), channel_id=1, source_target_pairs={{0,8},{8,16},{16,24},{24,28},{28,20},{20,12},{12,4},{4,0},{1,9},{9... | collective-permute-start | bytes 3268616 | tf_op jit(solution)/shard_map/ppermute | solution.py:432
  54.1 35.3 %collective-permute-start.16 = (bf16[2,224,1216]{2,1,0:T(8,128)(2,1)S(1)}, bf16[2,224,1216]{2,1,0:T(8,128)(2,1)}, u32[]{:S(2)}, u32[]{:S(2)}) collective-permute-start(bf16[2,224,1216]{2,1,0:T(8,128)(2,1)S(1)} %pad_maximum_fusion.refs_0_), channel_id=1, source_target_pairs={{0,4},{8,0},{16,8},{24,16},{28,24},{20,28},{12,20},{4,12},{1,5},{9... | collective-permute-start | bytes 3268616 | tf_op jit(solution)/shard_map/ppermute | solution.py:432
  68.0 30.9 %collective-permute-start.19 = (bf16[2,448,512]{2,1,0:T(8,128)(2,1)}, bf16[2,448,512]{2,1,0:T(8,128)(2,1)}, u32[]{:S(2)}, u32[]{:S(2)}) collective-permute-start(bf16[2,448,512]{2,1,0:T(8,128)(2,1)} %fusion.15.refs_0_), channel_id=1, source_target_pairs={{0,2},{1,3},{2,0},{3,1},{4,6},{5,7},{6,4},{7,5},{8,10},{9,11},{10,... | collective-permute-start | bytes 2752520 | tf_op jit(solution)/shard_map/ppermute | solution.py:52
  89.3 39.7 %collective-permute-start.18 = (bf16[2,448,512]{2,1,0:T(8,128)(2,1)}, bf16[2,448,512]{2,1,0:T(8,128)(2,1)}, u32[]{:S(2)}, u32[]{:S(2)}) collective-permute-start(bf16[2,448,512]{2,1,0:T(8,128)(2,1)} %fusion.15.refs_0_), channel_id=1, source_target_pairs={{0,1},{1,0},{2,3},{3,2},{4,5},{5,4},{6,7},{7,6},{8,9},{9,8},{10,11... | collective-permute-start | bytes 2752520 | tf_op jit(solution)/shard_map/ppermute | solution.py:52
  89.4 42.5 %collective-permute-start.21 = (bf16[2,224,1216]{2,1,0:T(8,128)(2,1)}, bf16[2,224,1216]{2,1,0:T(8,128)(2,1)}, u32[]{:S(2)}, u32[]{:S(2)}) collective-permute-start(bf16[2,224,1216]{2,1,0:T(8,128)(2,1)} %collective-permute-done.15.refs_1_), channel_id=1, source_target_pairs={{0,8},{8,16},{16,24},{24,28},{28,20},{20,12},{12,4},{4,0},{1,9},{9... | collective-permute-start | bytes 3268616 | tf_op jit(solution)/shard_map/ppermute | solution.py:432
  89.4 42.5 %collective-permute-start.22 = (bf16[2,224,1216]{2,1,0:T(8,128)(2,1)}, bf16[2,224,1216]{2,1,0:T(8,128)(2,1)}, u32[]{:S(2)}, u32[]{:S(2)}) collective-permute-start(bf16[2,224,1216]{2,1,0:T(8,128)(2,1)} %collective-permute-done.16.refs_5_), channel_id=1, source_target_pairs={{0,4},{8,0},{16,8},{24,16},{28,24},{20,28},{12,20},{4,12},{1,5},{9... | collective-permute-start | bytes 3268616 | tf_op jit(solution)/shard_map/ppermute | solution.py:432
  98.9 30.1 %collective-permute-start.20 = (bf16[2,448,512]{2,1,0:T(8,128)(2,1)}, bf16[2,448,512]{2,1,0:T(8,128)(2,1)}, u32[]{:S(2)}, u32[]{:S(2)}) collective-permute-start(bf16[2,448,512]{2,1,0:T(8,128)(2,1)} %collective-permute-done.19.refs_2_), channel_id=1, source_target_pairs={{0,1},{1,0},{2,3},{3,2},{4,5},{5,4},{6,7},{7,6},{8,9},{9,8},{10,11... | collective-permute-start | bytes 2752520 | tf_op jit(solution)/shard_map/ppermute | solution.py:52
  98.9 28.7 %collective-permute-start.23 = (bf16[2,4,160,128]{3,2,1,0:T(8,128)(2,1)}, bf16[2,4,160,128]{3,2,1,0:T(8,128)(2,1)}, u32[]{:S(2)}, u32[]{:S(2)}) collective-permute-start(bf16[2,4,160,128]{3,2,1,0:T(8,128)(2,1)} %add_convert_fusion.5), channel_id=1, source_target_pairs={{0,16},{4,20},{8,24},{12,28},{1,17},{5,21},{9,25},{13,29},{2,18},{... | collective-permute-start | bytes 983048 | tf_op jit(solution)/shard_map/ppermute | solution.py:616
  141.1 29.9 %collective-permute-start.27 = (bf16[2,224,1216]{2,1,0:T(8,128)(2,1)}, bf16[2,224,1216]{2,1,0:T(8,128)(2,1)S(1)}, u32[]{:S(2)}, u32[]{:S(2)}) collective-permute-start(bf16[2,224,1216]{2,1,0:T(8,128)(2,1)} %collective-permute-done.21.refs_2_), channel_id=1, source_target_pairs={{0,8},{8,16},{16,24},{24,28},{28,20},{20,12},{12,4},{4,0},{1,9},{9... | collective-permute-start | bytes 3268616 | tf_op jit(solution)/shard_map/ppermute | solution.py:432
  146.0 27.2 %collective-permute-start.28 = (bf16[2,224,1216]{2,1,0:T(8,128)(2,1)}, bf16[2,224,1216]{2,1,0:T(8,128)(2,1)S(1)}, u32[]{:S(2)}, u32[]{:S(2)}) collective-permute-start(bf16[2,224,1216]{2,1,0:T(8,128)(2,1)} %collective-permute-done.22.refs_6_), channel_id=1, source_target_pairs={{0,4},{8,0},{16,8},{24,16},{28,24},{20,28},{12,20},{4,12},{1,5},{9... | collective-permute-start | bytes 3268616 | tf_op jit(solution)/shard_map/ppermute | solution.py:432
  147.5 30.0 %collective-permute-start.26 = (bf16[2,448,512]{2,1,0:T(8,128)(2,1)S(1)}, bf16[2,448,512]{2,1,0:T(8,128)(2,1)S(1)}, u32[]{:S(2)}, u32[]{:S(2)}) collective-permute-start(bf16[2,448,512]{2,1,0:T(8,128)(2,1)S(1)} %get-tuple-element.240), channel_id=1, source_target_pairs={{0,2},{1,3},{2,0},{3,1},{4,6},{5,7},{6,4},{7,5},{8,10},{9,11},{10,... | collective-permute-start | bytes 2752520 | tf_op jit(solution)/shard_map/ppermute | solution.py:52
  175.5 23.9 %collective-permute-start.31 = (bf16[224,1216]{1,0:T(8,128)(2,1)S(1)}, bf16[224,1216]{1,0:T(8,128)(2,1)S(1)}, u32[]{:S(2)}, u32[]{:S(2)}) collective-permute-start(bf16[224,1216]{1,0:T(8,128)(2,1)S(1)} %bitcast.62), channel_id=1, source_target_pairs={{0,8},{8,16},{16,24},{24,28},{28,20},{20,12},{12,4},{4,0},{1,9},{9... | collective-permute-start | bytes 1634312 | tf_op jit(solution)/shard_map/ppermute | solution.py:432
  177.5 24.1 %collective-permute-start.32 = (bf16[224,1216]{1,0:T(8,128)(2,1)S(1)}, bf16[224,1216]{1,0:T(8,128)(2,1)S(1)}, u32[]{:S(2)}, u32[]{:S(2)}) collective-permute-start(bf16[224,1216]{1,0:T(8,128)(2,1)S(1)} %bitcast.63), channel_id=1, source_target_pairs={{0,4},{8,0},{16,8},{24,16},{28,24},{20,28},{12,20},{4,12},{1,5},{9... | collective-permute-start | bytes 1634312 | tf_op jit(solution)/shard_map/ppermute | solution.py:432
  179.2 36.1 %collective-permute-start.36 = (bf16[2,448,512]{2,1,0:T(8,128)(2,1)S(1)}, bf16[2,448,512]{2,1,0:T(8,128)(2,1)S(1)}, u32[]{:S(2)}, u32[]{:S(2)}) collective-permute-start(bf16[2,448,512]{2,1,0:T(8,128)(2,1)S(1)} %get-tuple-element.425.refs_0_), channel_id=1, source_target_pairs={{0,2},{1,3},{2,0},{3,1},{4,6},{5,7},{6,4},{7,5},{8,10},{9,11},{10,... | collective-permute-start | bytes 2752520 | tf_op jit(solution)/shard_map/ppermute | solution.py:52
  203.7 27.9 %collective-permute-start.35 = (bf16[2,448,512]{2,1,0:T(8,128)(2,1)S(1)}, bf16[2,448,512]{2,1,0:T(8,128)(2,1)S(1)}, u32[]{:S(2)}, u32[]{:S(2)}) collective-permute-start(bf16[2,448,512]{2,1,0:T(8,128)(2,1)S(1)} %get-tuple-element.425.refs_0_), channel_id=1, source_target_pairs={{0,1},{1,0},{2,3},{3,2},{4,5},{5,4},{6,7},{7,6},{8,9},{9,8},{10,11... | collective-permute-start | bytes 2752520 | tf_op jit(solution)/shard_map/ppermute | solution.py:52
  287.9 26.3 %collective-permute-start.46 = (bf16[2,456,512]{2,1,0:T(8,128)(2,1)S(1)}, bf16[2,456,512]{2,1,0:T(8,128)(2,1)S(1)}, u32[]{:S(2)}, u32[]{:S(2)}) collective-permute-start(bf16[2,456,512]{2,1,0:T(8,128)(2,1)S(1)} %get-tuple-element.282), channel_id=1, source_target_pairs={{0,2},{1,3},{2,0},{3,1},{4,6},{5,7},{6,4},{7,5},{8,10},{9,11},{10,... | collective-permute-start | bytes 2801672 | tf_op jit(solution)/shard_map/ppermute | solution.py:52
  340.0 26.9 %collective-permute-start.54 = (bf16[224,2432]{1,0:T(8,128)(2,1)S(1)}, bf16[224,2432]{1,0:T(8,128)(2,1)S(1)}, u32[]{:S(2)}, u32[]{:S(2)}) collective-permute-start(bf16[224,2432]{1,0:T(8,128)(2,1)S(1)} %copy-done.40), channel_id=1, source_target_pairs={{0,8},{8,16},{16,24},{24,28},{28,20},{20,12},{12,4},{4,0},{1,9},{9... | collective-permute-start | bytes 3268616 | tf_op jit(solution)/shard_map/ppermute | solution.py:432
  340.8 26.1 %collective-permute-start.55 = (bf16[224,2432]{1,0:T(8,128)(2,1)S(1)}, bf16[224,2432]{1,0:T(8,128)(2,1)S(1)}, u32[]{:S(2)}, u32[]{:S(2)}) collective-permute-start(bf16[224,2432]{1,0:T(8,128)(2,1)S(1)} %copy-done.38), channel_id=1, source_target_pairs={{0,4},{8,0},{16,8},{24,16},{28,24},{20,28},{12,20},{4,12},{1,5},{9... | collective-permute-start | bytes 3268616 | tf_op jit(solution)/shard_map/ppermute | solution.py:432
  374.8 30.2 %collective-permute-start.57 = (bf16[448,1024]{1,0:T(8,128)(2,1)}, bf16[448,1024]{1,0:T(8,128)(2,1)}, u32[]{:S(2)}, u32[]{:S(2)}) collective-permute-start(bf16[448,1024]{1,0:T(8,128)(2,1)} %get-tuple-element.325), channel_id=1, source_target_pairs={{0,1},{1,0},{2,3},{3,2},{4,5},{5,4},{6,7},{7,6},{8,9},{9,8},{10,11... | collective-permute-start | bytes 2752520 | tf_op jit(solution)/shard_map/ppermute | solution.py:52
  374.9 32.2 %collective-permute-start.59 = (bf16[448,1024]{1,0:T(8,128)(2,1)}, bf16[448,1024]{1,0:T(8,128)(2,1)}, u32[]{:S(2)}, u32[]{:S(2)}) collective-permute-start(bf16[448,1024]{1,0:T(8,128)(2,1)} %get-tuple-element.334), channel_id=1, source_target_pairs={{0,1},{1,0},{2,3},{3,2},{4,5},{5,4},{6,7},{7,6},{8,9},{9,8},{10,11... | collective-permute-start | bytes 2752520 | tf_op jit(solution)/shard_map/ppermute | solution.py:52
  387.5 40.8 %collective-permute-start.62 = (bf16[224,1216]{1,0:T(8,128)(2,1)}, bf16[224,1216]{1,0:T(8,128)(2,1)S(1)}, u32[]{:S(2)}, u32[]{:S(2)}) collective-permute-start(bf16[224,1216]{1,0:T(8,128)(2,1)} %copy-done.46), channel_id=1, source_target_pairs={{0,8},{8,16},{16,24},{24,28},{28,20},{20,12},{12,4},{4,0},{1,9},{9... | collective-permute-start | bytes 1634312 | tf_op jit(solution)/shard_map/ppermute | solution.py:432
  387.6 41.4 %collective-permute-start.63 = (bf16[224,1216]{1,0:T(8,128)(2,1)}, bf16[224,1216]{1,0:T(8,128)(2,1)S(1)}, u32[]{:S(2)}, u32[]{:S(2)}) collective-permute-start(bf16[224,1216]{1,0:T(8,128)(2,1)} %copy-done.45), channel_id=1, source_target_pairs={{0,4},{8,0},{16,8},{24,16},{28,24},{20,28},{12,20},{4,12},{1,5},{9... | collective-permute-start | bytes 1634312 | tf_op jit(solution)/shard_map/ppermute | solution.py:432
  403.8 34.5 %collective-permute-start.64 = (bf16[224,2432]{1,0:T(8,128)(2,1)}, bf16[224,2432]{1,0:T(8,128)(2,1)S(1)}, u32[]{:S(2)}, u32[]{:S(2)}) collective-permute-start(bf16[224,2432]{1,0:T(8,128)(2,1)} %get-tuple-element.330), channel_id=1, source_target_pairs={{0,8},{8,16},{16,24},{24,28},{28,20},{20,12},{12,4},{4,0},{1,9},{9... | collective-permute-start | bytes 3268616 | tf_op jit(solution)/shard_map/ppermute | solution.py:432
  405.0 33.4 %collective-permute-start.65 = (bf16[224,2432]{1,0:T(8,128)(2,1)}, bf16[224,2432]{1,0:T(8,128)(2,1)S(1)}, u32[]{:S(2)}, u32[]{:S(2)}) collective-permute-start(bf16[224,2432]{1,0:T(8,128)(2,1)} %get-tuple-element.331), channel_id=1, source_target_pairs={{0,4},{8,0},{16,8},{24,16},{28,24},{20,28},{12,20},{4,12},{1,5},{9... | collective-permute-start | bytes 3268616 | tf_op jit(solution)/shard_map/ppermute | solution.py:432
  444.1 27.4 %collective-permute-start.70 = (bf16[2,456,512]{2,1,0:T(8,128)(2,1)S(1)}, bf16[2,456,512]{2,1,0:T(8,128)(2,1)S(1)}, u32[]{:S(2)}, u32[]{:S(2)}) collective-permute-start(bf16[2,456,512]{2,1,0:T(8,128)(2,1)S(1)} %get-tuple-element.364), channel_id=1, source_target_pairs={{0,2},{1,3},{2,0},{3,1},{4,6},{5,7},{6,4},{7,5},{8,10},{9,11},{10,... | collective-permute-start | bytes 2801672 | tf_op jit(solution)/shard_map/ppermute | solution.py:52
  452.5 51.4 %collective-permute-start.80 = (bf16[224,2432]{1,0:T(8,128)(2,1)S(1)}, bf16[224,2432]{1,0:T(8,128)(2,1)S(1)}, u32[]{:S(2)}, u32[]{:S(2)}) collective-permute-start(bf16[224,2432]{1,0:T(8,128)(2,1)S(1)} %get-tuple-element.359), channel_id=1, source_target_pairs={{0,8},{8,16},{16,24},{24,28},{28,20},{20,12},{12,4},{4,0},{1,9},{9... | collective-permute-start | bytes 3268616 | tf_op jit(solution)/shard_map/ppermute | solution.py:432
  461.2 42.6 %collective-permute-start.81 = (bf16[224,2432]{1,0:T(8,128)(2,1)S(1)}, bf16[224,2432]{1,0:T(8,128)(2,1)S(1)}, u32[]{:S(2)}, u32[]{:S(2)}) collective-permute-start(bf16[224,2432]{1,0:T(8,128)(2,1)S(1)} %get-tuple-element.360), channel_id=1, source_target_pairs={{0,4},{8,0},{16,8},{24,16},{28,24},{20,28},{12,20},{4,12},{1,5},{9... | collective-permute-start | bytes 3268616 | tf_op jit(solution)/shard_map/ppermute | solution.py:432
  465.7 34.8 %collective-permute-start.83 = (bf16[224,1216]{1,0:T(8,128)(2,1)S(1)}, bf16[224,1216]{1,0:T(8,128)(2,1)S(1)}, u32[]{:S(2)}, u32[]{:S(2)}) collective-permute-start(bf16[224,1216]{1,0:T(8,128)(2,1)S(1)} %copy-done.44), channel_id=1, source_target_pairs={{0,4},{8,0},{16,8},{24,16},{28,24},{20,28},{12,20},{4,12},{1,5},{9... | collective-permute-start | bytes 1634312 | tf_op jit(solution)/shard_map/ppermute | solution.py:432
  471.5 36.5 %collective-permute-start.76 = (bf16[224,1024]{1,0:T(8,128)(2,1)S(1)}, bf16[224,1024]{1,0:T(8,128)(2,1)S(1)}, u32[]{:S(2)}, u32[]{:S(2)}) collective-permute-start(bf16[224,1024]{1,0:T(8,128)(2,1)S(1)} %get-tuple-element.379), channel_id=1, source_target_pairs={{0,8},{8,16},{16,24},{24,28},{28,20},{20,12},{12,4},{4,0},{1,9},{9... | collective-permute-start | bytes 1376264 | tf_op jit(solution)/shard_map/ppermute | solution.py:432
  473.5 34.5 %collective-permute-start.77 = (bf16[224,1024]{1,0:T(8,128)(2,1)S(1)}, bf16[224,1024]{1,0:T(8,128)(2,1)S(1)}, u32[]{:S(2)}, u32[]{:S(2)}) collective-permute-start(bf16[224,1024]{1,0:T(8,128)(2,1)S(1)} %get-tuple-element.380), channel_id=1, source_target_pairs={{0,4},{8,0},{16,8},{24,16},{28,24},{20,28},{12,20},{4,12},{1,5},{9... | collective-permute-start | bytes 1376264 | tf_op jit(solution)/shard_map/ppermute | solution.py:432
  (126 other events, 1602.4 us)

commit v5 on v4

--- a/solution.py
+++ b/solution.py
@@ -864,10 +864,8 @@
     fence(before.one)
     before.second(*token)
     fence(before.sent)
+    ring_down.advance(*token)
     spread_out.cross(*token)
-    blocks = spread_out.blocks()
-    grad_out_full = gathered(index, (turn(blocks[0]),) + blocks[1:])
-    fence(grad_out_full)
     fence(ring_gate_up.here())
     ring_gate_up.advance(*token)
 
@@ -879,10 +877,17 @@
         (("head", BF), ("row", F32)),
         1,
     )(turn(qkv), qkv, qkv, valid, state)
-    scatter_attn = Scatter(index, projected(index, w_attn, [mixed], "out_proj", columns), seqs)
+    fence(ring_down.here())
+    scatter_attn = Scatter(
+        index, projected(index, w_attn, [turn(mixed)], "out_proj", columns), seqs
+    )
     fence(scatter_attn.sent)
+    fence(ring_gate_up.here())
     scatter_attn.cross(*token)
     fence(scatter_attn.sent_far)
+    blocks = spread_out.blocks()
+    grad_out_full = gathered(index, (turn(blocks[0]),) + blocks[1:])
+    fence(grad_out_full)
     fence(ring_gate_up.here())
     ring_gate_up.advance(*token)
     ring_down.advance(*token)
@@ -900,8 +905,6 @@
     blocks = spread_resid.blocks()
     normed_two, inv_two = gathered(index, blocks, gains.blocks(), 1)
     fence(normed_two)
-    fence(ring_down.here())
-    ring_down.advance(*token)
     gate = mm_tn(gate_up[0], turn(normed_two))
     up = mm_tn(gate_up[1], normed_two)
     act = (gate * jax.nn.sigmoid(gate) * up).astype(BF)
@@ -964,6 +967,14 @@
     fence(after.other)
     after.first(*token)
     fence(after.total if ringed() else ())
+    local = call(
+        local_kernel,
+        "local",
+        ("query", "key", "value", "valid", "state", "ext"),
+        (("feat", BF), ("feat", F32), ("head", F32)),
+        2,
+    )(turn(qkv), qkv, qkv, valid, state, weighted)
+    fence(local)
     scatter_out = Scatter(index, [*lax.optimization_barrier((*ffn_out, *token))[:3]], seqs)
     fence(after.one)
     after.second(*token)
@@ -972,14 +983,6 @@
     fence(gate_up_ring.sent)
     scatter_out.cross(*token)
     fence(scatter_out.sent_far)
-    local = call(
-        local_kernel,
-        "local",
-        ("query", "key", "value", "valid", "state", "ext"),
-        (("feat", BF), ("feat", F32), ("head", F32)),
-        2,
-    )(turn(qkv), qkv, qkv, valid, state, weighted)
-    fence(local)
 
     def later(*refs):
         later_kernel(heads, *refs)

time: 532 us -> 514 us (0.966)
  waiting for transfers between devices: 240 us -> 225 us
  starting transfers between devices: 91.6 us -> 85.5 us
    ppermute x48, waiting for transfers between devices: 156 us -> 135 us  [hop(): return lax.ppermute(value, 'ctx', pairs)]
    ppermute x27, waiting for transfers between devices: 6.09 us -> 20.3 us  [swap(): return lax.ppermute(value, 'wt', [(i, i ^ bit) for i in range(count)])]
    ppermute x4, waiting for transfers between devices: 45.7 us -> 36.7 us  [shifted(): return lax.ppermute(value, 'ctx', pairs)]
    ppermute x48, starting transfers between devices: 61.7 us -> 56.1 us  [hop(): return lax.ppermute(value, 'ctx', pairs)]
    unnamed x158 -> x150, local copies, waits for them, and re-layouts: 21 us -> 23.1 us
  transfers between devices with their start and end apart: 84 -> 84, of which waited for: 36 -> 37; matrix products, arithmetic and copies ran while one was open for 7% -> 9% of each run, Pallas kernels for 16% -> 19%
where the time goes in v5:
time: 514 us; the launch traced here: 506 us
  waiting for transfers between devices  225 us (44%)
  Pallas kernels  111 us (22%)
  starting transfers between devices  85.5 us (17%)
  matrix products  32.6 us (6%)
  local copies, waits for them, and re-layouts  29.6 us (6%)
  other arithmetic  19.8 us (4%)
    ppermute x48, waiting for transfers between devices, hop(): return lax.ppermute(value, 'ctx', pairs)  135 us
    ppermute x48, starting transfers between devices, hop(): return lax.ppermute(value, 'ctx', pairs)  56.1 us
    ppermute x4, waiting for transfers between devices, shifted(): return lax.ppermute(value, 'ctx', pairs)  36.7 us
    dot_general x5, matrix products, mm_tn(): lax.dot_general(left, right, (((0,), (0,)), ((), ())), preferred_element_...  32.6 us
    pallas_call x4, Pallas kernels, projected(): pl.pallas_call(kernel, name=name, grid_spec=pltpu.PrefetchScalarGridSpec(...  28.9 us
    ppermute x2, waiting for transfers between devices, __init__(): self.other = lax.ppermute(value, 'ctx', [(i, i ^ 1) for i in range(count)])  27.4 us
    unnamed x150, local copies, waits for them, and re-layouts  23.1 us
    pallas_call x3, Pallas kernels, products(): pl.pallas_call(kernel, name=name, grid=(4,), in_specs=[pl.BlockSpec((rows...  22.1 us
  transfers between devices with their start and end apart: 84, of which 37 were waited for; matrix products, arithmetic and copies ran while one was open for 9% of the time, Pallas kernels for 19%

profile of v5, /device:TPU:0, one launch (start us, length us, event | category | flops | bytes accessed | tf_op | source)
XLA Modules:
  0.0 505.6 jit_solution(1864371788071714612)
XLA Ops:
  9.7 8.5 %collective-permute-done.refs_1_ = bf16[224,1024]{1,0:T(8,128)(2,1)S(1)} collective-permute-done((bf16[224,1024]{1,0:T(8,128)(2,1)S(1)}, bf16[224,1024]{1,0:T(8,128)(2,1)S(1)}, u32[]{:S(2)}, u32[]{:S(2)}) %collective-permute-start) | collective-permute-done | bytes 458784 | tf_op jit(solution)/shard_map/ppermute | solution.py:432
  23.1 7.9 %collective-permute-done.2.refs_2_ = bf16[224,1024]{1,0:T(8,128)(2,1)} collective-permute-done((bf16[224,1024]{1,0:T(8,128)(2,1)S(1)}, bf16[224,1024]{1,0:T(8,128)(2,1)}, u32[]{:S(2)}, u32[]{:S(2)}) %collective-permute-start.2) | collective-permute-done | bytes 458784 | tf_op jit(solution)/shard_map/ppermute | solution.py:432
  36.2 9.3 %collective-permute-done.4.refs_3_ = bf16[224,1024]{1,0:T(8,128)(2,1)S(1)} collective-permute-done((bf16[224,1024]{1,0:T(8,128)(2,1)}, bf16[224,1024]{1,0:T(8,128)(2,1)S(1)}, u32[]{:S(2)}, u32[]{:S(2)}) %collective-permute-start.4) | collective-permute-done | bytes 458784 | tf_op jit(solution)/shard_map/ppermute | solution.py:432
  66.6 21.3 %collective-permute-done.14 = bf16[2,4,160,128]{3,2,1,0:T(8,128)(2,1)S(1)} collective-permute-done((bf16[2,4,160,128]{3,2,1,0:T(8,128)(2,1)S(1)}, bf16[2,4,160,128]{3,2,1,0:T(8,128)(2,1)S(1)}, u32[]{:S(2)}, u32[]{:S(2)}) %collective-permute-start.14) | collective-permute-done | bytes 327712 | tf_op jit(solution)/shard_map/ppermute | solution.py:625
  91.4 6.0 %collective-permute-done.17 = bf16[2,4,160,128]{3,2,1,0:T(8,128)(2,1)S(1)} collective-permute-done((bf16[2,4,160,128]{3,2,1,0:T(8,128)(2,1)S(1)}, bf16[2,4,160,128]{3,2,1,0:T(8,128)(2,1)S(1)}, u32[]{:S(2)}, u32[]{:S(2)}) %collective-permute-start.17) | collective-permute-done | bytes 327712 | tf_op jit(solution)/shard_map/ppermute | solution.py:616
  98.9 5.6 %collective-permute-start.20 = (bf16[2,4,160,128]{3,2,1,0:T(8,128)(2,1)}, bf16[2,4,160,128]{3,2,1,0:T(8,128)(2,1)}, u32[]{:S(2)}, u32[]{:S(2)}) collective-permute-start(bf16[2,4,160,128]{3,2,1,0:T(8,128)(2,1)} %add_convert_fusion.5), channel_id=1, source_target_pairs={{0,16},{4,20},{8,24},{12,28},{1,17},{5,21},{9,25},{13,29},{2,18},{... | collective-permute-start | bytes 983048 | tf_op jit(solution)/shard_map/ppermute | solution.py:616
  108.5 20.7 %collective-permute-done.20 = bf16[2,4,160,128]{3,2,1,0:T(8,128)(2,1)} collective-permute-done((bf16[2,4,160,128]{3,2,1,0:T(8,128)(2,1)}, bf16[2,4,160,128]{3,2,1,0:T(8,128)(2,1)}, u32[]{:S(2)}, u32[]{:S(2)}) %collective-permute-start.20) | collective-permute-done | bytes 327712 | tf_op jit(solution)/shard_map/ppermute | solution.py:616
  135.7 4.8 attend.1
  148.4 16.1 %collective-permute-done.24.refs_3_ = bf16[2,224,1216]{2,1,0:T(8,128)(2,1)S(1)} collective-permute-done((bf16[2,224,1216]{2,1,0:T(8,128)(2,1)}, bf16[2,224,1216]{2,1,0:T(8,128)(2,1)S(1)}, u32[]{:S(2)}, u32[]{:S(2)}) %collective-permute-start.24) | collective-permute-done | bytes 1089568 | tf_op jit(solution)/shard_map/ppermute | solution.py:432
  174.4 14.4 %collective-permute-done.27 = bf16[2,448,512]{2,1,0:T(8,128)(2,1)S(1)} collective-permute-done((bf16[2,448,512]{2,1,0:T(8,128)(2,1)S(1)}, bf16[2,448,512]{2,1,0:T(8,128)(2,1)S(1)}, u32[]{:S(2)}, u32[]{:S(2)}) %collective-permute-start.27) | collective-permute-done | bytes 917536 | tf_op jit(solution)/shard_map/ppermute | solution.py:52
  192.0 4.9 collective-permute-done.33.refs_2_
  204.9 9.1 %collective-permute-done.35.refs_3_ = bf16[224,1216]{1,0:T(8,128)(2,1)S(1)} collective-permute-done((bf16[224,1216]{1,0:T(8,128)(2,1)S(1)}, bf16[224,1216]{1,0:T(8,128)(2,1)S(1)}, u32[]{:S(2)}, u32[]{:S(2)}) %collective-permute-start.35) | collective-permute-done | bytes 544800 | tf_op jit(solution)/shard_map/ppermute | solution.py:432
  219.8 6.5 %fusion.1 = f32[1216,1024]{1,0:T(8,128)} fusion(bf16[1792,1024]{1,0:T(8,128)(2,1)S(1)} %get-tuple-element.267.refs_0_, bf16[2,1792,1216]{2,1,0:T(8,128)(2,1)S(1)} %assemble.4.weight_ref), kind=kOutput, calls=%fused_computation.8 | convolution fusion | flops 4462739456 | bytes 13238272 | tf_op jit(solution)/shard_map/dot_general | solution.py:30
  226.3 8.8 %multiply_convert_fusion.2 = (bf16[1216,1024]{1,0:T(8,128)(2,1)S(1)}, f32[1216,1024]{1,0:T(8,128)}) fusion(f32[1216,1024]{1,0:T(8,128)} %fusion.1, bf16[1792,1024]{1,0:T(8,128)(2,1)S(1)} %get-tuple-element.267.refs_0_, bf16[2,1792,1216]{2,1,0:T(8,128)(2,1)S(1)} %assemble.4.weight_ref), kind=kOutput, calls=%fused_computation.3 | convolution fusion | flops 4470210560 | bytes 20709376 | tf_op jit(solution)/shard_map/dot_general | solution.py:30
  236.6 12.9 %add_reduce_fusion = (f32[1024]{0:T(1024)S(1)}, bf16[1216,1024]{1,0:T(8,128)(2,1)}, bf16[1216,1024]{1,0:T(8,128)(2,1)}) fusion(f32[1216,1024]{1,0:T(8,128)} %get-tuple-element.443, f32[1216,1024]{1,0:T(8,128)} %fusion.1, bf16[1792,1216]{1,0:T(8,128)(2,1)S(1)} %assemble.5.weight_ref, bf16[1792,1024]{1,0:T(8,128)(2,1)S(1)} %gather.2.refs_0_), kind=kOutput, calls=%fused_computation | convolution fusion | flops 4486396928 | bytes 22974464 | tf_op jit(solution)/shard_map/dot_general | solution.py:30
  252.9 11.9 %ffn_back.1 = (bf16[456,1024]{1,0:T(8,128)(2,1)S(1)}, bf16[456,1024]{1,0:T(8,128)(2,1)S(1)}, bf16[2,448,1024]{2,1,0:T(8,128)(2,1)S(1)}) custom-call(s32[9]{0:T(128)S(1)} %fusion.20.index_ref, bf16[2,1792,1216]{2,1,0:T(8,128)(2,1)S(1)} %assemble.4.weight_ref, bf16[1216,1024]{1,0:T(8,128)(2,1)S(1)} %copy-done.45, bf16[1216,1024]{1,0:T(8,128)(2,1)S(1)} %copy-done.43, ...), custom_call_target="tpu_custom_call" | custom-call | flops 8925478912 | bytes 8388608 | tf_op jit(solution)/shard_map/ffn_back/pallas_call | solution.py:155
  265.3 5.6 %down_grad.1.refs_0_.refs_2_.refs_3_.own = bf16[1792,1216]{1,0:T(8,128)(2,1)S(1)} custom-call(bf16[1792,1024]{1,0:T(8,128)(2,1)S(1)} %copy-done.10, bf16[1216,1024]{1,0:T(8,128)(2,1)S(1)} %get-tuple-element.307.refs_1_.refs_0_), custom_call_target="tpu_custom_call" | custom-call | flops 4462739456 | bytes 4358144 | tf_op jit(solution)/shard_map/down_grad/pallas_call | solution.py:513
  279.4 10.6 %gate_up_grad.1.refs_0_.refs_2_.refs_3_.own = bf16[1792,2432]{1,0:T(8,128)(2,1)S(1)} custom-call(bf16[1792,1024]{1,0:T(8,128)(2,1)S(1)} %copy-done.38, bf16[1216,1024]{1,0:T(8,128)(2,1)S(1)} %copy-done.46, bf16[1216,1024]{1,0:T(8,128)(2,1)S(1)} %copy-done.44), custom_call_target="tpu_custom_call" | custom-call | flops 8925478912 | bytes 8716288 | tf_op jit(solution)/shard_map/gate_up_grad/pallas_call | solution.py:513
  300.8 5.3 %collective-permute-done.47.refs_0_ = bf16[112,2432]{1,0:T(8,128)(2,1)S(1)} collective-permute-done((bf16[112,2432]{1,0:T(8,128)(2,1)S(1)}, bf16[112,2432]{1,0:T(8,128)(2,1)S(1)}, u32[]{:S(2)}, u32[]{:S(2)}) %collective-permute-start.47) | collective-permute-done | bytes 544800 | tf_op jit(solution)/shard_map/ppermute | solution.py:432
  309.7 7.6 %ffn_out.1 = (bf16[448,1024]{1,0:T(8,128)(2,1)}, bf16[448,1024]{1,0:T(8,128)(2,1)}, bf16[2,448,1024]{2,1,0:T(8,128)(2,1)S(1)}) custom-call(s32[9]{0:T(128)S(1)} %fusion.20.index_ref, bf16[1792,1216]{1,0:T(8,128)(2,1)S(1)} %bitcast.61, bf16[1216,1024]{1,0:T(8,128)(2,1)S(1)} %get-tuple-element.307.refs_1_.refs_0_), custom_call_target="tpu_custom_call" | custom-call | flops 4462739456 | bytes 8388608 | tf_op jit(solution)/shard_map/ffn_out/pallas_call | solution.py:155
  329.4 17.4 %collective-permute-done.54.refs_0_ = bf16[224,2432]{1,0:T(8,128)(2,1)S(1)} collective-permute-done((bf16[224,2432]{1,0:T(8,128)(2,1)}, bf16[224,2432]{1,0:T(8,128)(2,1)S(1)}, u32[]{:S(2)}, u32[]{:S(2)}) %collective-permute-start.54) | collective-permute-done | bytes 1089568 | tf_op jit(solution)/shard_map/ppermute | solution.py:432
  347.2 6.2 %collective-permute-done.56 = bf16[2,4,160,128]{3,2,1,0:T(8,128)(2,1)S(1)} collective-permute-done((bf16[2,4,160,128]{3,2,1,0:T(8,128)(2,1)S(1)}, bf16[2,4,160,128]{3,2,1,0:T(8,128)(2,1)S(1)}, u32[]{:S(2)}, u32[]{:S(2)}) %collective-permute-start.56) | collective-permute-done | bytes 327712 | tf_op jit(solution)/shard_map/ppermute | solution.py:625
  354.8 7.8 %local.1 = (bf16[64,1024]{1,0:T(8,128)(2,1)S(1)}, f32[64,1024]{1,0:T(8,128)S(1)}, f32[448,1024]{1,0:T(8,128)S(1)}) custom-call(bf16[576,1024]{1,0:T(8,128)(2,1)S(1)} %fusion.9.key_ref.value_ref.query_ref.refs_0_.refs_1_, bf16[576,1024]{1,0:T(8,128)(2,1)S(1)} %fusion.9.key_ref.value_ref.query_ref.refs_0_.refs_1_, ...), custom_call_target="tpu_custom_call" | custom-call | flops 2147483648 | bytes 4194304 | tf_op jit(solution)/shard_map/local/pallas_call | solution.py:970
  377.4 9.9 %collective-permute-done.61 = bf16[2,4,160,128]{3,2,1,0:T(8,128)(2,1)} collective-permute-done((bf16[2,4,160,128]{3,2,1,0:T(8,128)(2,1)}, bf16[2,4,160,128]{3,2,1,0:T(8,128)(2,1)}, u32[]{:S(2)}, u32[]{:S(2)}) %collective-permute-start.61) | collective-permute-done | bytes 327712 | tf_op jit(solution)/shard_map/ppermute | solution.py:616
  398.5 5.8 %qkv_back.1 = (bf16[456,1024]{1,0:T(8,128)(2,1)}, bf16[456,1024]{1,0:T(8,128)(2,1)}, bf16[2,448,1024]{2,1,0:T(8,128)(2,1)S(1)}) custom-call(s32[9]{0:T(128)S(1)} %fusion.20.index_ref, bf16[1792,1024]{1,0:T(8,128)(2,1)S(1)} %copy-done.8, bf16[576,1024]{1,0:T(8,128)(2,1)S(1)} %later.1.refs_0_.refs_2_, f32[1,1024]{1,0:T(1,128)S(1)} %bitcast.65), custom_call_target="tpu_custom_call" | custom-call | flops 2113929216 | bytes 8388608 | tf_op jit(solution)/shard_map/qkv_back/pallas_call | solution.py:155
  407.9 5.9 %attn_grad.1.refs_0_.refs_2_.refs_3_.own = bf16[1792,1024]{1,0:T(8,128)(2,1)S(1)} custom-call(bf16[1792,1024]{1,0:T(8,128)(2,1)S(1)} %copy-done.36, bf16[1792,1024]{1,0:T(8,128)(2,1)S(1)} %copy-done.12, bf16[576,1024]{1,0:T(8,128)(2,1)S(1)} %later.1.refs_0_.refs_2_, bf16[448,1024]{1,0:T(8,128)(2,1)S(1)} %copy-done.23), custom_call_target="tpu_custom_call" | custom-call | flops 3758096384 | bytes 3670016 | tf_op jit(solution)/shard_map/attn_grad/pallas_call | solution.py:513
  422.5 5.0 collective-permute-done.69.refs_1_
  432.4 9.5 %collective-permute-done.74.refs_0_ = bf16[224,1024]{1,0:T(8,128)(2,1)S(1)} collective-permute-done((bf16[224,1024]{1,0:T(8,128)(2,1)S(1)}, bf16[224,1024]{1,0:T(8,128)(2,1)S(1)}, u32[]{:S(2)}, u32[]{:S(2)}) %collective-permute-start.74) | collective-permute-done | bytes 458784 | tf_op jit(solution)/shard_map/ppermute | solution.py:432
  449.1 5.1 %collective-permute-done.82.right_ref = bf16[224,1216]{1,0:T(8,128)(2,1)S(1)} collective-permute-done((bf16[224,1216]{1,0:T(8,128)(2,1)S(1)}, bf16[224,1216]{1,0:T(8,128)(2,1)S(1)}, u32[]{:S(2)}, u32[]{:S(2)}) %collective-permute-start.82) | collective-permute-done | bytes 544800 | tf_op jit(solution)/shard_map/ppermute | solution.py:432
  459.0 22.2 %collective-permute-done.83.left_ref = bf16[224,1216]{1,0:T(8,128)(2,1)S(1)} collective-permute-done((bf16[224,1216]{1,0:T(8,128)(2,1)S(1)}, bf16[224,1216]{1,0:T(8,128)(2,1)S(1)}, u32[]{:S(2)}, u32[]{:S(2)}) %collective-permute-start.83) | collective-permute-done | bytes 544800 | tf_op jit(solution)/shard_map/ppermute | solution.py:432
  490.5 4.1 collective-permute-start.73
  496.4 4.1 collective-permute-done.73
  (376 shorter events, 202.8 us)
Async XLA Ops:
  7.7 24.6 %collective-permute-start.7 = (bf16[2,448,512]{2,1,0:T(8,128)(2,1)}, bf16[2,448,512]{2,1,0:T(8,128)(2,1)}, u32[]{:S(2)}, u32[]{:S(2)}) collective-permute-start(bf16[2,448,512]{2,1,0:T(8,128)(2,1)} %bitcast.57), channel_id=1, source_target_pairs={{0,2},{1,3},{2,0},{3,1},{4,6},{5,7},{6,4},{7,5},{8,10},{9,11},{10,... | collective-permute-start | bytes 2752520 | tf_op jit(solution)/shard_map/ppermute | solution.py:52
  21.7 29.6 %collective-permute-start.6 = (bf16[2,448,512]{2,1,0:T(8,128)(2,1)}, bf16[2,448,512]{2,1,0:T(8,128)(2,1)}, u32[]{:S(2)}, u32[]{:S(2)}) collective-permute-start(bf16[2,448,512]{2,1,0:T(8,128)(2,1)} %bitcast.58), channel_id=1, source_target_pairs={{0,1},{1,0},{2,3},{3,2},{4,5},{5,4},{6,7},{7,6},{8,9},{9,8},{10,11... | collective-permute-start | bytes 2752520 | tf_op jit(solution)/shard_map/ppermute | solution.py:52
  52.5 36.7 %collective-permute-start.15 = (bf16[2,224,1216]{2,1,0:T(8,128)(2,1)S(1)}, bf16[2,224,1216]{2,1,0:T(8,128)(2,1)}, u32[]{:S(2)}, u32[]{:S(2)}) collective-permute-start(bf16[2,224,1216]{2,1,0:T(8,128)(2,1)S(1)} %pad_maximum_fusion.refs_0_), channel_id=1, source_target_pairs={{0,8},{8,16},{16,24},{24,28},{28,20},{20,12},{12,4},{4,0},{1,9},{9... | collective-permute-start | bytes 3268616 | tf_op jit(solution)/shard_map/ppermute | solution.py:432
  54.1 35.2 %collective-permute-start.16 = (bf16[2,224,1216]{2,1,0:T(8,128)(2,1)S(1)}, bf16[2,224,1216]{2,1,0:T(8,128)(2,1)}, u32[]{:S(2)}, u32[]{:S(2)}) collective-permute-start(bf16[2,224,1216]{2,1,0:T(8,128)(2,1)S(1)} %pad_maximum_fusion.refs_0_), channel_id=1, source_target_pairs={{0,4},{8,0},{16,8},{24,16},{28,24},{20,28},{12,20},{4,12},{1,5},{9... | collective-permute-start | bytes 3268616 | tf_op jit(solution)/shard_map/ppermute | solution.py:432
  89.3 42.5 %collective-permute-start.18 = (bf16[2,224,1216]{2,1,0:T(8,128)(2,1)}, bf16[2,224,1216]{2,1,0:T(8,128)(2,1)}, u32[]{:S(2)}, u32[]{:S(2)}) collective-permute-start(bf16[2,224,1216]{2,1,0:T(8,128)(2,1)} %collective-permute-done.15.refs_1_), channel_id=1, source_target_pairs={{0,8},{8,16},{16,24},{24,28},{28,20},{20,12},{12,4},{4,0},{1,9},{9... | collective-permute-start | bytes 3268616 | tf_op jit(solution)/shard_map/ppermute | solution.py:432
  89.4 42.4 %collective-permute-start.19 = (bf16[2,224,1216]{2,1,0:T(8,128)(2,1)}, bf16[2,224,1216]{2,1,0:T(8,128)(2,1)}, u32[]{:S(2)}, u32[]{:S(2)}) collective-permute-start(bf16[2,224,1216]{2,1,0:T(8,128)(2,1)} %collective-permute-done.16.refs_5_), channel_id=1, source_target_pairs={{0,4},{8,0},{16,8},{24,16},{28,24},{20,28},{12,20},{4,12},{1,5},{9... | collective-permute-start | bytes 3268616 | tf_op jit(solution)/shard_map/ppermute | solution.py:432
  98.9 30.2 %collective-permute-start.20 = (bf16[2,4,160,128]{3,2,1,0:T(8,128)(2,1)}, bf16[2,4,160,128]{3,2,1,0:T(8,128)(2,1)}, u32[]{:S(2)}, u32[]{:S(2)}) collective-permute-start(bf16[2,4,160,128]{3,2,1,0:T(8,128)(2,1)} %add_convert_fusion.5), channel_id=1, source_target_pairs={{0,16},{4,20},{8,24},{12,28},{1,17},{5,21},{9,25},{13,29},{2,18},{... | collective-permute-start | bytes 983048 | tf_op jit(solution)/shard_map/ppermute | solution.py:616
  104.6 36.8 %collective-permute-start.21 = (bf16[224,1216]{1,0:T(8,128)(2,1)}, bf16[224,1216]{1,0:T(8,128)(2,1)S(1)}, u32[]{:S(2)}, u32[]{:S(2)}) collective-permute-start(bf16[224,1216]{1,0:T(8,128)(2,1)} %bitcast.62), channel_id=1, source_target_pairs={{0,8},{8,16},{16,24},{24,28},{28,20},{20,12},{12,4},{4,0},{1,9},{9... | collective-permute-start | bytes 1634312 | tf_op jit(solution)/shard_map/ppermute | solution.py:432
  107.1 34.3 %collective-permute-start.22 = (bf16[224,1216]{1,0:T(8,128)(2,1)}, bf16[224,1216]{1,0:T(8,128)(2,1)S(1)}, u32[]{:S(2)}, u32[]{:S(2)}) collective-permute-start(bf16[224,1216]{1,0:T(8,128)(2,1)} %bitcast.63), channel_id=1, source_target_pairs={{0,4},{8,0},{16,8},{24,16},{28,24},{20,28},{12,20},{4,12},{1,5},{9... | collective-permute-start | bytes 1634312 | tf_op jit(solution)/shard_map/ppermute | solution.py:432
  131.8 32.6 %collective-permute-start.24 = (bf16[2,224,1216]{2,1,0:T(8,128)(2,1)}, bf16[2,224,1216]{2,1,0:T(8,128)(2,1)S(1)}, u32[]{:S(2)}, u32[]{:S(2)}) collective-permute-start(bf16[2,224,1216]{2,1,0:T(8,128)(2,1)} %collective-permute-done.18.refs_2_), channel_id=1, source_target_pairs={{0,8},{8,16},{16,24},{24,28},{28,20},{20,12},{12,4},{4,0},{1,9},{9... | collective-permute-start | bytes 3268616 | tf_op jit(solution)/shard_map/ppermute | solution.py:432
  135.7 28.7 %collective-permute-start.25 = (bf16[2,224,1216]{2,1,0:T(8,128)(2,1)}, bf16[2,224,1216]{2,1,0:T(8,128)(2,1)S(1)}, u32[]{:S(2)}, u32[]{:S(2)}) collective-permute-start(bf16[2,224,1216]{2,1,0:T(8,128)(2,1)} %collective-permute-done.19.refs_6_), channel_id=1, source_target_pairs={{0,4},{8,0},{16,8},{24,16},{28,24},{20,28},{12,20},{4,12},{1,5},{9... | collective-permute-start | bytes 3268616 | tf_op jit(solution)/shard_map/ppermute | solution.py:432
  168.8 23.2 %collective-permute-start.31 = (bf16[2,112,1216]{2,1,0:T(8,128)(2,1)S(1)}, bf16[2,112,1216]{2,1,0:T(8,128)(2,1)S(1)}, u32[]{:S(2)}, u32[]{:S(2)}) collective-permute-start(bf16[2,112,1216]{2,1,0:T(8,128)(2,1)S(1)} %slice.111), channel_id=1, source_target_pairs={{0,8},{8,16},{16,24},{24,28},{28,20},{20,12},{12,4},{4,0},{1,9},{9... | collective-permute-start | bytes 1634312 | tf_op jit(solution)/shard_map/ppermute | solution.py:432
  172.0 24.9 %collective-permute-start.33 = (bf16[224,1216]{1,0:T(8,128)(2,1)S(1)}, bf16[224,1216]{1,0:T(8,128)(2,1)S(1)}, u32[]{:S(2)}, u32[]{:S(2)}) collective-permute-start(bf16[224,1216]{1,0:T(8,128)(2,1)S(1)} %collective-permute-done.21.refs_1_), channel_id=1, source_target_pairs={{0,8},{8,16},{16,24},{24,28},{28,20},{20,12},{12,4},{4,0},{1,9},{9... | collective-permute-start | bytes 1634312 | tf_op jit(solution)/shard_map/ppermute | solution.py:432
  174.4 25.4 %collective-permute-start.34 = (bf16[224,1216]{1,0:T(8,128)(2,1)S(1)}, bf16[224,1216]{1,0:T(8,128)(2,1)S(1)}, u32[]{:S(2)}, u32[]{:S(2)}) collective-permute-start(bf16[224,1216]{1,0:T(8,128)(2,1)S(1)} %collective-permute-done.22.refs_5_), channel_id=1, source_target_pairs={{0,4},{8,0},{16,8},{24,16},{28,24},{20,28},{12,20},{4,12},{1,5},{9... | collective-permute-start | bytes 1634312 | tf_op jit(solution)/shard_map/ppermute | solution.py:432
  190.5 24.7 %collective-permute-start.38 = (bf16[2,448,512]{2,1,0:T(8,128)(2,1)S(1)}, bf16[2,448,512]{2,1,0:T(8,128)(2,1)S(1)}, u32[]{:S(2)}, u32[]{:S(2)}) collective-permute-start(bf16[2,448,512]{2,1,0:T(8,128)(2,1)S(1)} %get-tuple-element.429.refs_0_), channel_id=1, source_target_pairs={{0,2},{1,3},{2,0},{3,1},{4,6},{5,7},{6,4},{7,5},{8,10},{9,11},{10,... | collective-permute-start | bytes 2752520 | tf_op jit(solution)/shard_map/ppermute | solution.py:52
  319.7 27.0 %collective-permute-start.54 = (bf16[224,2432]{1,0:T(8,128)(2,1)}, bf16[224,2432]{1,0:T(8,128)(2,1)S(1)}, u32[]{:S(2)}, u32[]{:S(2)}) collective-permute-start(bf16[224,2432]{1,0:T(8,128)(2,1)} %get-tuple-element.304), channel_id=1, source_target_pairs={{0,8},{8,16},{16,24},{24,28},{28,20},{20,12},{12,4},{4,0},{1,9},{9... | collective-permute-start | bytes 3268616 | tf_op jit(solution)/shard_map/ppermute | solution.py:432
  321.1 26.1 %collective-permute-start.55 = (bf16[224,2432]{1,0:T(8,128)(2,1)S(1)}, bf16[224,2432]{1,0:T(8,128)(2,1)S(1)}, u32[]{:S(2)}, u32[]{:S(2)}) collective-permute-start(bf16[224,2432]{1,0:T(8,128)(2,1)S(1)} %get-tuple-element.305), channel_id=1, source_target_pairs={{0,4},{8,0},{16,8},{24,16},{28,24},{20,28},{12,20},{4,12},{1,5},{9... | collective-permute-start | bytes 3268616 | tf_op jit(solution)/shard_map/ppermute | solution.py:432
  328.7 24.7 %collective-permute-start.56 = (bf16[2,4,160,128]{3,2,1,0:T(8,128)(2,1)S(1)}, bf16[2,4,160,128]{3,2,1,0:T(8,128)(2,1)S(1)}, u32[]{:S(2)}, u32[]{:S(2)}) collective-permute-start(bf16[2,4,160,128]{3,2,1,0:T(8,128)(2,1)S(1)} %get-tuple-element.322), channel_id=1, source_target_pairs={{0,4},{4,0},{8,12},{12,8},{16,20},{20,16},{24,28},{28,24},{1,5},{5... | collective-permute-start | bytes 983048 | tf_op jit(solution)/shard_map/ppermute | solution.py:625
  364.5 24.0 %collective-permute-start.57 = (bf16[448,1024]{1,0:T(8,128)(2,1)}, bf16[448,1024]{1,0:T(8,128)(2,1)}, u32[]{:S(2)}, u32[]{:S(2)}) collective-permute-start(bf16[448,1024]{1,0:T(8,128)(2,1)} %get-tuple-element.335), channel_id=1, source_target_pairs={{0,1},{1,0},{2,3},{3,2},{4,5},{5,4},{6,7},{7,6},{8,9},{9,8},{10,11... | collective-permute-start | bytes 2752520 | tf_op jit(solution)/shard_map/ppermute | solution.py:52
  364.5 26.3 %collective-permute-start.59 = (bf16[448,1024]{1,0:T(8,128)(2,1)}, bf16[448,1024]{1,0:T(8,128)(2,1)}, u32[]{:S(2)}, u32[]{:S(2)}) collective-permute-start(bf16[448,1024]{1,0:T(8,128)(2,1)} %get-tuple-element.344), channel_id=1, source_target_pairs={{0,1},{1,0},{2,3},{3,2},{4,5},{5,4},{6,7},{7,6},{8,9},{9,8},{10,11... | collective-permute-start | bytes 2752520 | tf_op jit(solution)/shard_map/ppermute | solution.py:52
  367.9 36.3 %collective-permute-start.62 = (bf16[224,1216]{1,0:T(8,128)(2,1)}, bf16[224,1216]{1,0:T(8,128)(2,1)S(1)}, u32[]{:S(2)}, u32[]{:S(2)}) collective-permute-start(bf16[224,1216]{1,0:T(8,128)(2,1)} %copy-done.40), channel_id=1, source_target_pairs={{0,8},{8,16},{16,24},{24,28},{28,20},{20,12},{12,4},{4,0},{1,9},{9... | collective-permute-start | bytes 1634312 | tf_op jit(solution)/shard_map/ppermute | solution.py:432
  370.6 34.2 %collective-permute-start.63 = (bf16[224,1216]{1,0:T(8,128)(2,1)}, bf16[224,1216]{1,0:T(8,128)(2,1)S(1)}, u32[]{:S(2)}, u32[]{:S(2)}) collective-permute-start(bf16[224,1216]{1,0:T(8,128)(2,1)} %copy-done.39), channel_id=1, source_target_pairs={{0,4},{8,0},{16,8},{24,16},{28,24},{20,28},{12,20},{4,12},{1,5},{9... | collective-permute-start | bytes 1634312 | tf_op jit(solution)/shard_map/ppermute | solution.py:432
  387.4 27.1 %collective-permute-start.64 = (bf16[224,2432]{1,0:T(8,128)(2,1)}, bf16[224,2432]{1,0:T(8,128)(2,1)S(1)}, u32[]{:S(2)}, u32[]{:S(2)}) collective-permute-start(bf16[224,2432]{1,0:T(8,128)(2,1)} %get-tuple-element.340), channel_id=1, source_target_pairs={{0,8},{8,16},{16,24},{24,28},{28,20},{20,12},{12,4},{4,0},{1,9},{9... | collective-permute-start | bytes 3268616 | tf_op jit(solution)/shard_map/ppermute | solution.py:432
  388.5 26.3 %collective-permute-start.65 = (bf16[224,2432]{1,0:T(8,128)(2,1)}, bf16[224,2432]{1,0:T(8,128)(2,1)S(1)}, u32[]{:S(2)}, u32[]{:S(2)}) collective-permute-start(bf16[224,2432]{1,0:T(8,128)(2,1)} %get-tuple-element.341), channel_id=1, source_target_pairs={{0,4},{8,0},{16,8},{24,16},{28,24},{20,28},{12,20},{4,12},{1,5},{9... | collective-permute-start | bytes 3268616 | tf_op jit(solution)/shard_map/ppermute | solution.py:432
  404.8 27.4 %collective-permute-start.60 = (bf16[2,448,512]{2,1,0:T(8,128)(2,1)}, bf16[2,448,512]{2,1,0:T(8,128)(2,1)}, u32[]{:S(2)}, u32[]{:S(2)}) collective-permute-start(bf16[2,448,512]{2,1,0:T(8,128)(2,1)} %get-tuple-element.346), channel_id=1, source_target_pairs={{0,2},{1,3},{2,0},{3,1},{4,6},{5,7},{6,4},{7,5},{8,10},{9,11},{10,... | collective-permute-start | bytes 2752520 | tf_op jit(solution)/shard_map/ppermute | solution.py:52
  420.0 28.7 %collective-permute-start.70 = (bf16[2,456,512]{2,1,0:T(8,128)(2,1)S(1)}, bf16[2,456,512]{2,1,0:T(8,128)(2,1)S(1)}, u32[]{:S(2)}, u32[]{:S(2)}) collective-permute-start(bf16[2,456,512]{2,1,0:T(8,128)(2,1)S(1)} %get-tuple-element.368), channel_id=1, source_target_pairs={{0,2},{1,3},{2,0},{3,1},{4,6},{5,7},{6,4},{7,5},{8,10},{9,11},{10,... | collective-permute-start | bytes 2801672 | tf_op jit(solution)/shard_map/ppermute | solution.py:52
  430.5 23.7 %collective-permute-start.82 = (bf16[224,1216]{1,0:T(8,128)(2,1)S(1)}, bf16[224,1216]{1,0:T(8,128)(2,1)S(1)}, u32[]{:S(2)}, u32[]{:S(2)}) collective-permute-start(bf16[224,1216]{1,0:T(8,128)(2,1)S(1)} %copy-done.42), channel_id=1, source_target_pairs={{0,8},{8,16},{16,24},{24,28},{28,20},{20,12},{12,4},{4,0},{1,9},{9... | collective-permute-start | bytes 1634312 | tf_op jit(solution)/shard_map/ppermute | solution.py:432
  432.3 51.6 %collective-permute-start.80 = (bf16[224,2432]{1,0:T(8,128)(2,1)S(1)}, bf16[224,2432]{1,0:T(8,128)(2,1)S(1)}, u32[]{:S(2)}, u32[]{:S(2)}) collective-permute-start(bf16[224,2432]{1,0:T(8,128)(2,1)S(1)} %get-tuple-element.363), channel_id=1, source_target_pairs={{0,8},{8,16},{16,24},{24,28},{28,20},{20,12},{12,4},{4,0},{1,9},{9... | collective-permute-start | bytes 3268616 | tf_op jit(solution)/shard_map/ppermute | solution.py:432
  441.9 42.0 %collective-permute-start.81 = (bf16[224,2432]{1,0:T(8,128)(2,1)S(1)}, bf16[224,2432]{1,0:T(8,128)(2,1)S(1)}, u32[]{:S(2)}, u32[]{:S(2)}) collective-permute-start(bf16[224,2432]{1,0:T(8,128)(2,1)S(1)} %get-tuple-element.364), channel_id=1, source_target_pairs={{0,4},{8,0},{16,8},{24,16},{28,24},{20,28},{12,20},{4,12},{1,5},{9... | collective-permute-start | bytes 3268616 | tf_op jit(solution)/shard_map/ppermute | solution.py:432
  446.2 35.0 %collective-permute-start.83 = (bf16[224,1216]{1,0:T(8,128)(2,1)S(1)}, bf16[224,1216]{1,0:T(8,128)(2,1)S(1)}, u32[]{:S(2)}, u32[]{:S(2)}) collective-permute-start(bf16[224,1216]{1,0:T(8,128)(2,1)S(1)} %get-tuple-element.355), channel_id=1, source_target_pairs={{0,4},{8,0},{16,8},{24,16},{28,24},{20,28},{12,20},{4,12},{1,5},{9... | collective-permute-start | bytes 1634312 | tf_op jit(solution)/shard_map/ppermute | solution.py:432
  448.7 38.2 %collective-permute-start.76 = (bf16[224,1024]{1,0:T(8,128)(2,1)S(1)}, bf16[224,1024]{1,0:T(8,128)(2,1)S(1)}, u32[]{:S(2)}, u32[]{:S(2)}) collective-permute-start(bf16[224,1024]{1,0:T(8,128)(2,1)S(1)} %get-tuple-element.383), channel_id=1, source_target_pairs={{0,8},{8,16},{16,24},{24,28},{28,20},{20,12},{12,4},{4,0},{1,9},{9... | collective-permute-start | bytes 1376264 | tf_op jit(solution)/shard_map/ppermute | solution.py:432
  454.2 32.7 %collective-permute-start.77 = (bf16[224,1024]{1,0:T(8,128)(2,1)S(1)}, bf16[224,1024]{1,0:T(8,128)(2,1)S(1)}, u32[]{:S(2)}, u32[]{:S(2)}) collective-permute-start(bf16[224,1024]{1,0:T(8,128)(2,1)S(1)} %get-tuple-element.384), channel_id=1, source_target_pairs={{0,4},{8,0},{16,8},{24,16},{28,24},{20,28},{12,20},{4,12},{1,5},{9... | collective-permute-start | bytes 1376264 | tf_op jit(solution)/shard_map/ppermute | solution.py:432
  (122 other events, 1497.5 us)

commit v6 on v5

--- a/solution.py
+++ b/solution.py
@@ -981,8 +981,10 @@
     fence(after.sent)
     gate_up_ring.advance(*token)
     fence(gate_up_ring.sent)
-    scatter_out.cross(*token)
-    fence(scatter_out.sent_far)
+
+    fence(down_ring.here())
+    down_ring.advance(*token)
+    fence(down_ring.sent)
 
     def later(*refs):
         later_kernel(heads, *refs)
@@ -999,13 +1001,12 @@
         index, projected(index, w_attn, [d_qkv], "qkv_back", row=inner), seqs, inner
     )
     fence(scatter_one.sent)
-    fence(down_ring.here())
-    down_ring.advance(*token)
-    fence(down_ring.sent)
     attn_ring = Products(
         index, products([turn(normed_one), resid_full], [d_qkv, mixed], "attn_grad")
     )
     fence(attn_ring.sent)
+    scatter_out.cross(*token)
+    fence(scatter_out.sent_far)
     fence(gate_up_ring.here())
     gate_up_ring.advance(*token)
     fence(gate_up_ring.sent)

time: 514 us -> 508 us (0.988)
    ppermute x27, waiting for transfers between devices: 20.3 us -> 41.3 us  [swap(): return lax.ppermute(value, 'wt', [(i, i ^ bit) for i in range(count)])]
    ppermute x48, waiting for transfers between devices: 135 us -> 117 us  [hop(): return lax.ppermute(value, 'ctx', pairs)]
    ppermute x4, waiting for transfers between devices: 36.7 us -> 31.3 us  [shifted(): return lax.ppermute(value, 'ctx', pairs)]
    unnamed x150 -> x146, local copies, waits for them, and re-layouts: 23.1 us -> 23.4 us
  transfers between devices with their start and end apart: 84 -> 84, of which waited for: 37 -> 35; matrix products, arithmetic and copies ran while one was open for 9% -> 9% of each run, Pallas kernels for 19% -> 19%
where the time goes in v6:
time: 508 us; the launch traced here: 499 us
  waiting for transfers between devices  221 us (44%)
  Pallas kernels  110 us (22%)
  starting transfers between devices  84.5 us (17%)
  matrix products  32.5 us (6%)
  local copies, waits for them, and re-layouts  29.9 us (6%)
  other arithmetic  18.7 us (4%)
    ppermute x48, waiting for transfers between devices, hop(): return lax.ppermute(value, 'ctx', pairs)  117 us
    ppermute x48, starting transfers between devices, hop(): return lax.ppermute(value, 'ctx', pairs)  56.5 us
    ppermute x27, waiting for transfers between devices, swap(): return lax.ppermute(value, 'wt', [(i, i ^ bit) for i in range(count)])  41.3 us
    dot_general x5, matrix products, mm_tn(): lax.dot_general(left, right, (((0,), (0,)), ((), ())), preferred_element_...  32.5 us
    ppermute x4, waiting for transfers between devices, shifted(): return lax.ppermute(value, 'ctx', pairs)  31.3 us
    pallas_call x4, Pallas kernels, projected(): pl.pallas_call(kernel, name=name, grid_spec=pltpu.PrefetchScalarGridSpec(...  28.2 us
    ppermute x2, waiting for transfers between devices, __init__(): self.other = lax.ppermute(value, 'ctx', [(i, i ^ 1) for i in range(count)])  27 us
    unnamed x146, local copies, waits for them, and re-layouts  23.4 us
  transfers between devices with their start and end apart: 84, of which 35 were waited for; matrix products, arithmetic and copies ran while one was open for 9% of the time, Pallas kernels for 19%

profile of v6, /device:TPU:0, one launch (start us, length us, event | category | flops | bytes accessed | tf_op | source)
XLA Modules:
  0.0 499.0 jit_solution(11936976312831378482)
XLA Ops:
  9.7 8.5 %collective-permute-done.refs_1_ = bf16[224,1024]{1,0:T(8,128)(2,1)S(1)} collective-permute-done((bf16[224,1024]{1,0:T(8,128)(2,1)S(1)}, bf16[224,1024]{1,0:T(8,128)(2,1)S(1)}, u32[]{:S(2)}, u32[]{:S(2)}) %collective-permute-start) | collective-permute-done | bytes 458784 | tf_op jit(solution)/shard_map/ppermute | solution.py:432
  23.1 7.9 %collective-permute-done.2.refs_2_ = bf16[224,1024]{1,0:T(8,128)(2,1)} collective-permute-done((bf16[224,1024]{1,0:T(8,128)(2,1)S(1)}, bf16[224,1024]{1,0:T(8,128)(2,1)}, u32[]{:S(2)}, u32[]{:S(2)}) %collective-permute-start.2) | collective-permute-done | bytes 458784 | tf_op jit(solution)/shard_map/ppermute | solution.py:432
  36.2 9.3 %collective-permute-done.4.refs_3_ = bf16[224,1024]{1,0:T(8,128)(2,1)S(1)} collective-permute-done((bf16[224,1024]{1,0:T(8,128)(2,1)}, bf16[224,1024]{1,0:T(8,128)(2,1)S(1)}, u32[]{:S(2)}, u32[]{:S(2)}) %collective-permute-start.4) | collective-permute-done | bytes 458784 | tf_op jit(solution)/shard_map/ppermute | solution.py:432
  66.6 21.3 %collective-permute-done.14 = bf16[2,4,160,128]{3,2,1,0:T(8,128)(2,1)S(1)} collective-permute-done((bf16[2,4,160,128]{3,2,1,0:T(8,128)(2,1)S(1)}, bf16[2,4,160,128]{3,2,1,0:T(8,128)(2,1)S(1)}, u32[]{:S(2)}, u32[]{:S(2)}) %collective-permute-start.14) | collective-permute-done | bytes 327712 | tf_op jit(solution)/shard_map/ppermute | solution.py:625
  91.4 6.0 %collective-permute-done.17 = bf16[2,4,160,128]{3,2,1,0:T(8,128)(2,1)S(1)} collective-permute-done((bf16[2,4,160,128]{3,2,1,0:T(8,128)(2,1)S(1)}, bf16[2,4,160,128]{3,2,1,0:T(8,128)(2,1)S(1)}, u32[]{:S(2)}, u32[]{:S(2)}) %collective-permute-start.17) | collective-permute-done | bytes 327712 | tf_op jit(solution)/shard_map/ppermute | solution.py:616
  98.9 5.6 %collective-permute-start.20 = (bf16[2,4,160,128]{3,2,1,0:T(8,128)(2,1)}, bf16[2,4,160,128]{3,2,1,0:T(8,128)(2,1)}, u32[]{:S(2)}, u32[]{:S(2)}) collective-permute-start(bf16[2,4,160,128]{3,2,1,0:T(8,128)(2,1)} %add_convert_fusion.5), channel_id=1, source_target_pairs={{0,16},{4,20},{8,24},{12,28},{1,17},{5,21},{9,25},{13,29},{2,18},{... | collective-permute-start | bytes 983048 | tf_op jit(solution)/shard_map/ppermute | solution.py:616
  108.5 20.7 %collective-permute-done.20 = bf16[2,4,160,128]{3,2,1,0:T(8,128)(2,1)} collective-permute-done((bf16[2,4,160,128]{3,2,1,0:T(8,128)(2,1)}, bf16[2,4,160,128]{3,2,1,0:T(8,128)(2,1)}, u32[]{:S(2)}, u32[]{:S(2)}) %collective-permute-start.20) | collective-permute-done | bytes 327712 | tf_op jit(solution)/shard_map/ppermute | solution.py:616
  131.8 3.9 collective-permute-start.24
  135.7 4.8 attend.1
  148.4 16.1 %collective-permute-done.24.refs_3_ = bf16[2,224,1216]{2,1,0:T(8,128)(2,1)S(1)} collective-permute-done((bf16[2,224,1216]{2,1,0:T(8,128)(2,1)}, bf16[2,224,1216]{2,1,0:T(8,128)(2,1)S(1)}, u32[]{:S(2)}, u32[]{:S(2)}) %collective-permute-start.24) | collective-permute-done | bytes 1089568 | tf_op jit(solution)/shard_map/ppermute | solution.py:432
  174.4 14.4 %collective-permute-done.27 = bf16[2,448,512]{2,1,0:T(8,128)(2,1)S(1)} collective-permute-done((bf16[2,448,512]{2,1,0:T(8,128)(2,1)S(1)}, bf16[2,448,512]{2,1,0:T(8,128)(2,1)S(1)}, u32[]{:S(2)}, u32[]{:S(2)}) %collective-permute-start.27) | collective-permute-done | bytes 917536 | tf_op jit(solution)/shard_map/ppermute | solution.py:52
  192.0 4.9 collective-permute-done.33.refs_2_
  204.9 9.1 %collective-permute-done.35.refs_3_ = bf16[224,1216]{1,0:T(8,128)(2,1)S(1)} collective-permute-done((bf16[224,1216]{1,0:T(8,128)(2,1)S(1)}, bf16[224,1216]{1,0:T(8,128)(2,1)S(1)}, u32[]{:S(2)}, u32[]{:S(2)}) %collective-permute-start.35) | collective-permute-done | bytes 544800 | tf_op jit(solution)/shard_map/ppermute | solution.py:432
  219.8 6.5 %fusion.1 = f32[1216,1024]{1,0:T(8,128)} fusion(bf16[1792,1024]{1,0:T(8,128)(2,1)S(1)} %get-tuple-element.267.refs_0_, bf16[2,1792,1216]{2,1,0:T(8,128)(2,1)S(1)} %assemble.4.weight_ref), kind=kOutput, calls=%fused_computation.8 | convolution fusion | flops 4462739456 | bytes 13238272 | tf_op jit(solution)/shard_map/dot_general | solution.py:30
  226.3 8.8 %multiply_convert_fusion.2 = (bf16[1216,1024]{1,0:T(8,128)(2,1)S(1)}, f32[1216,1024]{1,0:T(8,128)}) fusion(f32[1216,1024]{1,0:T(8,128)} %fusion.1, bf16[1792,1024]{1,0:T(8,128)(2,1)S(1)} %get-tuple-element.267.refs_0_, bf16[2,1792,1216]{2,1,0:T(8,128)(2,1)S(1)} %assemble.4.weight_ref), kind=kOutput, calls=%fused_computation.3 | convolution fusion | flops 4470210560 | bytes 20709376 | tf_op jit(solution)/shard_map/dot_general | solution.py:30
  236.6 12.9 %add_reduce_fusion = (f32[1024]{0:T(1024)S(1)}, bf16[1216,1024]{1,0:T(8,128)(2,1)}, bf16[1216,1024]{1,0:T(8,128)(2,1)}) fusion(f32[1216,1024]{1,0:T(8,128)} %get-tuple-element.443, f32[1216,1024]{1,0:T(8,128)} %fusion.1, bf16[1792,1216]{1,0:T(8,128)(2,1)S(1)} %assemble.5.weight_ref, bf16[1792,1024]{1,0:T(8,128)(2,1)S(1)} %gather.2.refs_0_), kind=kOutput, calls=%fused_computation | convolution fusion | flops 4486396928 | bytes 22974464 | tf_op jit(solution)/shard_map/dot_general | solution.py:30
  252.9 11.9 %ffn_back.1 = (bf16[456,1024]{1,0:T(8,128)(2,1)S(1)}, bf16[456,1024]{1,0:T(8,128)(2,1)S(1)}, bf16[2,448,1024]{2,1,0:T(8,128)(2,1)S(1)}) custom-call(s32[9]{0:T(128)S(1)} %fusion.20.index_ref, bf16[2,1792,1216]{2,1,0:T(8,128)(2,1)S(1)} %assemble.4.weight_ref, bf16[1216,1024]{1,0:T(8,128)(2,1)S(1)} %copy-done.43, bf16[1216,1024]{1,0:T(8,128)(2,1)S(1)} %copy-done.41, ...), custom_call_target="tpu_custom_call" | custom-call | flops 8925478912 | bytes 8388608 | tf_op jit(solution)/shard_map/ffn_back/pallas_call | solution.py:155
  265.3 5.6 %down_grad.1.refs_0_.refs_2_.refs_3_.own = bf16[1792,1216]{1,0:T(8,128)(2,1)S(1)} custom-call(bf16[1792,1024]{1,0:T(8,128)(2,1)S(1)} %copy-done.11, bf16[1216,1024]{1,0:T(8,128)(2,1)S(1)} %get-tuple-element.307.refs_1_.refs_0_), custom_call_target="tpu_custom_call" | custom-call | flops 4462739456 | bytes 4358144 | tf_op jit(solution)/shard_map/down_grad/pallas_call | solution.py:513
  279.4 10.6 %gate_up_grad.1.refs_0_.refs_2_.refs_3_.own = bf16[1792,2432]{1,0:T(8,128)(2,1)S(1)} custom-call(bf16[1792,1024]{1,0:T(8,128)(2,1)S(1)} %copy-done.37, bf16[1216,1024]{1,0:T(8,128)(2,1)S(1)} %copy-done.44, bf16[1216,1024]{1,0:T(8,128)(2,1)S(1)} %copy-done.42), custom_call_target="tpu_custom_call" | custom-call | flops 8925478912 | bytes 8716288 | tf_op jit(solution)/shard_map/gate_up_grad/pallas_call | solution.py:513
  300.8 5.3 %collective-permute-done.47.refs_0_ = bf16[112,2432]{1,0:T(8,128)(2,1)S(1)} collective-permute-done((bf16[112,2432]{1,0:T(8,128)(2,1)S(1)}, bf16[112,2432]{1,0:T(8,128)(2,1)S(1)}, u32[]{:S(2)}, u32[]{:S(2)}) %collective-permute-start.47) | collective-permute-done | bytes 544800 | tf_op jit(solution)/shard_map/ppermute | solution.py:432
  309.6 7.3 %ffn_out.1 = (bf16[448,1024]{1,0:T(8,128)(2,1)}, bf16[448,1024]{1,0:T(8,128)(2,1)S(1)}, bf16[2,448,1024]{2,1,0:T(8,128)(2,1)S(1)}) custom-call(s32[9]{0:T(128)S(1)} %fusion.20.index_ref, bf16[1792,1216]{1,0:T(8,128)(2,1)S(1)} %bitcast.61, bf16[1216,1024]{1,0:T(8,128)(2,1)S(1)} %get-tuple-element.307.refs_1_.refs_0_), custom_call_target="tpu_custom_call" | custom-call | flops 4462739456 | bytes 8388608 | tf_op jit(solution)/shard_map/ffn_out/pallas_call | solution.py:155
  329.4 17.8 %collective-permute-done.54.refs_0_ = bf16[224,2432]{1,0:T(8,128)(2,1)S(1)} collective-permute-done((bf16[224,2432]{1,0:T(8,128)(2,1)}, bf16[224,2432]{1,0:T(8,128)(2,1)S(1)}, u32[]{:S(2)}, u32[]{:S(2)}) %collective-permute-start.54) | collective-permute-done | bytes 1089568 | tf_op jit(solution)/shard_map/ppermute | solution.py:432
  348.0 5.8 %collective-permute-done.56 = bf16[2,4,160,128]{3,2,1,0:T(8,128)(2,1)S(1)} collective-permute-done((bf16[2,4,160,128]{3,2,1,0:T(8,128)(2,1)S(1)}, bf16[2,4,160,128]{3,2,1,0:T(8,128)(2,1)S(1)}, u32[]{:S(2)}, u32[]{:S(2)}) %collective-permute-start.56) | collective-permute-done | bytes 327712 | tf_op jit(solution)/shard_map/ppermute | solution.py:625
  357.9 7.8 %local.1 = (bf16[64,1024]{1,0:T(8,128)(2,1)S(1)}, f32[64,1024]{1,0:T(8,128)S(1)}, f32[448,1024]{1,0:T(8,128)S(1)}) custom-call(bf16[576,1024]{1,0:T(8,128)(2,1)S(1)} %fusion.9.key_ref.value_ref.query_ref.refs_0_.refs_1_, bf16[576,1024]{1,0:T(8,128)(2,1)S(1)} %fusion.9.key_ref.value_ref.query_ref.refs_0_.refs_1_, ...), custom_call_target="tpu_custom_call" | custom-call | flops 2147483648 | bytes 4194304 | tf_op jit(solution)/shard_map/local/pallas_call | solution.py:970
  385.0 4.6 collective-permute-done.61
  394.1 5.4 %qkv_back.1 = (bf16[456,1024]{1,0:T(8,128)(2,1)}, bf16[456,1024]{1,0:T(8,128)(2,1)S(1)}, bf16[2,448,1024]{2,1,0:T(8,128)(2,1)S(1)}) custom-call(s32[9]{0:T(128)S(1)} %fusion.20.index_ref, bf16[1792,1024]{1,0:T(8,128)(2,1)S(1)} %copy-done.9, bf16[576,1024]{1,0:T(8,128)(2,1)S(1)} %later.1.refs_0_.refs_2_, f32[1,1024]{1,0:T(1,128)S(1)} %bitcast.65), custom_call_target="tpu_custom_call" | custom-call | flops 2113929216 | bytes 8388608 | tf_op jit(solution)/shard_map/qkv_back/pallas_call | solution.py:155
  400.0 5.9 %attn_grad.1.refs_0_.refs_2_.refs_3_.own = bf16[1792,1024]{1,0:T(8,128)(2,1)S(1)} custom-call(bf16[1792,1024]{1,0:T(8,128)(2,1)S(1)} %copy-done.35, bf16[1792,1024]{1,0:T(8,128)(2,1)S(1)} %copy-done.13, bf16[576,1024]{1,0:T(8,128)(2,1)S(1)} %later.1.refs_0_.refs_2_, bf16[448,1024]{1,0:T(8,128)(2,1)S(1)} %copy-done.22), custom_call_target="tpu_custom_call" | custom-call | flops 3758096384 | bytes 3670016 | tf_op jit(solution)/shard_map/attn_grad/pallas_call | solution.py:513
  416.8 5.0 %collective-permute-done.68.refs_0_ = bf16[112,1024]{1,0:T(8,128)(2,1)S(1)} collective-permute-done((bf16[112,1024]{1,0:T(8,128)(2,1)S(1)}, bf16[112,1024]{1,0:T(8,128)(2,1)S(1)}, u32[]{:S(2)}, u32[]{:S(2)}) %collective-permute-start.68) | collective-permute-done | bytes 229408 | tf_op jit(solution)/shard_map/ppermute | solution.py:432
  425.1 8.1 %collective-permute-done.63 = bf16[2,448,512]{2,1,0:T(8,128)(2,1)S(1)} collective-permute-done((bf16[2,448,512]{2,1,0:T(8,128)(2,1)S(1)}, bf16[2,448,512]{2,1,0:T(8,128)(2,1)S(1)}, u32[]{:S(2)}, u32[]{:S(2)}) %collective-permute-start.63) | collective-permute-done | bytes 917536 | tf_op jit(solution)/shard_map/ppermute | solution.py:52
  439.0 13.3 %collective-permute-done.70 = bf16[2,456,512]{2,1,0:T(8,128)(2,1)S(1)} collective-permute-done((bf16[2,456,512]{2,1,0:T(8,128)(2,1)S(1)}, bf16[2,456,512]{2,1,0:T(8,128)(2,1)S(1)}, u32[]{:S(2)}, u32[]{:S(2)}) %collective-permute-start.70) | collective-permute-done | bytes 933920 | tf_op jit(solution)/shard_map/ppermute | solution.py:52
  460.9 18.4 %collective-permute-done.76.refs_0_ = bf16[224,1024]{1,0:T(8,128)(2,1)S(1)} collective-permute-done((bf16[224,1024]{1,0:T(8,128)(2,1)S(1)}, bf16[224,1024]{1,0:T(8,128)(2,1)S(1)}, u32[]{:S(2)}, u32[]{:S(2)}) %collective-permute-start.76) | collective-permute-done | bytes 458784 | tf_op jit(solution)/shard_map/ppermute | solution.py:432
  489.1 4.6 collective-permute-done.73
  (372 shorter events, 198.8 us)
Async XLA Ops:
  7.7 24.6 %collective-permute-start.7 = (bf16[2,448,512]{2,1,0:T(8,128)(2,1)}, bf16[2,448,512]{2,1,0:T(8,128)(2,1)}, u32[]{:S(2)}, u32[]{:S(2)}) collective-permute-start(bf16[2,448,512]{2,1,0:T(8,128)(2,1)} %bitcast.57), channel_id=1, source_target_pairs={{0,2},{1,3},{2,0},{3,1},{4,6},{5,7},{6,4},{7,5},{8,10},{9,11},{10,... | collective-permute-start | bytes 2752520 | tf_op jit(solution)/shard_map/ppermute | solution.py:52
  21.7 29.6 %collective-permute-start.6 = (bf16[2,448,512]{2,1,0:T(8,128)(2,1)}, bf16[2,448,512]{2,1,0:T(8,128)(2,1)}, u32[]{:S(2)}, u32[]{:S(2)}) collective-permute-start(bf16[2,448,512]{2,1,0:T(8,128)(2,1)} %bitcast.58), channel_id=1, source_target_pairs={{0,1},{1,0},{2,3},{3,2},{4,5},{5,4},{6,7},{7,6},{8,9},{9,8},{10,11... | collective-permute-start | bytes 2752520 | tf_op jit(solution)/shard_map/ppermute | solution.py:52
  52.5 36.7 %collective-permute-start.15 = (bf16[2,224,1216]{2,1,0:T(8,128)(2,1)S(1)}, bf16[2,224,1216]{2,1,0:T(8,128)(2,1)}, u32[]{:S(2)}, u32[]{:S(2)}) collective-permute-start(bf16[2,224,1216]{2,1,0:T(8,128)(2,1)S(1)} %pad_maximum_fusion.refs_0_), channel_id=1, source_target_pairs={{0,8},{8,16},{16,24},{24,28},{28,20},{20,12},{12,4},{4,0},{1,9},{9... | collective-permute-start | bytes 3268616 | tf_op jit(solution)/shard_map/ppermute | solution.py:432
  54.1 35.2 %collective-permute-start.16 = (bf16[2,224,1216]{2,1,0:T(8,128)(2,1)S(1)}, bf16[2,224,1216]{2,1,0:T(8,128)(2,1)}, u32[]{:S(2)}, u32[]{:S(2)}) collective-permute-start(bf16[2,224,1216]{2,1,0:T(8,128)(2,1)S(1)} %pad_maximum_fusion.refs_0_), channel_id=1, source_target_pairs={{0,4},{8,0},{16,8},{24,16},{28,24},{20,28},{12,20},{4,12},{1,5},{9... | collective-permute-start | bytes 3268616 | tf_op jit(solution)/shard_map/ppermute | solution.py:432
  89.3 42.5 %collective-permute-start.18 = (bf16[2,224,1216]{2,1,0:T(8,128)(2,1)}, bf16[2,224,1216]{2,1,0:T(8,128)(2,1)}, u32[]{:S(2)}, u32[]{:S(2)}) collective-permute-start(bf16[2,224,1216]{2,1,0:T(8,128)(2,1)} %collective-permute-done.15.refs_1_), channel_id=1, source_target_pairs={{0,8},{8,16},{16,24},{24,28},{28,20},{20,12},{12,4},{4,0},{1,9},{9... | collective-permute-start | bytes 3268616 | tf_op jit(solution)/shard_map/ppermute | solution.py:432
  89.4 42.4 %collective-permute-start.19 = (bf16[2,224,1216]{2,1,0:T(8,128)(2,1)}, bf16[2,224,1216]{2,1,0:T(8,128)(2,1)}, u32[]{:S(2)}, u32[]{:S(2)}) collective-permute-start(bf16[2,224,1216]{2,1,0:T(8,128)(2,1)} %collective-permute-done.16.refs_5_), channel_id=1, source_target_pairs={{0,4},{8,0},{16,8},{24,16},{28,24},{20,28},{12,20},{4,12},{1,5},{9... | collective-permute-start | bytes 3268616 | tf_op jit(solution)/shard_map/ppermute | solution.py:432
  98.9 30.2 %collective-permute-start.20 = (bf16[2,4,160,128]{3,2,1,0:T(8,128)(2,1)}, bf16[2,4,160,128]{3,2,1,0:T(8,128)(2,1)}, u32[]{:S(2)}, u32[]{:S(2)}) collective-permute-start(bf16[2,4,160,128]{3,2,1,0:T(8,128)(2,1)} %add_convert_fusion.5), channel_id=1, source_target_pairs={{0,16},{4,20},{8,24},{12,28},{1,17},{5,21},{9,25},{13,29},{2,18},{... | collective-permute-start | bytes 983048 | tf_op jit(solution)/shard_map/ppermute | solution.py:616
  104.6 36.8 %collective-permute-start.21 = (bf16[224,1216]{1,0:T(8,128)(2,1)}, bf16[224,1216]{1,0:T(8,128)(2,1)S(1)}, u32[]{:S(2)}, u32[]{:S(2)}) collective-permute-start(bf16[224,1216]{1,0:T(8,128)(2,1)} %bitcast.62), channel_id=1, source_target_pairs={{0,8},{8,16},{16,24},{24,28},{28,20},{20,12},{12,4},{4,0},{1,9},{9... | collective-permute-start | bytes 1634312 | tf_op jit(solution)/shard_map/ppermute | solution.py:432
  107.1 34.3 %collective-permute-start.22 = (bf16[224,1216]{1,0:T(8,128)(2,1)}, bf16[224,1216]{1,0:T(8,128)(2,1)S(1)}, u32[]{:S(2)}, u32[]{:S(2)}) collective-permute-start(bf16[224,1216]{1,0:T(8,128)(2,1)} %bitcast.63), channel_id=1, source_target_pairs={{0,4},{8,0},{16,8},{24,16},{28,24},{20,28},{12,20},{4,12},{1,5},{9... | collective-permute-start | bytes 1634312 | tf_op jit(solution)/shard_map/ppermute | solution.py:432
  131.8 32.6 %collective-permute-start.24 = (bf16[2,224,1216]{2,1,0:T(8,128)(2,1)}, bf16[2,224,1216]{2,1,0:T(8,128)(2,1)S(1)}, u32[]{:S(2)}, u32[]{:S(2)}) collective-permute-start(bf16[2,224,1216]{2,1,0:T(8,128)(2,1)} %collective-permute-done.18.refs_2_), channel_id=1, source_target_pairs={{0,8},{8,16},{16,24},{24,28},{28,20},{20,12},{12,4},{4,0},{1,9},{9... | collective-permute-start | bytes 3268616 | tf_op jit(solution)/shard_map/ppermute | solution.py:432
  135.7 28.7 %collective-permute-start.25 = (bf16[2,224,1216]{2,1,0:T(8,128)(2,1)}, bf16[2,224,1216]{2,1,0:T(8,128)(2,1)S(1)}, u32[]{:S(2)}, u32[]{:S(2)}) collective-permute-start(bf16[2,224,1216]{2,1,0:T(8,128)(2,1)} %collective-permute-done.19.refs_6_), channel_id=1, source_target_pairs={{0,4},{8,0},{16,8},{24,16},{28,24},{20,28},{12,20},{4,12},{1,5},{9... | collective-permute-start | bytes 3268616 | tf_op jit(solution)/shard_map/ppermute | solution.py:432
  166.0 22.8 %collective-permute-start.27 = (bf16[2,448,512]{2,1,0:T(8,128)(2,1)S(1)}, bf16[2,448,512]{2,1,0:T(8,128)(2,1)S(1)}, u32[]{:S(2)}, u32[]{:S(2)}) collective-permute-start(bf16[2,448,512]{2,1,0:T(8,128)(2,1)S(1)} %get-tuple-element.245), channel_id=1, source_target_pairs={{0,2},{1,3},{2,0},{3,1},{4,6},{5,7},{6,4},{7,5},{8,10},{9,11},{10,... | collective-permute-start | bytes 2752520 | tf_op jit(solution)/shard_map/ppermute | solution.py:52
  168.8 23.2 %collective-permute-start.31 = (bf16[2,112,1216]{2,1,0:T(8,128)(2,1)S(1)}, bf16[2,112,1216]{2,1,0:T(8,128)(2,1)S(1)}, u32[]{:S(2)}, u32[]{:S(2)}) collective-permute-start(bf16[2,112,1216]{2,1,0:T(8,128)(2,1)S(1)} %slice.111), channel_id=1, source_target_pairs={{0,8},{8,16},{16,24},{24,28},{28,20},{20,12},{12,4},{4,0},{1,9},{9... | collective-permute-start | bytes 1634312 | tf_op jit(solution)/shard_map/ppermute | solution.py:432
  172.0 24.9 %collective-permute-start.33 = (bf16[224,1216]{1,0:T(8,128)(2,1)S(1)}, bf16[224,1216]{1,0:T(8,128)(2,1)S(1)}, u32[]{:S(2)}, u32[]{:S(2)}) collective-permute-start(bf16[224,1216]{1,0:T(8,128)(2,1)S(1)} %collective-permute-done.21.refs_1_), channel_id=1, source_target_pairs={{0,8},{8,16},{16,24},{24,28},{28,20},{20,12},{12,4},{4,0},{1,9},{9... | collective-permute-start | bytes 1634312 | tf_op jit(solution)/shard_map/ppermute | solution.py:432
  174.4 25.4 %collective-permute-start.34 = (bf16[224,1216]{1,0:T(8,128)(2,1)S(1)}, bf16[224,1216]{1,0:T(8,128)(2,1)S(1)}, u32[]{:S(2)}, u32[]{:S(2)}) collective-permute-start(bf16[224,1216]{1,0:T(8,128)(2,1)S(1)} %collective-permute-done.22.refs_5_), channel_id=1, source_target_pairs={{0,4},{8,0},{16,8},{24,16},{28,24},{20,28},{12,20},{4,12},{1,5},{9... | collective-permute-start | bytes 1634312 | tf_op jit(solution)/shard_map/ppermute | solution.py:432
  190.5 24.7 %collective-permute-start.38 = (bf16[2,448,512]{2,1,0:T(8,128)(2,1)S(1)}, bf16[2,448,512]{2,1,0:T(8,128)(2,1)S(1)}, u32[]{:S(2)}, u32[]{:S(2)}) collective-permute-start(bf16[2,448,512]{2,1,0:T(8,128)(2,1)S(1)} %get-tuple-element.429.refs_0_), channel_id=1, source_target_pairs={{0,2},{1,3},{2,0},{3,1},{4,6},{5,7},{6,4},{7,5},{8,10},{9,11},{10,... | collective-permute-start | bytes 2752520 | tf_op jit(solution)/shard_map/ppermute | solution.py:52
  273.1 22.8 %collective-permute-start.46 = (bf16[2,456,512]{2,1,0:T(8,128)(2,1)S(1)}, bf16[2,456,512]{2,1,0:T(8,128)(2,1)S(1)}, u32[]{:S(2)}, u32[]{:S(2)}) collective-permute-start(bf16[2,456,512]{2,1,0:T(8,128)(2,1)S(1)} %get-tuple-element.286), channel_id=1, source_target_pairs={{0,2},{1,3},{2,0},{3,1},{4,6},{5,7},{6,4},{7,5},{8,10},{9,11},{10,... | collective-permute-start | bytes 2801672 | tf_op jit(solution)/shard_map/ppermute | solution.py:52
  320.1 27.1 %collective-permute-start.54 = (bf16[224,2432]{1,0:T(8,128)(2,1)}, bf16[224,2432]{1,0:T(8,128)(2,1)S(1)}, u32[]{:S(2)}, u32[]{:S(2)}) collective-permute-start(bf16[224,2432]{1,0:T(8,128)(2,1)} %get-tuple-element.304), channel_id=1, source_target_pairs={{0,8},{8,16},{16,24},{24,28},{28,20},{20,12},{12,4},{4,0},{1,9},{9... | collective-permute-start | bytes 3268616 | tf_op jit(solution)/shard_map/ppermute | solution.py:432
  321.9 26.1 %collective-permute-start.55 = (bf16[224,2432]{1,0:T(8,128)(2,1)S(1)}, bf16[224,2432]{1,0:T(8,128)(2,1)S(1)}, u32[]{:S(2)}, u32[]{:S(2)}) collective-permute-start(bf16[224,2432]{1,0:T(8,128)(2,1)S(1)} %get-tuple-element.305), channel_id=1, source_target_pairs={{0,4},{8,0},{16,8},{24,16},{28,24},{20,28},{12,20},{4,12},{1,5},{9... | collective-permute-start | bytes 3268616 | tf_op jit(solution)/shard_map/ppermute | solution.py:432
  329.1 24.7 %collective-permute-start.56 = (bf16[2,4,160,128]{3,2,1,0:T(8,128)(2,1)S(1)}, bf16[2,4,160,128]{3,2,1,0:T(8,128)(2,1)S(1)}, u32[]{:S(2)}, u32[]{:S(2)}) collective-permute-start(bf16[2,4,160,128]{3,2,1,0:T(8,128)(2,1)S(1)} %get-tuple-element.322), channel_id=1, source_target_pairs={{0,4},{4,0},{8,12},{12,8},{16,20},{20,16},{24,28},{28,24},{1,5},{5... | collective-permute-start | bytes 983048 | tf_op jit(solution)/shard_map/ppermute | solution.py:625
  370.4 29.1 %collective-permute-start.57 = (bf16[448,1024]{1,0:T(8,128)(2,1)}, bf16[448,1024]{1,0:T(8,128)(2,1)}, u32[]{:S(2)}, u32[]{:S(2)}) collective-permute-start(bf16[448,1024]{1,0:T(8,128)(2,1)} %get-tuple-element.335), channel_id=1, source_target_pairs={{0,1},{1,0},{2,3},{3,2},{4,5},{5,4},{6,7},{7,6},{8,9},{9,8},{10,11... | collective-permute-start | bytes 2752520 | tf_op jit(solution)/shard_map/ppermute | solution.py:52
  370.4 36.2 %collective-permute-start.62 = (bf16[448,1024]{1,0:T(8,128)(2,1)}, bf16[448,1024]{1,0:T(8,128)(2,1)}, u32[]{:S(2)}, u32[]{:S(2)}) collective-permute-start(bf16[448,1024]{1,0:T(8,128)(2,1)} %copy-done.38), channel_id=1, source_target_pairs={{0,1},{1,0},{2,3},{3,2},{4,5},{5,4},{6,7},{7,6},{8,9},{9,8},{10,11... | collective-permute-start | bytes 2752520 | tf_op jit(solution)/shard_map/ppermute | solution.py:52
  376.8 34.1 %collective-permute-start.64 = (bf16[224,2432]{1,0:T(8,128)(2,1)S(1)}, bf16[224,2432]{1,0:T(8,128)(2,1)S(1)}, u32[]{:S(2)}, u32[]{:S(2)}) collective-permute-start(bf16[224,2432]{1,0:T(8,128)(2,1)S(1)} %get-tuple-element.340), channel_id=1, source_target_pairs={{0,8},{8,16},{16,24},{24,28},{28,20},{20,12},{12,4},{4,0},{1,9},{9... | collective-permute-start | bytes 3268616 | tf_op jit(solution)/shard_map/ppermute | solution.py:432
  379.8 31.1 %collective-permute-start.65 = (bf16[224,2432]{1,0:T(8,128)(2,1)S(1)}, bf16[224,2432]{1,0:T(8,128)(2,1)S(1)}, u32[]{:S(2)}, u32[]{:S(2)}) collective-permute-start(bf16[224,2432]{1,0:T(8,128)(2,1)S(1)} %get-tuple-element.341), channel_id=1, source_target_pairs={{0,4},{8,0},{16,8},{24,16},{28,24},{20,28},{12,20},{4,12},{1,5},{9... | collective-permute-start | bytes 3268616 | tf_op jit(solution)/shard_map/ppermute | solution.py:432
  409.9 23.3 %collective-permute-start.63 = (bf16[2,448,512]{2,1,0:T(8,128)(2,1)S(1)}, bf16[2,448,512]{2,1,0:T(8,128)(2,1)S(1)}, u32[]{:S(2)}, u32[]{:S(2)}) collective-permute-start(bf16[2,448,512]{2,1,0:T(8,128)(2,1)S(1)} %get-tuple-element.359), channel_id=1, source_target_pairs={{0,2},{1,3},{2,0},{3,1},{4,6},{5,7},{6,4},{7,5},{8,10},{9,11},{10,... | collective-permute-start | bytes 2752520 | tf_op jit(solution)/shard_map/ppermute | solution.py:52
  413.5 38.8 %collective-permute-start.70 = (bf16[2,456,512]{2,1,0:T(8,128)(2,1)S(1)}, bf16[2,456,512]{2,1,0:T(8,128)(2,1)S(1)}, u32[]{:S(2)}, u32[]{:S(2)}) collective-permute-start(bf16[2,456,512]{2,1,0:T(8,128)(2,1)S(1)} %get-tuple-element.368), channel_id=1, source_target_pairs={{0,2},{1,3},{2,0},{3,1},{4,6},{5,7},{6,4},{7,5},{8,10},{9,11},{10,... | collective-permute-start | bytes 2801672 | tf_op jit(solution)/shard_map/ppermute | solution.py:52
  424.8 27.6 %collective-permute-start.82 = (bf16[224,1216]{1,0:T(8,128)(2,1)S(1)}, bf16[224,1216]{1,0:T(8,128)(2,1)S(1)}, u32[]{:S(2)}, u32[]{:S(2)}) collective-permute-start(bf16[224,1216]{1,0:T(8,128)(2,1)S(1)} %copy-done.40), channel_id=1, source_target_pairs={{0,8},{8,16},{16,24},{24,28},{28,20},{20,12},{12,4},{4,0},{1,9},{9... | collective-permute-start | bytes 1634312 | tf_op jit(solution)/shard_map/ppermute | solution.py:432
  433.2 24.5 %collective-permute-start.83 = (bf16[224,1216]{1,0:T(8,128)(2,1)S(1)}, bf16[224,1216]{1,0:T(8,128)(2,1)S(1)}, u32[]{:S(2)}, u32[]{:S(2)}) collective-permute-start(bf16[224,1216]{1,0:T(8,128)(2,1)S(1)} %get-tuple-element.346), channel_id=1, source_target_pairs={{0,4},{8,0},{16,8},{24,16},{28,24},{20,28},{12,20},{4,12},{1,5},{9... | collective-permute-start | bytes 1634312 | tf_op jit(solution)/shard_map/ppermute | solution.py:432
  436.2 47.9 %collective-permute-start.80 = (bf16[224,2432]{1,0:T(8,128)(2,1)S(1)}, bf16[224,2432]{1,0:T(8,128)(2,1)S(1)}, u32[]{:S(2)}, u32[]{:S(2)}) collective-permute-start(bf16[224,2432]{1,0:T(8,128)(2,1)S(1)} %get-tuple-element.363), channel_id=1, source_target_pairs={{0,8},{8,16},{16,24},{24,28},{28,20},{20,12},{12,4},{4,0},{1,9},{9... | collective-permute-start | bytes 3268616 | tf_op jit(solution)/shard_map/ppermute | solution.py:432
  436.8 47.3 %collective-permute-start.81 = (bf16[224,2432]{1,0:T(8,128)(2,1)S(1)}, bf16[224,2432]{1,0:T(8,128)(2,1)S(1)}, u32[]{:S(2)}, u32[]{:S(2)}) collective-permute-start(bf16[224,2432]{1,0:T(8,128)(2,1)S(1)} %get-tuple-element.364), channel_id=1, source_target_pairs={{0,4},{8,0},{16,8},{24,16},{28,24},{20,28},{12,20},{4,12},{1,5},{9... | collective-permute-start | bytes 3268616 | tf_op jit(solution)/shard_map/ppermute | solution.py:432
  452.4 26.9 %collective-permute-start.76 = (bf16[224,1024]{1,0:T(8,128)(2,1)S(1)}, bf16[224,1024]{1,0:T(8,128)(2,1)S(1)}, u32[]{:S(2)}, u32[]{:S(2)}) collective-permute-start(bf16[224,1024]{1,0:T(8,128)(2,1)S(1)} %get-tuple-element.383), channel_id=1, source_target_pairs={{0,8},{8,16},{16,24},{24,28},{28,20},{20,12},{12,4},{4,0},{1,9},{9... | collective-permute-start | bytes 1376264 | tf_op jit(solution)/shard_map/ppermute | solution.py:432
  452.4 27.2 %collective-permute-start.77 = (bf16[224,1024]{1,0:T(8,128)(2,1)S(1)}, bf16[224,1024]{1,0:T(8,128)(2,1)S(1)}, u32[]{:S(2)}, u32[]{:S(2)}) collective-permute-start(bf16[224,1024]{1,0:T(8,128)(2,1)S(1)} %get-tuple-element.384), channel_id=1, source_target_pairs={{0,4},{8,0},{16,8},{24,16},{28,24},{20,28},{12,20},{4,12},{1,5},{9... | collective-permute-start | bytes 1376264 | tf_op jit(solution)/shard_map/ppermute | solution.py:432
  (120 other events, 1549.7 us)

commit v7 on v6

--- a/solution.py
+++ b/solution.py
@@ -1015,8 +1015,6 @@
     fence(attn_ring.here())
     attn_ring.advance(*token)
     fence(attn_ring.sent)
-    layer_out = (resid + scatter_out.sums(*token)).astype(BF)
-    fence(layer_out)
     d_norm, inner = scatter_one.sums(*token)
     value = hidden.astype(F32)
     gain_one_part = jnp.sum(value * inv_one * d_norm, (0, 2))
@@ -1024,6 +1022,8 @@
         d_resid + inv_one * gain_one * d_norm - value * (inv_one * inv_one * inner / D)
     )
     fence(gain_one_part, grad_input)
+    layer_out = (resid + scatter_out.sums(*token)).astype(BF)
+    fence(layer_out)
     gain_grads = ctx_total(jnp.stack([gain_one_part, gain_two_part]) + token[0][:1, :1])
     fence(attn_ring.here())
     attn_ring.advance(*token)

time: 508 us -> 504 us (level)
    ppermute x48, waiting for transfers between devices: 117 us -> 126 us  [hop(): return lax.ppermute(value, 'ctx', pairs)]
    ppermute x27, waiting for transfers between devices: 41.3 us -> 33.4 us  [swap(): return lax.ppermute(value, 'wt', [(i, i ^ bit) for i in range(count)])]
    unnamed x146 -> x150, local copies, waits for them, and re-layouts: 23.4 us -> 23.4 us
  transfers between devices with their start and end apart: 84 -> 84, of which waited for: 35 -> 36; matrix products, arithmetic and copies ran while one was open for 9% -> 9% of each run, Pallas kernels for 19% -> 19%
where the time goes in v7:
time: 504 us; the launch traced here: 495 us
  waiting for transfers between devices  220 us (44%)
  Pallas kernels  109 us (22%)
  starting transfers between devices  82.3 us (16%)
  matrix products  32.5 us (6%)
  local copies, waits for them, and re-layouts  29.9 us (6%)
  other arithmetic  18.7 us (4%)
    ppermute x48, waiting for transfers between devices, hop(): return lax.ppermute(value, 'ctx', pairs)  126 us
    ppermute x48, starting transfers between devices, hop(): return lax.ppermute(value, 'ctx', pairs)  56.2 us
    ppermute x27, waiting for transfers between devices, swap(): return lax.ppermute(value, 'wt', [(i, i ^ bit) for i in range(count)])  33.4 us
    dot_general x5, matrix products, mm_tn(): lax.dot_general(left, right, (((0,), (0,)), ((), ())), preferred_element_...  32.5 us
    ppermute x4, waiting for transfers between devices, shifted(): return lax.ppermute(value, 'ctx', pairs)  31.3 us
    pallas_call x4, Pallas kernels, projected(): pl.pallas_call(kernel, name=name, grid_spec=pltpu.PrefetchScalarGridSpec(...  27.3 us
    ppermute x2, waiting for transfers between devices, __init__(): self.other = lax.ppermute(value, 'ctx', [(i, i ^ 1) for i in range(count)])  27 us
    unnamed x150, local copies, waits for them, and re-layouts  23.4 us
  transfers between devices with their start and end apart: 84, of which 36 were waited for; matrix products, arithmetic and copies ran while one was open for 9% of the time, Pallas kernels for 19%

profile of v7, /device:TPU:0, one launch (start us, length us, event | category | flops | bytes accessed | tf_op | source)
XLA Modules:
  0.0 495.0 jit_solution(2443897442104279260)
XLA Ops:
  9.7 8.5 %collective-permute-done.refs_1_ = bf16[224,1024]{1,0:T(8,128)(2,1)S(1)} collective-permute-done((bf16[224,1024]{1,0:T(8,128)(2,1)S(1)}, bf16[224,1024]{1,0:T(8,128)(2,1)S(1)}, u32[]{:S(2)}, u32[]{:S(2)}) %collective-permute-start) | collective-permute-done | bytes 458784 | tf_op jit(solution)/shard_map/ppermute | solution.py:432
  23.1 7.9 %collective-permute-done.2.refs_2_ = bf16[224,1024]{1,0:T(8,128)(2,1)} collective-permute-done((bf16[224,1024]{1,0:T(8,128)(2,1)S(1)}, bf16[224,1024]{1,0:T(8,128)(2,1)}, u32[]{:S(2)}, u32[]{:S(2)}) %collective-permute-start.2) | collective-permute-done | bytes 458784 | tf_op jit(solution)/shard_map/ppermute | solution.py:432
  36.2 9.3 %collective-permute-done.4.refs_3_ = bf16[224,1024]{1,0:T(8,128)(2,1)S(1)} collective-permute-done((bf16[224,1024]{1,0:T(8,128)(2,1)}, bf16[224,1024]{1,0:T(8,128)(2,1)S(1)}, u32[]{:S(2)}, u32[]{:S(2)}) %collective-permute-start.4) | collective-permute-done | bytes 458784 | tf_op jit(solution)/shard_map/ppermute | solution.py:432
  66.6 21.3 %collective-permute-done.14 = bf16[2,4,160,128]{3,2,1,0:T(8,128)(2,1)S(1)} collective-permute-done((bf16[2,4,160,128]{3,2,1,0:T(8,128)(2,1)S(1)}, bf16[2,4,160,128]{3,2,1,0:T(8,128)(2,1)S(1)}, u32[]{:S(2)}, u32[]{:S(2)}) %collective-permute-start.14) | collective-permute-done | bytes 327712 | tf_op jit(solution)/shard_map/ppermute | solution.py:625
  91.4 6.0 %collective-permute-done.17 = bf16[2,4,160,128]{3,2,1,0:T(8,128)(2,1)S(1)} collective-permute-done((bf16[2,4,160,128]{3,2,1,0:T(8,128)(2,1)S(1)}, bf16[2,4,160,128]{3,2,1,0:T(8,128)(2,1)S(1)}, u32[]{:S(2)}, u32[]{:S(2)}) %collective-permute-start.17) | collective-permute-done | bytes 327712 | tf_op jit(solution)/shard_map/ppermute | solution.py:616
  98.9 5.6 %collective-permute-start.20 = (bf16[2,4,160,128]{3,2,1,0:T(8,128)(2,1)}, bf16[2,4,160,128]{3,2,1,0:T(8,128)(2,1)}, u32[]{:S(2)}, u32[]{:S(2)}) collective-permute-start(bf16[2,4,160,128]{3,2,1,0:T(8,128)(2,1)} %add_convert_fusion.5), channel_id=1, source_target_pairs={{0,16},{4,20},{8,24},{12,28},{1,17},{5,21},{9,25},{13,29},{2,18},{... | collective-permute-start | bytes 983048 | tf_op jit(solution)/shard_map/ppermute | solution.py:616
  108.5 20.7 %collective-permute-done.20 = bf16[2,4,160,128]{3,2,1,0:T(8,128)(2,1)} collective-permute-done((bf16[2,4,160,128]{3,2,1,0:T(8,128)(2,1)}, bf16[2,4,160,128]{3,2,1,0:T(8,128)(2,1)}, u32[]{:S(2)}, u32[]{:S(2)}) %collective-permute-start.20) | collective-permute-done | bytes 327712 | tf_op jit(solution)/shard_map/ppermute | solution.py:616
  131.8 3.9 collective-permute-start.24
  135.7 4.8 attend.1
  141.4 3.7 out_proj.1
  148.4 16.1 %collective-permute-done.24.refs_3_ = bf16[2,224,1216]{2,1,0:T(8,128)(2,1)S(1)} collective-permute-done((bf16[2,224,1216]{2,1,0:T(8,128)(2,1)}, bf16[2,224,1216]{2,1,0:T(8,128)(2,1)S(1)}, u32[]{:S(2)}, u32[]{:S(2)}) %collective-permute-start.24) | collective-permute-done | bytes 1089568 | tf_op jit(solution)/shard_map/ppermute | solution.py:432
  174.4 14.4 %collective-permute-done.27 = bf16[2,448,512]{2,1,0:T(8,128)(2,1)S(1)} collective-permute-done((bf16[2,448,512]{2,1,0:T(8,128)(2,1)S(1)}, bf16[2,448,512]{2,1,0:T(8,128)(2,1)S(1)}, u32[]{:S(2)}, u32[]{:S(2)}) %collective-permute-start.27) | collective-permute-done | bytes 917536 | tf_op jit(solution)/shard_map/ppermute | solution.py:52
  192.0 4.9 collective-permute-done.33.refs_2_
  204.9 9.1 %collective-permute-done.35.refs_3_ = bf16[224,1216]{1,0:T(8,128)(2,1)S(1)} collective-permute-done((bf16[224,1216]{1,0:T(8,128)(2,1)S(1)}, bf16[224,1216]{1,0:T(8,128)(2,1)S(1)}, u32[]{:S(2)}, u32[]{:S(2)}) %collective-permute-start.35) | collective-permute-done | bytes 544800 | tf_op jit(solution)/shard_map/ppermute | solution.py:432
  219.8 6.5 %fusion.1 = f32[1216,1024]{1,0:T(8,128)} fusion(bf16[1792,1024]{1,0:T(8,128)(2,1)S(1)} %get-tuple-element.267.refs_0_, bf16[2,1792,1216]{2,1,0:T(8,128)(2,1)S(1)} %assemble.4.weight_ref), kind=kOutput, calls=%fused_computation.8 | convolution fusion | flops 4462739456 | bytes 13238272 | tf_op jit(solution)/shard_map/dot_general | solution.py:30
  226.3 8.8 %multiply_convert_fusion.2 = (bf16[1216,1024]{1,0:T(8,128)(2,1)S(1)}, f32[1216,1024]{1,0:T(8,128)}) fusion(f32[1216,1024]{1,0:T(8,128)} %fusion.1, bf16[1792,1024]{1,0:T(8,128)(2,1)S(1)} %get-tuple-element.267.refs_0_, bf16[2,1792,1216]{2,1,0:T(8,128)(2,1)S(1)} %assemble.4.weight_ref), kind=kOutput, calls=%fused_computation.3 | convolution fusion | flops 4470210560 | bytes 20709376 | tf_op jit(solution)/shard_map/dot_general | solution.py:30
  236.6 12.9 %add_reduce_fusion = (f32[1024]{0:T(1024)S(1)}, bf16[1216,1024]{1,0:T(8,128)(2,1)}, bf16[1216,1024]{1,0:T(8,128)(2,1)}) fusion(f32[1216,1024]{1,0:T(8,128)} %get-tuple-element.443, f32[1216,1024]{1,0:T(8,128)} %fusion.1, bf16[1792,1216]{1,0:T(8,128)(2,1)S(1)} %assemble.5.weight_ref, bf16[1792,1024]{1,0:T(8,128)(2,1)S(1)} %gather.2.refs_0_), kind=kOutput, calls=%fused_computation | convolution fusion | flops 4486396928 | bytes 22974464 | tf_op jit(solution)/shard_map/dot_general | solution.py:30
  252.9 11.9 %ffn_back.1 = (bf16[456,1024]{1,0:T(8,128)(2,1)S(1)}, bf16[456,1024]{1,0:T(8,128)(2,1)S(1)}, bf16[2,448,1024]{2,1,0:T(8,128)(2,1)S(1)}) custom-call(s32[9]{0:T(128)S(1)} %fusion.20.index_ref, bf16[2,1792,1216]{2,1,0:T(8,128)(2,1)S(1)} %assemble.4.weight_ref, bf16[1216,1024]{1,0:T(8,128)(2,1)S(1)} %copy-done.45, bf16[1216,1024]{1,0:T(8,128)(2,1)S(1)} %copy-done.43, ...), custom_call_target="tpu_custom_call" | custom-call | flops 8925478912 | bytes 8388608 | tf_op jit(solution)/shard_map/ffn_back/pallas_call | solution.py:155
  265.3 5.6 %down_grad.1.refs_0_.refs_2_.refs_3_.own = bf16[1792,1216]{1,0:T(8,128)(2,1)S(1)} custom-call(bf16[1792,1024]{1,0:T(8,128)(2,1)S(1)} %copy-done.11, bf16[1216,1024]{1,0:T(8,128)(2,1)S(1)} %get-tuple-element.307.refs_1_.refs_0_), custom_call_target="tpu_custom_call" | custom-call | flops 4462739456 | bytes 4358144 | tf_op jit(solution)/shard_map/down_grad/pallas_call | solution.py:513
  279.4 10.6 %gate_up_grad.1.refs_0_.refs_2_.refs_3_.own = bf16[1792,2432]{1,0:T(8,128)(2,1)S(1)} custom-call(bf16[1792,1024]{1,0:T(8,128)(2,1)S(1)} %copy-done.37, bf16[1216,1024]{1,0:T(8,128)(2,1)S(1)} %copy-done.46, bf16[1216,1024]{1,0:T(8,128)(2,1)S(1)} %copy-done.44), custom_call_target="tpu_custom_call" | custom-call | flops 8925478912 | bytes 8716288 | tf_op jit(solution)/shard_map/gate_up_grad/pallas_call | solution.py:513
  300.8 5.3 %collective-permute-done.47.refs_0_ = bf16[112,2432]{1,0:T(8,128)(2,1)S(1)} collective-permute-done((bf16[112,2432]{1,0:T(8,128)(2,1)S(1)}, bf16[112,2432]{1,0:T(8,128)(2,1)S(1)}, u32[]{:S(2)}, u32[]{:S(2)}) %collective-permute-start.47) | collective-permute-done | bytes 544800 | tf_op jit(solution)/shard_map/ppermute | solution.py:432
  309.6 7.3 %ffn_out.1 = (bf16[448,1024]{1,0:T(8,128)(2,1)}, bf16[448,1024]{1,0:T(8,128)(2,1)S(1)}, bf16[2,448,1024]{2,1,0:T(8,128)(2,1)S(1)}) custom-call(s32[9]{0:T(128)S(1)} %fusion.20.index_ref, bf16[1792,1216]{1,0:T(8,128)(2,1)S(1)} %bitcast.61, bf16[1216,1024]{1,0:T(8,128)(2,1)S(1)} %get-tuple-element.307.refs_1_.refs_0_), custom_call_target="tpu_custom_call" | custom-call | flops 4462739456 | bytes 8388608 | tf_op jit(solution)/shard_map/ffn_out/pallas_call | solution.py:155
  329.4 17.8 %collective-permute-done.54.refs_0_ = bf16[224,2432]{1,0:T(8,128)(2,1)S(1)} collective-permute-done((bf16[224,2432]{1,0:T(8,128)(2,1)}, bf16[224,2432]{1,0:T(8,128)(2,1)S(1)}, u32[]{:S(2)}, u32[]{:S(2)}) %collective-permute-start.54) | collective-permute-done | bytes 1089568 | tf_op jit(solution)/shard_map/ppermute | solution.py:432
  348.0 5.8 %collective-permute-done.56 = bf16[2,4,160,128]{3,2,1,0:T(8,128)(2,1)S(1)} collective-permute-done((bf16[2,4,160,128]{3,2,1,0:T(8,128)(2,1)S(1)}, bf16[2,4,160,128]{3,2,1,0:T(8,128)(2,1)S(1)}, u32[]{:S(2)}, u32[]{:S(2)}) %collective-permute-start.56) | collective-permute-done | bytes 327712 | tf_op jit(solution)/shard_map/ppermute | solution.py:625
  357.9 7.8 %local.1 = (bf16[64,1024]{1,0:T(8,128)(2,1)S(1)}, f32[64,1024]{1,0:T(8,128)S(1)}, f32[448,1024]{1,0:T(8,128)S(1)}) custom-call(bf16[576,1024]{1,0:T(8,128)(2,1)S(1)} %fusion.9.key_ref.value_ref.query_ref.refs_0_.refs_1_, bf16[576,1024]{1,0:T(8,128)(2,1)S(1)} %fusion.9.key_ref.value_ref.query_ref.refs_0_.refs_1_, ...), custom_call_target="tpu_custom_call" | custom-call | flops 2147483648 | bytes 4194304 | tf_op jit(solution)/shard_map/local/pallas_call | solution.py:970
  385.1 4.6 collective-permute-done.61
  394.1 4.5 qkv_back.1
  399.2 5.9 %attn_grad.1.refs_0_.refs_2_.refs_3_.own = bf16[1792,1024]{1,0:T(8,128)(2,1)S(1)} custom-call(bf16[1792,1024]{1,0:T(8,128)(2,1)S(1)} %copy-done.35, bf16[1792,1024]{1,0:T(8,128)(2,1)S(1)} %copy-done.13, bf16[576,1024]{1,0:T(8,128)(2,1)S(1)} %later.1.refs_0_.refs_2_, bf16[448,1024]{1,0:T(8,128)(2,1)S(1)} %copy-done.22), custom_call_target="tpu_custom_call" | custom-call | flops 3758096384 | bytes 3670016 | tf_op jit(solution)/shard_map/attn_grad/pallas_call | solution.py:513
  415.3 4.7 collective-permute-done.68.refs_0_
  425.7 9.8 %collective-permute-done.74.refs_0_ = bf16[224,1024]{1,0:T(8,128)(2,1)S(1)} collective-permute-done((bf16[224,1024]{1,0:T(8,128)(2,1)S(1)}, bf16[224,1024]{1,0:T(8,128)(2,1)S(1)}, u32[]{:S(2)}, u32[]{:S(2)}) %collective-permute-start.74) | collective-permute-done | bytes 458784 | tf_op jit(solution)/shard_map/ppermute | solution.py:432
  441.1 13.5 %collective-permute-done.63 = bf16[2,448,512]{2,1,0:T(8,128)(2,1)S(1)} collective-permute-done((bf16[2,448,512]{2,1,0:T(8,128)(2,1)S(1)}, bf16[2,448,512]{2,1,0:T(8,128)(2,1)S(1)}, u32[]{:S(2)}, u32[]{:S(2)}) %collective-permute-start.63) | collective-permute-done | bytes 917536 | tf_op jit(solution)/shard_map/ppermute | solution.py:52
  462.1 15.4 %collective-permute-done.76.refs_0_ = bf16[224,1024]{1,0:T(8,128)(2,1)S(1)} collective-permute-done((bf16[224,1024]{1,0:T(8,128)(2,1)S(1)}, bf16[224,1024]{1,0:T(8,128)(2,1)S(1)}, u32[]{:S(2)}, u32[]{:S(2)}) %collective-permute-start.76) | collective-permute-done | bytes 458784 | tf_op jit(solution)/shard_map/ppermute | solution.py:432
  (376 shorter events, 197.9 us)
Async XLA Ops:
  7.7 24.6 %collective-permute-start.7 = (bf16[2,448,512]{2,1,0:T(8,128)(2,1)}, bf16[2,448,512]{2,1,0:T(8,128)(2,1)}, u32[]{:S(2)}, u32[]{:S(2)}) collective-permute-start(bf16[2,448,512]{2,1,0:T(8,128)(2,1)} %bitcast.57), channel_id=1, source_target_pairs={{0,2},{1,3},{2,0},{3,1},{4,6},{5,7},{6,4},{7,5},{8,10},{9,11},{10,... | collective-permute-start | bytes 2752520 | tf_op jit(solution)/shard_map/ppermute | solution.py:52
  21.7 29.6 %collective-permute-start.6 = (bf16[2,448,512]{2,1,0:T(8,128)(2,1)}, bf16[2,448,512]{2,1,0:T(8,128)(2,1)}, u32[]{:S(2)}, u32[]{:S(2)}) collective-permute-start(bf16[2,448,512]{2,1,0:T(8,128)(2,1)} %bitcast.58), channel_id=1, source_target_pairs={{0,1},{1,0},{2,3},{3,2},{4,5},{5,4},{6,7},{7,6},{8,9},{9,8},{10,11... | collective-permute-start | bytes 2752520 | tf_op jit(solution)/shard_map/ppermute | solution.py:52
  52.5 36.7 %collective-permute-start.15 = (bf16[2,224,1216]{2,1,0:T(8,128)(2,1)S(1)}, bf16[2,224,1216]{2,1,0:T(8,128)(2,1)}, u32[]{:S(2)}, u32[]{:S(2)}) collective-permute-start(bf16[2,224,1216]{2,1,0:T(8,128)(2,1)S(1)} %pad_maximum_fusion.refs_0_), channel_id=1, source_target_pairs={{0,8},{8,16},{16,24},{24,28},{28,20},{20,12},{12,4},{4,0},{1,9},{9... | collective-permute-start | bytes 3268616 | tf_op jit(solution)/shard_map/ppermute | solution.py:432
  54.1 35.2 %collective-permute-start.16 = (bf16[2,224,1216]{2,1,0:T(8,128)(2,1)S(1)}, bf16[2,224,1216]{2,1,0:T(8,128)(2,1)}, u32[]{:S(2)}, u32[]{:S(2)}) collective-permute-start(bf16[2,224,1216]{2,1,0:T(8,128)(2,1)S(1)} %pad_maximum_fusion.refs_0_), channel_id=1, source_target_pairs={{0,4},{8,0},{16,8},{24,16},{28,24},{20,28},{12,20},{4,12},{1,5},{9... | collective-permute-start | bytes 3268616 | tf_op jit(solution)/shard_map/ppermute | solution.py:432
  89.3 42.5 %collective-permute-start.18 = (bf16[2,224,1216]{2,1,0:T(8,128)(2,1)}, bf16[2,224,1216]{2,1,0:T(8,128)(2,1)}, u32[]{:S(2)}, u32[]{:S(2)}) collective-permute-start(bf16[2,224,1216]{2,1,0:T(8,128)(2,1)} %collective-permute-done.15.refs_1_), channel_id=1, source_target_pairs={{0,8},{8,16},{16,24},{24,28},{28,20},{20,12},{12,4},{4,0},{1,9},{9... | collective-permute-start | bytes 3268616 | tf_op jit(solution)/shard_map/ppermute | solution.py:432
  89.4 42.4 %collective-permute-start.19 = (bf16[2,224,1216]{2,1,0:T(8,128)(2,1)}, bf16[2,224,1216]{2,1,0:T(8,128)(2,1)}, u32[]{:S(2)}, u32[]{:S(2)}) collective-permute-start(bf16[2,224,1216]{2,1,0:T(8,128)(2,1)} %collective-permute-done.16.refs_5_), channel_id=1, source_target_pairs={{0,4},{8,0},{16,8},{24,16},{28,24},{20,28},{12,20},{4,12},{1,5},{9... | collective-permute-start | bytes 3268616 | tf_op jit(solution)/shard_map/ppermute | solution.py:432
  98.9 30.2 %collective-permute-start.20 = (bf16[2,4,160,128]{3,2,1,0:T(8,128)(2,1)}, bf16[2,4,160,128]{3,2,1,0:T(8,128)(2,1)}, u32[]{:S(2)}, u32[]{:S(2)}) collective-permute-start(bf16[2,4,160,128]{3,2,1,0:T(8,128)(2,1)} %add_convert_fusion.5), channel_id=1, source_target_pairs={{0,16},{4,20},{8,24},{12,28},{1,17},{5,21},{9,25},{13,29},{2,18},{... | collective-permute-start | bytes 983048 | tf_op jit(solution)/shard_map/ppermute | solution.py:616
  104.6 36.8 %collective-permute-start.21 = (bf16[224,1216]{1,0:T(8,128)(2,1)}, bf16[224,1216]{1,0:T(8,128)(2,1)S(1)}, u32[]{:S(2)}, u32[]{:S(2)}) collective-permute-start(bf16[224,1216]{1,0:T(8,128)(2,1)} %bitcast.62), channel_id=1, source_target_pairs={{0,8},{8,16},{16,24},{24,28},{28,20},{20,12},{12,4},{4,0},{1,9},{9... | collective-permute-start | bytes 1634312 | tf_op jit(solution)/shard_map/ppermute | solution.py:432
  107.1 34.3 %collective-permute-start.22 = (bf16[224,1216]{1,0:T(8,128)(2,1)}, bf16[224,1216]{1,0:T(8,128)(2,1)S(1)}, u32[]{:S(2)}, u32[]{:S(2)}) collective-permute-start(bf16[224,1216]{1,0:T(8,128)(2,1)} %bitcast.63), channel_id=1, source_target_pairs={{0,4},{8,0},{16,8},{24,16},{28,24},{20,28},{12,20},{4,12},{1,5},{9... | collective-permute-start | bytes 1634312 | tf_op jit(solution)/shard_map/ppermute | solution.py:432
  131.8 32.6 %collective-permute-start.24 = (bf16[2,224,1216]{2,1,0:T(8,128)(2,1)}, bf16[2,224,1216]{2,1,0:T(8,128)(2,1)S(1)}, u32[]{:S(2)}, u32[]{:S(2)}) collective-permute-start(bf16[2,224,1216]{2,1,0:T(8,128)(2,1)} %collective-permute-done.18.refs_2_), channel_id=1, source_target_pairs={{0,8},{8,16},{16,24},{24,28},{28,20},{20,12},{12,4},{4,0},{1,9},{9... | collective-permute-start | bytes 3268616 | tf_op jit(solution)/shard_map/ppermute | solution.py:432
  135.7 28.7 %collective-permute-start.25 = (bf16[2,224,1216]{2,1,0:T(8,128)(2,1)}, bf16[2,224,1216]{2,1,0:T(8,128)(2,1)S(1)}, u32[]{:S(2)}, u32[]{:S(2)}) collective-permute-start(bf16[2,224,1216]{2,1,0:T(8,128)(2,1)} %collective-permute-done.19.refs_6_), channel_id=1, source_target_pairs={{0,4},{8,0},{16,8},{24,16},{28,24},{20,28},{12,20},{4,12},{1,5},{9... | collective-permute-start | bytes 3268616 | tf_op jit(solution)/shard_map/ppermute | solution.py:432
  166.0 22.8 %collective-permute-start.27 = (bf16[2,448,512]{2,1,0:T(8,128)(2,1)S(1)}, bf16[2,448,512]{2,1,0:T(8,128)(2,1)S(1)}, u32[]{:S(2)}, u32[]{:S(2)}) collective-permute-start(bf16[2,448,512]{2,1,0:T(8,128)(2,1)S(1)} %get-tuple-element.245), channel_id=1, source_target_pairs={{0,2},{1,3},{2,0},{3,1},{4,6},{5,7},{6,4},{7,5},{8,10},{9,11},{10,... | collective-permute-start | bytes 2752520 | tf_op jit(solution)/shard_map/ppermute | solution.py:52
  168.8 23.2 %collective-permute-start.31 = (bf16[2,112,1216]{2,1,0:T(8,128)(2,1)S(1)}, bf16[2,112,1216]{2,1,0:T(8,128)(2,1)S(1)}, u32[]{:S(2)}, u32[]{:S(2)}) collective-permute-start(bf16[2,112,1216]{2,1,0:T(8,128)(2,1)S(1)} %slice.111), channel_id=1, source_target_pairs={{0,8},{8,16},{16,24},{24,28},{28,20},{20,12},{12,4},{4,0},{1,9},{9... | collective-permute-start | bytes 1634312 | tf_op jit(solution)/shard_map/ppermute | solution.py:432
  172.0 24.9 %collective-permute-start.33 = (bf16[224,1216]{1,0:T(8,128)(2,1)S(1)}, bf16[224,1216]{1,0:T(8,128)(2,1)S(1)}, u32[]{:S(2)}, u32[]{:S(2)}) collective-permute-start(bf16[224,1216]{1,0:T(8,128)(2,1)S(1)} %collective-permute-done.21.refs_1_), channel_id=1, source_target_pairs={{0,8},{8,16},{16,24},{24,28},{28,20},{20,12},{12,4},{4,0},{1,9},{9... | collective-permute-start | bytes 1634312 | tf_op jit(solution)/shard_map/ppermute | solution.py:432
  174.4 25.4 %collective-permute-start.34 = (bf16[224,1216]{1,0:T(8,128)(2,1)S(1)}, bf16[224,1216]{1,0:T(8,128)(2,1)S(1)}, u32[]{:S(2)}, u32[]{:S(2)}) collective-permute-start(bf16[224,1216]{1,0:T(8,128)(2,1)S(1)} %collective-permute-done.22.refs_5_), channel_id=1, source_target_pairs={{0,4},{8,0},{16,8},{24,16},{28,24},{20,28},{12,20},{4,12},{1,5},{9... | collective-permute-start | bytes 1634312 | tf_op jit(solution)/shard_map/ppermute | solution.py:432
  190.5 24.7 %collective-permute-start.38 = (bf16[2,448,512]{2,1,0:T(8,128)(2,1)S(1)}, bf16[2,448,512]{2,1,0:T(8,128)(2,1)S(1)}, u32[]{:S(2)}, u32[]{:S(2)}) collective-permute-start(bf16[2,448,512]{2,1,0:T(8,128)(2,1)S(1)} %get-tuple-element.429.refs_0_), channel_id=1, source_target_pairs={{0,2},{1,3},{2,0},{3,1},{4,6},{5,7},{6,4},{7,5},{8,10},{9,11},{10,... | collective-permute-start | bytes 2752520 | tf_op jit(solution)/shard_map/ppermute | solution.py:52
  273.1 22.8 %collective-permute-start.46 = (bf16[2,456,512]{2,1,0:T(8,128)(2,1)S(1)}, bf16[2,456,512]{2,1,0:T(8,128)(2,1)S(1)}, u32[]{:S(2)}, u32[]{:S(2)}) collective-permute-start(bf16[2,456,512]{2,1,0:T(8,128)(2,1)S(1)} %get-tuple-element.286), channel_id=1, source_target_pairs={{0,2},{1,3},{2,0},{3,1},{4,6},{5,7},{6,4},{7,5},{8,10},{9,11},{10,... | collective-permute-start | bytes 2801672 | tf_op jit(solution)/shard_map/ppermute | solution.py:52
  320.1 27.1 %collective-permute-start.54 = (bf16[224,2432]{1,0:T(8,128)(2,1)}, bf16[224,2432]{1,0:T(8,128)(2,1)S(1)}, u32[]{:S(2)}, u32[]{:S(2)}) collective-permute-start(bf16[224,2432]{1,0:T(8,128)(2,1)} %get-tuple-element.304), channel_id=1, source_target_pairs={{0,8},{8,16},{16,24},{24,28},{28,20},{20,12},{12,4},{4,0},{1,9},{9... | collective-permute-start | bytes 3268616 | tf_op jit(solution)/shard_map/ppermute | solution.py:432
  321.9 26.1 %collective-permute-start.55 = (bf16[224,2432]{1,0:T(8,128)(2,1)S(1)}, bf16[224,2432]{1,0:T(8,128)(2,1)S(1)}, u32[]{:S(2)}, u32[]{:S(2)}) collective-permute-start(bf16[224,2432]{1,0:T(8,128)(2,1)S(1)} %get-tuple-element.305), channel_id=1, source_target_pairs={{0,4},{8,0},{16,8},{24,16},{28,24},{20,28},{12,20},{4,12},{1,5},{9... | collective-permute-start | bytes 3268616 | tf_op jit(solution)/shard_map/ppermute | solution.py:432
  329.1 24.7 %collective-permute-start.56 = (bf16[2,4,160,128]{3,2,1,0:T(8,128)(2,1)S(1)}, bf16[2,4,160,128]{3,2,1,0:T(8,128)(2,1)S(1)}, u32[]{:S(2)}, u32[]{:S(2)}) collective-permute-start(bf16[2,4,160,128]{3,2,1,0:T(8,128)(2,1)S(1)} %get-tuple-element.322), channel_id=1, source_target_pairs={{0,4},{4,0},{8,12},{12,8},{16,20},{20,16},{24,28},{28,24},{1,5},{5... | collective-permute-start | bytes 983048 | tf_op jit(solution)/shard_map/ppermute | solution.py:625
  370.4 28.3 %collective-permute-start.57 = (bf16[448,1024]{1,0:T(8,128)(2,1)}, bf16[448,1024]{1,0:T(8,128)(2,1)}, u32[]{:S(2)}, u32[]{:S(2)}) collective-permute-start(bf16[448,1024]{1,0:T(8,128)(2,1)} %get-tuple-element.335), channel_id=1, source_target_pairs={{0,1},{1,0},{2,3},{3,2},{4,5},{5,4},{6,7},{7,6},{8,9},{9,8},{10,11... | collective-permute-start | bytes 2752520 | tf_op jit(solution)/shard_map/ppermute | solution.py:52
  370.5 35.3 %collective-permute-start.62 = (bf16[448,1024]{1,0:T(8,128)(2,1)}, bf16[448,1024]{1,0:T(8,128)(2,1)}, u32[]{:S(2)}, u32[]{:S(2)}) collective-permute-start(bf16[448,1024]{1,0:T(8,128)(2,1)} %copy-done.38), channel_id=1, source_target_pairs={{0,1},{1,0},{2,3},{3,2},{4,5},{5,4},{6,7},{7,6},{8,9},{9,8},{10,11... | collective-permute-start | bytes 2752520 | tf_op jit(solution)/shard_map/ppermute | solution.py:52
  376.8 32.3 %collective-permute-start.64 = (bf16[224,2432]{1,0:T(8,128)(2,1)S(1)}, bf16[224,2432]{1,0:T(8,128)(2,1)S(1)}, u32[]{:S(2)}, u32[]{:S(2)}) collective-permute-start(bf16[224,2432]{1,0:T(8,128)(2,1)S(1)} %get-tuple-element.340), channel_id=1, source_target_pairs={{0,8},{8,16},{16,24},{24,28},{28,20},{20,12},{12,4},{4,0},{1,9},{9... | collective-permute-start | bytes 3268616 | tf_op jit(solution)/shard_map/ppermute | solution.py:432
  379.8 30.6 %collective-permute-start.65 = (bf16[224,2432]{1,0:T(8,128)(2,1)S(1)}, bf16[224,2432]{1,0:T(8,128)(2,1)S(1)}, u32[]{:S(2)}, u32[]{:S(2)}) collective-permute-start(bf16[224,2432]{1,0:T(8,128)(2,1)S(1)} %get-tuple-element.341), channel_id=1, source_target_pairs={{0,4},{8,0},{16,8},{24,16},{28,24},{20,28},{12,20},{4,12},{1,5},{9... | collective-permute-start | bytes 3268616 | tf_op jit(solution)/shard_map/ppermute | solution.py:432
  413.1 25.2 %collective-permute-start.70 = (bf16[2,456,512]{2,1,0:T(8,128)(2,1)S(1)}, bf16[2,456,512]{2,1,0:T(8,128)(2,1)S(1)}, u32[]{:S(2)}, u32[]{:S(2)}) collective-permute-start(bf16[2,456,512]{2,1,0:T(8,128)(2,1)S(1)} %get-tuple-element.368), channel_id=1, source_target_pairs={{0,2},{1,3},{2,0},{3,1},{4,6},{5,7},{6,4},{7,5},{8,10},{9,11},{10,... | collective-permute-start | bytes 2801672 | tf_op jit(solution)/shard_map/ppermute | solution.py:52
  424.1 30.6 %collective-permute-start.63 = (bf16[2,448,512]{2,1,0:T(8,128)(2,1)S(1)}, bf16[2,448,512]{2,1,0:T(8,128)(2,1)S(1)}, u32[]{:S(2)}, u32[]{:S(2)}) collective-permute-start(bf16[2,448,512]{2,1,0:T(8,128)(2,1)S(1)} %get-tuple-element.359), channel_id=1, source_target_pairs={{0,2},{1,3},{2,0},{3,1},{4,6},{5,7},{6,4},{7,5},{8,10},{9,11},{10,... | collective-permute-start | bytes 2752520 | tf_op jit(solution)/shard_map/ppermute | solution.py:52
  425.6 29.8 %collective-permute-start.82 = (bf16[224,1216]{1,0:T(8,128)(2,1)S(1)}, bf16[224,1216]{1,0:T(8,128)(2,1)S(1)}, u32[]{:S(2)}, u32[]{:S(2)}) collective-permute-start(bf16[224,1216]{1,0:T(8,128)(2,1)S(1)} %copy-done.42), channel_id=1, source_target_pairs={{0,8},{8,16},{16,24},{24,28},{28,20},{20,12},{12,4},{4,0},{1,9},{9... | collective-permute-start | bytes 1634312 | tf_op jit(solution)/shard_map/ppermute | solution.py:432
  435.5 23.9 %collective-permute-start.83 = (bf16[224,1216]{1,0:T(8,128)(2,1)S(1)}, bf16[224,1216]{1,0:T(8,128)(2,1)S(1)}, u32[]{:S(2)}, u32[]{:S(2)}) collective-permute-start(bf16[224,1216]{1,0:T(8,128)(2,1)S(1)} %copy-done.40), channel_id=1, source_target_pairs={{0,4},{8,0},{16,8},{24,16},{28,24},{20,28},{12,20},{4,12},{1,5},{9... | collective-permute-start | bytes 1634312 | tf_op jit(solution)/shard_map/ppermute | solution.py:432
  436.1 46.4 %collective-permute-start.80 = (bf16[224,2432]{1,0:T(8,128)(2,1)S(1)}, bf16[224,2432]{1,0:T(8,128)(2,1)S(1)}, u32[]{:S(2)}, u32[]{:S(2)}) collective-permute-start(bf16[224,2432]{1,0:T(8,128)(2,1)S(1)} %get-tuple-element.363), channel_id=1, source_target_pairs={{0,8},{8,16},{16,24},{24,28},{28,20},{20,12},{12,4},{4,0},{1,9},{9... | collective-permute-start | bytes 3268616 | tf_op jit(solution)/shard_map/ppermute | solution.py:432
  438.3 44.3 %collective-permute-start.81 = (bf16[224,2432]{1,0:T(8,128)(2,1)S(1)}, bf16[224,2432]{1,0:T(8,128)(2,1)S(1)}, u32[]{:S(2)}, u32[]{:S(2)}) collective-permute-start(bf16[224,2432]{1,0:T(8,128)(2,1)S(1)} %get-tuple-element.364), channel_id=1, source_target_pairs={{0,4},{8,0},{16,8},{24,16},{28,24},{20,28},{12,20},{4,12},{1,5},{9... | collective-permute-start | bytes 3268616 | tf_op jit(solution)/shard_map/ppermute | solution.py:432
  454.7 22.8 %collective-permute-start.76 = (bf16[224,1024]{1,0:T(8,128)(2,1)S(1)}, bf16[224,1024]{1,0:T(8,128)(2,1)S(1)}, u32[]{:S(2)}, u32[]{:S(2)}) collective-permute-start(bf16[224,1024]{1,0:T(8,128)(2,1)S(1)} %get-tuple-element.383), channel_id=1, source_target_pairs={{0,8},{8,16},{16,24},{24,28},{28,20},{20,12},{12,4},{4,0},{1,9},{9... | collective-permute-start | bytes 1376264 | tf_op jit(solution)/shard_map/ppermute | solution.py:432
  455.4 22.1 %collective-permute-start.77 = (bf16[224,1024]{1,0:T(8,128)(2,1)S(1)}, bf16[224,1024]{1,0:T(8,128)(2,1)S(1)}, u32[]{:S(2)}, u32[]{:S(2)}) collective-permute-start(bf16[224,1024]{1,0:T(8,128)(2,1)S(1)} %get-tuple-element.384), channel_id=1, source_target_pairs={{0,4},{8,0},{16,8},{24,16},{28,24},{20,28},{12,20},{4,12},{1,5},{9... | collective-permute-start | bytes 1376264 | tf_op jit(solution)/shard_map/ppermute | solution.py:432
  (122 other events, 1559.9 us)
